TPU v7x, 128 devices: a whole 4x4x4 slice. The times are simulated.
128 devices in a mesh: gz: 64 (over z, x_lo, y, core), gy: 2 (over x_hi).
Axes of the slice: x: 4 (x_hi: 2, x_lo: 2; x = x_hi * 2 + x_lo), y: 4, z: 4, core: 2. Of those that a mesh axis runs over, the one named last changes fastest.
Arguments:
- moving_image: float32 [2048, 128, 512], P('gz', 'gy'), may hold values from -6 to 6
- fixed_image: float32 [2048, 128, 512], P('gz', 'gy'), may hold values from -36 to 36
Outputs:
- solution: float32 [3, 128, 8, 32], P(None, 'gz')
- residual: float32 [3, 128, 8, 32], P(None, 'gz')
All inputs are finite; a program needn't handle non-finite values.
Results may differ from a plain program's by a relative error of at most 0.0003.
Values sent between devices are 32-bit elements; how exact they have to be, the bound alone decides.
No kernel may reach another device: no remote copies, remote signals or barrier semaphores. Data moves between devices by JAX's collectives and lax.ppermute only.
A program may use at most 192 MiB of HBM per device.

v0:
```python
import jax
import jax.numpy as jnp
from jax import lax
from jax.sharding import PartitionSpec as P

KNOT = 16
ITERS = 2


data_weight = 1.0 / 256.0
smooth_weight = 0.1


def extended_2(block, sides, width):
    for axis, dim in sides:
        count = lax.axis_size(axis)
        forward = [(i, i + 1) for i in range(count - 1)]
        backward = [(target, source) for source, target in forward]
        low = lax.ppermute(
            lax.slice_in_dim(block, block.shape[dim] - width, None, axis=dim), axis, forward
        )
        high = lax.ppermute(lax.slice_in_dim(block, 0, width, axis=dim), axis, backward)
        block = jnp.concatenate([low, block, high], axis=dim)
    return block


def passed_along(value, axis, steps):
    count = lax.axis_size(axis)
    initial, last = (max(0, -steps), min(count, count - steps))
    return lax.ppermute(value, axis, [(source, source + steps) for source in range(initial, last)])


def spline_weights(knot_len):
    t = (jnp.arange(knot_len, dtype=jnp.float32) + 0.5) / knot_len
    return jnp.stack(
        [
            (1.0 - t) ** 3 / 6.0,
            (3.0 * t**3 - 6.0 * t**2 + 4.0) / 6.0,
            (-3.0 * t**3 + 3.0 * t**2 + 3.0 * t + 1.0) / 6.0,
            t**3 / 6.0,
        ]
    )


def expand(coeffs, axis_pos, spline_table):
    turned = jnp.moveaxis(coeffs, axis_pos, -1)
    blocks = turned.shape[-1] - 3
    knot_len = spline_table.shape[1]
    summed = turned[..., 0:blocks, None] * spline_table[0]
    for j in range(1, 4):
        summed = summed + turned[..., j : j + blocks, None] * spline_table[j]
    summed = summed.reshape(turned.shape[:-1] + (blocks * knot_len,))
    return jnp.moveaxis(summed, -1, axis_pos)


def contract(spline_field, axis_pos, spline_table):
    turned = jnp.moveaxis(spline_field, axis_pos, -1)
    knot_len = spline_table.shape[1]
    blocks = turned.shape[-1] // knot_len
    pieces = turned.reshape(turned.shape[:-1] + (blocks, knot_len))
    widths = [(0, 0)] * (turned.ndim - 1)
    summed = jnp.zeros(turned.shape[:-1] + (blocks + 3,), spline_field.dtype)
    for j in range(4):
        folded = jnp.sum(pieces * spline_table[j], axis=-1)
        summed = summed + jnp.pad(folded, widths + [(j, 3 - j)])
    return jnp.moveaxis(summed, -1, axis_pos)


def central(extended, axis_pos):
    length = extended.shape[axis_pos] - 4

    def window(offset):
        return lax.slice_in_dim(extended, offset, offset + length, axis=axis_pos)

    return (8.0 * (window(3) - window(1)) - (window(4) - window(0))) / 12.0


def rim_pad(field_in, axis_pos):
    widths = [(0, 0)] * field_in.ndim
    widths[axis_pos] = (2, 2)
    return jnp.pad(field_in, widths)


def squares(residual):
    return lax.psum(jnp.sum(residual * residual), "gz")


def local(moving_image, fixed_image):
    spline_table = spline_weights(KNOT)
    z_blocks = moving_image.shape[0] // KNOT
    y_blocks = moving_image.shape[1] // KNOT
    ctl_x = moving_image.shape[2] // KNOT
    ctl_y = y_blocks * lax.axis_size("gy")
    row_block = lax.axis_index("gy") * y_blocks
    planes = extended_2(moving_image, (("gz", 0),), 2)
    along_z = central(planes, 0)
    row_halo = extended_2(moving_image, (("gy", 1),), 2)
    along_y = central(row_halo, 1)
    along_x = central(rim_pad(moving_image, 2), 2)
    gradient = jnp.stack([along_z, along_y, along_x])

    def adjoint(weighted):
        returned = contract(weighted, 3, spline_table)[..., 1 : ctl_x + 1]
        returned = contract(contract(returned, 2, spline_table), 1, spline_table)
        placed = jnp.zeros((3, z_blocks + 3, ctl_y + 3, ctl_x), jnp.float32)
        placed = lax.dynamic_update_slice_in_dim(placed, returned, row_block, 2)[
            :, :, 1 : ctl_y + 1
        ]
        summed = lax.psum(placed, "gy")
        from_above = passed_along(summed[:, :1], "gz", -1)
        from_below = passed_along(summed[:, -2:], "gz", 1)
        owned = summed[:, 1:-2]
        owned = owned + from_below
        return owned + jnp.pad(from_above, ((0, 0), (z_blocks - 1, 0), (0, 0), (0, 0)))

    right_side = -data_weight * adjoint(gradient * (moving_image - fixed_image)[None])
    solution = jnp.zeros_like(right_side)
    residual = right_side
    direction = right_side
    norm_now = squares(residual)
    for iteration in range(ITERS):
        lower_rim = passed_along(direction[:, -1:], "gz", 1)
        upper_rim = passed_along(direction, "gz", -1)
        z_padded = jnp.concatenate([lower_rim, direction, upper_rim], 1)
        padded = jnp.pad(z_padded, ((0, 0), (0, 0), (1, 2), (1, 2)))
        pieces = lax.dynamic_slice_in_dim(padded, row_block, y_blocks + 3, 2)
        spline_field = expand(
            expand(expand(pieces, 1, spline_table), 2, spline_table), 3, spline_table
        )
        weights = jnp.sum(gradient * spline_field, 0)
        data_term = adjoint(gradient * weights[None])
        side_pad = jnp.pad(direction, ((0, 0), (0, 0), (1, 1), (1, 1)))
        neighbours = z_padded[:, :-3] + z_padded[:, 2:-1]
        neighbours = neighbours + side_pad[:, :, :-2, 1:-1] + side_pad[:, :, 2:, 1:-1]
        neighbours = neighbours + side_pad[:, :, 1:-1, :-2] + side_pad[:, :, 1:-1, 2:]
        image_vec = data_weight * data_term + smooth_weight * (6.0 * direction - neighbours)
        step_size = norm_now / lax.psum(jnp.sum(direction * image_vec), "gz")
        solution = solution + step_size * direction
        residual = residual - step_size * image_vec
        norm_next = squares(residual)
        direction = residual + norm_next / norm_now * direction
        norm_now = norm_next
    return (solution, residual)


def solution(mesh):
    in_specs = (P("gz", "gy", None), P("gz", "gy", None))
    out_specs = (P(None, "gz", None, None), P(None, "gz", None, None))
    return jax.shard_map(local, mesh=mesh, in_specs=in_specs, out_specs=out_specs, check_vma=False)
```

profile of v0, /device:TPU:0, one launch (start us, length us, event | category | flops | bytes accessed | tf_op | source)
XLA Modules:
  0.0 865.0 jit_solution(11955002290748199332)
XLA Ops:
  0.6 6.9 copy.112
  15.8 6.1 collective-permute-start.3
  21.9 6.7 sub.121
  28.7 6.9 copy.122
  35.6 4.6 copy.117
  40.2 4.6 copy.119
  44.8 68.7 %fusion.4 = (f32[32,64,512]{1,2,0:T(8,128)}, f32[32,64,512]{1,2,0:T(8,128)}, f32[32,64,512]{1,2,0:T(8,128)}) fusion(f32[2,64,512]{1,2,0:T(8,128)S(1)} %collective-permute-done.1, f32[32,64,512]{1,2,0:T(8,128)} %copy.112, f32[2,64,512]{1,2,0:T(8,128)S(1)} %collective-permute-done, f32[32,2,512]{1,2,0:T(8,128)} %copy.119, f32[32,2,512]{1,2,0:T(8,128)} %copy.117), kind=kLoop, calls=%fused_computation.23 | loop fusion | flops 24117248 | bytes 17563648 | tf_op jit(solution)/shard_map/div | solution.py:75
  113.5 49.6 %multiply_reduce_fusion.13 = (f32[3,32,64,32]{2,3,1,0:T(8,128)S(1)}, f32[3,32,64,32]{2,3,1,0:T(8,128)S(1)}, f32[3,32,64,32]{2,3,1,0:T(8,128)S(1)}, f32[3,32,64,32]{2,3,1,0:T(8,128)S(1)}) fusion(f32[16]{0:T(128)S(1)} %get-tuple-element.80, f32[32,64,32,16]{1,3,2,0:T(8,128)} %bitcast.115, f32[1,32,64,32,16]{2,4,3,1,0:T(8,128)} %bitcast.103, ...), kind=kLoop, calls=%fused_computation.14 | loop fusion | flops 33816576 | bytes 19923200 | tf_op jit(solution)/shard_map/reduce_sum | solution.py:64
  171.7 9.2 %psum.49 = f32[3,5,8,32]{3,2,1,0:T(8,128)S(1)} all-reduce(f32[3,5,8,32]{3,2,1,0:T(8,128)S(1)} %slice.298), channel_id=1, replica_groups=mesh['gz'=64,'gy'=2] {'gy'}, use_global_device_ids=true, to_apply=%region_12.13 | all-reduce | flops 3840 | bytes 30720 | tf_op jit(solution)/shard_map/psum | solution.py:109
  188.4 5.0 collective-permute-start.6
  195.7 6.1 fusion.74
  201.8 3.7 copy.124
  214.0 19.9 %multiply_reduce_fusion.9 = f32[32,64,32,16]{1,3,2,0:T(8,128)} fusion(f32[3,32,64,32]{2,3,1,0:T(8,128)} %copy.127, f32[3,32,64,32]{2,3,1,0:T(8,128)} %copy.126, f32[3,32,64,32]{2,3,1,0:T(8,128)} %copy.125, f32[3,32,64,32]{2,3,1,0:T(8,128)} %copy.124, f32[16]{0:T(128)S(1)} %get-tuple-element.83, f32[16]{0:T(128)S(1)} %get-tuple-element.81, ...), kind=kLoop, calls=%fused_computation.10 | loop fusion | flops 33554432 | bytes 19923200 | tf_op jit(solution)/shard_map/reduce_sum | solution.py:130
  233.8 49.6 %multiply_reduce_fusion.8 = (f32[3,32,64,32]{2,3,1,0:T(8,128)S(1)}, f32[3,32,64,32]{2,3,1,0:T(8,128)S(1)}, f32[3,32,64,32]{2,3,1,0:T(8,128)S(1)}, f32[3,32,64,32]{2,3,1,0:T(8,128)S(1)}) fusion(f32[32,64,32,16]{1,3,2,0:T(8,128)} %multiply_reduce_fusion.9, f32[16]{0:T(128)S(1)} %get-tuple-element.80, f32[1,32,64,32,16]{2,4,3,1,0:T(8,128)} %bitcast.105, ...), kind=kLoop, calls=%fused_computation.9 | loop fusion | flops 33816576 | bytes 19923200 | tf_op jit(solution)/shard_map/reduce_sum | solution.py:64
  291.9 12.3 %psum.51 = f32[3,5,8,32]{3,2,1,0:T(8,128)S(1)} all-reduce(f32[3,5,8,32]{3,2,1,0:T(8,128)S(1)} %slice.315), channel_id=1, replica_groups=mesh['gz'=64,'gy'=2] {'gy'}, use_global_device_ids=true, to_apply=%region_28.29 | all-reduce | flops 3840 | bytes 30720 | tf_op jit(solution)/shard_map/psum | solution.py:109
  307.4 5.1 collective-permute-done.9
  313.3 145.0 %all-reduce.44 = (f32[]{:T(128)}, f32[]{:T(128)}) all-reduce(f32[]{:T(128)} %get-tuple-element.39, f32[]{:T(128)} %get-tuple-element.38), channel_id=1, replica_groups=mesh['gz'=64,'gy'=2] {'gz'}, use_global_device_ids=true, to_apply=%region_14.15 | all-reduce | flops 2 | bytes 16 | tf_op jit(solution)/shard_map/psum | solution.py:85
  460.2 139.1 %psum.53 = f32[]{:T(128)} all-reduce(f32[]{:T(128)} %multiply_reduce_fusion.39), channel_id=1, replica_groups=mesh['gz'=64,'gy'=2] {'gz'}, use_global_device_ids=true, to_apply=%region_32.33 | all-reduce | flops 1 | bytes 8 | tf_op jit(solution)/shard_map/psum | solution.py:85
  607.2 6.1 fusion.73
  625.3 19.9 %multiply_reduce_fusion.4 = f32[32,64,32,16]{1,3,2,0:T(8,128)} fusion(f32[3,32,64,32]{2,3,1,0:T(8,128)} %copy.132, f32[3,32,64,32]{2,3,1,0:T(8,128)} %copy.131, f32[3,32,64,32]{2,3,1,0:T(8,128)} %copy.130, f32[3,32,64,32]{2,3,1,0:T(8,128)} %copy.129, f32[16]{0:T(128)S(1)} %get-tuple-element.83, f32[16]{0:T(128)S(1)} %get-tuple-element.81, ...), kind=kLoop, calls=%fused_computation.5 | loop fusion | flops 33554432 | bytes 19923200 | tf_op jit(solution)/shard_map/reduce_sum | solution.py:130
  645.2 49.7 %multiply_reduce_fusion.3 = (f32[3,32,64,32]{2,3,1,0:T(8,128)S(1)}, f32[3,32,64,32]{2,3,1,0:T(8,128)S(1)}, f32[3,32,64,32]{2,3,1,0:T(8,128)S(1)}, f32[3,32,64,32]{2,3,1,0:T(8,128)S(1)}) fusion(f32[32,64,32,16]{1,3,2,0:T(8,128)} %multiply_reduce_fusion.4, f32[16]{0:T(128)S(1)} %get-tuple-element.80, f32[1,32,64,32,16]{2,4,3,1,0:T(8,128)} %bitcast.107, ...), kind=kLoop, calls=%fused_computation.4 | loop fusion | flops 33816576 | bytes 19923200 | tf_op jit(solution)/shard_map/reduce_sum | solution.py:64
  703.2 9.7 %psum.54 = f32[3,5,8,32]{3,2,1,0:T(8,128)S(1)} all-reduce(f32[3,5,8,32]{3,2,1,0:T(8,128)S(1)} %slice.332), channel_id=1, replica_groups=mesh['gz'=64,'gy'=2] {'gy'}, use_global_device_ids=true, to_apply=%region_46.47 | all-reduce | flops 3840 | bytes 30720 | tf_op jit(solution)/shard_map/psum | solution.py:109
  715.5 5.1 collective-permute-done.13
  721.3 141.5 %psum.55 = f32[]{:T(128)} all-reduce(f32[]{:T(128)} %get-tuple-element.42), channel_id=1, replica_groups=mesh['gz'=64,'gy'=2] {'gz'}, use_global_device_ids=true, to_apply=%region_48.49 | all-reduce | flops 1 | bytes 8 | tf_op jit(solution)/shard_map/psum | solution.py:137
  (113 shorter events, 78.6 us)
Async XLA Ops:
  8.8 36.0 %collective-permute-start = (f32[2,64,512]{1,2,0:T(8,128)S(1)}, f32[2,64,512]{1,2,0:T(8,128)S(1)}, u32[]{:S(2)}, u32[]{:S(2)}) collective-permute-start(f32[2,64,512]{1,2,0:T(8,128)S(1)} %get-tuple-element.50), channel_id=1, source_target_pairs={{2,0},{4,2},{6,4},{8,6},{10,8},{12,10},{14,12},{16,14},{18,16},{20... | collective-permute-start | bytes 786440 | tf_op jit(solution)/shard_map/ppermute | solution.py:22
  10.1 34.7 %collective-permute-start.1 = (f32[2,64,512]{1,2,0:T(8,128)S(1)}, f32[2,64,512]{1,2,0:T(8,128)S(1)}, u32[]{:S(2)}, u32[]{:S(2)}) collective-permute-start(f32[2,64,512]{1,2,0:T(8,128)S(1)} %get-tuple-element.51), channel_id=1, source_target_pairs={{0,2},{2,4},{4,6},{6,8},{8,10},{10,12},{12,14},{14,16},{16,18},{18... | collective-permute-start | bytes 786440 | tf_op jit(solution)/shard_map/ppermute | solution.py:19
  14.5 21.0 %collective-permute-start.2 = (f32[32,2,512]{2,0,1:T(8,128)S(1)}, f32[32,2,512]{2,0,1:T(8,128)S(1)}, u32[]{:S(2)}, u32[]{:S(2)}) collective-permute-start(f32[32,2,512]{2,0,1:T(8,128)S(1)} %copy.134), channel_id=1, source_target_pairs={{1,0},{3,2},{5,4},{7,6},{9,8},{11,10},{13,12},{15,14},{17,16},{19,... | collective-permute-start | bytes 393224 | tf_op jit(solution)/shard_map/ppermute | solution.py:22
  15.8 24.4 %collective-permute-start.3 = (f32[32,2,512]{2,0,1:T(8,128)S(1)}, f32[32,2,512]{2,0,1:T(8,128)S(1)}, u32[]{:S(2)}, u32[]{:S(2)}) collective-permute-start(f32[32,2,512]{2,0,1:T(8,128)S(1)} %copy.135), channel_id=1, source_target_pairs={{0,1},{2,3},{4,5},{6,7},{8,9},{10,11},{12,13},{14,15},{16,17},{18,... | collective-permute-start | bytes 393224 | tf_op jit(solution)/shard_map/ppermute | solution.py:19
  180.9 6.2 collective-permute-start.4
  182.2 4.9 collective-permute-start.5
  187.1 7.1 collective-permute-start.7
  188.4 5.8 collective-permute-start.6
  304.2 8.4 collective-permute-start.8
  306.1 6.4 collective-permute-start.9
  600.6 5.2 collective-permute-start.11
  601.9 3.9 collective-permute-start.10
  712.9 7.7 collective-permute-start.12
  714.2 6.4 collective-permute-start.13
where the time goes:
time: 871 us; the launch traced here: 865 us
  blocking collectives  457 us (52%)
  other arithmetic  287 us (33%)
  local copies, waits for them, and re-layouts  70.4 us (8%)
  starting transfers between devices  30.7 us (4%)
  waiting for transfers between devices  14.7 us (2%)
    psum x2, blocking collectives, squares(): return lax.psum(jnp.sum(residual * residual), 'gz')  284 us
    reduce_sum x9, other arithmetic, contract(): folded = jnp.sum(pieces * spline_table[j], axis=-1)  160 us
    psum x1, blocking collectives, local(): step_size = norm_now / lax.psum(jnp.sum(direction * image_vec), 'gz')  141 us
    div x1, other arithmetic, central(): return (8.0 * (window(3) - window(1)) - (window(4) - window(0))) / 12.0  68.7 us
    reduce_sum x2, other arithmetic, local(): weights = jnp.sum(gradient * spline_field, 0)  39.8 us
    psum x3, blocking collectives, adjoint(): summed = lax.psum(placed, 'gy')  31.2 us
    slice x8, local copies, waits for them, and re-layouts, expand(): summed = turned[..., 0:blocks, None] * spline_table[0]  19.6 us
    ppermute x10, starting transfers between devices, passed_along(): lax.ppermute(value, axis, [(source, source + steps) for source in range(i...  19 us
  transfers between devices with their start and end apart: 14, of which 5 were waited for; matrix products, arithmetic and copies ran while one was open for 3% of the time, Pallas kernels for 0%

commit v1 on v0

v1 whole, which is shorter than its diff:
```python
import functools

import jax
import jax.numpy as jnp
import ml_dtypes
import numpy as np
from jax import lax
from jax.experimental import pallas as pl
from jax.experimental.pallas import tpu as pltpu
from jax.sharding import PartitionSpec as P

KNOT = 16
data_weight = 1.0 / 256.0
smooth_weight = 0.1

BF = jnp.bfloat16
F32 = jnp.float32
NZ, NY, NX = 32, 64, 512
CHUNK = 8
STEPS = NZ // CHUNK
ROWS = CHUNK * NY
PLANES, CY, CX = 5, 8, 32
CTL = PLANES * CY
KPAD = 48


def split(array):
    high = array.astype(ml_dtypes.bfloat16)
    low = (array - high.astype(np.float64)).astype(ml_dtypes.bfloat16)
    return high, low


def tables():
    t = (np.arange(KNOT) + 0.5) / KNOT
    weights = np.stack(
        [
            (1 - t) ** 3 / 6,
            (3 * t**3 - 6 * t**2 + 4) / 6,
            (-3 * t**3 + 3 * t**2 + 3 * t + 1) / 6,
            t**3 / 6,
        ]
    )

    def along(blocks, first_block, points, first_point):
        out = np.zeros((blocks * KNOT, points))
        for block in range(blocks):
            for j in range(4):
                point = first_block + block + j - 1 - first_point
                if 0 <= point < points:
                    out[block * KNOT : (block + 1) * KNOT, point] = weights[j]
        return out

    along_z = along(NZ // KNOT, 0, PLANES, -1)
    halves = []
    for half in range(2):
        along_y = along(NY // KNOT, half * (NY // KNOT), CY, 0)
        halves.append(np.einsum("zp,yq->zypq", along_z, along_y).reshape(NZ * NY, CTL))
    high, low = split(np.stack(halves))
    widths = ((0, 0), (0, 0), (0, KPAD - CTL))
    high48, low48 = (np.pad(a, widths) for a in (high, low))
    out_table = np.concatenate([high48, low48, high48, low48], axis=2)
    back_table = np.concatenate([high, low], axis=2).transpose(0, 2, 1)
    along_x = along(NX // KNOT, 0, CX, 0)
    rows = np.zeros((128, 3 * NX))
    for c in range(3):
        rows[c * CX : (c + 1) * CX, c * NX : (c + 1) * NX] = along_x.T
    x_table = np.concatenate(split(rows), axis=0)
    return out_table, np.ascontiguousarray(back_table), x_table


def halves_of(value):
    high = value.astype(BF)
    return high, (value - high.astype(F32)).astype(BF)


def contracted(parts, back_ref, x_ref):
    both = lax.dot_general(
        parts[...], x_ref[...], (((1,), (1,)), ((), ())), preferred_element_type=F32
    )
    rows = both[:ROWS, :128] + (both[:ROWS, 128:] + both[ROWS:, :128])
    high, low = halves_of(rows)
    back = back_ref[0]
    terms = jnp.dot(back, high, preferred_element_type=F32)
    rest = jnp.dot(back[:CTL], low, preferred_element_type=F32)
    return terms[:CTL] + (terms[CTL:] + rest)


def put_parts(parts, z, c, value):
    high, low = halves_of(value)
    at = pl.multiple_of(z * NY, NY)
    parts[pl.ds(at, NY), c * NX : (c + 1) * NX] = high
    parts[pl.ds(ROWS + at, NY), c * NX : (c + 1) * NX] = low


def first_kernel(
    half, moving, z_low, z_high, fixed, y_rows, back, xt, grad, out, padded, parts, sems
):
    step = pl.program_id(0)

    def chunk_copy(j):
        return pltpu.make_async_copy(
            moving.at[pl.ds(j * CHUNK, CHUNK)],
            padded.at[pl.ds(2 + j * CHUNK, CHUNK), pl.ds(8, NY)],
            sems.at[j],
        )

    def low_copy():
        return pltpu.make_async_copy(
            z_low, padded.at[pl.ds(0, 2), pl.ds(8, NY)], sems.at[STEPS]
        )

    def high_copy():
        return pltpu.make_async_copy(
            z_high, padded.at[pl.ds(2 + NZ, 2), pl.ds(8, NY)], sems.at[STEPS + 1]
        )

    @pl.when(step == 0)
    def _():
        low_copy().start()
        for j in range(STEPS):
            chunk_copy(j).start()
        high_copy().start()
        low_copy().wait()
        chunk_copy(0).wait()
        out[...] = jnp.zeros_like(out)

    for j in range(1, STEPS):

        @pl.when(step == j - 1)
        def _(j=j):
            chunk_copy(j).wait()

    @pl.when(step == STEPS - 1)
    def _():
        high_copy().wait()

    upper = half[0] == 0
    lane = lax.broadcasted_iota(jnp.int32, (NY, NX), 1)

    def plane(z, carry):
        at = 2 + step * CHUNK + z
        rows = y_rows[z]
        blank = jnp.zeros_like(rows)
        padded[at, 6:8, :] = jnp.where(upper, blank, rows)
        padded[at, 72:74, :] = jnp.where(upper, rows, blank)
        center = padded[at, 8:72, :]

        def at_z(k):
            return padded[at + k, 8:72, :]

        def at_y(k):
            return padded[at, 8 + k : 72 + k, :]

        def at_x(k):
            moved = pltpu.roll(center, (-k) % NX, 1)
            inside = lane < NX - k if k > 0 else lane >= -k
            return jnp.where(inside, moved, 0.0)

        difference = center - fixed[z]
        for c, near in enumerate((at_z, at_y, at_x)):
            slope = 8.0 * (near(1) - near(-1)) - (near(2) - near(-2))
            grad[c, z] = slope
            put_parts(parts, z, c, slope * difference)
        return carry

    lax.fori_loop(0, CHUNK, plane, 0)
    out[...] += contracted(parts, back, xt)

    @pl.when(step == STEPS - 1)
    def _():
        out[...] = out[...] * (-data_weight / 12.0)


def hessian_kernel(
    half, ctl, base, grad, front, back, xt, out, sums, spread, field, parts, square
):
    step = pl.program_id(0)

    @pl.when(step == 0)
    def _():
        high, low = halves_of(ctl[...])
        first, second = xt[:128], xt[128:]
        value = jnp.dot(high, first, preferred_element_type=F32)
        value += jnp.dot(low, first, preferred_element_type=F32)
        value += jnp.dot(high, second, preferred_element_type=F32)
        value = jnp.concatenate([value, jnp.zeros((KPAD - CTL, 3 * NX), F32)], 0)
        high, low = halves_of(value)
        for j, part in enumerate((high, high, low, low)):
            spread[j * KPAD : (j + 1) * KPAD] = part
        out[...] = jnp.zeros_like(out)
        square[...] = jnp.zeros_like(square)

    field[...] = jnp.dot(front[0], spread[...], preferred_element_type=F32)

    def plane(z, carry):
        at = pl.multiple_of(z * NY, NY)
        rows = pl.ds(at, NY)
        slopes = [grad[c, z] for c in range(3)]
        weight = slopes[0] * field[rows, 0:NX]
        weight += slopes[1] * field[rows, NX : 2 * NX]
        weight += slopes[2] * field[rows, 2 * NX : 3 * NX]
        squared = weight * weight
        square[...] += jnp.sum(squared.reshape(NY // 8, 8, NX), axis=0)
        for c in range(3):
            put_parts(parts, z, c, slopes[c] * weight)
        return carry

    lax.fori_loop(0, CHUNK, plane, 0)
    out[...] += contracted(parts, back, xt)

    @pl.when(step == STEPS - 1)
    def _():
        scale = data_weight / 144.0
        whole = ctl[...]
        owned = whole[CY : 3 * CY]
        sub = lax.broadcasted_iota(jnp.int32, (2 * CY, 128), 0) % CY
        lane = lax.broadcasted_iota(jnp.int32, (2 * CY, 128), 1) % CX
        near = whole[0 : 2 * CY] + whole[2 * CY : 4 * CY]
        near += jnp.where(sub > 0, pltpu.roll(owned, 1, 0), 0.0)
        near += jnp.where(sub < CY - 1, pltpu.roll(owned, 2 * CY - 1, 0), 0.0)
        near += jnp.where(lane > 0, pltpu.roll(owned, 1, 1), 0.0)
        near += jnp.where(lane < CX - 1, pltpu.roll(owned, 127, 1), 0.0)
        smooth = (0.5 * smooth_weight) * (6.0 * owned - near)
        out[...] = out[...] * scale
        out[CY : 3 * CY] += smooth
        first = base[...]

        def total(value):
            return jnp.sum(jnp.sum(value, axis=0, keepdims=True), axis=1, keepdims=True)

        whole_square = total(square[...]) * scale + total(smooth * owned)
        lines = [
            0.5 * total(first * first),
            0.5 * total(first * owned),
            0.5 * total(owned * owned),
            whole_square,
        ]
        which = lax.broadcasted_iota(jnp.int32, (8, 128), 0)
        tile = jnp.zeros((8, 128), F32)
        for j, line in enumerate(lines):
            tile = jnp.where(which == j, line, tile)
        sums[...] = tile


def vmem_params():
    return pltpu.CompilerParams(
        dimension_semantics=("arbitrary",), vmem_limit_bytes=48 * 1024 * 1024
    )


def whole_spec(shape):
    return pl.BlockSpec(shape, lambda i, h: (0,) * len(shape))


BACK_SPEC = ((1, 2 * CTL, ROWS), lambda i, h: (h[0], 0, i))
GRAD_SPEC = ((3, CHUNK, NY, NX), lambda i, h: (0, i, 0, 0))


def first_pass(half, moving, z_low, z_high, fixed, y_rows, back_table, x_table):
    return pl.pallas_call(
        first_kernel,
        grid_spec=pltpu.PrefetchScalarGridSpec(
            num_scalar_prefetch=1,
            grid=(STEPS,),
            in_specs=[
                pl.BlockSpec(memory_space=pl.ANY),
                pl.BlockSpec(memory_space=pl.ANY),
                pl.BlockSpec(memory_space=pl.ANY),
                pl.BlockSpec((CHUNK, NY, NX), lambda i, h: (i, 0, 0)),
                pl.BlockSpec((CHUNK, 2, NX), lambda i, h: (i, 0, 0)),
                pl.BlockSpec(*BACK_SPEC),
                whole_spec((256, 3 * NX)),
            ],
            out_specs=[pl.BlockSpec(*GRAD_SPEC), whole_spec((CTL, 128))],
            scratch_shapes=[
                pltpu.VMEM((NZ + 4, NY + 16, NX), F32),
                pltpu.VMEM((2 * ROWS, 3 * NX), BF),
                pltpu.SemaphoreType.DMA((STEPS + 2,)),
            ],
        ),
        out_shape=[
            jax.ShapeDtypeStruct((3, NZ, NY, NX), F32),
            jax.ShapeDtypeStruct((CTL, 128), F32),
        ],
        compiler_params=vmem_params(),
        name="first",
    )(half, moving, z_low, z_high, fixed, y_rows, back_table, x_table)


def hessian_pass(half, ctl, base, grad, front_table, back_table, x_table):
    return pl.pallas_call(
        hessian_kernel,
        grid_spec=pltpu.PrefetchScalarGridSpec(
            num_scalar_prefetch=1,
            grid=(STEPS,),
            in_specs=[
                whole_spec((CTL, 128)),
                whole_spec((2 * CY, 128)),
                pl.BlockSpec(*GRAD_SPEC),
                pl.BlockSpec((1, ROWS, 4 * KPAD), lambda i, h: (h[0], i, 0)),
                pl.BlockSpec(*BACK_SPEC),
                whole_spec((256, 3 * NX)),
            ],
            out_specs=[whole_spec((CTL, 128)), whole_spec((8, 128))],
            scratch_shapes=[
                pltpu.VMEM((4 * KPAD, 3 * NX), BF),
                pltpu.VMEM((ROWS, 3 * NX), F32),
                pltpu.VMEM((2 * ROWS, 3 * NX), BF),
                pltpu.VMEM((8, NX), F32),
            ],
        ),
        out_shape=[
            jax.ShapeDtypeStruct((CTL, 128), F32),
            jax.ShapeDtypeStruct((8, 128), F32),
        ],
        compiler_params=vmem_params(),
        name="hessian",
    )(half, ctl, base, grad, front_table, back_table, x_table)


def passed_along(value, axis, steps):
    count = lax.axis_size(axis)
    initial, last = (max(0, -steps), min(count, count - steps))
    return lax.ppermute(value, axis, [(source, source + steps) for source in range(initial, last)])


def swapped(value):
    return lax.ppermute(value, "gy", [(0, 1), (1, 0)])


def owned_sum(whole):
    from_above = passed_along(whole[:CY], "gz", -1)
    from_below = passed_along(whole[3 * CY :], "gz", 1)
    owned = whole[CY : 3 * CY] + from_below
    return owned + jnp.pad(from_above, ((CY, 0), (0, 0)))


def with_rims(owned):
    lower = passed_along(owned[CY:], "gz", 1)
    upper = passed_along(owned, "gz", -1)
    return jnp.concatenate([lower, owned, upper], 0)


def local(moving, fixed):
    half_id = lax.axis_index("gy").astype(jnp.int32)
    half = half_id.reshape(1)
    front, back, xt = (jnp.asarray(a) for a in tables())

    z_low = passed_along(moving[-2:], "gz", 1)
    z_high = passed_along(moving[:2], "gz", -1)
    y_rows = swapped(jnp.where(half_id == 0, moving[:, -2:], moving[:, :2]))

    grad, part = first_pass(half, moving, z_low, z_high, fixed, y_rows, back, xt)
    b = owned_sum(part + swapped(part))
    part, _ = hessian_pass(half, with_rims(b), b, grad, front, back, xt)
    u = owned_sum(part + swapped(part))
    part, sums = hessian_pass(half, with_rims(u), b, grad, front, back, xt)
    both = jnp.concatenate([part, sums], 0)
    both = both + swapped(both)
    v = owned_sum(both[:CTL])
    sums = both[CTL:]
    for mask in (1, 2, 6, 8, 16, 48):
        sums = sums + lax.ppermute(sums, "gz", [(i, i ^ mask) for i in range(64)])

    bb, bu, uu, uv = (sums[j : j + 1] for j in range(4))
    a0 = bb / bu
    rr1 = bb - 2.0 * a0 * bu + a0 * a0 * uu
    beta = rr1 / bb
    more = 1.0 + beta
    a1 = rr1 / (more * more * bu - 2.0 * more * a0 * uu + a0 * a0 * uv)
    solution = a0 * b + a1 * (more * b - a0 * u)
    residual = (b - a0 * u) - a1 * (more * u - a0 * v)

    def placed(value):
        turned = value.reshape(2, CY, 128)[:, :, : 3 * CX].reshape(2, CY, 3, CX)
        return turned.transpose(2, 0, 1, 3)

    return placed(solution), placed(residual)


def solution(mesh):
    in_specs = (P("gz", "gy", None), P("gz", "gy", None))
    out_specs = (P(None, "gz", None, None), P(None, "gz", None, None))
    return jax.shard_map(local, mesh=mesh, in_specs=in_specs, out_specs=out_specs, check_vma=False)
```

time: 871 us -> 166 us (0.19)
  the two profiles are of different devices: /device:TPU:0 before, /device:TPU:27 now
where the time goes in v1:
time: 166 us
  starting transfers between devices  67.9 us (41%)
  Pallas kernels  48 us (29%)
  waiting for transfers between devices  43 us (26%)
  local copies, waits for them, and re-layouts  4.71 us (3%)
    ppermute x12, starting transfers between devices, passed_along(): lax.ppermute(value, axis, [(source, source + steps) for source in range(i...  55 us
    pallas_call x2, Pallas kernels, hessian_pass(): pl.pallas_call(hessian_kernel, grid_spec=pltpu.PrefetchScalarGridSpec(num...  27.4 us
    pallas_call x1, Pallas kernels, first_pass(): pl.pallas_call(first_kernel, grid_spec=pltpu.PrefetchScalarGridSpec(num_s...  20.6 us
    ppermute x12, waiting for transfers between devices, passed_along(): lax.ppermute(value, axis, [(source, source + steps) for source in range(i...  19.4 us
    ppermute x4, waiting for transfers between devices, swapped(): return lax.ppermute(value, 'gy', [(0, 1), (1, 0)])  12.8 us
    ppermute x6, waiting for transfers between devices, local(): sums = sums + lax.ppermute(sums, 'gz', [(i, i ^ mask) for i in range(64)])  10.7 us
    ppermute x6, starting transfers between devices, local(): sums = sums + lax.ppermute(sums, 'gz', [(i, i ^ mask) for i in range(64)])  6.59 us
    ppermute x4, starting transfers between devices, swapped(): return lax.ppermute(value, 'gy', [(0, 1), (1, 0)])  6.34 us
  transfers between devices with their start and end apart: 22, of which 14 were waited for; matrix products, arithmetic and copies ran while one was open for 1% of the time, Pallas kernels for 0%

profile of v1, /device:TPU:27, one launch (start us, length us, event | category | flops | bytes accessed | tf_op | source)
XLA Modules:
  0.0 165.8 jit_solution(2594506117603061228)
XLA Ops:
  1.7 2.6 %collective-permute-start.1 = (f32[2,64,512]{2,1,0:T(8,128)S(1)}, f32[2,64,512]{2,1,0:T(8,128)S(1)}, u32[]{:S(2)}, u32[]{:S(2)}) collective-permute-start(f32[2,64,512]{2,1,0:T(8,128)S(1)} %get-tuple-element.18), channel_id=1, source_target_pairs={{2,0},{4,2},{6,4},{8,6},{10,8},{12,10},{14,12},{16,14},{18,16},{20... | collective-permute-start | bytes 786440 | tf_op jit(solution)/shard_map/ppermute | solution.py:324
  4.3 6.0 %collective-permute-start = (f32[2,64,512]{2,1,0:T(8,128)S(1)}, f32[2,64,512]{2,1,0:T(8,128)S(1)}, u32[]{:S(2)}, u32[]{:S(2)}) collective-permute-start(f32[2,64,512]{2,1,0:T(8,128)S(1)} %get-tuple-element.19), channel_id=1, source_target_pairs={{0,2},{2,4},{4,6},{6,8},{8,10},{10,12},{12,14},{14,16},{16,18},{18... | collective-permute-start | bytes 786440 | tf_op jit(solution)/shard_map/ppermute | solution.py:324
  11.6 1.9 %collective-permute-start.2 = (f32[32,2,512]{2,1,0:T(2,128)S(1)}, f32[32,2,512]{2,1,0:T(2,128)S(1)}, u32[]{:S(2)}, u32[]{:S(2)}) collective-permute-start(f32[32,2,512]{2,1,0:T(2,128)S(1)} %slice_select_fusion), channel_id=1, source_target_pairs={{0,1},{1,0},{2,3},{3,2},{4,5},{5,4},{6,7},{7,6},{8,9},{9,8},{10,11... | collective-permute-start | bytes 393224 | tf_op jit(solution)/shard_map/ppermute | solution.py:328
  13.5 4.6 %collective-permute-done.2.y_rows = f32[32,2,512]{2,1,0:T(2,128)S(1)} collective-permute-done((f32[32,2,512]{2,1,0:T(2,128)S(1)}, f32[32,2,512]{2,1,0:T(2,128)S(1)}, u32[]{:S(2)}, u32[]{:S(2)}) %collective-permute-start.2) | collective-permute-done | bytes 131104 | tf_op jit(solution)/shard_map/ppermute | solution.py:328
  20.3 20.6 %first.1 = (f32[3,32,64,512]{3,2,1,0:T(8,128)}, f32[40,128]{1,0:T(8,128)S(1)}) custom-call(s32[1]{0:T(128)} %bitcast.half, f32[32,64,512]{2,1,0:T(8,128)} %moving.1, f32[2,64,512]{2,1,0:T(8,128)S(1)} %collective-permute-done.z_low, f32[2,64,512]{2,1,0:T(8,128)S(1)} %collective-permute-done.1.z_high, f32[32,64,512]{2,1,0:T(8,128)} %fixed.1, ...), custom_call_target="tpu_custom_call" | custom-call | tf_op jit(solution)/shard_map/first/pallas_call | solution.py:260
  42.8 2.4 %collective-permute-done.3 = f32[40,128]{1,0:T(8,128)S(1)} collective-permute-done((f32[40,128]{1,0:T(8,128)S(1)}, f32[40,128]{1,0:T(8,128)S(1)}, u32[]{:S(2)}, u32[]{:S(2)}) %collective-permute-start.3) | collective-permute-done | bytes 20512 | tf_op jit(solution)/shard_map/ppermute | solution.py:328
  45.2 5.4 %collective-permute-start.4 = (f32[16,128]{1,0:T(8,128)S(1)}, f32[16,128]{1,0:T(8,128)S(1)}, u32[]{:S(2)}, u32[]{:S(2)}) collective-permute-start(f32[16,128]{1,0:T(8,128)S(1)} %slice.93), channel_id=1, source_target_pairs={{0,2},{2,4},{4,6},{6,8},{8,10},{10,12},{12,14},{14,16},{16,18},{18... | collective-permute-start | bytes 24584 | tf_op jit(solution)/shard_map/ppermute | solution.py:324
  52.6 6.0 %collective-permute-done.5 = f32[8,128]{1,0:T(8,128)S(1)} collective-permute-done((f32[8,128]{1,0:T(8,128)S(1)}, f32[8,128]{1,0:T(8,128)S(1)}, u32[]{:S(2)}, u32[]{:S(2)}) %collective-permute-start.5) | collective-permute-done | bytes 4128 | tf_op jit(solution)/shard_map/ppermute | solution.py:324
  60.5 6.7 %collective-permute-start.6 = (f32[8,128]{1,0:T(8,128)S(1)}, f32[8,128]{1,0:T(8,128)S(1)}, u32[]{:S(2)}, u32[]{:S(2)}) collective-permute-start(f32[8,128]{1,0:T(8,128)S(1)} %slice.95), channel_id=1, source_target_pairs={{0,2},{2,4},{4,6},{6,8},{8,10},{10,12},{12,14},{14,16},{16,18},{18... | collective-permute-start | bytes 12296 | tf_op jit(solution)/shard_map/ppermute | solution.py:324
  67.9 14.0 %hessian.2 = (f32[40,128]{1,0:T(8,128)S(1)}, f32[8,128]{1,0:T(8,128)}) custom-call(s32[1]{0:T(128)} %bitcast.half, f32[40,128]{1,0:T(8,128)S(1)} %pad_maximum_fusion.ctl, f32[16,128]{1,0:T(8,128)S(1)} %fusion.7.base, f32[3,32,64,512]{3,2,1,0:T(8,128)} %get-tuple-element.8.grad, bf16[2,2048,192]{2,1,0:T(8,128)(2,1)S(1)} %copy-done, ...), custom_call_target="tpu_custom_call" | custom-call | tf_op jit(solution)/shard_map/hessian/pallas_call | solution.py:291
  83.2 2.9 %collective-permute-done.8 = f32[40,128]{1,0:T(8,128)S(1)} collective-permute-done((f32[40,128]{1,0:T(8,128)S(1)}, f32[40,128]{1,0:T(8,128)S(1)}, u32[]{:S(2)}, u32[]{:S(2)}) %collective-permute-start.8) | collective-permute-done | bytes 20512 | tf_op jit(solution)/shard_map/ppermute | solution.py:328
  86.1 8.3 %collective-permute-start.9 = (f32[16,128]{1,0:T(8,128)S(1)}, f32[16,128]{1,0:T(8,128)S(1)}, u32[]{:S(2)}, u32[]{:S(2)}) collective-permute-start(f32[16,128]{1,0:T(8,128)S(1)} %slice.97), channel_id=1, source_target_pairs={{0,2},{2,4},{4,6},{6,8},{8,10},{10,12},{12,14},{14,16},{16,18},{18... | collective-permute-start | bytes 24584 | tf_op jit(solution)/shard_map/ppermute | solution.py:324
  96.4 6.0 %collective-permute-done.10 = f32[8,128]{1,0:T(8,128)S(1)} collective-permute-done((f32[8,128]{1,0:T(8,128)S(1)}, f32[8,128]{1,0:T(8,128)S(1)}, u32[]{:S(2)}, u32[]{:S(2)}) %collective-permute-start.10) | collective-permute-done | bytes 4128 | tf_op jit(solution)/shard_map/ppermute | solution.py:324
  104.3 6.7 %collective-permute-start.11 = (f32[8,128]{1,0:T(8,128)S(1)}, f32[8,128]{1,0:T(8,128)S(1)}, u32[]{:S(2)}, u32[]{:S(2)}) collective-permute-start(f32[8,128]{1,0:T(8,128)S(1)} %slice.99), channel_id=1, source_target_pairs={{0,2},{2,4},{4,6},{6,8},{8,10},{10,12},{12,14},{14,16},{16,18},{18... | collective-permute-start | bytes 12296 | tf_op jit(solution)/shard_map/ppermute | solution.py:324
  111.7 13.4 %hessian.3 = (f32[40,128]{1,0:T(8,128)S(1)}, f32[8,128]{1,0:T(8,128)S(1)}) custom-call(s32[1]{0:T(128)} %bitcast.half, f32[40,128]{1,0:T(8,128)S(1)} %pad_maximum_fusion.1.ctl, f32[16,128]{1,0:T(8,128)S(1)} %fusion.7.base, f32[3,32,64,512]{3,2,1,0:T(8,128)} %get-tuple-element.8.grad, bf16[2,2048,192]{2,1,0:T(8,128)(2,1)S(1)} %copy-done, ...), custom_call_target="tpu_custom_call" | custom-call | tf_op jit(solution)/shard_map/hessian/pallas_call | solution.py:291
  126.4 2.9 %collective-permute-done.13 = f32[48,128]{1,0:T(8,128)S(1)} collective-permute-done((f32[48,128]{1,0:T(8,128)S(1)}, f32[48,128]{1,0:T(8,128)S(1)}, u32[]{:S(2)}, u32[]{:S(2)}) %collective-permute-start.13) | collective-permute-done | bytes 24608 | tf_op jit(solution)/shard_map/ppermute | solution.py:328
  130.6 2.5 %collective-permute-done.15 = f32[8,128]{1,0:T(8,128)S(1)} collective-permute-done((f32[8,128]{1,0:T(8,128)S(1)}, f32[8,128]{1,0:T(8,128)S(1)}, u32[]{:S(2)}, u32[]{:S(2)}) %collective-permute-start.15) | collective-permute-done | bytes 4128 | tf_op jit(solution)/shard_map/ppermute | solution.py:363
  133.1 3.7 %collective-permute-done.16 = f32[8,128]{1,0:T(8,128)S(1)} collective-permute-done((f32[8,128]{1,0:T(8,128)S(1)}, f32[8,128]{1,0:T(8,128)S(1)}, u32[]{:S(2)}, u32[]{:S(2)}) %collective-permute-start.16) | collective-permute-done | bytes 4128 | tf_op jit(solution)/shard_map/ppermute | solution.py:363
  136.7 2.5 %collective-permute-done.17 = f32[8,128]{1,0:T(8,128)S(1)} collective-permute-done((f32[8,128]{1,0:T(8,128)S(1)}, f32[8,128]{1,0:T(8,128)S(1)}, u32[]{:S(2)}, u32[]{:S(2)}) %collective-permute-start.17) | collective-permute-done | bytes 4128 | tf_op jit(solution)/shard_map/ppermute | solution.py:363
  139.2 2.6 %collective-permute-start.18 = (f32[8,128]{1,0:T(8,128)S(1)}, f32[8,128]{1,0:T(8,128)S(1)}, u32[]{:S(2)}, u32[]{:S(2)}) collective-permute-start(f32[8,128]{1,0:T(8,128)S(1)} %add.76), channel_id=1, source_target_pairs={{0,32},{2,34},{4,36},{6,38},{8,40},{10,42},{12,44},{14,46},{16,48}... | collective-permute-start | bytes 12296 | tf_op jit(solution)/shard_map/ppermute | solution.py:363
  142.8 3.9 %collective-permute-start.19 = (f32[8,128]{1,0:T(8,128)S(1)}, f32[8,128]{1,0:T(8,128)S(1)}, u32[]{:S(2)}, u32[]{:S(2)}) collective-permute-start(f32[8,128]{1,0:T(8,128)S(1)} %add.77), channel_id=1, source_target_pairs={{0,96},{2,98},{4,100},{6,102},{8,104},{10,106},{12,108},{14,110},{... | collective-permute-start | bytes 12296 | tf_op jit(solution)/shard_map/ppermute | solution.py:363
  146.7 9.8 %collective-permute-start.20 = (f32[16,128]{1,0:T(8,128)S(1)}, f32[16,128]{1,0:T(8,128)S(1)}, u32[]{:S(2)}, u32[]{:S(2)}) collective-permute-start(f32[16,128]{1,0:T(8,128)S(1)} %slice.103), channel_id=1, source_target_pairs={{0,2},{2,4},{4,6},{6,8},{8,10},{10,12},{12,14},{14,16},{16,18},{18... | collective-permute-start | bytes 24584 | tf_op jit(solution)/shard_map/ppermute | solution.py:324
  156.5 1.9 %collective-permute-start.21 = (f32[8,128]{1,0:T(8,128)S(1)}, f32[8,128]{1,0:T(8,128)S(1)}, u32[]{:S(2)}, u32[]{:S(2)}) collective-permute-start(f32[8,128]{1,0:T(8,128)S(1)} %get-tuple-element.20), channel_id=1, source_target_pairs={{2,0},{4,2},{6,4},{8,6},{10,8},{12,10},{14,12},{16,14},{18,16},{20... | collective-permute-start | bytes 12296 | tf_op jit(solution)/shard_map/ppermute | solution.py:324
  158.5 5.9 %collective-permute-done.21 = f32[8,128]{1,0:T(8,128)S(1)} collective-permute-done((f32[8,128]{1,0:T(8,128)S(1)}, f32[8,128]{1,0:T(8,128)S(1)}, u32[]{:S(2)}, u32[]{:S(2)}) %collective-permute-start.21) | collective-permute-done | bytes 4128 | tf_op jit(solution)/shard_map/ppermute | solution.py:324
  (63 shorter events, 21.9 us)
Async XLA Ops:
  1.7 16.4 %collective-permute-start.1 = (f32[2,64,512]{2,1,0:T(8,128)S(1)}, f32[2,64,512]{2,1,0:T(8,128)S(1)}, u32[]{:S(2)}, u32[]{:S(2)}) collective-permute-start(f32[2,64,512]{2,1,0:T(8,128)S(1)} %get-tuple-element.18), channel_id=1, source_target_pairs={{2,0},{4,2},{6,4},{8,6},{10,8},{12,10},{14,12},{16,14},{18,16},{20... | collective-permute-start | bytes 786440 | tf_op jit(solution)/shard_map/ppermute | solution.py:324
  4.3 13.8 %collective-permute-start = (f32[2,64,512]{2,1,0:T(8,128)S(1)}, f32[2,64,512]{2,1,0:T(8,128)S(1)}, u32[]{:S(2)}, u32[]{:S(2)}) collective-permute-start(f32[2,64,512]{2,1,0:T(8,128)S(1)} %get-tuple-element.19), channel_id=1, source_target_pairs={{0,2},{2,4},{4,6},{6,8},{8,10},{10,12},{12,14},{14,16},{16,18},{18... | collective-permute-start | bytes 786440 | tf_op jit(solution)/shard_map/ppermute | solution.py:324
  11.6 6.5 %collective-permute-start.2 = (f32[32,2,512]{2,1,0:T(2,128)S(1)}, f32[32,2,512]{2,1,0:T(2,128)S(1)}, u32[]{:S(2)}, u32[]{:S(2)}) collective-permute-start(f32[32,2,512]{2,1,0:T(2,128)S(1)} %slice_select_fusion), channel_id=1, source_target_pairs={{0,1},{1,0},{2,3},{3,2},{4,5},{5,4},{6,7},{7,6},{8,9},{9,8},{10,11... | collective-permute-start | bytes 393224 | tf_op jit(solution)/shard_map/ppermute | solution.py:328
  20.3 47.6 %copy-start = (bf16[2,2048,192]{2,1,0:T(8,128)(2,1)S(1)}, bf16[2,2048,192]{2,1,0:T(8,128)(2,1)}, u32[]{:S(2)}) copy-start(bf16[2,2048,192]{2,1,0:T(8,128)(2,1)} %constant.18.clone.front) | copy-start | bytes 4718596
  20.3 47.6 %copy-start.2 = (bf16[256,1536]{1,0:T(8,128)(2,1)S(1)}, bf16[256,1536]{1,0:T(8,128)(2,1)}, u32[]{:S(2)}) copy-start(bf16[256,1536]{1,0:T(8,128)(2,1)} %constant.20.clone.xt) | copy-start | bytes 2359300
  41.0 4.2 %collective-permute-start.3 = (f32[40,128]{1,0:T(8,128)S(1)}, f32[40,128]{1,0:T(8,128)S(1)}, u32[]{:S(2)}, u32[]{:S(2)}) collective-permute-start(f32[40,128]{1,0:T(8,128)S(1)} %get-tuple-element.7), channel_id=1, source_target_pairs={{0,1},{1,0},{2,3},{3,2},{4,5},{5,4},{6,7},{7,6},{8,9},{9,8},{10,11... | collective-permute-start | bytes 61448 | tf_op jit(solution)/shard_map/ppermute | solution.py:328
  45.2 13.4 %collective-permute-start.4 = (f32[16,128]{1,0:T(8,128)S(1)}, f32[16,128]{1,0:T(8,128)S(1)}, u32[]{:S(2)}, u32[]{:S(2)}) collective-permute-start(f32[16,128]{1,0:T(8,128)S(1)} %slice.93), channel_id=1, source_target_pairs={{0,2},{2,4},{4,6},{6,8},{8,10},{10,12},{12,14},{14,16},{16,18},{18... | collective-permute-start | bytes 24584 | tf_op jit(solution)/shard_map/ppermute | solution.py:324
  50.7 7.9 %collective-permute-start.5 = (f32[8,128]{1,0:T(8,128)S(1)}, f32[8,128]{1,0:T(8,128)S(1)}, u32[]{:S(2)}, u32[]{:S(2)}) collective-permute-start(f32[8,128]{1,0:T(8,128)S(1)} %slice.94), channel_id=1, source_target_pairs={{2,0},{4,2},{6,4},{8,6},{10,8},{12,10},{14,12},{16,14},{18,16},{20... | collective-permute-start | bytes 12296 | tf_op jit(solution)/shard_map/ppermute | solution.py:324
  58.6 9.3 %collective-permute-start.7 = (f32[16,128]{1,0:T(8,128)S(1)}, f32[16,128]{1,0:T(8,128)S(1)}, u32[]{:S(2)}, u32[]{:S(2)}) collective-permute-start(f32[16,128]{1,0:T(8,128)S(1)} %fusion.7.base), channel_id=1, source_target_pairs={{2,0},{4,2},{6,4},{8,6},{10,8},{12,10},{14,12},{16,14},{18,16},{20... | collective-permute-start | bytes 24584 | tf_op jit(solution)/shard_map/ppermute | solution.py:324
  60.5 7.4 %collective-permute-start.6 = (f32[8,128]{1,0:T(8,128)S(1)}, f32[8,128]{1,0:T(8,128)S(1)}, u32[]{:S(2)}, u32[]{:S(2)}) collective-permute-start(f32[8,128]{1,0:T(8,128)S(1)} %slice.95), channel_id=1, source_target_pairs={{0,2},{2,4},{4,6},{6,8},{8,10},{10,12},{12,14},{14,16},{16,18},{18... | collective-permute-start | bytes 12296 | tf_op jit(solution)/shard_map/ppermute | solution.py:324
  82.0 4.1 %collective-permute-start.8 = (f32[40,128]{1,0:T(8,128)S(1)}, f32[40,128]{1,0:T(8,128)S(1)}, u32[]{:S(2)}, u32[]{:S(2)}) collective-permute-start(f32[40,128]{1,0:T(8,128)S(1)} %get-tuple-element.9), channel_id=1, source_target_pairs={{0,1},{1,0},{2,3},{3,2},{4,5},{5,4},{6,7},{7,6},{8,9},{9,8},{10,11... | collective-permute-start | bytes 61448 | tf_op jit(solution)/shard_map/ppermute | solution.py:328
  86.1 16.3 %collective-permute-start.9 = (f32[16,128]{1,0:T(8,128)S(1)}, f32[16,128]{1,0:T(8,128)S(1)}, u32[]{:S(2)}, u32[]{:S(2)}) collective-permute-start(f32[16,128]{1,0:T(8,128)S(1)} %slice.97), channel_id=1, source_target_pairs={{0,2},{2,4},{4,6},{6,8},{8,10},{10,12},{12,14},{14,16},{16,18},{18... | collective-permute-start | bytes 24584 | tf_op jit(solution)/shard_map/ppermute | solution.py:324
  94.4 7.9 %collective-permute-start.10 = (f32[8,128]{1,0:T(8,128)S(1)}, f32[8,128]{1,0:T(8,128)S(1)}, u32[]{:S(2)}, u32[]{:S(2)}) collective-permute-start(f32[8,128]{1,0:T(8,128)S(1)} %slice.98), channel_id=1, source_target_pairs={{2,0},{4,2},{6,4},{8,6},{10,8},{12,10},{14,12},{16,14},{18,16},{20... | collective-permute-start | bytes 12296 | tf_op jit(solution)/shard_map/ppermute | solution.py:324
  102.4 9.3 %collective-permute-start.12 = (f32[16,128]{1,0:T(8,128)S(1)}, f32[16,128]{1,0:T(8,128)S(1)}, u32[]{:S(2)}, u32[]{:S(2)}) collective-permute-start(f32[16,128]{1,0:T(8,128)S(1)} %fusion.6), channel_id=1, source_target_pairs={{2,0},{4,2},{6,4},{8,6},{10,8},{12,10},{14,12},{16,14},{18,16},{20... | collective-permute-start | bytes 24584 | tf_op jit(solution)/shard_map/ppermute | solution.py:324
  104.3 7.4 %collective-permute-start.11 = (f32[8,128]{1,0:T(8,128)S(1)}, f32[8,128]{1,0:T(8,128)S(1)}, u32[]{:S(2)}, u32[]{:S(2)}) collective-permute-start(f32[8,128]{1,0:T(8,128)S(1)} %slice.99), channel_id=1, source_target_pairs={{0,2},{2,4},{4,6},{6,8},{8,10},{10,12},{12,14},{14,16},{16,18},{18... | collective-permute-start | bytes 12296 | tf_op jit(solution)/shard_map/ppermute | solution.py:324
  125.1 4.3 %collective-permute-start.13 = (f32[48,128]{1,0:T(8,128)S(1)}, f32[48,128]{1,0:T(8,128)S(1)}, u32[]{:S(2)}, u32[]{:S(2)}) collective-permute-start(f32[48,128]{1,0:T(8,128)S(1)} %constant_dynamic-update-slice_fusion), channel_id=1, source_target_pairs={{0,1},{1,0},{2,3},{3,2},{4,5},{5,4},{6,7},{7,6},{8,9},{9,8},{10,11... | collective-permute-start | bytes 73736 | tf_op jit(solution)/shard_map/ppermute | solution.py:328
  129.3 1.2 collective-permute-start.14
  130.6 2.5 %collective-permute-start.15 = (f32[8,128]{1,0:T(8,128)S(1)}, f32[8,128]{1,0:T(8,128)S(1)}, u32[]{:S(2)}, u32[]{:S(2)}) collective-permute-start(f32[8,128]{1,0:T(8,128)S(1)} %get-tuple-element.21), channel_id=1, source_target_pairs={{0,4},{2,6},{4,0},{6,2},{8,12},{10,14},{12,8},{14,10},{16,20},{18,... | collective-permute-start | bytes 12296 | tf_op jit(solution)/shard_map/ppermute | solution.py:363
  133.1 3.7 %collective-permute-start.16 = (f32[8,128]{1,0:T(8,128)S(1)}, f32[8,128]{1,0:T(8,128)S(1)}, u32[]{:S(2)}, u32[]{:S(2)}) collective-permute-start(f32[8,128]{1,0:T(8,128)S(1)} %add.74), channel_id=1, source_target_pairs={{0,12},{2,14},{4,8},{6,10},{8,4},{10,6},{12,0},{14,2},{16,28},{18,... | collective-permute-start | bytes 12296 | tf_op jit(solution)/shard_map/ppermute | solution.py:363
  136.7 2.5 %collective-permute-start.17 = (f32[8,128]{1,0:T(8,128)S(1)}, f32[8,128]{1,0:T(8,128)S(1)}, u32[]{:S(2)}, u32[]{:S(2)}) collective-permute-start(f32[8,128]{1,0:T(8,128)S(1)} %add.75), channel_id=1, source_target_pairs={{0,16},{2,18},{4,20},{6,22},{8,24},{10,26},{12,28},{14,30},{16,0},... | collective-permute-start | bytes 12296 | tf_op jit(solution)/shard_map/ppermute | solution.py:363
  139.2 3.6 %collective-permute-start.18 = (f32[8,128]{1,0:T(8,128)S(1)}, f32[8,128]{1,0:T(8,128)S(1)}, u32[]{:S(2)}, u32[]{:S(2)}) collective-permute-start(f32[8,128]{1,0:T(8,128)S(1)} %add.76), channel_id=1, source_target_pairs={{0,32},{2,34},{4,36},{6,38},{8,40},{10,42},{12,44},{14,46},{16,48}... | collective-permute-start | bytes 12296 | tf_op jit(solution)/shard_map/ppermute | solution.py:363
  142.8 15.6 %collective-permute-start.19 = (f32[8,128]{1,0:T(8,128)S(1)}, f32[8,128]{1,0:T(8,128)S(1)}, u32[]{:S(2)}, u32[]{:S(2)}) collective-permute-start(f32[8,128]{1,0:T(8,128)S(1)} %add.77), channel_id=1, source_target_pairs={{0,96},{2,98},{4,100},{6,102},{8,104},{10,106},{12,108},{14,110},{... | collective-permute-start | bytes 12296 | tf_op jit(solution)/shard_map/ppermute | solution.py:363
  146.7 17.7 %collective-permute-start.20 = (f32[16,128]{1,0:T(8,128)S(1)}, f32[16,128]{1,0:T(8,128)S(1)}, u32[]{:S(2)}, u32[]{:S(2)}) collective-permute-start(f32[16,128]{1,0:T(8,128)S(1)} %slice.103), channel_id=1, source_target_pairs={{0,2},{2,4},{4,6},{6,8},{8,10},{10,12},{12,14},{14,16},{16,18},{18... | collective-permute-start | bytes 24584 | tf_op jit(solution)/shard_map/ppermute | solution.py:324
  156.5 7.9 %collective-permute-start.21 = (f32[8,128]{1,0:T(8,128)S(1)}, f32[8,128]{1,0:T(8,128)S(1)}, u32[]{:S(2)}, u32[]{:S(2)}) collective-permute-start(f32[8,128]{1,0:T(8,128)S(1)} %get-tuple-element.20), channel_id=1, source_target_pairs={{2,0},{4,2},{6,4},{8,6},{10,8},{12,10},{14,12},{16,14},{18,16},{20... | collective-permute-start | bytes 12296 | tf_op jit(solution)/shard_map/ppermute | solution.py:324
  (2 other events, 2.2 us)

commit v2 on v1

--- a/solution.py
+++ b/solution.py
@@ -328,22 +328,44 @@
     return lax.ppermute(value, "gy", [(0, 1), (1, 0)])
 
 
-def owned_sum(whole):
-    from_above = passed_along(whole[:CY], "gz", -1)
-    from_below = passed_along(whole[3 * CY :], "gz", 1)
-    owned = whole[CY : 3 * CY] + from_below
-    return owned + jnp.pad(from_above, ((CY, 0), (0, 0)))
-
-
-def with_rims(owned):
-    lower = passed_along(owned[CY:], "gz", 1)
-    upper = passed_along(owned, "gz", -1)
-    return jnp.concatenate([lower, owned, upper], 0)
+def paired(value, mask):
+    count = lax.axis_size("gz")
+    return lax.ppermute(value, "gz", [(i, i ^ mask) for i in range(count)])
+
+
+def outer_paired(value):
+    count = lax.axis_size("gz")
+    pairs = [(i, i + 1) for i in range(1, count - 1, 2)]
+    return lax.ppermute(value, "gz", pairs + [(j, i) for i, j in pairs])
+
+
+def pair_sum(lower, own, other):
+    first, second = jnp.where(lower, own, other), jnp.where(lower, other, own)
+    widths = ((0, 2 * CY), (0, 0)), ((2 * CY, 0), (0, 0))
+    return jnp.pad(first, widths[0]) + jnp.pad(second, widths[1])
+
+
+def outer_terms(lower, seven):
+    return outer_paired(jnp.where(lower, seven[: 3 * CY], seven[4 * CY :]))
+
+
+def all_planes(lower, part):
+    part = part + swapped(part)
+    seven = pair_sum(lower, part, paired(part, 1))
+    three = outer_terms(lower, seven)
+    one = paired(jnp.where(lower, three[2 * CY :], three[:CY]), 1)
+    low = jnp.concatenate([three, jnp.zeros((CY, 128), F32), one], 0) + seven[: 5 * CY]
+    high = jnp.concatenate([one, jnp.zeros((CY, 128), F32), three], 0) + seven[2 * CY :]
+    row = lax.broadcasted_iota(jnp.int32, (CTL, 128), 0)
+    at = lax.axis_index("gz") * (2 * CY) - CY + row
+    inside = (at >= 0) & (at < lax.axis_size("gz") * (2 * CY))
+    return jnp.where(inside, jnp.where(lower, low, high), 0.0)
 
 
 def local(moving, fixed):
     half_id = lax.axis_index("gy").astype(jnp.int32)
     half = half_id.reshape(1)
+    lower = lax.axis_index("gz") % 2 == 0
     front, back, xt = (jnp.asarray(a) for a in tables())
 
     z_low = passed_along(moving[-2:], "gz", 1)
@@ -351,16 +373,25 @@
     y_rows = swapped(jnp.where(half_id == 0, moving[:, -2:], moving[:, :2]))
 
     grad, part = first_pass(half, moving, z_low, z_high, fixed, y_rows, back, xt)
-    b = owned_sum(part + swapped(part))
-    part, _ = hessian_pass(half, with_rims(b), b, grad, front, back, xt)
-    u = owned_sum(part + swapped(part))
-    part, sums = hessian_pass(half, with_rims(u), b, grad, front, back, xt)
+    b_planes = all_planes(lower, part)
+    b = b_planes[CY : 3 * CY]
+    part, _ = hessian_pass(half, b_planes, b, grad, front, back, xt)
+    u_planes = all_planes(lower, part)
+    u = u_planes[CY : 3 * CY]
+    part, sums = hessian_pass(half, u_planes, b, grad, front, back, xt)
     both = jnp.concatenate([part, sums], 0)
     both = both + swapped(both)
-    v = owned_sum(both[:CTL])
-    sums = both[CTL:]
-    for mask in (1, 2, 6, 8, 16, 48):
-        sums = sums + lax.ppermute(sums, "gz", [(i, i ^ mask) for i in range(64)])
+    other = paired(both, 1)
+    seven = pair_sum(lower, both[:CTL], other[:CTL])
+    sums = both[CTL:] + other[CTL:]
+    three = outer_terms(lower, seven)
+    sums = sums + paired(sums, 2)
+    sums, three = lax.optimization_barrier((sums, three))
+    for mask in (6, 8, 16, 48):
+        sums = sums + paired(sums, mask)
+    v_low = seven[CY : 3 * CY] + three[CY:]
+    v_high = seven[3 * CY : 5 * CY] + jnp.pad(three[:CY], ((CY, 0), (0, 0)))
+    v = jnp.where(lower, v_low, v_high)
 
     bb, bu, uu, uv = (sums[j : j + 1] for j in range(4))
     a0 = bb / bu

time: 166 us -> 142 us (0.86)
  the two profiles are of different devices: /device:TPU:27 before, /device:TPU:0 now
where the time goes in v2:
time: 142 us
  starting transfers between devices  57.9 us (41%)
  Pallas kernels  47.8 us (34%)
  waiting for transfers between devices  22.4 us (16%)
  local copies, waits for them, and re-layouts  8.59 us (6%)
  other arithmetic  4.34 us (3%)
    ppermute x10, starting transfers between devices, paired(): return lax.ppermute(value, 'gz', [(i, i ^ mask) for i in range(count)])  39.9 us
    pallas_call x2, Pallas kernels, hessian_pass(): pl.pallas_call(hessian_kernel, grid_spec=pltpu.PrefetchScalarGridSpec(num...  27.3 us
    pallas_call x1, Pallas kernels, first_pass(): pl.pallas_call(first_kernel, grid_spec=pltpu.PrefetchScalarGridSpec(num_s...  20.5 us
    ppermute x4, starting transfers between devices, swapped(): return lax.ppermute(value, 'gy', [(0, 1), (1, 0)])  13.4 us
    ppermute x10, waiting for transfers between devices, paired(): return lax.ppermute(value, 'gz', [(i, i ^ mask) for i in range(count)])  13.1 us
    ppermute x4, waiting for transfers between devices, swapped(): return lax.ppermute(value, 'gy', [(0, 1), (1, 0)])  9.28 us
    unnamed x25, local copies, waits for them, and re-layouts  7.36 us
  transfers between devices with their start and end apart: 19, of which 14 were waited for; matrix products, arithmetic and copies ran while one was open for 1% of the time, Pallas kernels for 0%

profile of v2, /device:TPU:0, one launch (start us, length us, event | category | flops | bytes accessed | tf_op | source)
XLA Modules:
  0.0 141.8 jit_solution(13309838380009892687)
XLA Ops:
  1.7 1.3 collective-permute-start
  5.6 3.6 %collective-permute-start.2 = (f32[32,2,512]{2,1,0:T(2,128)S(1)}, f32[32,2,512]{2,1,0:T(2,128)S(1)}, u32[]{:S(2)}, u32[]{:S(2)}) collective-permute-start(f32[32,2,512]{2,1,0:T(2,128)S(1)} %slice_select_fusion), channel_id=1, source_target_pairs={{0,1},{1,0},{2,3},{3,2},{4,5},{5,4},{6,7},{7,6},{8,9},{9,8},{10,11... | collective-permute-start | bytes 393224 | tf_op jit(solution)/shard_map/ppermute | solution.py:328
  9.3 2.9 %collective-permute-done.2.y_rows = f32[32,2,512]{2,1,0:T(2,128)S(1)} collective-permute-done((f32[32,2,512]{2,1,0:T(2,128)S(1)}, f32[32,2,512]{2,1,0:T(2,128)S(1)}, u32[]{:S(2)}, u32[]{:S(2)}) %collective-permute-start.2) | collective-permute-done | bytes 131104 | tf_op jit(solution)/shard_map/ppermute | solution.py:328
  17.7 20.5 %first.1 = (f32[3,32,64,512]{3,2,1,0:T(8,128)}, f32[40,128]{1,0:T(8,128)S(1)}) custom-call(s32[1]{0:T(128)} %bitcast.half, f32[32,64,512]{2,1,0:T(8,128)} %moving.1, f32[2,64,512]{2,1,0:T(8,128)S(1)} %copy-done.6, f32[2,64,512]{2,1,0:T(8,128)S(1)} %copy-done.8, f32[32,64,512]{2,1,0:T(8,128)} %fixed.1, f32[32,2,512]{2,1,0:T(2,128)S(1)} %collective-permute-done.2.y_rows, ...), custom_call_target="tpu_custom_call" | custom-call | tf_op jit(solution)/shard_map/first/pallas_call | solution.py:260
  38.2 3.6 %collective-permute-start.3 = (f32[40,128]{1,0:T(8,128)S(1)}, f32[40,128]{1,0:T(8,128)S(1)}, u32[]{:S(2)}, u32[]{:S(2)}) collective-permute-start(f32[40,128]{1,0:T(8,128)S(1)} %get-tuple-element.9), channel_id=1, source_target_pairs={{0,1},{1,0},{2,3},{3,2},{4,5},{5,4},{6,7},{7,6},{8,9},{9,8},{10,11... | collective-permute-start | bytes 61448 | tf_op jit(solution)/shard_map/ppermute | solution.py:328
  41.8 1.8 %collective-permute-done.3 = f32[40,128]{1,0:T(8,128)S(1)} collective-permute-done((f32[40,128]{1,0:T(8,128)S(1)}, f32[40,128]{1,0:T(8,128)S(1)}, u32[]{:S(2)}, u32[]{:S(2)}) %collective-permute-start.3) | collective-permute-done | bytes 20512 | tf_op jit(solution)/shard_map/ppermute | solution.py:328
  48.7 7.6 %collective-permute-start.6 = (f32[8,128]{1,0:T(8,128)S(1)}, f32[8,128]{1,0:T(8,128)S(1)}, u32[]{:S(2)}, u32[]{:S(2)}) collective-permute-start(f32[8,128]{1,0:T(8,128)S(1)} %slice_select_fusion.4), channel_id=1, source_target_pairs={{0,2},{2,0},{4,6},{6,4},{8,10},{10,8},{12,14},{14,12},{16,18},{18,... | collective-permute-start | bytes 12296 | tf_op jit(solution)/shard_map/ppermute | solution.py:333
  58.1 14.0 %hessian.2 = (f32[40,128]{1,0:T(8,128)S(1)}, f32[8,128]{1,0:T(8,128)}) custom-call(s32[1]{0:T(128)} %bitcast.half, f32[40,128]{1,0:T(8,128)S(1)} %fusion.3.ctl, f32[16,128]{1,0:T(8,128)S(1)} %slice.144.base, f32[3,32,64,512]{3,2,1,0:T(8,128)} %get-tuple-element.10.grad, bf16[2,2048,192]{2,1,0:T(8,128)(2,1)S(1)} %copy-done, ...), custom_call_target="tpu_custom_call" | custom-call | tf_op jit(solution)/shard_map/hessian/pallas_call | solution.py:291
  72.0 3.0 %collective-permute-start.7 = (f32[40,128]{1,0:T(8,128)S(1)}, f32[40,128]{1,0:T(8,128)S(1)}, u32[]{:S(2)}, u32[]{:S(2)}) collective-permute-start(f32[40,128]{1,0:T(8,128)S(1)} %get-tuple-element.11), channel_id=1, source_target_pairs={{0,1},{1,0},{2,3},{3,2},{4,5},{5,4},{6,7},{7,6},{8,9},{9,8},{10,11... | collective-permute-start | bytes 61448 | tf_op jit(solution)/shard_map/ppermute | solution.py:328
  75.1 2.3 %collective-permute-done.7 = f32[40,128]{1,0:T(8,128)S(1)} collective-permute-done((f32[40,128]{1,0:T(8,128)S(1)}, f32[40,128]{1,0:T(8,128)S(1)}, u32[]{:S(2)}, u32[]{:S(2)}) %collective-permute-start.7) | collective-permute-done | bytes 20512 | tf_op jit(solution)/shard_map/ppermute | solution.py:328
  79.2 4.7 %collective-permute-start.10 = (f32[8,128]{1,0:T(8,128)S(1)}, f32[8,128]{1,0:T(8,128)S(1)}, u32[]{:S(2)}, u32[]{:S(2)}) collective-permute-start(f32[8,128]{1,0:T(8,128)S(1)} %slice_select_fusion.3), channel_id=1, source_target_pairs={{0,2},{2,0},{4,6},{6,4},{8,10},{10,8},{12,14},{14,12},{16,18},{18,... | collective-permute-start | bytes 12296 | tf_op jit(solution)/shard_map/ppermute | solution.py:333
  84.8 13.4 %hessian.3 = (f32[40,128]{1,0:T(8,128)S(1)}, f32[8,128]{1,0:T(8,128)S(1)}) custom-call(s32[1]{0:T(128)} %bitcast.half, f32[40,128]{1,0:T(8,128)S(1)} %fusion.7.ctl, f32[16,128]{1,0:T(8,128)S(1)} %slice.144.base, f32[3,32,64,512]{3,2,1,0:T(8,128)} %get-tuple-element.10.grad, bf16[2,2048,192]{2,1,0:T(8,128)(2,1)S(1)} %copy-done, ...), custom_call_target="tpu_custom_call" | custom-call | tf_op jit(solution)/shard_map/hessian/pallas_call | solution.py:291
  98.2 3.1 %collective-permute-start.11 = (f32[48,128]{1,0:T(8,128)S(1)}, f32[48,128]{1,0:T(8,128)S(1)}, u32[]{:S(2)}, u32[]{:S(2)}) collective-permute-start(f32[48,128]{1,0:T(8,128)S(1)} %constant_dynamic-update-slice_fusion), channel_id=1, source_target_pairs={{0,1},{1,0},{2,3},{3,2},{4,5},{5,4},{6,7},{7,6},{8,9},{9,8},{10,11... | collective-permute-start | bytes 73736 | tf_op jit(solution)/shard_map/ppermute | solution.py:328
  101.3 2.3 %collective-permute-done.11 = f32[48,128]{1,0:T(8,128)S(1)} collective-permute-done((f32[48,128]{1,0:T(8,128)S(1)}, f32[48,128]{1,0:T(8,128)S(1)}, u32[]{:S(2)}, u32[]{:S(2)}) %collective-permute-start.11) | collective-permute-done | bytes 24608 | tf_op jit(solution)/shard_map/ppermute | solution.py:328
  105.5 3.3 %collective-permute-start.13 = (f32[8,128]{1,0:T(8,128)S(1)}, f32[8,128]{1,0:T(8,128)S(1)}, u32[]{:S(2)}, u32[]{:S(2)}) collective-permute-start(f32[8,128]{1,0:T(8,128)S(1)} %slice_add_fusion), channel_id=1, source_target_pairs={{0,4},{2,6},{4,0},{6,2},{8,12},{10,14},{12,8},{14,10},{16,20},{18,... | collective-permute-start | bytes 12296 | tf_op jit(solution)/shard_map/ppermute | solution.py:333
  108.8 1.6 %collective-permute-done.13 = f32[8,128]{1,0:T(8,128)S(1)} collective-permute-done((f32[8,128]{1,0:T(8,128)S(1)}, f32[8,128]{1,0:T(8,128)S(1)}, u32[]{:S(2)}, u32[]{:S(2)}) %collective-permute-start.13) | collective-permute-done | bytes 4128 | tf_op jit(solution)/shard_map/ppermute | solution.py:333
  110.4 7.6 %collective-permute-start.15 = (f32[8,128]{1,0:T(8,128)S(1)}, f32[8,128]{1,0:T(8,128)S(1)}, u32[]{:S(2)}, u32[]{:S(2)}) collective-permute-start(f32[8,128]{1,0:T(8,128)S(1)} %add.110), channel_id=1, source_target_pairs={{0,12},{2,14},{4,8},{6,10},{8,4},{10,6},{12,0},{14,2},{16,28},{18,... | collective-permute-start | bytes 12296 | tf_op jit(solution)/shard_map/ppermute | solution.py:333
  118.0 1.6 %collective-permute-done.15 = f32[8,128]{1,0:T(8,128)S(1)} collective-permute-done((f32[8,128]{1,0:T(8,128)S(1)}, f32[8,128]{1,0:T(8,128)S(1)}, u32[]{:S(2)}, u32[]{:S(2)}) %collective-permute-start.15) | collective-permute-done | bytes 4128 | tf_op jit(solution)/shard_map/ppermute | solution.py:333
  119.5 6.1 %collective-permute-start.16 = (f32[8,128]{1,0:T(8,128)S(1)}, f32[8,128]{1,0:T(8,128)S(1)}, u32[]{:S(2)}, u32[]{:S(2)}) collective-permute-start(f32[8,128]{1,0:T(8,128)S(1)} %add.112), channel_id=1, source_target_pairs={{0,16},{2,18},{4,20},{6,22},{8,24},{10,26},{12,28},{14,30},{16,0},... | collective-permute-start | bytes 12296 | tf_op jit(solution)/shard_map/ppermute | solution.py:333
  125.7 1.6 %collective-permute-done.16 = f32[8,128]{1,0:T(8,128)S(1)} collective-permute-done((f32[8,128]{1,0:T(8,128)S(1)}, f32[8,128]{1,0:T(8,128)S(1)}, u32[]{:S(2)}, u32[]{:S(2)}) %collective-permute-start.16) | collective-permute-done | bytes 4128 | tf_op jit(solution)/shard_map/ppermute | solution.py:333
  127.3 5.8 %collective-permute-start.17 = (f32[8,128]{1,0:T(8,128)S(1)}, f32[8,128]{1,0:T(8,128)S(1)}, u32[]{:S(2)}, u32[]{:S(2)}) collective-permute-start(f32[8,128]{1,0:T(8,128)S(1)} %add.113), channel_id=1, source_target_pairs={{0,32},{2,34},{4,36},{6,38},{8,40},{10,42},{12,44},{14,46},{16,48}... | collective-permute-start | bytes 12296 | tf_op jit(solution)/shard_map/ppermute | solution.py:333
  133.1 1.6 %collective-permute-done.17 = f32[8,128]{1,0:T(8,128)S(1)} collective-permute-done((f32[8,128]{1,0:T(8,128)S(1)}, f32[8,128]{1,0:T(8,128)S(1)}, u32[]{:S(2)}, u32[]{:S(2)}) %collective-permute-start.17) | collective-permute-done | bytes 4128 | tf_op jit(solution)/shard_map/ppermute | solution.py:333
  134.7 4.2 %collective-permute-start.18 = (f32[8,128]{1,0:T(8,128)S(1)}, f32[8,128]{1,0:T(8,128)S(1)}, u32[]{:S(2)}, u32[]{:S(2)}) collective-permute-start(f32[8,128]{1,0:T(8,128)S(1)} %add.114), channel_id=1, source_target_pairs={{0,96},{2,98},{4,100},{6,102},{8,104},{10,106},{12,108},{14,110},{... | collective-permute-start | bytes 12296 | tf_op jit(solution)/shard_map/ppermute | solution.py:333
  138.8 1.6 %collective-permute-done.18 = f32[8,128]{1,0:T(8,128)S(1)} collective-permute-done((f32[8,128]{1,0:T(8,128)S(1)}, f32[8,128]{1,0:T(8,128)S(1)}, u32[]{:S(2)}, u32[]{:S(2)}) %collective-permute-start.18) | collective-permute-done | bytes 4128 | tf_op jit(solution)/shard_map/ppermute | solution.py:333
  (73 shorter events, 22.1 us)
Async XLA Ops:
  1.7 10.5 %collective-permute-start = (f32[2,64,512]{2,1,0:T(8,128)S(1)}, f32[2,64,512]{2,1,0:T(8,128)S(1)}, u32[]{:S(2)}, u32[]{:S(2)}) collective-permute-start(f32[2,64,512]{2,1,0:T(8,128)S(1)} %get-tuple-element.23), channel_id=1, source_target_pairs={{0,2},{2,4},{4,6},{6,8},{8,10},{10,12},{12,14},{14,16},{16,18},{18... | collective-permute-start | bytes 786440 | tf_op jit(solution)/shard_map/ppermute | solution.py:324
  3.0 9.9 %collective-permute-start.1 = (f32[2,64,512]{2,1,0:T(8,128)S(1)}, f32[2,64,512]{2,1,0:T(8,128)S(1)}, u32[]{:S(2)}, u32[]{:S(2)}) collective-permute-start(f32[2,64,512]{2,1,0:T(8,128)S(1)} %get-tuple-element.22), channel_id=1, source_target_pairs={{2,0},{4,2},{6,4},{8,6},{10,8},{12,10},{14,12},{16,14},{18,16},{20... | collective-permute-start | bytes 786440 | tf_op jit(solution)/shard_map/ppermute | solution.py:324
  5.6 6.6 %collective-permute-start.2 = (f32[32,2,512]{2,1,0:T(2,128)S(1)}, f32[32,2,512]{2,1,0:T(2,128)S(1)}, u32[]{:S(2)}, u32[]{:S(2)}) collective-permute-start(f32[32,2,512]{2,1,0:T(2,128)S(1)} %slice_select_fusion), channel_id=1, source_target_pairs={{0,1},{1,0},{2,3},{3,2},{4,5},{5,4},{6,7},{7,6},{8,9},{9,8},{10,11... | collective-permute-start | bytes 393224 | tf_op jit(solution)/shard_map/ppermute | solution.py:328
  13.6 1.1 copy-start.1
  17.7 40.3 %copy-start = (bf16[2,2048,192]{2,1,0:T(8,128)(2,1)S(1)}, bf16[2,2048,192]{2,1,0:T(8,128)(2,1)}, u32[]{:S(2)}) copy-start(bf16[2,2048,192]{2,1,0:T(8,128)(2,1)} %constant.44.clone.front) | copy-start | bytes 4718596
  17.7 40.3 %copy-start.2 = (bf16[256,1536]{1,0:T(8,128)(2,1)S(1)}, bf16[256,1536]{1,0:T(8,128)(2,1)}, u32[]{:S(2)}) copy-start(bf16[256,1536]{1,0:T(8,128)(2,1)} %constant.46.clone.xt) | copy-start | bytes 2359300
  17.7 40.3 %copy-start.4 = (bf16[2,80,2048]{2,1,0:T(8,128)(2,1)S(1)}, bf16[2,80,2048]{2,1,0:T(8,128)(2,1)}, u32[]{:S(2)}) copy-start(bf16[2,80,2048]{2,1,0:T(8,128)(2,1)} %constant.45.clone.back) | copy-start | bytes 1966084
  38.2 5.4 %collective-permute-start.3 = (f32[40,128]{1,0:T(8,128)S(1)}, f32[40,128]{1,0:T(8,128)S(1)}, u32[]{:S(2)}, u32[]{:S(2)}) collective-permute-start(f32[40,128]{1,0:T(8,128)S(1)} %get-tuple-element.9), channel_id=1, source_target_pairs={{0,1},{1,0},{2,3},{3,2},{4,5},{5,4},{6,7},{7,6},{8,9},{9,8},{10,11... | collective-permute-start | bytes 61448 | tf_op jit(solution)/shard_map/ppermute | solution.py:328
  44.2 1.9 %collective-permute-start.4 = (f32[40,128]{1,0:T(8,128)}, f32[40,128]{1,0:T(8,128)}, u32[]{:S(2)}, u32[]{:S(2)}) collective-permute-start(f32[40,128]{1,0:T(8,128)} %add.100), channel_id=1, source_target_pairs={{0,2},{2,0},{4,6},{6,4},{8,10},{10,8},{12,14},{14,12},{16,18},{18,... | collective-permute-start | bytes 61448 | tf_op jit(solution)/shard_map/ppermute | solution.py:333
  46.8 1.2 copy-start.10
  48.0 0.7 collective-permute-start.5
  48.7 8.4 %collective-permute-start.6 = (f32[8,128]{1,0:T(8,128)S(1)}, f32[8,128]{1,0:T(8,128)S(1)}, u32[]{:S(2)}, u32[]{:S(2)}) collective-permute-start(f32[8,128]{1,0:T(8,128)S(1)} %slice_select_fusion.4), channel_id=1, source_target_pairs={{0,2},{2,0},{4,6},{6,4},{8,10},{10,8},{12,14},{14,12},{16,18},{18,... | collective-permute-start | bytes 12296 | tf_op jit(solution)/shard_map/ppermute | solution.py:333
  72.0 5.3 %collective-permute-start.7 = (f32[40,128]{1,0:T(8,128)S(1)}, f32[40,128]{1,0:T(8,128)S(1)}, u32[]{:S(2)}, u32[]{:S(2)}) collective-permute-start(f32[40,128]{1,0:T(8,128)S(1)} %get-tuple-element.11), channel_id=1, source_target_pairs={{0,1},{1,0},{2,3},{3,2},{4,5},{5,4},{6,7},{7,6},{8,9},{9,8},{10,11... | collective-permute-start | bytes 61448 | tf_op jit(solution)/shard_map/ppermute | solution.py:328
  77.3 1.2 collective-permute-start.8
  78.5 0.7 collective-permute-start.9
  79.2 5.5 %collective-permute-start.10 = (f32[8,128]{1,0:T(8,128)S(1)}, f32[8,128]{1,0:T(8,128)S(1)}, u32[]{:S(2)}, u32[]{:S(2)}) collective-permute-start(f32[8,128]{1,0:T(8,128)S(1)} %slice_select_fusion.3), channel_id=1, source_target_pairs={{0,2},{2,0},{4,6},{6,4},{8,10},{10,8},{12,14},{14,12},{16,18},{18,... | collective-permute-start | bytes 12296 | tf_op jit(solution)/shard_map/ppermute | solution.py:333
  98.2 5.4 %collective-permute-start.11 = (f32[48,128]{1,0:T(8,128)S(1)}, f32[48,128]{1,0:T(8,128)S(1)}, u32[]{:S(2)}, u32[]{:S(2)}) collective-permute-start(f32[48,128]{1,0:T(8,128)S(1)} %constant_dynamic-update-slice_fusion), channel_id=1, source_target_pairs={{0,1},{1,0},{2,3},{3,2},{4,5},{5,4},{6,7},{7,6},{8,9},{9,8},{10,11... | collective-permute-start | bytes 73736 | tf_op jit(solution)/shard_map/ppermute | solution.py:328
  103.6 1.2 collective-permute-start.12
  104.8 5.6 %collective-permute-start.14 = (f32[24,128]{1,0:T(8,128)S(1)}, f32[24,128]{1,0:T(8,128)S(1)}, u32[]{:S(2)}, u32[]{:S(2)}) collective-permute-start(f32[24,128]{1,0:T(8,128)S(1)} %fusion.21), channel_id=1, source_target_pairs={{2,4},{6,8},{10,12},{14,16},{18,20},{22,24},{26,28},{30,32},{34,36... | collective-permute-start | bytes 36872 | tf_op jit(solution)/shard_map/ppermute | solution.py:339
  105.5 4.9 %collective-permute-start.13 = (f32[8,128]{1,0:T(8,128)S(1)}, f32[8,128]{1,0:T(8,128)S(1)}, u32[]{:S(2)}, u32[]{:S(2)}) collective-permute-start(f32[8,128]{1,0:T(8,128)S(1)} %slice_add_fusion), channel_id=1, source_target_pairs={{0,4},{2,6},{4,0},{6,2},{8,12},{10,14},{12,8},{14,10},{16,20},{18,... | collective-permute-start | bytes 12296 | tf_op jit(solution)/shard_map/ppermute | solution.py:333
  110.4 9.2 %collective-permute-start.15 = (f32[8,128]{1,0:T(8,128)S(1)}, f32[8,128]{1,0:T(8,128)S(1)}, u32[]{:S(2)}, u32[]{:S(2)}) collective-permute-start(f32[8,128]{1,0:T(8,128)S(1)} %add.110), channel_id=1, source_target_pairs={{0,12},{2,14},{4,8},{6,10},{8,4},{10,6},{12,0},{14,2},{16,28},{18,... | collective-permute-start | bytes 12296 | tf_op jit(solution)/shard_map/ppermute | solution.py:333
  119.5 7.7 %collective-permute-start.16 = (f32[8,128]{1,0:T(8,128)S(1)}, f32[8,128]{1,0:T(8,128)S(1)}, u32[]{:S(2)}, u32[]{:S(2)}) collective-permute-start(f32[8,128]{1,0:T(8,128)S(1)} %add.112), channel_id=1, source_target_pairs={{0,16},{2,18},{4,20},{6,22},{8,24},{10,26},{12,28},{14,30},{16,0},... | collective-permute-start | bytes 12296 | tf_op jit(solution)/shard_map/ppermute | solution.py:333
  127.3 7.4 %collective-permute-start.17 = (f32[8,128]{1,0:T(8,128)S(1)}, f32[8,128]{1,0:T(8,128)S(1)}, u32[]{:S(2)}, u32[]{:S(2)}) collective-permute-start(f32[8,128]{1,0:T(8,128)S(1)} %add.113), channel_id=1, source_target_pairs={{0,32},{2,34},{4,36},{6,38},{8,40},{10,42},{12,44},{14,46},{16,48}... | collective-permute-start | bytes 12296 | tf_op jit(solution)/shard_map/ppermute | solution.py:333
  134.7 5.7 %collective-permute-start.18 = (f32[8,128]{1,0:T(8,128)S(1)}, f32[8,128]{1,0:T(8,128)S(1)}, u32[]{:S(2)}, u32[]{:S(2)}) collective-permute-start(f32[8,128]{1,0:T(8,128)S(1)} %add.114), channel_id=1, source_target_pairs={{0,96},{2,98},{4,100},{6,102},{8,104},{10,106},{12,108},{14,110},{... | collective-permute-start | bytes 12296 | tf_op jit(solution)/shard_map/ppermute | solution.py:333
  (6 other events, 5.0 us)

commit v3 on v2

v3 whole, which is shorter than its diff:
```python
import jax
import jax.numpy as jnp
import ml_dtypes
import numpy as np
from jax import lax
from jax.experimental import pallas as pl
from jax.experimental.pallas import tpu as pltpu
from jax.sharding import PartitionSpec as P

KNOT = 16
data_weight = 1.0 / 256.0
smooth_weight = 0.1

BF = jnp.bfloat16
F32 = jnp.float32
NZ, NY, NX = 32, 64, 512
ROWS = KNOT * NY
PLANES, CY, CX = 5, 8, 32
CTL = PLANES * CY
KPAD = 48
TILE = 16
WIDE = 128


def split(array):
    high = array.astype(ml_dtypes.bfloat16)
    low = (array - high.astype(np.float64)).astype(ml_dtypes.bfloat16)
    return high, low


def spline_weights():
    t = (np.arange(KNOT) + 0.5) / KNOT
    return np.stack(
        [
            (1 - t) ** 3 / 6,
            (3 * t**3 - 6 * t**2 + 4) / 6,
            (-3 * t**3 + 3 * t**2 + 3 * t + 1) / 6,
            t**3 / 6,
        ]
    )


def tables():
    weights = spline_weights()

    def along(blocks, first_block, points, first_point):
        out = np.zeros((blocks * KNOT, points))
        for block in range(blocks):
            for j in range(4):
                point = first_block + block + j - 1 - first_point
                if 0 <= point < points:
                    out[block * KNOT : (block + 1) * KNOT, point] = weights[j]
        return out

    along_z = along(NZ // KNOT, 0, PLANES, -1)
    halves = []
    for half in range(2):
        along_y = along(NY // KNOT, half * (NY // KNOT), CY, 0)
        halves.append(np.einsum("zp,yq->zypq", along_z, along_y).reshape(NZ * NY, CTL))
    high, low = split(np.stack(halves))
    widths = ((0, 0), (0, 0), (0, KPAD - CTL))
    high48, low48 = (np.pad(a, widths) for a in (high, low))
    out_table = np.concatenate([high48, low48, high48, low48], axis=2)
    backs = []
    for half in range(2):
        along_y = along(NY // KNOT, half * (NY // KNOT), CY, 0)
        backs.append(np.concatenate(split(np.kron(np.eye(PLANES), along_y).T), axis=0))
    back_table = np.stack(backs)
    along_x = along(NX // KNOT, 0, CX, 0)
    rows = np.zeros((128, 3 * NX))
    for c in range(3):
        rows[c * CX : (c + 1) * CX, c * NX : (c + 1) * NX] = along_x.T
    x_table = np.concatenate(split(rows), axis=0)
    return out_table, back_table, x_table


def halves_of(value):
    high = value.astype(BF)
    return high, (value - high.astype(F32)).astype(BF)


def block_terms(block, grad, weight_at, planes):
    weights = spline_weights()
    even = (weights[:2] + weights[:2, ::-1]) / 2
    odd = (weights[:2] - weights[:2, ::-1]) / 2

    def strip(y, carry):
        rows = pl.ds(pl.multiple_of(y * 8, 8), 8)
        for x in range(0, NX, WIDE):
            lanes = slice(x, x + WIDE)
            sums = [[[0.0, 0.0], [0.0, 0.0]] for _ in range(3)]
            for i in range(KNOT // 2):
                pair = []
                for z in (i, KNOT - 1 - i):
                    slopes = [grad[c, block * KNOT + z, rows, lanes] for c in range(3)]
                    weight, carry = weight_at(block * KNOT + z, y, lanes, slopes, carry)
                    pair.append([slope * weight for slope in slopes])
                for c in range(3):
                    both, apart = pair[0][c] + pair[1][c], pair[0][c] - pair[1][c]
                    for j in range(2):
                        sums[c][0][j] = sums[c][0][j] + float(even[j, i]) * both
                        sums[c][1][j] = sums[c][1][j] + float(odd[j, i]) * apart
            for c in range(3):
                (e0, e1), (o0, o1) = sums[c]
                at = slice(c * NX + x, c * NX + x + WIDE)
                for j, value in enumerate((e0 + o0, e1 + o1, e1 - o1, e0 - o0)):
                    if block == 0 or j == 3:
                        planes[block + j, rows, at] = value
                    else:
                        planes[block + j, rows, at] += value
        return carry

    return strip


def contracted(planes, back, x_table):
    high, low = halves_of(planes[...].reshape(PLANES * NY, 3 * NX))
    terms = jnp.dot(back, high, preferred_element_type=F32)
    rest = jnp.dot(back[:CTL], low, preferred_element_type=F32)
    high, low = halves_of(terms[:CTL] + (terms[CTL:] + rest))
    both = lax.dot_general(
        jnp.concatenate([high, low], 0),
        x_table[...],
        (((1,), (1,)), ((), ())),
        preferred_element_type=F32,
    )
    return both[:CTL, :128] + (both[:CTL, 128:] + both[CTL:, :128])


def first_kernel(half, moving, z_low, z_high, fixed, y_rows, back, xt, grad, out, planes):
    upper = half[0] == 0
    lane = lax.broadcasted_iota(jnp.int32, (TILE, NX), 1)

    def plane(z, near_planes):
        rows = y_rows[z]
        blank = jnp.zeros_like(rows)
        low_rows = jnp.where(upper, blank, rows)
        high_rows = jnp.where(upper, rows, blank)
        center = near_planes[2]
        for y in range(0, NY, TILE):
            here = slice(y, y + TILE)
            value = center[here]

            def at_z(k):
                return near_planes[2 + k][here]

            def at_y(k):
                first = y + k
                if first < 0:
                    return jnp.concatenate([low_rows[2 + first :], center[0 : TILE + first]], 0)
                if first + TILE > NY:
                    return jnp.concatenate([center[first:NY], high_rows[: first + TILE - NY]], 0)
                return center[first : first + TILE]

            def at_x(k):
                moved = pltpu.roll(value, (-k) % NX, 1)
                inside = lane < NX - k if k > 0 else lane >= -k
                return jnp.where(inside, moved, 0.0)

            for c, near in enumerate((at_z, at_y, at_x)):
                slope = 8.0 * (near(1) - near(-1)) - (near(2) - near(-2))
                grad[c, z, here] = slope

    def ref_of(z):
        if z < 0:
            return z_low.at[2 + z]
        if z >= NZ:
            return z_high.at[z - NZ]
        return moving.at[z]

    for z in (0, 1, NZ - 2, NZ - 1):
        plane(z, [ref_of(z + k) for k in range(-2, 3)])

    def body(z, carry):
        plane(z, [moving.at[z + k] for k in range(-2, 3)])
        return carry

    lax.fori_loop(2, NZ - 2, body, 0)

    def weight_at(z, y, lanes, slopes, carry):
        rows = pl.ds(pl.multiple_of(y * 8, 8), 8)
        return moving[z, rows, lanes] - fixed[z, rows, lanes], carry

    for block in range(NZ // KNOT):
        lax.fori_loop(0, NY // 8, block_terms(block, grad, weight_at, planes), 0)
    out[...] = contracted(planes, back[half[0]], xt) * (-data_weight / 12.0)


def hessian_kernel(half, ctl, base, grad, front, back, xt, out, sums, spread, field, planes):
    high, low = halves_of(ctl[...])
    first, second = xt[:128], xt[128:]
    value = jnp.dot(high, first, preferred_element_type=F32)
    value += jnp.dot(low, first, preferred_element_type=F32)
    value += jnp.dot(high, second, preferred_element_type=F32)
    value = jnp.concatenate([value, jnp.zeros((KPAD - CTL, 3 * NX), F32)], 0)
    high, low = halves_of(value)
    for j, part in enumerate((high, high, low, low)):
        spread[j * KPAD : (j + 1) * KPAD] = part
    square = jnp.zeros((8, WIDE), F32)

    for block in range(NZ // KNOT):
        at_rows = slice(block * ROWS, (block + 1) * ROWS)
        field[...] = jnp.dot(front[half[0], at_rows], spread[...], preferred_element_type=F32)

        def weight_at(z, y, lanes, slopes, carry):
            rows = pl.ds(pl.multiple_of(z % KNOT * NY + y * 8, 8), 8)
            weight = 0.0
            for c in range(3):
                at = slice(c * NX + lanes.start, c * NX + lanes.stop)
                weight = weight + slopes[c] * field[rows, at]
            return weight, carry + weight * weight

        strip = block_terms(block, grad, weight_at, planes)
        square = lax.fori_loop(0, NY // 8, strip, square)

    scale = data_weight / 144.0
    whole = ctl[...]
    owned = whole[CY : 3 * CY]
    sub = lax.broadcasted_iota(jnp.int32, (2 * CY, 128), 0) % CY
    lane = lax.broadcasted_iota(jnp.int32, (2 * CY, 128), 1) % CX
    near = whole[0 : 2 * CY] + whole[2 * CY : 4 * CY]
    near += jnp.where(sub > 0, pltpu.roll(owned, 1, 0), 0.0)
    near += jnp.where(sub < CY - 1, pltpu.roll(owned, 2 * CY - 1, 0), 0.0)
    near += jnp.where(lane > 0, pltpu.roll(owned, 1, 1), 0.0)
    near += jnp.where(lane < CX - 1, pltpu.roll(owned, 127, 1), 0.0)
    smooth = (0.5 * smooth_weight) * (6.0 * owned - near)
    out[...] = contracted(planes, back[half[0]], xt) * scale
    out[CY : 3 * CY] += smooth
    first = base[...]

    def total(value):
        return jnp.sum(jnp.sum(value, axis=0, keepdims=True), axis=1, keepdims=True)

    whole_square = total(square) * scale + total(smooth * owned)
    lines = [
        0.5 * total(first * first),
        0.5 * total(first * owned),
        0.5 * total(owned * owned),
        whole_square,
    ]
    which = lax.broadcasted_iota(jnp.int32, (8, 128), 0)
    tile = jnp.zeros((8, 128), F32)
    for j, line in enumerate(lines):
        tile = jnp.where(which == j, line, tile)
    sums[...] = tile


VMEM_SPEC = pl.BlockSpec(memory_space=pltpu.VMEM)
SMEM_SPEC = pl.BlockSpec(memory_space=pltpu.SMEM)
PARAMS = pltpu.CompilerParams(vmem_limit_bytes=24 * 1024 * 1024)


def first_pass(half, moving, z_low, z_high, fixed, y_rows, back_table, x_table):
    return pl.pallas_call(
        first_kernel,
        in_specs=[SMEM_SPEC] + [VMEM_SPEC] * 7,
        out_specs=[VMEM_SPEC] * 2,
        scratch_shapes=[pltpu.VMEM((PLANES, NY, 3 * NX), F32)],
        out_shape=[
            jax.ShapeDtypeStruct((3, NZ, NY, NX), F32),
            jax.ShapeDtypeStruct((CTL, 128), F32),
        ],
        compiler_params=PARAMS,
        name="first",
    )(half, moving, z_low, z_high, fixed, y_rows, back_table, x_table)


def hessian_pass(half, ctl, base, grad, front_table, back_table, x_table):
    return pl.pallas_call(
        hessian_kernel,
        in_specs=[SMEM_SPEC] + [VMEM_SPEC] * 6,
        out_specs=[VMEM_SPEC] * 2,
        scratch_shapes=[
            pltpu.VMEM((4 * KPAD, 3 * NX), BF),
            pltpu.VMEM((ROWS, 3 * NX), F32),
            pltpu.VMEM((PLANES, NY, 3 * NX), F32),
        ],
        out_shape=[
            jax.ShapeDtypeStruct((CTL, 128), F32),
            jax.ShapeDtypeStruct((8, 128), F32),
        ],
        compiler_params=PARAMS,
        name="hessian",
    )(half, ctl, base, grad, front_table, back_table, x_table)


def passed_along(value, axis, steps):
    count = lax.axis_size(axis)
    initial, last = (max(0, -steps), min(count, count - steps))
    return lax.ppermute(value, axis, [(source, source + steps) for source in range(initial, last)])


def swapped(value):
    return lax.ppermute(value, "gy", [(0, 1), (1, 0)])


def paired(value, mask):
    count = lax.axis_size("gz")
    return lax.ppermute(value, "gz", [(i, i ^ mask) for i in range(count)])


def outer_paired(value):
    count = lax.axis_size("gz")
    pairs = [(i, i + 1) for i in range(1, count - 1, 2)]
    return lax.ppermute(value, "gz", pairs + [(j, i) for i, j in pairs])


def pair_sum(lower, own, other):
    first, second = jnp.where(lower, own, other), jnp.where(lower, other, own)
    widths = ((0, 2 * CY), (0, 0)), ((2 * CY, 0), (0, 0))
    return jnp.pad(first, widths[0]) + jnp.pad(second, widths[1])


def outer_terms(lower, seven):
    return outer_paired(jnp.where(lower, seven[: 3 * CY], seven[4 * CY :]))


def all_planes(lower, part):
    part = part + swapped(part)
    seven = pair_sum(lower, part, paired(part, 1))
    three = outer_terms(lower, seven)
    one = paired(jnp.where(lower, three[2 * CY :], three[:CY]), 1)
    low = jnp.concatenate([three, jnp.zeros((CY, 128), F32), one], 0) + seven[: 5 * CY]
    high = jnp.concatenate([one, jnp.zeros((CY, 128), F32), three], 0) + seven[2 * CY :]
    row = lax.broadcasted_iota(jnp.int32, (CTL, 128), 0)
    at = lax.axis_index("gz") * (2 * CY) - CY + row
    inside = (at >= 0) & (at < lax.axis_size("gz") * (2 * CY))
    return jnp.where(inside, jnp.where(lower, low, high), 0.0)


def local(moving, fixed):
    half_id = lax.axis_index("gy").astype(jnp.int32)
    half = half_id.reshape(1)
    lower = lax.axis_index("gz") % 2 == 0
    front, back, xt = (jnp.asarray(a) for a in tables())

    z_low = passed_along(moving[-2:], "gz", 1)
    z_high = passed_along(moving[:2], "gz", -1)
    y_rows = swapped(jnp.where(half_id == 0, moving[:, -2:], moving[:, :2]))

    grad, part = first_pass(half, moving, z_low, z_high, fixed, y_rows, back, xt)
    b_planes = all_planes(lower, part)
    b = b_planes[CY : 3 * CY]
    part, _ = hessian_pass(half, b_planes, b, grad, front, back, xt)
    u_planes = all_planes(lower, part)
    u = u_planes[CY : 3 * CY]
    part, sums = hessian_pass(half, u_planes, b, grad, front, back, xt)
    both = jnp.concatenate([part, sums], 0)
    both = both + swapped(both)
    other = paired(both, 1)
    seven = pair_sum(lower, both[:CTL], other[:CTL])
    sums = both[CTL:] + other[CTL:]
    three = outer_terms(lower, seven)
    sums = sums + paired(sums, 2)
    sums, three = lax.optimization_barrier((sums, three))
    for mask in (6, 8, 16, 48):
        sums = sums + paired(sums, mask)
    v_low = seven[CY : 3 * CY] + three[CY:]
    v_high = seven[3 * CY : 5 * CY] + jnp.pad(three[:CY], ((CY, 0), (0, 0)))
    v = jnp.where(lower, v_low, v_high)

    bb, bu, uu, uv = (sums[j : j + 1] for j in range(4))
    a0 = bb / bu
    rr1 = bb - 2.0 * a0 * bu + a0 * a0 * uu
    beta = rr1 / bb
    more = 1.0 + beta
    a1 = rr1 / (more * more * bu - 2.0 * more * a0 * uu + a0 * a0 * uv)
    solution = a0 * b + a1 * (more * b - a0 * u)
    residual = (b - a0 * u) - a1 * (more * u - a0 * v)

    def placed(value):
        turned = value.reshape(2, CY, 128)[:, :, : 3 * CX].reshape(2, CY, 3, CX)
        return turned.transpose(2, 0, 1, 3)

    return placed(solution), placed(residual)


def solution(mesh):
    in_specs = (P("gz", "gy", None), P("gz", "gy", None))
    out_specs = (P(None, "gz", None, None), P(None, "gz", None, None))
    return jax.shard_map(local, mesh=mesh, in_specs=in_specs, out_specs=out_specs, check_vma=False)
```

time: 142 us -> 128 us (0.901)
  Pallas kernels: 47.8 us -> 27.8 us
  local copies, waits for them, and re-layouts: 8.59 us -> 18 us
  other arithmetic: 4.34 us -> 1.6 us
    pallas_call x3, Pallas kernels: 47.8 us -> 27.8 us  [the longest x2 17.1 us: hessian_pass(): pl.pallas_call(hessian_kernel, in_specs=[SMEM_SPEC] + [VMEM_SPEC] * 6, ou...]
    unnamed x25 -> x21, local copies, waits for them, and re-layouts: 7.36 us -> 16.7 us
where the time goes in v3:
time: 128 us
  starting transfers between devices  57.6 us (45%)
  Pallas kernels  27.8 us (22%)
  waiting for transfers between devices  22.1 us (17%)
  local copies, waits for them, and re-layouts  18 us (14%)
  other arithmetic  1.6 us (1%)
    ppermute x10, starting transfers between devices, paired(): return lax.ppermute(value, 'gz', [(i, i ^ mask) for i in range(count)])  39.7 us
    pallas_call x2, Pallas kernels, hessian_pass(): pl.pallas_call(hessian_kernel, in_specs=[SMEM_SPEC] + [VMEM_SPEC] * 6, ou...  17.1 us
    unnamed x21, local copies, waits for them, and re-layouts  16.7 us
    ppermute x4, starting transfers between devices, swapped(): return lax.ppermute(value, 'gy', [(0, 1), (1, 0)])  13.3 us
    ppermute x10, waiting for transfers between devices, paired(): return lax.ppermute(value, 'gz', [(i, i ^ mask) for i in range(count)])  12.8 us
    pallas_call x1, Pallas kernels, first_pass(): pl.pallas_call(first_kernel, in_specs=[SMEM_SPEC] + [VMEM_SPEC] * 7, out_...  10.7 us
    ppermute x4, waiting for transfers between devices, swapped(): return lax.ppermute(value, 'gy', [(0, 1), (1, 0)])  9.27 us
    ppermute x2, starting transfers between devices, passed_along(): lax.ppermute(value, axis, [(source, source + steps) for source in range(i...  2.6 us
  transfers between devices with their start and end apart: 19, of which 14 were waited for; matrix products, arithmetic and copies ran while one was open for 1% of the time, Pallas kernels for 0%

profile of v3, /device:TPU:0, one launch (start us, length us, event | category | flops | bytes accessed | tf_op | source)
XLA Modules:
  0.0 127.8 jit_solution(8426196666006406729)
XLA Ops:
  5.6 3.6 %collective-permute-start.2 = (f32[32,2,512]{2,1,0:T(2,128)S(1)}, f32[32,2,512]{2,1,0:T(2,128)S(1)}, u32[]{:S(2)}, u32[]{:S(2)}) collective-permute-start(f32[32,2,512]{2,1,0:T(2,128)S(1)} %slice_select_fusion), channel_id=1, source_target_pairs={{0,1},{1,0},{2,3},{3,2},{4,5},{5,4},{6,7},{7,6},{8,9},{9,8},{10,11... | collective-permute-start | bytes 393224 | tf_op jit(solution)/shard_map/ppermute | solution.py:294
  9.3 2.9 %collective-permute-done.2.y_rows = f32[32,2,512]{2,1,0:T(2,128)S(1)} collective-permute-done((f32[32,2,512]{2,1,0:T(2,128)S(1)}, f32[32,2,512]{2,1,0:T(2,128)S(1)}, u32[]{:S(2)}, u32[]{:S(2)}) %collective-permute-start.2) | collective-permute-done | bytes 131104 | tf_op jit(solution)/shard_map/ppermute | solution.py:294
  13.4 2.2 %copy-done.5 = f32[32,64,512]{2,1,0:T(8,128)S(1)} copy-done((f32[32,64,512]{2,1,0:T(8,128)S(1)}, f32[32,64,512]{2,1,0:T(8,128)}, u32[]{:S(2)}) %copy-start.5) | copy-done | bytes 4194328
  15.5 2.2 %copy-done.6 = f32[32,64,512]{2,1,0:T(8,128)S(1)} copy-done((f32[32,64,512]{2,1,0:T(8,128)S(1)}, f32[32,64,512]{2,1,0:T(8,128)}, u32[]{:S(2)}) %copy-start.6) | copy-done | bytes 4194328
  18.6 10.7 %first.1 = (f32[3,32,64,512]{3,2,1,0:T(8,128)S(1)}, f32[40,128]{1,0:T(8,128)S(1)}) custom-call(s32[1]{0:T(128)} %bitcast.half, f32[32,64,512]{2,1,0:T(8,128)S(1)} %copy-done.5, f32[2,64,512]{2,1,0:T(8,128)S(1)} %collective-permute-done.z_low, f32[2,64,512]{2,1,0:T(8,128)S(1)} %collective-permute-done.1.z_high, f32[32,64,512]{2,1,0:T(8,128)S(1)} %copy-done.6, ...), custom_call_target="tpu_custom_call" | custom-call | tf_op jit(solution)/shard_map/first/pallas_call | solution.py:254
  29.4 4.5 %copy-done = f32[3,32,64,512]{3,2,1,0:T(8,128)} copy-done((f32[3,32,64,512]{3,2,1,0:T(8,128)}, f32[3,32,64,512]{3,2,1,0:T(8,128)S(1)}, u32[]{:S(2)}) %copy-start) | copy-done | bytes 12582936
  33.9 3.5 %collective-permute-start.3 = (f32[40,128]{1,0:T(8,128)S(1)}, f32[40,128]{1,0:T(8,128)S(1)}, u32[]{:S(2)}, u32[]{:S(2)}) collective-permute-start(f32[40,128]{1,0:T(8,128)S(1)} %get-tuple-element.9), channel_id=1, source_target_pairs={{0,1},{1,0},{2,3},{3,2},{4,5},{5,4},{6,7},{7,6},{8,9},{9,8},{10,11... | collective-permute-start | bytes 61448 | tf_op jit(solution)/shard_map/ppermute | solution.py:294
  37.4 1.8 %collective-permute-done.3 = f32[40,128]{1,0:T(8,128)S(1)} collective-permute-done((f32[40,128]{1,0:T(8,128)S(1)}, f32[40,128]{1,0:T(8,128)S(1)}, u32[]{:S(2)}, u32[]{:S(2)}) %collective-permute-start.3) | collective-permute-done | bytes 20512 | tf_op jit(solution)/shard_map/ppermute | solution.py:294
  41.4 7.4 %collective-permute-start.6 = (f32[8,128]{1,0:T(8,128)S(1)}, f32[8,128]{1,0:T(8,128)S(1)}, u32[]{:S(2)}, u32[]{:S(2)}) collective-permute-start(f32[8,128]{1,0:T(8,128)S(1)} %slice_select_fusion.4), channel_id=1, source_target_pairs={{0,2},{2,0},{4,6},{6,4},{8,10},{10,8},{12,14},{14,12},{16,18},{18,... | collective-permute-start | bytes 12296 | tf_op jit(solution)/shard_map/ppermute | solution.py:299
  49.7 4.6 %copy-done.1 = f32[3,32,64,512]{3,2,1,0:T(8,128)S(1)} copy-done((f32[3,32,64,512]{3,2,1,0:T(8,128)S(1)}, f32[3,32,64,512]{3,2,1,0:T(8,128)}, u32[]{:S(2)}) %copy-start.1) | copy-done | bytes 12582936
  54.3 8.8 %hessian.2 = (f32[40,128]{1,0:T(8,128)S(1)}, f32[8,128]{1,0:T(8,128)}) custom-call(s32[1]{0:T(128)} %bitcast.half, f32[40,128]{1,0:T(8,128)S(1)} %fusion.3.ctl, f32[16,128]{1,0:T(8,128)S(1)} %slice.144.base, f32[3,32,64,512]{3,2,1,0:T(8,128)S(1)} %copy-done.1, bf16[2,2048,192]{2,1,0:T(8,128)(2,1)S(1)} %copy-done.2, bf16[2,80,320]{2,1,0:T(8,128)(2,1)S(1)} %copy-done.8, ...), custom_call_target="tpu_custom_call" | custom-call | tf_op jit(solution)/shard_map/hessian/pallas_call | solution.py:269
  63.1 3.0 %collective-permute-start.7 = (f32[40,128]{1,0:T(8,128)S(1)}, f32[40,128]{1,0:T(8,128)S(1)}, u32[]{:S(2)}, u32[]{:S(2)}) collective-permute-start(f32[40,128]{1,0:T(8,128)S(1)} %get-tuple-element.11), channel_id=1, source_target_pairs={{0,1},{1,0},{2,3},{3,2},{4,5},{5,4},{6,7},{7,6},{8,9},{9,8},{10,11... | collective-permute-start | bytes 61448 | tf_op jit(solution)/shard_map/ppermute | solution.py:294
  66.1 2.2 %collective-permute-done.7 = f32[40,128]{1,0:T(8,128)S(1)} collective-permute-done((f32[40,128]{1,0:T(8,128)S(1)}, f32[40,128]{1,0:T(8,128)S(1)}, u32[]{:S(2)}, u32[]{:S(2)}) %collective-permute-start.7) | collective-permute-done | bytes 20512 | tf_op jit(solution)/shard_map/ppermute | solution.py:294
  70.3 4.7 %collective-permute-start.10 = (f32[8,128]{1,0:T(8,128)S(1)}, f32[8,128]{1,0:T(8,128)S(1)}, u32[]{:S(2)}, u32[]{:S(2)}) collective-permute-start(f32[8,128]{1,0:T(8,128)S(1)} %slice_select_fusion.3), channel_id=1, source_target_pairs={{0,2},{2,0},{4,6},{6,4},{8,10},{10,8},{12,14},{14,12},{16,18},{18,... | collective-permute-start | bytes 12296 | tf_op jit(solution)/shard_map/ppermute | solution.py:299
  75.9 8.3 %hessian.3 = (f32[40,128]{1,0:T(8,128)S(1)}, f32[8,128]{1,0:T(8,128)S(1)}) custom-call(s32[1]{0:T(128)} %bitcast.half, f32[40,128]{1,0:T(8,128)S(1)} %fusion.7.ctl, f32[16,128]{1,0:T(8,128)S(1)} %slice.144.base, f32[3,32,64,512]{3,2,1,0:T(8,128)S(1)} %copy-done.1, bf16[2,2048,192]{2,1,0:T(8,128)(2,1)S(1)} %copy-done.2, bf16[2,80,320]{2,1,0:T(8,128)(2,1)S(1)} %copy-done.8, ...), custom_call_target="tpu_custom_call" | custom-call | tf_op jit(solution)/shard_map/hessian/pallas_call | solution.py:269
  84.2 3.1 %collective-permute-start.11 = (f32[48,128]{1,0:T(8,128)S(1)}, f32[48,128]{1,0:T(8,128)S(1)}, u32[]{:S(2)}, u32[]{:S(2)}) collective-permute-start(f32[48,128]{1,0:T(8,128)S(1)} %constant_dynamic-update-slice_fusion), channel_id=1, source_target_pairs={{0,1},{1,0},{2,3},{3,2},{4,5},{5,4},{6,7},{7,6},{8,9},{9,8},{10,11... | collective-permute-start | bytes 73736 | tf_op jit(solution)/shard_map/ppermute | solution.py:294
  87.3 2.3 %collective-permute-done.11 = f32[48,128]{1,0:T(8,128)S(1)} collective-permute-done((f32[48,128]{1,0:T(8,128)S(1)}, f32[48,128]{1,0:T(8,128)S(1)}, u32[]{:S(2)}, u32[]{:S(2)}) %collective-permute-start.11) | collective-permute-done | bytes 24608 | tf_op jit(solution)/shard_map/ppermute | solution.py:294
  91.5 3.3 %collective-permute-start.13 = (f32[8,128]{1,0:T(8,128)S(1)}, f32[8,128]{1,0:T(8,128)S(1)}, u32[]{:S(2)}, u32[]{:S(2)}) collective-permute-start(f32[8,128]{1,0:T(8,128)S(1)} %slice_add_fusion), channel_id=1, source_target_pairs={{0,4},{2,6},{4,0},{6,2},{8,12},{10,14},{12,8},{14,10},{16,20},{18,... | collective-permute-start | bytes 12296 | tf_op jit(solution)/shard_map/ppermute | solution.py:299
  94.8 1.6 %collective-permute-done.13 = f32[8,128]{1,0:T(8,128)S(1)} collective-permute-done((f32[8,128]{1,0:T(8,128)S(1)}, f32[8,128]{1,0:T(8,128)S(1)}, u32[]{:S(2)}, u32[]{:S(2)}) %collective-permute-start.13) | collective-permute-done | bytes 4128 | tf_op jit(solution)/shard_map/ppermute | solution.py:299
  96.4 7.5 %collective-permute-start.15 = (f32[8,128]{1,0:T(8,128)S(1)}, f32[8,128]{1,0:T(8,128)S(1)}, u32[]{:S(2)}, u32[]{:S(2)}) collective-permute-start(f32[8,128]{1,0:T(8,128)S(1)} %add.110), channel_id=1, source_target_pairs={{0,12},{2,14},{4,8},{6,10},{8,4},{10,6},{12,0},{14,2},{16,28},{18,... | collective-permute-start | bytes 12296 | tf_op jit(solution)/shard_map/ppermute | solution.py:299
  103.9 1.6 %collective-permute-done.15 = f32[8,128]{1,0:T(8,128)S(1)} collective-permute-done((f32[8,128]{1,0:T(8,128)S(1)}, f32[8,128]{1,0:T(8,128)S(1)}, u32[]{:S(2)}, u32[]{:S(2)}) %collective-permute-start.15) | collective-permute-done | bytes 4128 | tf_op jit(solution)/shard_map/ppermute | solution.py:299
  105.5 6.1 %collective-permute-start.16 = (f32[8,128]{1,0:T(8,128)S(1)}, f32[8,128]{1,0:T(8,128)S(1)}, u32[]{:S(2)}, u32[]{:S(2)}) collective-permute-start(f32[8,128]{1,0:T(8,128)S(1)} %add.112), channel_id=1, source_target_pairs={{0,16},{2,18},{4,20},{6,22},{8,24},{10,26},{12,28},{14,30},{16,0},... | collective-permute-start | bytes 12296 | tf_op jit(solution)/shard_map/ppermute | solution.py:299
  113.2 5.8 %collective-permute-start.17 = (f32[8,128]{1,0:T(8,128)S(1)}, f32[8,128]{1,0:T(8,128)S(1)}, u32[]{:S(2)}, u32[]{:S(2)}) collective-permute-start(f32[8,128]{1,0:T(8,128)S(1)} %add.113), channel_id=1, source_target_pairs={{0,32},{2,34},{4,36},{6,38},{8,40},{10,42},{12,44},{14,46},{16,48}... | collective-permute-start | bytes 12296 | tf_op jit(solution)/shard_map/ppermute | solution.py:299
  120.6 4.2 %collective-permute-start.18 = (f32[8,128]{1,0:T(8,128)S(1)}, f32[8,128]{1,0:T(8,128)S(1)}, u32[]{:S(2)}, u32[]{:S(2)}) collective-permute-start(f32[8,128]{1,0:T(8,128)S(1)} %add.114), channel_id=1, source_target_pairs={{0,96},{2,98},{4,100},{6,102},{8,104},{10,106},{12,108},{14,110},{... | collective-permute-start | bytes 12296 | tf_op jit(solution)/shard_map/ppermute | solution.py:299
  (69 shorter events, 21.0 us)
Async XLA Ops:
  1.7 10.5 %collective-permute-start = (f32[2,64,512]{2,1,0:T(8,128)S(1)}, f32[2,64,512]{2,1,0:T(8,128)S(1)}, u32[]{:S(2)}, u32[]{:S(2)}) collective-permute-start(f32[2,64,512]{2,1,0:T(8,128)S(1)} %get-tuple-element.23), channel_id=1, source_target_pairs={{0,2},{2,4},{4,6},{6,8},{8,10},{10,12},{12,14},{14,16},{16,18},{18... | collective-permute-start | bytes 786440 | tf_op jit(solution)/shard_map/ppermute | solution.py:290
  3.0 9.2 %collective-permute-start.1 = (f32[2,64,512]{2,1,0:T(8,128)S(1)}, f32[2,64,512]{2,1,0:T(8,128)S(1)}, u32[]{:S(2)}, u32[]{:S(2)}) collective-permute-start(f32[2,64,512]{2,1,0:T(8,128)S(1)} %get-tuple-element.22), channel_id=1, source_target_pairs={{2,0},{4,2},{6,4},{8,6},{10,8},{12,10},{14,12},{16,14},{18,16},{20... | collective-permute-start | bytes 786440 | tf_op jit(solution)/shard_map/ppermute | solution.py:290
  5.6 6.6 %collective-permute-start.2 = (f32[32,2,512]{2,1,0:T(2,128)S(1)}, f32[32,2,512]{2,1,0:T(2,128)S(1)}, u32[]{:S(2)}, u32[]{:S(2)}) collective-permute-start(f32[32,2,512]{2,1,0:T(2,128)S(1)} %slice_select_fusion), channel_id=1, source_target_pairs={{0,1},{1,0},{2,3},{3,2},{4,5},{5,4},{6,7},{7,6},{8,9},{9,8},{10,11... | collective-permute-start | bytes 393224 | tf_op jit(solution)/shard_map/ppermute | solution.py:294
  18.6 31.1 %copy-start.2 = (bf16[2,2048,192]{2,1,0:T(8,128)(2,1)S(1)}, bf16[2,2048,192]{2,1,0:T(8,128)(2,1)}, u32[]{:S(2)}) copy-start(bf16[2,2048,192]{2,1,0:T(8,128)(2,1)} %constant.44.clone.front) | copy-start | bytes 4718596
  18.6 31.1 %copy-start.4 = (bf16[256,1536]{1,0:T(8,128)(2,1)S(1)}, bf16[256,1536]{1,0:T(8,128)(2,1)}, u32[]{:S(2)}) copy-start(bf16[256,1536]{1,0:T(8,128)(2,1)} %constant.46.clone.xt) | copy-start | bytes 2359300
  18.6 31.1 %copy-start.8 = (bf16[2,80,320]{2,1,0:T(8,128)(2,1)S(1)}, bf16[2,80,320]{2,1,0:T(8,128)(2,1)}, u32[]{:S(2)}) copy-start(bf16[2,80,320]{2,1,0:T(8,128)(2,1)} %constant.45.clone.back) | copy-start | bytes 307204
  29.4 4.5 %copy-start = (f32[3,32,64,512]{3,2,1,0:T(8,128)}, f32[3,32,64,512]{3,2,1,0:T(8,128)S(1)}, u32[]{:S(2)}) copy-start(f32[3,32,64,512]{3,2,1,0:T(8,128)S(1)} %get-tuple-element.10.grad) | copy-start | bytes 37748740
  33.9 5.3 %collective-permute-start.3 = (f32[40,128]{1,0:T(8,128)S(1)}, f32[40,128]{1,0:T(8,128)S(1)}, u32[]{:S(2)}, u32[]{:S(2)}) collective-permute-start(f32[40,128]{1,0:T(8,128)S(1)} %get-tuple-element.9), channel_id=1, source_target_pairs={{0,1},{1,0},{2,3},{3,2},{4,5},{5,4},{6,7},{7,6},{8,9},{9,8},{10,11... | collective-permute-start | bytes 61448 | tf_op jit(solution)/shard_map/ppermute | solution.py:294
  39.2 1.5 %collective-permute-start.4 = (f32[40,128]{1,0:T(8,128)S(1)}, f32[40,128]{1,0:T(8,128)S(1)}, u32[]{:S(2)}, u32[]{:S(2)}) collective-permute-start(f32[40,128]{1,0:T(8,128)S(1)} %add.100), channel_id=1, source_target_pairs={{0,2},{2,0},{4,6},{6,4},{8,10},{10,8},{12,14},{14,12},{16,18},{18,... | collective-permute-start | bytes 61448 | tf_op jit(solution)/shard_map/ppermute | solution.py:299
  40.7 0.7 collective-permute-start.5
  41.4 8.2 %collective-permute-start.6 = (f32[8,128]{1,0:T(8,128)S(1)}, f32[8,128]{1,0:T(8,128)S(1)}, u32[]{:S(2)}, u32[]{:S(2)}) collective-permute-start(f32[8,128]{1,0:T(8,128)S(1)} %slice_select_fusion.4), channel_id=1, source_target_pairs={{0,2},{2,0},{4,6},{6,4},{8,10},{10,8},{12,14},{14,12},{16,18},{18,... | collective-permute-start | bytes 12296 | tf_op jit(solution)/shard_map/ppermute | solution.py:299
  49.7 4.6 %copy-start.1 = (f32[3,32,64,512]{3,2,1,0:T(8,128)S(1)}, f32[3,32,64,512]{3,2,1,0:T(8,128)}, u32[]{:S(2)}) copy-start(f32[3,32,64,512]{3,2,1,0:T(8,128)} %copy-done) | copy-start | bytes 37748740
  63.1 5.3 %collective-permute-start.7 = (f32[40,128]{1,0:T(8,128)S(1)}, f32[40,128]{1,0:T(8,128)S(1)}, u32[]{:S(2)}, u32[]{:S(2)}) collective-permute-start(f32[40,128]{1,0:T(8,128)S(1)} %get-tuple-element.11), channel_id=1, source_target_pairs={{0,1},{1,0},{2,3},{3,2},{4,5},{5,4},{6,7},{7,6},{8,9},{9,8},{10,11... | collective-permute-start | bytes 61448 | tf_op jit(solution)/shard_map/ppermute | solution.py:294
  68.4 1.2 collective-permute-start.8
  69.6 0.7 collective-permute-start.9
  70.3 5.5 %collective-permute-start.10 = (f32[8,128]{1,0:T(8,128)S(1)}, f32[8,128]{1,0:T(8,128)S(1)}, u32[]{:S(2)}, u32[]{:S(2)}) collective-permute-start(f32[8,128]{1,0:T(8,128)S(1)} %slice_select_fusion.3), channel_id=1, source_target_pairs={{0,2},{2,0},{4,6},{6,4},{8,10},{10,8},{12,14},{14,12},{16,18},{18,... | collective-permute-start | bytes 12296 | tf_op jit(solution)/shard_map/ppermute | solution.py:299
  84.2 5.4 %collective-permute-start.11 = (f32[48,128]{1,0:T(8,128)S(1)}, f32[48,128]{1,0:T(8,128)S(1)}, u32[]{:S(2)}, u32[]{:S(2)}) collective-permute-start(f32[48,128]{1,0:T(8,128)S(1)} %constant_dynamic-update-slice_fusion), channel_id=1, source_target_pairs={{0,1},{1,0},{2,3},{3,2},{4,5},{5,4},{6,7},{7,6},{8,9},{9,8},{10,11... | collective-permute-start | bytes 73736 | tf_op jit(solution)/shard_map/ppermute | solution.py:294
  89.6 1.2 collective-permute-start.12
  90.8 5.6 %collective-permute-start.14 = (f32[24,128]{1,0:T(8,128)S(1)}, f32[24,128]{1,0:T(8,128)S(1)}, u32[]{:S(2)}, u32[]{:S(2)}) collective-permute-start(f32[24,128]{1,0:T(8,128)S(1)} %fusion.21), channel_id=1, source_target_pairs={{2,4},{6,8},{10,12},{14,16},{18,20},{22,24},{26,28},{30,32},{34,36... | collective-permute-start | bytes 36872 | tf_op jit(solution)/shard_map/ppermute | solution.py:305
  91.5 4.9 %collective-permute-start.13 = (f32[8,128]{1,0:T(8,128)S(1)}, f32[8,128]{1,0:T(8,128)S(1)}, u32[]{:S(2)}, u32[]{:S(2)}) collective-permute-start(f32[8,128]{1,0:T(8,128)S(1)} %slice_add_fusion), channel_id=1, source_target_pairs={{0,4},{2,6},{4,0},{6,2},{8,12},{10,14},{12,8},{14,10},{16,20},{18,... | collective-permute-start | bytes 12296 | tf_op jit(solution)/shard_map/ppermute | solution.py:299
  96.4 9.1 %collective-permute-start.15 = (f32[8,128]{1,0:T(8,128)S(1)}, f32[8,128]{1,0:T(8,128)S(1)}, u32[]{:S(2)}, u32[]{:S(2)}) collective-permute-start(f32[8,128]{1,0:T(8,128)S(1)} %add.110), channel_id=1, source_target_pairs={{0,12},{2,14},{4,8},{6,10},{8,4},{10,6},{12,0},{14,2},{16,28},{18,... | collective-permute-start | bytes 12296 | tf_op jit(solution)/shard_map/ppermute | solution.py:299
  105.5 7.7 %collective-permute-start.16 = (f32[8,128]{1,0:T(8,128)S(1)}, f32[8,128]{1,0:T(8,128)S(1)}, u32[]{:S(2)}, u32[]{:S(2)}) collective-permute-start(f32[8,128]{1,0:T(8,128)S(1)} %add.112), channel_id=1, source_target_pairs={{0,16},{2,18},{4,20},{6,22},{8,24},{10,26},{12,28},{14,30},{16,0},... | collective-permute-start | bytes 12296 | tf_op jit(solution)/shard_map/ppermute | solution.py:299
  113.2 7.4 %collective-permute-start.17 = (f32[8,128]{1,0:T(8,128)S(1)}, f32[8,128]{1,0:T(8,128)S(1)}, u32[]{:S(2)}, u32[]{:S(2)}) collective-permute-start(f32[8,128]{1,0:T(8,128)S(1)} %add.113), channel_id=1, source_target_pairs={{0,32},{2,34},{4,36},{6,38},{8,40},{10,42},{12,44},{14,46},{16,48}... | collective-permute-start | bytes 12296 | tf_op jit(solution)/shard_map/ppermute | solution.py:299
  120.6 5.7 %collective-permute-start.18 = (f32[8,128]{1,0:T(8,128)S(1)}, f32[8,128]{1,0:T(8,128)S(1)}, u32[]{:S(2)}, u32[]{:S(2)}) collective-permute-start(f32[8,128]{1,0:T(8,128)S(1)} %add.114), channel_id=1, source_target_pairs={{0,96},{2,98},{4,100},{6,102},{8,104},{10,106},{12,108},{14,110},{... | collective-permute-start | bytes 12296 | tf_op jit(solution)/shard_map/ppermute | solution.py:299
  (4 other events, 6.4 us)

commit v4 on v3

--- a/solution.py
+++ b/solution.py
@@ -20,6 +20,9 @@
 KPAD = 48
 TILE = 16
 WIDE = 128
+CHUNK = 8
+STEPS = NZ // CHUNK
+EDGES = (0, 1, NZ - 2, NZ - 1)
 
 
 def split(array):
@@ -127,29 +130,38 @@
     return both[:CTL, :128] + (both[:CTL, 128:] + both[CTL:, :128])
 
 
-def first_kernel(half, moving, z_low, z_high, fixed, y_rows, back, xt, grad, out, planes):
-    upper = half[0] == 0
+def interior_kernel(
+    half, moving_hbm, fixed_hbm, grad_hbm, planes, z_edges, y_edges, z_slopes, y_slopes, grad, moving, fixed, sems, out_sems
+):
+    def copies(j):
+        part = pl.ds(j * CHUNK, CHUNK)
+        return [
+            pltpu.make_async_copy(source.at[part], target.at[part], sems.at[which, j])
+            for which, (source, target) in enumerate(((moving_hbm, moving), (fixed_hbm, fixed)))
+        ]
+
+    for j in range(STEPS):
+        copies(j)[0].start()
+    for j in range(STEPS):
+        copies(j)[1].start()
     lane = lax.broadcasted_iota(jnp.int32, (TILE, NX), 1)
-
-    def plane(z, near_planes):
-        rows = y_rows[z]
-        blank = jnp.zeros_like(rows)
-        low_rows = jnp.where(upper, blank, rows)
-        high_rows = jnp.where(upper, rows, blank)
-        center = near_planes[2]
+    two = jnp.zeros((2, NX), F32)
+
+    def plane(z, shifts):
+        center = moving.at[z]
         for y in range(0, NY, TILE):
             here = slice(y, y + TILE)
             value = center[here]
 
             def at_z(k):
-                return near_planes[2 + k][here]
+                return moving[z + k, here] if k in shifts else 0.0
 
             def at_y(k):
                 first = y + k
                 if first < 0:
-                    return jnp.concatenate([low_rows[2 + first :], center[0 : TILE + first]], 0)
+                    return jnp.concatenate([two[: -first], center[0 : TILE + first]], 0)
                 if first + TILE > NY:
-                    return jnp.concatenate([center[first:NY], high_rows[: first + TILE - NY]], 0)
+                    return jnp.concatenate([center[first:NY], two[: first + TILE - NY]], 0)
                 return center[first : first + TILE]
 
             def at_x(k):
@@ -158,24 +170,31 @@
                 return jnp.where(inside, moved, 0.0)
 
             for c, near in enumerate((at_z, at_y, at_x)):
-                slope = 8.0 * (near(1) - near(-1)) - (near(2) - near(-2))
-                grad[c, z, here] = slope
-
-    def ref_of(z):
-        if z < 0:
-            return z_low.at[2 + z]
-        if z >= NZ:
-            return z_high.at[z - NZ]
-        return moving.at[z]
-
-    for z in (0, 1, NZ - 2, NZ - 1):
-        plane(z, [ref_of(z + k) for k in range(-2, 3)])
+                grad[c, z, here] = 8.0 * (near(1) - near(-1)) - (near(2) - near(-2))
+
+    every = (-2, -1, 1, 2)
 
     def body(z, carry):
-        plane(z, [moving.at[z + k] for k in range(-2, 3)])
+        plane(z, every)
         return carry
 
-    lax.fori_loop(2, NZ - 2, body, 0)
+    bounds = [0] + [(j + 1) * CHUNK - 2 for j in range(STEPS - 1)] + [NZ]
+    written = [
+        pltpu.make_async_copy(grad.at[:, first:last], grad_hbm.at[:, first:last], out_sems.at[j])
+        for j, (first, last) in enumerate(zip(bounds, bounds[1:]))
+    ]
+    for j in range(STEPS):
+        copies(j)[0].wait()
+        if j == 0:
+            plane(0, (1, 2))
+            plane(1, (-1, 1, 2))
+        lax.fori_loop(max(2, j * CHUNK - 2), (j + 1) * CHUNK - 2, body, 0)
+        if j == STEPS - 1:
+            plane(NZ - 2, (-2, -1, 1))
+            plane(NZ - 1, (-2, -1))
+        written[j].start()
+    for j in range(STEPS):
+        copies(j)[1].wait()
 
     def weight_at(z, y, lanes, slopes, carry):
         rows = pl.ds(pl.multiple_of(y * 8, 8), 8)
@@ -183,10 +202,103 @@
 
     for block in range(NZ // KNOT):
         lax.fori_loop(0, NY // 8, block_terms(block, grad, weight_at, planes), 0)
+    for e, z in enumerate(EDGES):
+        z_edges[e] = moving[z] - fixed[z]
+        z_slopes[e] = grad[0, z]
+    rows = pl.ds(pl.multiple_of((1 - half[0]) * (NY - 8), 8), 8)
+    y_edges[...] = moving[:, rows, :] - fixed[:, rows, :]
+    y_slopes[...] = grad[1, :, rows, :]
+    for copy in written:
+        copy.wait()
+
+
+def edge_kernel(
+    half,
+    z_low,
+    z_high,
+    y_rows,
+    z_edges,
+    y_edges,
+    z_slopes,
+    y_slopes,
+    back,
+    xt,
+    grad_in,
+    planes_in,
+    grad_hbm,
+    out,
+    planes,
+    z_new,
+    y_new,
+    sems,
+):
+    del grad_in
+    planes[...] = planes_in[...]
+    weights = spline_weights()
+
+    def strip(y, carry):
+        rows = pl.ds(pl.multiple_of(y * 8, 8), 8)
+        near, far = z_low[1, rows], z_low[0, rows]
+        above, beyond = z_high[0, rows], z_high[1, rows]
+        slopes = (far - 8.0 * near, near, -above, 8.0 * above - beyond)
+        for e, z in enumerate(EDGES):
+            z_new[e, rows] = z_slopes[e, rows] + slopes[e]
+            term = slopes[e] * z_edges[e, rows]
+            for j in range(4):
+                at = z // KNOT + j
+                planes[at, rows, 0:NX] += float(weights[j, z % KNOT]) * term
+        return carry
+
+    lax.fori_loop(0, NY // 8, strip, 0)
+    copies = [
+        pltpu.make_async_copy(z_new.at[pl.ds(e, 2)], grad_hbm.at[0, pl.ds(EDGES[e], 2)], sems.at[e // 2])
+        for e in (0, 2)
+    ]
+    for copy in copies:
+        copy.start()
+
+    upper = half[0] == 0
+    rows = pl.ds(pl.multiple_of((1 - half[0]) * (NY - 8), 8), 8)
+    sub = lax.broadcasted_iota(jnp.int32, (8, NX), 0)
+
+    def coefficient(when_upper, otherwise):
+        def column(entries):
+            value = jnp.zeros((8, NX), F32)
+            for row, entry in entries.items():
+                value = jnp.where(sub == row, entry, value)
+            return value
+
+        return jnp.where(upper, column(when_upper), column(otherwise))
+
+    on_first = coefficient({6: -1.0, 7: 8.0}, {0: 1.0})
+    on_second = coefficient({7: -1.0}, {0: -8.0, 1: 1.0})
+    for block in range(NZ // KNOT):
+        sums = [0.0] * 4
+        for i in range(KNOT):
+            z = block * KNOT + i
+            slope = on_first * y_rows[z, 0:1] + on_second * y_rows[z, 1:2]
+            y_new[z] = y_slopes[z] + slope
+            term = slope * y_edges[z]
+            sums = [total + float(weights[j, i]) * term for j, total in enumerate(sums)]
+        for j, total in enumerate(sums):
+            planes[block + j, rows, NX : 2 * NX] += total
+    copies.append(pltpu.make_async_copy(y_new, grad_hbm.at[1, :, rows], sems.at[2]))
+    copies[-1].start()
     out[...] = contracted(planes, back[half[0]], xt) * (-data_weight / 12.0)
-
-
-def hessian_kernel(half, ctl, base, grad, front, back, xt, out, sums, spread, field, planes):
+    for copy in copies:
+        copy.wait()
+
+
+def hessian_kernel(
+    half, ctl, base, grad_hbm, front, back, xt, out, sums, grad, spread, field, planes, sems
+):
+    copies = []
+    for block in range(NZ // KNOT):
+        part = pl.ds(block * KNOT, KNOT)
+        copies.append(
+            pltpu.make_async_copy(grad_hbm.at[:, part], grad.at[:, part], sems.at[block])
+        )
+        copies[-1].start()
     high, low = halves_of(ctl[...])
     first, second = xt[:128], xt[128:]
     value = jnp.dot(high, first, preferred_element_type=F32)
@@ -210,6 +322,7 @@
                 weight = weight + slopes[c] * field[rows, at]
             return weight, carry + weight * weight
 
+        copies[block].wait()
         strip = block_terms(block, grad, weight_at, planes)
         square = lax.fori_loop(0, NY // 8, strip, square)
 
@@ -247,33 +360,71 @@
 
 VMEM_SPEC = pl.BlockSpec(memory_space=pltpu.VMEM)
 SMEM_SPEC = pl.BlockSpec(memory_space=pltpu.SMEM)
-PARAMS = pltpu.CompilerParams(vmem_limit_bytes=24 * 1024 * 1024)
-
-
-def first_pass(half, moving, z_low, z_high, fixed, y_rows, back_table, x_table):
+PARAMS = pltpu.CompilerParams(vmem_limit_bytes=52 * 1024 * 1024)
+EDGE_PARAMS = pltpu.CompilerParams(vmem_limit_bytes=50 * 1024 * 1024)
+INTERIOR_MIB = 48
+
+
+GRAD_SHAPE = jax.ShapeDtypeStruct((3, NZ, NY, NX), F32)
+PLANES_SHAPE = jax.ShapeDtypeStruct((PLANES, NY, 3 * NX), F32)
+CTL_SHAPE = jax.ShapeDtypeStruct((CTL, 128), F32)
+
+
+Z_SHAPE = (len(EDGES), NY, NX)
+Y_SHAPE = (NZ, 8, NX)
+HBM_SPEC = pl.BlockSpec(memory_space=pltpu.HBM)
+
+
+def interior_pass(half, moving, fixed):
     return pl.pallas_call(
-        first_kernel,
-        in_specs=[SMEM_SPEC] + [VMEM_SPEC] * 7,
-        out_specs=[VMEM_SPEC] * 2,
-        scratch_shapes=[pltpu.VMEM((PLANES, NY, 3 * NX), F32)],
-        out_shape=[
-            jax.ShapeDtypeStruct((3, NZ, NY, NX), F32),
-            jax.ShapeDtypeStruct((CTL, 128), F32),
+        interior_kernel,
+        in_specs=[SMEM_SPEC] + [HBM_SPEC] * 2,
+        out_specs=[HBM_SPEC] + [VMEM_SPEC] * 5,
+        scratch_shapes=[
+            pltpu.VMEM((3, NZ, NY, NX), F32),
+            pltpu.VMEM((NZ, NY, NX), F32),
+            pltpu.VMEM((NZ, NY, NX), F32),
+            pltpu.SemaphoreType.DMA((2, STEPS)),
+            pltpu.SemaphoreType.DMA((STEPS,)),
         ],
-        compiler_params=PARAMS,
-        name="first",
-    )(half, moving, z_low, z_high, fixed, y_rows, back_table, x_table)
+        out_shape=[GRAD_SHAPE, PLANES_SHAPE]
+        + [jax.ShapeDtypeStruct(shape, F32) for shape in (Z_SHAPE, Y_SHAPE) * 2],
+        compiler_params=pltpu.CompilerParams(vmem_limit_bytes=INTERIOR_MIB * 1024 * 1024),
+        cost_estimate=pl.CostEstimate(flops=100_000_000, bytes_accessed=40_000_000, transcendentals=0),
+        name="interior",
+    )(half, moving, fixed)
+
+
+def edge_pass(half, z_low, z_high, y_rows, edges, back_table, x_table, grad, planes):
+    grad, part = pl.pallas_call(
+        edge_kernel,
+        in_specs=[SMEM_SPEC] + [VMEM_SPEC] * 9 + [HBM_SPEC, VMEM_SPEC],
+        out_specs=[HBM_SPEC, VMEM_SPEC],
+        out_shape=[GRAD_SHAPE, CTL_SHAPE],
+        scratch_shapes=[
+            pltpu.VMEM((PLANES, NY, 3 * NX), F32),
+            pltpu.VMEM(Z_SHAPE, F32),
+            pltpu.VMEM(Y_SHAPE, F32),
+            pltpu.SemaphoreType.DMA((3,)),
+        ],
+        input_output_aliases={10: 0},
+        compiler_params=EDGE_PARAMS,
+        name="edge",
+    )(half, z_low, z_high, y_rows, *edges, back_table, x_table, grad, planes)
+    return grad, part
 
 
 def hessian_pass(half, ctl, base, grad, front_table, back_table, x_table):
     return pl.pallas_call(
         hessian_kernel,
-        in_specs=[SMEM_SPEC] + [VMEM_SPEC] * 6,
+        in_specs=[SMEM_SPEC] + [VMEM_SPEC] * 2 + [HBM_SPEC] + [VMEM_SPEC] * 3,
         out_specs=[VMEM_SPEC] * 2,
         scratch_shapes=[
+            pltpu.VMEM((3, NZ, NY, NX), F32),
             pltpu.VMEM((4 * KPAD, 3 * NX), BF),
             pltpu.VMEM((ROWS, 3 * NX), F32),
             pltpu.VMEM((PLANES, NY, 3 * NX), F32),
+            pltpu.SemaphoreType.DMA((NZ // KNOT,)),
         ],
         out_shape=[
             jax.ShapeDtypeStruct((CTL, 128), F32),
@@ -338,7 +489,8 @@
     z_high = passed_along(moving[:2], "gz", -1)
     y_rows = swapped(jnp.where(half_id == 0, moving[:, -2:], moving[:, :2]))
 
-    grad, part = first_pass(half, moving, z_low, z_high, fixed, y_rows, back, xt)
+    grad, planes, *edges = interior_pass(half, moving, fixed)
+    grad, part = edge_pass(half, z_low, z_high, y_rows, edges, back, xt, grad, planes)
     b_planes = all_planes(lower, part)
     b = b_planes[CY : 3 * CY]
     part, _ = hessian_pass(half, b_planes, b, grad, front, back, xt)

time: 128 us -> 121 us (0.945)
  local copies, waits for them, and re-layouts: 18 us -> 3.73 us
  Pallas kernels: 27.8 us -> 39 us
  starting transfers between devices: 57.6 us -> 47.7 us
  waiting for transfers between devices: 22.1 us -> 27.7 us
    unnamed x21 -> x9, local copies, waits for them, and re-layouts: 16.7 us -> 2.5 us
    pallas_call x3 -> x4, Pallas kernels: 27.8 us -> 39 us  [the longest x2 23 us: hessian_pass(): pl.pallas_call(hessian_kernel, in_specs=[SMEM_SPEC] + [VMEM_SPEC] * 2 + [...]
    ppermute x4, starting transfers between devices: 13.3 us -> 4.88 us  [swapped(): return lax.ppermute(value, 'gy', [(0, 1), (1, 0)])]
    ppermute x4, waiting for transfers between devices: 9.27 us -> 14.9 us  [swapped(): return lax.ppermute(value, 'gy', [(0, 1), (1, 0)])]
    ppermute x10, starting transfers between devices: 39.7 us -> 38.3 us  [paired(): return lax.ppermute(value, 'gz', [(i, i ^ mask) for i in range(count)])]
  transfers between devices with their start and end apart: 19 -> 19, of which waited for: 14 -> 13; matrix products, arithmetic and copies ran while one was open for 1% -> 1% of each run, Pallas kernels for 0% -> 10%
where the time goes in v4:
time: 121 us
  starting transfers between devices  47.7 us (39%)
  Pallas kernels  39 us (32%)
  waiting for transfers between devices  27.7 us (23%)
  local copies, waits for them, and re-layouts  3.73 us (3%)
  other arithmetic  1.6 us (1%)
    ppermute x10, starting transfers between devices, paired(): return lax.ppermute(value, 'gz', [(i, i ^ mask) for i in range(count)])  38.3 us
    pallas_call x2, Pallas kernels, hessian_pass(): pl.pallas_call(hessian_kernel, in_specs=[SMEM_SPEC] + [VMEM_SPEC] * 2 + [...  23 us
    ppermute x4, waiting for transfers between devices, swapped(): return lax.ppermute(value, 'gy', [(0, 1), (1, 0)])  14.9 us
    ppermute x10, waiting for transfers between devices, paired(): return lax.ppermute(value, 'gz', [(i, i ^ mask) for i in range(count)])  12.8 us
    pallas_call x1, Pallas kernels, interior_pass(): pl.pallas_call(interior_kernel, in_specs=[SMEM_SPEC] + [HBM_SPEC] * 2, ou...  12.4 us
    ppermute x4, starting transfers between devices, swapped(): return lax.ppermute(value, 'gy', [(0, 1), (1, 0)])  4.88 us
    pallas_call x1, Pallas kernels, edge_pass(): pl.pallas_call(edge_kernel, in_specs=[SMEM_SPEC] + [VMEM_SPEC] * 9 + [HBM...  3.63 us
    ppermute x2, starting transfers between devices, passed_along(): lax.ppermute(value, axis, [(source, source + steps) for source in range(i...  2.6 us
  transfers between devices with their start and end apart: 19, of which 13 were waited for; matrix products, arithmetic and copies ran while one was open for 1% of the time, Pallas kernels for 10%

profile of v4, /device:TPU:0, one launch (start us, length us, event | category | flops | bytes accessed | tf_op | source)
XLA Modules:
  0.0 120.6 jit_solution(11371694344181792293)
XLA Ops:
  1.7 1.3 %collective-permute-start = (f32[2,64,512]{2,1,0:T(8,128)S(1)}, f32[2,64,512]{2,1,0:T(8,128)S(1)}, u32[]{:S(2)}, u32[]{:S(2)}) collective-permute-start(f32[2,64,512]{2,1,0:T(8,128)S(1)} %get-tuple-element.35), channel_id=1, source_target_pairs={{0,2},{2,4},{4,6},{6,8},{8,10},{10,12},{12,14},{14,16},{16,18},{18... | collective-permute-start | bytes 786440 | tf_op jit(solution)/shard_map/ppermute | solution.py:441
  3.0 1.3 %collective-permute-start.1 = (f32[2,64,512]{2,1,0:T(8,128)S(1)}, f32[2,64,512]{2,1,0:T(8,128)S(1)}, u32[]{:S(2)}, u32[]{:S(2)}) collective-permute-start(f32[2,64,512]{2,1,0:T(8,128)S(1)} %get-tuple-element.34), channel_id=1, source_target_pairs={{2,0},{4,2},{6,4},{8,6},{10,8},{12,10},{14,12},{16,14},{18,16},{20... | collective-permute-start | bytes 786440 | tf_op jit(solution)/shard_map/ppermute | solution.py:441
  4.3 1.3 %slice_select_fusion = f32[32,2,512]{2,1,0:T(2,128)S(1)} fusion(f32[32,64,512]{2,1,0:T(8,128)} %moving_hbm.1, pred[]{:T(512)S(6)} %eq.9), kind=kLoop, calls=%fused_computation | loop fusion | flops 32768 | bytes 393217 | tf_op jit(solution)/shard_map/jit(_where)/select_n | solution.py:490
  5.6 3.6 %collective-permute-start.2 = (f32[32,2,512]{2,1,0:T(2,128)S(1)}, f32[32,2,512]{2,1,0:T(2,128)S(1)}, u32[]{:S(2)}, u32[]{:S(2)}) collective-permute-start(f32[32,2,512]{2,1,0:T(2,128)S(1)} %slice_select_fusion), channel_id=1, source_target_pairs={{0,1},{1,0},{2,3},{3,2},{4,5},{5,4},{6,7},{7,6},{8,9},{9,8},{10,11... | collective-permute-start | bytes 393224 | tf_op jit(solution)/shard_map/ppermute | solution.py:445
  9.3 12.4 %interior.1 = (f32[3,32,64,512]{3,2,1,0:T(8,128)}, f32[5,64,1536]{2,1,0:T(8,128)S(1)}, f32[4,64,512]{2,1,0:T(8,128)S(1)}, f32[32,8,512]{2,1,0:T(8,128)S(1)}, f32...) custom-call(s32[1]{0:T(128)} %bitcast.half, f32[32,64,512]{2,1,0:T(8,128)} %moving_hbm.1, f32[32,64,512]{2,1,0:T(8,128)} %fixed_hbm.1), custom_call_target="tpu_custom_call" | custom-call | flops 100000000 | bytes 40000000 | tf_op jit(solution)/shard_map/interior/pallas_call | solution.py:379
  21.7 1.3 %copy-done.1 = f32[5,64,1536]{2,1,0:T(8,128)} copy-done((f32[5,64,1536]{2,1,0:T(8,128)}, f32[5,64,1536]{2,1,0:T(8,128)S(1)}, u32[]{:S(2)}) %copy-start.1) | copy-done | bytes 1966104
  22.9 3.6 %edge.1 = (f32[3,32,64,512]{3,2,1,0:T(8,128)}, f32[40,128]{1,0:T(8,128)S(1)}) custom-call(s32[1]{0:T(128)} %bitcast.half, f32[2,64,512]{2,1,0:T(8,128)S(1)} %collective-permute-done.z_low, f32[2,64,512]{2,1,0:T(8,128)S(1)} %collective-permute-done.1.z_high, f32[32,2,512]{2,1,0:T(2,128)S(1)} %collective-permute-done.2.y_rows, ...), custom_call_target="tpu_custom_call", output_to_operand_aliasing={{0}: (10, {})} | custom-call | tf_op jit(solution)/shard_map/edge/pallas_call | solution.py:399
  26.7 5.3 %collective-permute-done.3 = f32[40,128]{1,0:T(8,128)S(1)} collective-permute-done((f32[40,128]{1,0:T(8,128)S(1)}, f32[40,128]{1,0:T(8,128)S(1)}, u32[]{:S(2)}, u32[]{:S(2)}) %collective-permute-start.3) | collective-permute-done | bytes 20512 | tf_op jit(solution)/shard_map/ppermute | solution.py:445
  34.6 6.1 %collective-permute-start.6 = (f32[8,128]{1,0:T(8,128)S(1)}, f32[8,128]{1,0:T(8,128)S(1)}, u32[]{:S(2)}, u32[]{:S(2)}) collective-permute-start(f32[8,128]{1,0:T(8,128)S(1)} %slice_select_fusion.4), channel_id=1, source_target_pairs={{0,2},{2,0},{4,6},{6,4},{8,10},{10,8},{12,14},{14,12},{16,18},{18,... | collective-permute-start | bytes 12296 | tf_op jit(solution)/shard_map/ppermute | solution.py:450
  41.6 11.8 %hessian.2 = (f32[40,128]{1,0:T(8,128)S(1)}, f32[8,128]{1,0:T(8,128)}) custom-call(s32[1]{0:T(128)} %bitcast.half, f32[40,128]{1,0:T(8,128)S(1)} %fusion.3.ctl, f32[16,128]{1,0:T(8,128)S(1)} %slice.144.base, f32[3,32,64,512]{3,2,1,0:T(8,128)} %get-tuple-element.22.grad_hbm, bf16[2,2048,192]{2,1,0:T(8,128)(2,1)} %constant.44.clone.front, ...), custom_call_target="tpu_custom_call" | custom-call | tf_op jit(solution)/shard_map/hessian/pallas_call | solution.py:418
  53.9 4.8 %collective-permute-done.7 = f32[40,128]{1,0:T(8,128)S(1)} collective-permute-done((f32[40,128]{1,0:T(8,128)S(1)}, f32[40,128]{1,0:T(8,128)S(1)}, u32[]{:S(2)}, u32[]{:S(2)}) %collective-permute-start.7) | collective-permute-done | bytes 20512 | tf_op jit(solution)/shard_map/ppermute | solution.py:445
  60.6 4.7 %collective-permute-start.10 = (f32[8,128]{1,0:T(8,128)S(1)}, f32[8,128]{1,0:T(8,128)S(1)}, u32[]{:S(2)}, u32[]{:S(2)}) collective-permute-start(f32[8,128]{1,0:T(8,128)S(1)} %slice_select_fusion.3), channel_id=1, source_target_pairs={{0,2},{2,0},{4,6},{6,4},{8,10},{10,8},{12,14},{14,12},{16,18},{18,... | collective-permute-start | bytes 12296 | tf_op jit(solution)/shard_map/ppermute | solution.py:450
  66.2 11.2 %hessian.3 = (f32[40,128]{1,0:T(8,128)S(1)}, f32[8,128]{1,0:T(8,128)S(1)}) custom-call(s32[1]{0:T(128)} %bitcast.half, f32[40,128]{1,0:T(8,128)S(1)} %fusion.7.ctl, f32[16,128]{1,0:T(8,128)S(1)} %slice.144.base, f32[3,32,64,512]{3,2,1,0:T(8,128)} %get-tuple-element.22.grad_hbm, bf16[2,2048,192]{2,1,0:T(8,128)(2,1)} %constant.44.clone.front, ...), custom_call_target="tpu_custom_call" | custom-call | tf_op jit(solution)/shard_map/hessian/pallas_call | solution.py:418
  78.0 4.8 %collective-permute-done.11 = f32[48,128]{1,0:T(8,128)S(1)} collective-permute-done((f32[48,128]{1,0:T(8,128)S(1)}, f32[48,128]{1,0:T(8,128)S(1)}, u32[]{:S(2)}, u32[]{:S(2)}) %collective-permute-start.11) | collective-permute-done | bytes 24608 | tf_op jit(solution)/shard_map/ppermute | solution.py:445
  84.8 3.3 %collective-permute-start.13 = (f32[8,128]{1,0:T(8,128)S(1)}, f32[8,128]{1,0:T(8,128)S(1)}, u32[]{:S(2)}, u32[]{:S(2)}) collective-permute-start(f32[8,128]{1,0:T(8,128)S(1)} %slice_add_fusion), channel_id=1, source_target_pairs={{0,4},{2,6},{4,0},{6,2},{8,12},{10,14},{12,8},{14,10},{16,20},{18,... | collective-permute-start | bytes 12296 | tf_op jit(solution)/shard_map/ppermute | solution.py:450
  88.1 1.6 %collective-permute-done.13 = f32[8,128]{1,0:T(8,128)S(1)} collective-permute-done((f32[8,128]{1,0:T(8,128)S(1)}, f32[8,128]{1,0:T(8,128)S(1)}, u32[]{:S(2)}, u32[]{:S(2)}) %collective-permute-start.13) | collective-permute-done | bytes 4128 | tf_op jit(solution)/shard_map/ppermute | solution.py:450
  89.7 7.3 %collective-permute-start.15 = (f32[8,128]{1,0:T(8,128)S(1)}, f32[8,128]{1,0:T(8,128)S(1)}, u32[]{:S(2)}, u32[]{:S(2)}) collective-permute-start(f32[8,128]{1,0:T(8,128)S(1)} %add.110), channel_id=1, source_target_pairs={{0,12},{2,14},{4,8},{6,10},{8,4},{10,6},{12,0},{14,2},{16,28},{18,... | collective-permute-start | bytes 12296 | tf_op jit(solution)/shard_map/ppermute | solution.py:450
  97.0 1.6 %collective-permute-done.15 = f32[8,128]{1,0:T(8,128)S(1)} collective-permute-done((f32[8,128]{1,0:T(8,128)S(1)}, f32[8,128]{1,0:T(8,128)S(1)}, u32[]{:S(2)}, u32[]{:S(2)}) %collective-permute-start.15) | collective-permute-done | bytes 4128 | tf_op jit(solution)/shard_map/ppermute | solution.py:450
  98.6 4.8 %collective-permute-start.16 = (f32[8,128]{1,0:T(8,128)S(1)}, f32[8,128]{1,0:T(8,128)S(1)}, u32[]{:S(2)}, u32[]{:S(2)}) collective-permute-start(f32[8,128]{1,0:T(8,128)S(1)} %add.112), channel_id=1, source_target_pairs={{0,16},{2,18},{4,20},{6,22},{8,24},{10,26},{12,28},{14,30},{16,0},... | collective-permute-start | bytes 12296 | tf_op jit(solution)/shard_map/ppermute | solution.py:450
  103.3 1.6 %collective-permute-done.16 = f32[8,128]{1,0:T(8,128)S(1)} collective-permute-done((f32[8,128]{1,0:T(8,128)S(1)}, f32[8,128]{1,0:T(8,128)S(1)}, u32[]{:S(2)}, u32[]{:S(2)}) %collective-permute-start.16) | collective-permute-done | bytes 4128 | tf_op jit(solution)/shard_map/ppermute | solution.py:450
  104.9 6.9 %collective-permute-start.17 = (f32[8,128]{1,0:T(8,128)S(1)}, f32[8,128]{1,0:T(8,128)S(1)}, u32[]{:S(2)}, u32[]{:S(2)}) collective-permute-start(f32[8,128]{1,0:T(8,128)S(1)} %add.113), channel_id=1, source_target_pairs={{0,32},{2,34},{4,36},{6,38},{8,40},{10,42},{12,44},{14,46},{16,48}... | collective-permute-start | bytes 12296 | tf_op jit(solution)/shard_map/ppermute | solution.py:450
  111.9 1.6 %collective-permute-done.17 = f32[8,128]{1,0:T(8,128)S(1)} collective-permute-done((f32[8,128]{1,0:T(8,128)S(1)}, f32[8,128]{1,0:T(8,128)S(1)}, u32[]{:S(2)}, u32[]{:S(2)}) %collective-permute-start.17) | collective-permute-done | bytes 4128 | tf_op jit(solution)/shard_map/ppermute | solution.py:450
  113.5 4.1 %collective-permute-start.18 = (f32[8,128]{1,0:T(8,128)S(1)}, f32[8,128]{1,0:T(8,128)S(1)}, u32[]{:S(2)}, u32[]{:S(2)}) collective-permute-start(f32[8,128]{1,0:T(8,128)S(1)} %add.114), channel_id=1, source_target_pairs={{0,96},{2,98},{4,100},{6,102},{8,104},{10,106},{12,108},{14,110},{... | collective-permute-start | bytes 12296 | tf_op jit(solution)/shard_map/ppermute | solution.py:450
  117.6 1.6 %collective-permute-done.18 = f32[8,128]{1,0:T(8,128)S(1)} collective-permute-done((f32[8,128]{1,0:T(8,128)S(1)}, f32[8,128]{1,0:T(8,128)S(1)}, u32[]{:S(2)}, u32[]{:S(2)}) %collective-permute-start.18) | collective-permute-done | bytes 4128 | tf_op jit(solution)/shard_map/ppermute | solution.py:450
  (58 shorter events, 11.9 us)
Async XLA Ops:
  1.7 21.2 %collective-permute-start = (f32[2,64,512]{2,1,0:T(8,128)S(1)}, f32[2,64,512]{2,1,0:T(8,128)S(1)}, u32[]{:S(2)}, u32[]{:S(2)}) collective-permute-start(f32[2,64,512]{2,1,0:T(8,128)S(1)} %get-tuple-element.35), channel_id=1, source_target_pairs={{0,2},{2,4},{4,6},{6,8},{8,10},{10,12},{12,14},{14,16},{16,18},{18... | collective-permute-start | bytes 786440 | tf_op jit(solution)/shard_map/ppermute | solution.py:441
  3.0 19.9 %collective-permute-start.1 = (f32[2,64,512]{2,1,0:T(8,128)S(1)}, f32[2,64,512]{2,1,0:T(8,128)S(1)}, u32[]{:S(2)}, u32[]{:S(2)}) collective-permute-start(f32[2,64,512]{2,1,0:T(8,128)S(1)} %get-tuple-element.34), channel_id=1, source_target_pairs={{2,0},{4,2},{6,4},{8,6},{10,8},{12,10},{14,12},{16,14},{18,16},{20... | collective-permute-start | bytes 786440 | tf_op jit(solution)/shard_map/ppermute | solution.py:441
  5.6 17.3 %collective-permute-start.2 = (f32[32,2,512]{2,1,0:T(2,128)S(1)}, f32[32,2,512]{2,1,0:T(2,128)S(1)}, u32[]{:S(2)}, u32[]{:S(2)}) collective-permute-start(f32[32,2,512]{2,1,0:T(2,128)S(1)} %slice_select_fusion), channel_id=1, source_target_pairs={{0,1},{1,0},{2,3},{3,2},{4,5},{5,4},{6,7},{7,6},{8,9},{9,8},{10,11... | collective-permute-start | bytes 393224 | tf_op jit(solution)/shard_map/ppermute | solution.py:445
  9.3 13.7 %copy-start = (bf16[256,1536]{1,0:T(8,128)(2,1)S(1)}, bf16[256,1536]{1,0:T(8,128)(2,1)}, u32[]{:S(2)}) copy-start(bf16[256,1536]{1,0:T(8,128)(2,1)} %constant.46.clone.xt) | copy-start | bytes 2359300
  9.3 13.7 %copy-start.2 = (bf16[2,80,320]{2,1,0:T(8,128)(2,1)S(1)}, bf16[2,80,320]{2,1,0:T(8,128)(2,1)}, u32[]{:S(2)}) copy-start(bf16[2,80,320]{2,1,0:T(8,128)(2,1)} %constant.45.clone.back) | copy-start | bytes 307204
  21.6 1.3 %copy-start.1 = (f32[5,64,1536]{2,1,0:T(8,128)}, f32[5,64,1536]{2,1,0:T(8,128)S(1)}, u32[]{:S(2)}) copy-start(f32[5,64,1536]{2,1,0:T(8,128)S(1)} %get-tuple-element.20.planes_in) | copy-start | bytes 5898244
  26.6 5.4 %collective-permute-start.3 = (f32[40,128]{1,0:T(8,128)S(1)}, f32[40,128]{1,0:T(8,128)S(1)}, u32[]{:S(2)}, u32[]{:S(2)}) collective-permute-start(f32[40,128]{1,0:T(8,128)S(1)} %get-tuple-element.21), channel_id=1, source_target_pairs={{0,1},{1,0},{2,3},{3,2},{4,5},{5,4},{6,7},{7,6},{8,9},{9,8},{10,11... | collective-permute-start | bytes 61448 | tf_op jit(solution)/shard_map/ppermute | solution.py:445
  32.0 1.9 %collective-permute-start.4 = (f32[40,128]{1,0:T(8,128)S(1)}, f32[40,128]{1,0:T(8,128)S(1)}, u32[]{:S(2)}, u32[]{:S(2)}) collective-permute-start(f32[40,128]{1,0:T(8,128)S(1)} %add.100), channel_id=1, source_target_pairs={{0,2},{2,0},{4,6},{6,4},{8,10},{10,8},{12,14},{14,12},{16,18},{18,... | collective-permute-start | bytes 61448 | tf_op jit(solution)/shard_map/ppermute | solution.py:450
  33.9 0.7 collective-permute-start.5
  34.6 6.9 %collective-permute-start.6 = (f32[8,128]{1,0:T(8,128)S(1)}, f32[8,128]{1,0:T(8,128)S(1)}, u32[]{:S(2)}, u32[]{:S(2)}) collective-permute-start(f32[8,128]{1,0:T(8,128)S(1)} %slice_select_fusion.4), channel_id=1, source_target_pairs={{0,2},{2,0},{4,6},{6,4},{8,10},{10,8},{12,14},{14,12},{16,18},{18,... | collective-permute-start | bytes 12296 | tf_op jit(solution)/shard_map/ppermute | solution.py:450
  53.3 5.4 %collective-permute-start.7 = (f32[40,128]{1,0:T(8,128)S(1)}, f32[40,128]{1,0:T(8,128)S(1)}, u32[]{:S(2)}, u32[]{:S(2)}) collective-permute-start(f32[40,128]{1,0:T(8,128)S(1)} %get-tuple-element.23), channel_id=1, source_target_pairs={{0,1},{1,0},{2,3},{3,2},{4,5},{5,4},{6,7},{7,6},{8,9},{9,8},{10,11... | collective-permute-start | bytes 61448 | tf_op jit(solution)/shard_map/ppermute | solution.py:445
  58.7 1.2 collective-permute-start.8
  59.9 0.7 collective-permute-start.9
  60.6 5.5 %collective-permute-start.10 = (f32[8,128]{1,0:T(8,128)S(1)}, f32[8,128]{1,0:T(8,128)S(1)}, u32[]{:S(2)}, u32[]{:S(2)}) collective-permute-start(f32[8,128]{1,0:T(8,128)S(1)} %slice_select_fusion.3), channel_id=1, source_target_pairs={{0,2},{2,0},{4,6},{6,4},{8,10},{10,8},{12,14},{14,12},{16,18},{18,... | collective-permute-start | bytes 12296 | tf_op jit(solution)/shard_map/ppermute | solution.py:450
  77.5 5.4 %collective-permute-start.11 = (f32[48,128]{1,0:T(8,128)S(1)}, f32[48,128]{1,0:T(8,128)S(1)}, u32[]{:S(2)}, u32[]{:S(2)}) collective-permute-start(f32[48,128]{1,0:T(8,128)S(1)} %constant_dynamic-update-slice_fusion), channel_id=1, source_target_pairs={{0,1},{1,0},{2,3},{3,2},{4,5},{5,4},{6,7},{7,6},{8,9},{9,8},{10,11... | collective-permute-start | bytes 73736 | tf_op jit(solution)/shard_map/ppermute | solution.py:445
  82.9 1.2 collective-permute-start.12
  84.1 5.6 %collective-permute-start.14 = (f32[24,128]{1,0:T(8,128)S(1)}, f32[24,128]{1,0:T(8,128)S(1)}, u32[]{:S(2)}, u32[]{:S(2)}) collective-permute-start(f32[24,128]{1,0:T(8,128)S(1)} %fusion.21), channel_id=1, source_target_pairs={{2,4},{6,8},{10,12},{14,16},{18,20},{22,24},{26,28},{30,32},{34,36... | collective-permute-start | bytes 36872 | tf_op jit(solution)/shard_map/ppermute | solution.py:456
  84.8 4.9 %collective-permute-start.13 = (f32[8,128]{1,0:T(8,128)S(1)}, f32[8,128]{1,0:T(8,128)S(1)}, u32[]{:S(2)}, u32[]{:S(2)}) collective-permute-start(f32[8,128]{1,0:T(8,128)S(1)} %slice_add_fusion), channel_id=1, source_target_pairs={{0,4},{2,6},{4,0},{6,2},{8,12},{10,14},{12,8},{14,10},{16,20},{18,... | collective-permute-start | bytes 12296 | tf_op jit(solution)/shard_map/ppermute | solution.py:450
  89.7 8.9 %collective-permute-start.15 = (f32[8,128]{1,0:T(8,128)S(1)}, f32[8,128]{1,0:T(8,128)S(1)}, u32[]{:S(2)}, u32[]{:S(2)}) collective-permute-start(f32[8,128]{1,0:T(8,128)S(1)} %add.110), channel_id=1, source_target_pairs={{0,12},{2,14},{4,8},{6,10},{8,4},{10,6},{12,0},{14,2},{16,28},{18,... | collective-permute-start | bytes 12296 | tf_op jit(solution)/shard_map/ppermute | solution.py:450
  98.6 6.3 %collective-permute-start.16 = (f32[8,128]{1,0:T(8,128)S(1)}, f32[8,128]{1,0:T(8,128)S(1)}, u32[]{:S(2)}, u32[]{:S(2)}) collective-permute-start(f32[8,128]{1,0:T(8,128)S(1)} %add.112), channel_id=1, source_target_pairs={{0,16},{2,18},{4,20},{6,22},{8,24},{10,26},{12,28},{14,30},{16,0},... | collective-permute-start | bytes 12296 | tf_op jit(solution)/shard_map/ppermute | solution.py:450
  104.9 8.5 %collective-permute-start.17 = (f32[8,128]{1,0:T(8,128)S(1)}, f32[8,128]{1,0:T(8,128)S(1)}, u32[]{:S(2)}, u32[]{:S(2)}) collective-permute-start(f32[8,128]{1,0:T(8,128)S(1)} %add.113), channel_id=1, source_target_pairs={{0,32},{2,34},{4,36},{6,38},{8,40},{10,42},{12,44},{14,46},{16,48}... | collective-permute-start | bytes 12296 | tf_op jit(solution)/shard_map/ppermute | solution.py:450
  113.5 5.7 %collective-permute-start.18 = (f32[8,128]{1,0:T(8,128)S(1)}, f32[8,128]{1,0:T(8,128)S(1)}, u32[]{:S(2)}, u32[]{:S(2)}) collective-permute-start(f32[8,128]{1,0:T(8,128)S(1)} %add.114), channel_id=1, source_target_pairs={{0,96},{2,98},{4,100},{6,102},{8,104},{10,106},{12,108},{14,110},{... | collective-permute-start | bytes 12296 | tf_op jit(solution)/shard_map/ppermute | solution.py:450

commit v5 on v4

--- a/solution.py
+++ b/solution.py
@@ -294,11 +294,13 @@
 ):
     copies = []
     for block in range(NZ // KNOT):
-        part = pl.ds(block * KNOT, KNOT)
-        copies.append(
-            pltpu.make_async_copy(grad_hbm.at[:, part], grad.at[:, part], sems.at[block])
-        )
-        copies[-1].start()
+        for y in range(2):
+            part = (slice(None), pl.ds(block * KNOT, KNOT), pl.ds(y * NY // 2, NY // 2))
+            copies.append(
+                pltpu.make_async_copy(grad_hbm.at[part], grad.at[part], sems.at[block, y])
+            )
+    for copy in copies:
+        copy.start()
     high, low = halves_of(ctl[...])
     first, second = xt[:128], xt[128:]
     value = jnp.dot(high, first, preferred_element_type=F32)
@@ -322,9 +324,10 @@
                 weight = weight + slopes[c] * field[rows, at]
             return weight, carry + weight * weight
 
-        copies[block].wait()
         strip = block_terms(block, grad, weight_at, planes)
-        square = lax.fori_loop(0, NY // 8, strip, square)
+        for y in range(2):
+            copies[2 * block + y].wait()
+            square = lax.fori_loop(y * NY // 16, (y + 1) * NY // 16, strip, square)
 
     scale = data_weight / 144.0
     whole = ctl[...]
@@ -360,8 +363,8 @@
 
 VMEM_SPEC = pl.BlockSpec(memory_space=pltpu.VMEM)
 SMEM_SPEC = pl.BlockSpec(memory_space=pltpu.SMEM)
-PARAMS = pltpu.CompilerParams(vmem_limit_bytes=52 * 1024 * 1024)
-EDGE_PARAMS = pltpu.CompilerParams(vmem_limit_bytes=50 * 1024 * 1024)
+PARAMS = pltpu.CompilerParams(vmem_limit_bytes=48 * 1024 * 1024)
+EDGE_PARAMS = pltpu.CompilerParams(vmem_limit_bytes=47 * 1024 * 1024)
 INTERIOR_MIB = 48
 
 
@@ -424,7 +427,7 @@
             pltpu.VMEM((4 * KPAD, 3 * NX), BF),
             pltpu.VMEM((ROWS, 3 * NX), F32),
             pltpu.VMEM((PLANES, NY, 3 * NX), F32),
-            pltpu.SemaphoreType.DMA((NZ // KNOT,)),
+            pltpu.SemaphoreType.DMA((NZ // KNOT, 2)),
         ],
         out_shape=[
             jax.ShapeDtypeStruct((CTL, 128), F32),
@@ -448,6 +451,10 @@
 def paired(value, mask):
     count = lax.axis_size("gz")
     return lax.ppermute(value, "gz", [(i, i ^ mask) for i in range(count)])
+
+
+def stage(value, *masks):
+    return value + sum(paired(value, mask) for mask in masks)
 
 
 def outer_paired(value):
@@ -503,10 +510,9 @@
     seven = pair_sum(lower, both[:CTL], other[:CTL])
     sums = both[CTL:] + other[CTL:]
     three = outer_terms(lower, seven)
-    sums = sums + paired(sums, 2)
+    sums = stage(sums, 2, 4, 6)
     sums, three = lax.optimization_barrier((sums, three))
-    for mask in (6, 8, 16, 48):
-        sums = sums + paired(sums, mask)
+    sums = stage(stage(sums, 8), 16, 32, 48)
     v_low = seven[CY : 3 * CY] + three[CY:]
     v_high = seven[3 * CY : 5 * CY] + jnp.pad(three[:CY], ((CY, 0), (0, 0)))
     v = jnp.where(lower, v_low, v_high)

time: 121 us -> 114 us (0.942)
  Pallas kernels: 39 us -> 32.5 us
  waiting for transfers between devices: 27.7 us -> 30.1 us
  starting transfers between devices: 47.7 us -> 46.3 us
  local copies, waits for them, and re-layouts: 3.73 us -> 2.48 us
    pallas_call x2, Pallas kernels: 23 us -> 18.1 us  [hessian_pass(): pl.pallas_call(hessian_kernel, in_specs=[SMEM_SPEC] + [VMEM_SPEC] * 2 + [...]
    ppermute x10 -> x12, waiting for transfers between devices: 12.8 us -> 15.4 us  [paired(): return lax.ppermute(value, 'gz', [(i, i ^ mask) for i in range(count)])]
    ppermute x10 -> x12, starting transfers between devices: 38.3 us -> 36.7 us  [paired(): return lax.ppermute(value, 'gz', [(i, i ^ mask) for i in range(count)])]
    pallas_call x1, Pallas kernels: 3.63 us -> 2.03 us  [edge_pass(): pl.pallas_call(edge_kernel, in_specs=[SMEM_SPEC] + [VMEM_SPEC] * 9 + [HBM...]
    unnamed x9, local copies, waits for them, and re-layouts: 2.5 us -> 1.25 us
  transfers between devices with their start and end apart: 19 -> 21, of which waited for: 13 -> 13; matrix products, arithmetic and copies ran while one was open for 1% -> 1% of each run, Pallas kernels for 10% -> 11%
where the time goes in v5:
time: 114 us
  starting transfers between devices  46.3 us (41%)
  Pallas kernels  32.5 us (29%)
  waiting for transfers between devices  30.1 us (26%)
  local copies, waits for them, and re-layouts  2.48 us (2%)
  other arithmetic  1.59 us (1%)
    ppermute x12, starting transfers between devices, paired(): return lax.ppermute(value, 'gz', [(i, i ^ mask) for i in range(count)])  36.7 us
    pallas_call x2, Pallas kernels, hessian_pass(): pl.pallas_call(hessian_kernel, in_specs=[SMEM_SPEC] + [VMEM_SPEC] * 2 + [...  18.1 us
    ppermute x12, waiting for transfers between devices, paired(): return lax.ppermute(value, 'gz', [(i, i ^ mask) for i in range(count)])  15.4 us
    ppermute x4, waiting for transfers between devices, swapped(): return lax.ppermute(value, 'gy', [(0, 1), (1, 0)])  14.8 us
    pallas_call x1, Pallas kernels, interior_pass(): pl.pallas_call(interior_kernel, in_specs=[SMEM_SPEC] + [HBM_SPEC] * 2, ou...  12.4 us
    ppermute x4, starting transfers between devices, swapped(): return lax.ppermute(value, 'gy', [(0, 1), (1, 0)])  5.01 us
    ppermute x2, starting transfers between devices, passed_along(): lax.ppermute(value, axis, [(source, source + steps) for source in range(i...  2.6 us
  transfers between devices with their start and end apart: 21, of which 13 were waited for; matrix products, arithmetic and copies ran while one was open for 1% of the time, Pallas kernels for 11%

profile of v5, /device:TPU:0, one launch (start us, length us, event | category | flops | bytes accessed | tf_op | source)
XLA Modules:
  0.0 113.9 jit_solution(5386765227277130312)
XLA Ops:
  1.7 1.3 %collective-permute-start = (f32[2,64,512]{2,1,0:T(8,128)S(1)}, f32[2,64,512]{2,1,0:T(8,128)S(1)}, u32[]{:S(2)}, u32[]{:S(2)}) collective-permute-start(f32[2,64,512]{2,1,0:T(8,128)S(1)} %get-tuple-element.35), channel_id=1, source_target_pairs={{0,2},{2,4},{4,6},{6,8},{8,10},{10,12},{12,14},{14,16},{16,18},{18... | collective-permute-start | bytes 786440 | tf_op jit(solution)/shard_map/ppermute | solution.py:444
  3.0 1.3 %collective-permute-start.1 = (f32[2,64,512]{2,1,0:T(8,128)S(1)}, f32[2,64,512]{2,1,0:T(8,128)S(1)}, u32[]{:S(2)}, u32[]{:S(2)}) collective-permute-start(f32[2,64,512]{2,1,0:T(8,128)S(1)} %get-tuple-element.34), channel_id=1, source_target_pairs={{2,0},{4,2},{6,4},{8,6},{10,8},{12,10},{14,12},{16,14},{18,16},{20... | collective-permute-start | bytes 786440 | tf_op jit(solution)/shard_map/ppermute | solution.py:444
  4.3 1.3 %slice_select_fusion = f32[32,2,512]{2,1,0:T(2,128)S(1)} fusion(f32[32,64,512]{2,1,0:T(8,128)} %moving_hbm.1, pred[]{:T(512)S(6)} %eq.9), kind=kLoop, calls=%fused_computation | loop fusion | flops 32768 | bytes 393217 | tf_op jit(solution)/shard_map/jit(_where)/select_n | solution.py:497
  5.6 3.6 %collective-permute-start.2 = (f32[32,2,512]{2,1,0:T(2,128)S(1)}, f32[32,2,512]{2,1,0:T(2,128)S(1)}, u32[]{:S(2)}, u32[]{:S(2)}) collective-permute-start(f32[32,2,512]{2,1,0:T(2,128)S(1)} %slice_select_fusion), channel_id=1, source_target_pairs={{0,1},{1,0},{2,3},{3,2},{4,5},{5,4},{6,7},{7,6},{8,9},{9,8},{10,11... | collective-permute-start | bytes 393224 | tf_op jit(solution)/shard_map/ppermute | solution.py:448
  9.3 12.4 %interior.1 = (f32[3,32,64,512]{3,2,1,0:T(8,128)}, f32[5,64,1536]{2,1,0:T(8,128)S(1)}, f32[4,64,512]{2,1,0:T(8,128)S(1)}, f32[32,8,512]{2,1,0:T(8,128)S(1)}, f32...) custom-call(s32[1]{0:T(128)} %bitcast.half, f32[32,64,512]{2,1,0:T(8,128)} %moving_hbm.1, f32[32,64,512]{2,1,0:T(8,128)} %fixed_hbm.1), custom_call_target="tpu_custom_call" | custom-call | flops 100000000 | bytes 40000000 | tf_op jit(solution)/shard_map/interior/pallas_call | solution.py:382
  21.7 2.0 %edge.1 = (f32[3,32,64,512]{3,2,1,0:T(8,128)}, f32[40,128]{1,0:T(8,128)S(1)}) custom-call(s32[1]{0:T(128)} %bitcast.half, f32[2,64,512]{2,1,0:T(8,128)S(1)} %collective-permute-done.z_low, f32[2,64,512]{2,1,0:T(8,128)S(1)} %collective-permute-done.1.z_high, f32[32,2,512]{2,1,0:T(2,128)S(1)} %collective-permute-done.2.y_rows, ...), custom_call_target="tpu_custom_call", output_to_operand_aliasing={{0}: (10, {})} | custom-call | tf_op jit(solution)/shard_map/edge/pallas_call | solution.py:402
  23.9 5.2 %collective-permute-done.3 = f32[40,128]{1,0:T(8,128)S(1)} collective-permute-done((f32[40,128]{1,0:T(8,128)S(1)}, f32[40,128]{1,0:T(8,128)S(1)}, u32[]{:S(2)}, u32[]{:S(2)}) %collective-permute-start.3) | collective-permute-done | bytes 20512 | tf_op jit(solution)/shard_map/ppermute | solution.py:448
  31.7 6.1 %collective-permute-start.6 = (f32[8,128]{1,0:T(8,128)S(1)}, f32[8,128]{1,0:T(8,128)S(1)}, u32[]{:S(2)}, u32[]{:S(2)}) collective-permute-start(f32[8,128]{1,0:T(8,128)S(1)} %slice_select_fusion.4), channel_id=1, source_target_pairs={{0,2},{2,0},{4,6},{6,4},{8,10},{10,8},{12,14},{14,12},{16,18},{18,... | collective-permute-start | bytes 12296 | tf_op jit(solution)/shard_map/ppermute | solution.py:453
  38.7 9.3 %hessian.2 = (f32[40,128]{1,0:T(8,128)S(1)}, f32[8,128]{1,0:T(8,128)}) custom-call(s32[1]{0:T(128)} %bitcast.half, f32[40,128]{1,0:T(8,128)S(1)} %fusion.3.ctl, f32[16,128]{1,0:T(8,128)S(1)} %slice.144.base, f32[3,32,64,512]{3,2,1,0:T(8,128)} %get-tuple-element.22.grad_hbm, bf16[2,2048,192]{2,1,0:T(8,128)(2,1)S(1)} %copy-done, ...), custom_call_target="tpu_custom_call" | custom-call | tf_op jit(solution)/shard_map/hessian/pallas_call | solution.py:421
  48.7 4.7 %collective-permute-done.7 = f32[40,128]{1,0:T(8,128)S(1)} collective-permute-done((f32[40,128]{1,0:T(8,128)S(1)}, f32[40,128]{1,0:T(8,128)S(1)}, u32[]{:S(2)}, u32[]{:S(2)}) %collective-permute-start.7) | collective-permute-done | bytes 20512 | tf_op jit(solution)/shard_map/ppermute | solution.py:448
  53.4 1.2 %collective-permute-done.8 = f32[40,128]{1,0:T(8,128)S(1)} collective-permute-done((f32[40,128]{1,0:T(8,128)S(1)}, f32[40,128]{1,0:T(8,128)S(1)}, u32[]{:S(2)}, u32[]{:S(2)}) %collective-permute-start.8) | collective-permute-done | bytes 20512 | tf_op jit(solution)/shard_map/ppermute | solution.py:453
  55.3 4.7 %collective-permute-start.10 = (f32[8,128]{1,0:T(8,128)S(1)}, f32[8,128]{1,0:T(8,128)S(1)}, u32[]{:S(2)}, u32[]{:S(2)}) collective-permute-start(f32[8,128]{1,0:T(8,128)S(1)} %slice_select_fusion.3), channel_id=1, source_target_pairs={{0,2},{2,0},{4,6},{6,4},{8,10},{10,8},{12,14},{14,12},{16,18},{18,... | collective-permute-start | bytes 12296 | tf_op jit(solution)/shard_map/ppermute | solution.py:453
  60.9 8.8 %hessian.3 = (f32[40,128]{1,0:T(8,128)S(1)}, f32[8,128]{1,0:T(8,128)S(1)}) custom-call(s32[1]{0:T(128)} %bitcast.half, f32[40,128]{1,0:T(8,128)S(1)} %fusion.7.ctl, f32[16,128]{1,0:T(8,128)S(1)} %slice.144.base, f32[3,32,64,512]{3,2,1,0:T(8,128)} %get-tuple-element.22.grad_hbm, bf16[2,2048,192]{2,1,0:T(8,128)(2,1)S(1)} %copy-done, ...), custom_call_target="tpu_custom_call" | custom-call | tf_op jit(solution)/shard_map/hessian/pallas_call | solution.py:421
  70.3 4.8 %collective-permute-done.11 = f32[48,128]{1,0:T(8,128)S(1)} collective-permute-done((f32[48,128]{1,0:T(8,128)S(1)}, f32[48,128]{1,0:T(8,128)S(1)}, u32[]{:S(2)}, u32[]{:S(2)}) %collective-permute-start.11) | collective-permute-done | bytes 24608 | tf_op jit(solution)/shard_map/ppermute | solution.py:448
  75.1 1.2 %collective-permute-done.12 = f32[48,128]{1,0:T(8,128)S(1)} collective-permute-done((f32[48,128]{1,0:T(8,128)S(1)}, f32[48,128]{1,0:T(8,128)S(1)}, u32[]{:S(2)}, u32[]{:S(2)}) %collective-permute-start.12) | collective-permute-done | bytes 24608 | tf_op jit(solution)/shard_map/ppermute | solution.py:453
  76.3 2.0 %collective-permute-start.13 = (f32[8,128]{1,0:T(8,128)S(1)}, f32[8,128]{1,0:T(8,128)S(1)}, u32[]{:S(2)}, u32[]{:S(2)}) collective-permute-start(f32[8,128]{1,0:T(8,128)S(1)} %slice_add_fusion), channel_id=1, source_target_pairs={{0,4},{2,6},{4,0},{6,2},{8,12},{10,14},{12,8},{14,10},{16,20},{18,... | collective-permute-start | bytes 12296 | tf_op jit(solution)/shard_map/ppermute | solution.py:453
  78.3 6.8 %collective-permute-start.14 = (f32[8,128]{1,0:T(8,128)S(1)}, f32[8,128]{1,0:T(8,128)S(1)}, u32[]{:S(2)}, u32[]{:S(2)}) collective-permute-start(f32[8,128]{1,0:T(8,128)S(1)} %slice_add_fusion), channel_id=1, source_target_pairs={{0,8},{2,10},{4,12},{6,14},{8,0},{10,2},{12,4},{14,6},{16,24},{18,... | collective-permute-start | bytes 12296 | tf_op jit(solution)/shard_map/ppermute | solution.py:453
  86.7 3.2 %collective-permute-done.15 = f32[8,128]{1,0:T(8,128)S(1)} collective-permute-done((f32[8,128]{1,0:T(8,128)S(1)}, f32[8,128]{1,0:T(8,128)S(1)}, u32[]{:S(2)}, u32[]{:S(2)}) %collective-permute-start.15) | collective-permute-done | bytes 4128 | tf_op jit(solution)/shard_map/ppermute | solution.py:453
  89.9 5.6 %collective-permute-start.17 = (f32[8,128]{1,0:T(8,128)S(1)}, f32[8,128]{1,0:T(8,128)S(1)}, u32[]{:S(2)}, u32[]{:S(2)}) collective-permute-start(f32[8,128]{1,0:T(8,128)S(1)} %add_add_fusion.1), channel_id=1, source_target_pairs={{0,16},{2,18},{4,20},{6,22},{8,24},{10,26},{12,28},{14,30},{16,0},... | collective-permute-start | bytes 12296 | tf_op jit(solution)/shard_map/ppermute | solution.py:453
  95.5 1.6 %collective-permute-done.17 = f32[8,128]{1,0:T(8,128)S(1)} collective-permute-done((f32[8,128]{1,0:T(8,128)S(1)}, f32[8,128]{1,0:T(8,128)S(1)}, u32[]{:S(2)}, u32[]{:S(2)}) %collective-permute-start.17) | collective-permute-done | bytes 4128 | tf_op jit(solution)/shard_map/ppermute | solution.py:453
  97.1 6.9 %collective-permute-start.18 = (f32[8,128]{1,0:T(8,128)S(1)}, f32[8,128]{1,0:T(8,128)S(1)}, u32[]{:S(2)}, u32[]{:S(2)}) collective-permute-start(f32[8,128]{1,0:T(8,128)S(1)} %add.120), channel_id=1, source_target_pairs={{0,32},{2,34},{4,36},{6,38},{8,40},{10,42},{12,44},{14,46},{16,48}... | collective-permute-start | bytes 12296 | tf_op jit(solution)/shard_map/ppermute | solution.py:453
  104.0 3.6 %collective-permute-start.19 = (f32[8,128]{1,0:T(8,128)S(1)}, f32[8,128]{1,0:T(8,128)S(1)}, u32[]{:S(2)}, u32[]{:S(2)}) collective-permute-start(f32[8,128]{1,0:T(8,128)S(1)} %add.120), channel_id=1, source_target_pairs={{0,64},{2,66},{4,68},{6,70},{8,72},{10,74},{12,76},{14,78},{16,80}... | collective-permute-start | bytes 12296 | tf_op jit(solution)/shard_map/ppermute | solution.py:453
  107.6 1.6 %collective-permute-done.19 = f32[8,128]{1,0:T(8,128)S(1)} collective-permute-done((f32[8,128]{1,0:T(8,128)S(1)}, f32[8,128]{1,0:T(8,128)S(1)}, u32[]{:S(2)}, u32[]{:S(2)}) %collective-permute-start.19) | collective-permute-done | bytes 4128 | tf_op jit(solution)/shard_map/ppermute | solution.py:453
  109.2 3.2 %collective-permute-done.20 = f32[8,128]{1,0:T(8,128)S(1)} collective-permute-done((f32[8,128]{1,0:T(8,128)S(1)}, f32[8,128]{1,0:T(8,128)S(1)}, u32[]{:S(2)}, u32[]{:S(2)}) %collective-permute-start.20) | collective-permute-done | bytes 4128 | tf_op jit(solution)/shard_map/ppermute | solution.py:453
  (60 shorter events, 10.6 us)
Async XLA Ops:
  1.7 20.0 %collective-permute-start = (f32[2,64,512]{2,1,0:T(8,128)S(1)}, f32[2,64,512]{2,1,0:T(8,128)S(1)}, u32[]{:S(2)}, u32[]{:S(2)}) collective-permute-start(f32[2,64,512]{2,1,0:T(8,128)S(1)} %get-tuple-element.35), channel_id=1, source_target_pairs={{0,2},{2,4},{4,6},{6,8},{8,10},{10,12},{12,14},{14,16},{16,18},{18... | collective-permute-start | bytes 786440 | tf_op jit(solution)/shard_map/ppermute | solution.py:444
  3.0 18.7 %collective-permute-start.1 = (f32[2,64,512]{2,1,0:T(8,128)S(1)}, f32[2,64,512]{2,1,0:T(8,128)S(1)}, u32[]{:S(2)}, u32[]{:S(2)}) collective-permute-start(f32[2,64,512]{2,1,0:T(8,128)S(1)} %get-tuple-element.34), channel_id=1, source_target_pairs={{2,0},{4,2},{6,4},{8,6},{10,8},{12,10},{14,12},{16,14},{18,16},{20... | collective-permute-start | bytes 786440 | tf_op jit(solution)/shard_map/ppermute | solution.py:444
  5.6 16.0 %collective-permute-start.2 = (f32[32,2,512]{2,1,0:T(2,128)S(1)}, f32[32,2,512]{2,1,0:T(2,128)S(1)}, u32[]{:S(2)}, u32[]{:S(2)}) collective-permute-start(f32[32,2,512]{2,1,0:T(2,128)S(1)} %slice_select_fusion), channel_id=1, source_target_pairs={{0,1},{1,0},{2,3},{3,2},{4,5},{5,4},{6,7},{7,6},{8,9},{9,8},{10,11... | collective-permute-start | bytes 393224 | tf_op jit(solution)/shard_map/ppermute | solution.py:448
  9.3 12.4 %copy-start.1 = (bf16[256,1536]{1,0:T(8,128)(2,1)S(1)}, bf16[256,1536]{1,0:T(8,128)(2,1)}, u32[]{:S(2)}) copy-start(bf16[256,1536]{1,0:T(8,128)(2,1)} %constant.46.clone.xt) | copy-start | bytes 2359300
  9.3 12.4 %copy-start.2 = (bf16[2,80,320]{2,1,0:T(8,128)(2,1)S(1)}, bf16[2,80,320]{2,1,0:T(8,128)(2,1)}, u32[]{:S(2)}) copy-start(bf16[2,80,320]{2,1,0:T(8,128)(2,1)} %constant.45.clone.back) | copy-start | bytes 307204
  21.7 17.0 %copy-start = (bf16[2,2048,192]{2,1,0:T(8,128)(2,1)S(1)}, bf16[2,2048,192]{2,1,0:T(8,128)(2,1)}, u32[]{:S(2)}) copy-start(bf16[2,2048,192]{2,1,0:T(8,128)(2,1)} %constant.44.clone.front) | copy-start | bytes 4718596
  23.8 5.4 %collective-permute-start.3 = (f32[40,128]{1,0:T(8,128)S(1)}, f32[40,128]{1,0:T(8,128)S(1)}, u32[]{:S(2)}, u32[]{:S(2)}) collective-permute-start(f32[40,128]{1,0:T(8,128)S(1)} %get-tuple-element.21), channel_id=1, source_target_pairs={{0,1},{1,0},{2,3},{3,2},{4,5},{5,4},{6,7},{7,6},{8,9},{9,8},{10,11... | collective-permute-start | bytes 61448 | tf_op jit(solution)/shard_map/ppermute | solution.py:448
  29.1 1.9 %collective-permute-start.4 = (f32[40,128]{1,0:T(8,128)S(1)}, f32[40,128]{1,0:T(8,128)S(1)}, u32[]{:S(2)}, u32[]{:S(2)}) collective-permute-start(f32[40,128]{1,0:T(8,128)S(1)} %add.106), channel_id=1, source_target_pairs={{0,2},{2,0},{4,6},{6,4},{8,10},{10,8},{12,14},{14,12},{16,18},{18,... | collective-permute-start | bytes 61448 | tf_op jit(solution)/shard_map/ppermute | solution.py:453
  31.0 0.7 collective-permute-start.5
  31.7 6.9 %collective-permute-start.6 = (f32[8,128]{1,0:T(8,128)S(1)}, f32[8,128]{1,0:T(8,128)S(1)}, u32[]{:S(2)}, u32[]{:S(2)}) collective-permute-start(f32[8,128]{1,0:T(8,128)S(1)} %slice_select_fusion.4), channel_id=1, source_target_pairs={{0,2},{2,0},{4,6},{6,4},{8,10},{10,8},{12,14},{14,12},{16,18},{18,... | collective-permute-start | bytes 12296 | tf_op jit(solution)/shard_map/ppermute | solution.py:453
  48.1 5.4 %collective-permute-start.7 = (f32[40,128]{1,0:T(8,128)S(1)}, f32[40,128]{1,0:T(8,128)S(1)}, u32[]{:S(2)}, u32[]{:S(2)}) collective-permute-start(f32[40,128]{1,0:T(8,128)S(1)} %get-tuple-element.23), channel_id=1, source_target_pairs={{0,1},{1,0},{2,3},{3,2},{4,5},{5,4},{6,7},{7,6},{8,9},{9,8},{10,11... | collective-permute-start | bytes 61448 | tf_op jit(solution)/shard_map/ppermute | solution.py:448
  53.4 1.2 %collective-permute-start.8 = (f32[40,128]{1,0:T(8,128)S(1)}, f32[40,128]{1,0:T(8,128)S(1)}, u32[]{:S(2)}, u32[]{:S(2)}) collective-permute-start(f32[40,128]{1,0:T(8,128)S(1)} %add.110), channel_id=1, source_target_pairs={{0,2},{2,0},{4,6},{6,4},{8,10},{10,8},{12,14},{14,12},{16,18},{18,... | collective-permute-start | bytes 61448 | tf_op jit(solution)/shard_map/ppermute | solution.py:453
  54.6 0.7 collective-permute-start.9
  55.3 5.5 %collective-permute-start.10 = (f32[8,128]{1,0:T(8,128)S(1)}, f32[8,128]{1,0:T(8,128)S(1)}, u32[]{:S(2)}, u32[]{:S(2)}) collective-permute-start(f32[8,128]{1,0:T(8,128)S(1)} %slice_select_fusion.3), channel_id=1, source_target_pairs={{0,2},{2,0},{4,6},{6,4},{8,10},{10,8},{12,14},{14,12},{16,18},{18,... | collective-permute-start | bytes 12296 | tf_op jit(solution)/shard_map/ppermute | solution.py:453
  69.7 5.4 %collective-permute-start.11 = (f32[48,128]{1,0:T(8,128)S(1)}, f32[48,128]{1,0:T(8,128)S(1)}, u32[]{:S(2)}, u32[]{:S(2)}) collective-permute-start(f32[48,128]{1,0:T(8,128)S(1)} %constant_dynamic-update-slice_fusion), channel_id=1, source_target_pairs={{0,1},{1,0},{2,3},{3,2},{4,5},{5,4},{6,7},{7,6},{8,9},{9,8},{10,11... | collective-permute-start | bytes 73736 | tf_op jit(solution)/shard_map/ppermute | solution.py:448
  75.1 1.2 %collective-permute-start.12 = (f32[48,128]{1,0:T(8,128)S(1)}, f32[48,128]{1,0:T(8,128)S(1)}, u32[]{:S(2)}, u32[]{:S(2)}) collective-permute-start(f32[48,128]{1,0:T(8,128)S(1)} %add.114), channel_id=1, source_target_pairs={{0,2},{2,0},{4,6},{6,4},{8,10},{10,8},{12,14},{14,12},{16,18},{18,... | collective-permute-start | bytes 73736 | tf_op jit(solution)/shard_map/ppermute | solution.py:453
  76.3 9.4 %collective-permute-start.13 = (f32[8,128]{1,0:T(8,128)S(1)}, f32[8,128]{1,0:T(8,128)S(1)}, u32[]{:S(2)}, u32[]{:S(2)}) collective-permute-start(f32[8,128]{1,0:T(8,128)S(1)} %slice_add_fusion), channel_id=1, source_target_pairs={{0,4},{2,6},{4,0},{6,2},{8,12},{10,14},{12,8},{14,10},{16,20},{18,... | collective-permute-start | bytes 12296 | tf_op jit(solution)/shard_map/ppermute | solution.py:453
  78.3 8.4 %collective-permute-start.14 = (f32[8,128]{1,0:T(8,128)S(1)}, f32[8,128]{1,0:T(8,128)S(1)}, u32[]{:S(2)}, u32[]{:S(2)}) collective-permute-start(f32[8,128]{1,0:T(8,128)S(1)} %slice_add_fusion), channel_id=1, source_target_pairs={{0,8},{2,10},{4,12},{6,14},{8,0},{10,2},{12,4},{14,6},{16,24},{18,... | collective-permute-start | bytes 12296 | tf_op jit(solution)/shard_map/ppermute | solution.py:453
  85.0 4.8 %collective-permute-start.15 = (f32[8,128]{1,0:T(8,128)S(1)}, f32[8,128]{1,0:T(8,128)S(1)}, u32[]{:S(2)}, u32[]{:S(2)}) collective-permute-start(f32[8,128]{1,0:T(8,128)S(1)} %slice_add_fusion), channel_id=1, source_target_pairs={{0,12},{2,14},{4,8},{6,10},{8,4},{10,6},{12,0},{14,2},{16,28},{18,... | collective-permute-start | bytes 12296 | tf_op jit(solution)/shard_map/ppermute | solution.py:453
  85.1 4.8 %collective-permute-start.16 = (f32[24,128]{1,0:T(8,128)S(1)}, f32[24,128]{1,0:T(8,128)S(1)}, u32[]{:S(2)}, u32[]{:S(2)}) collective-permute-start(f32[24,128]{1,0:T(8,128)S(1)} %fusion.21), channel_id=1, source_target_pairs={{2,4},{6,8},{10,12},{14,16},{18,20},{22,24},{26,28},{30,32},{34,36... | collective-permute-start | bytes 36872 | tf_op jit(solution)/shard_map/ppermute | solution.py:463
  89.9 7.2 %collective-permute-start.17 = (f32[8,128]{1,0:T(8,128)S(1)}, f32[8,128]{1,0:T(8,128)S(1)}, u32[]{:S(2)}, u32[]{:S(2)}) collective-permute-start(f32[8,128]{1,0:T(8,128)S(1)} %add_add_fusion.1), channel_id=1, source_target_pairs={{0,16},{2,18},{4,20},{6,22},{8,24},{10,26},{12,28},{14,30},{16,0},... | collective-permute-start | bytes 12296 | tf_op jit(solution)/shard_map/ppermute | solution.py:453
  97.1 10.5 %collective-permute-start.18 = (f32[8,128]{1,0:T(8,128)S(1)}, f32[8,128]{1,0:T(8,128)S(1)}, u32[]{:S(2)}, u32[]{:S(2)}) collective-permute-start(f32[8,128]{1,0:T(8,128)S(1)} %add.120), channel_id=1, source_target_pairs={{0,32},{2,34},{4,36},{6,38},{8,40},{10,42},{12,44},{14,46},{16,48}... | collective-permute-start | bytes 12296 | tf_op jit(solution)/shard_map/ppermute | solution.py:453
  104.0 5.2 %collective-permute-start.19 = (f32[8,128]{1,0:T(8,128)S(1)}, f32[8,128]{1,0:T(8,128)S(1)}, u32[]{:S(2)}, u32[]{:S(2)}) collective-permute-start(f32[8,128]{1,0:T(8,128)S(1)} %add.120), channel_id=1, source_target_pairs={{0,64},{2,66},{4,68},{6,70},{8,72},{10,74},{12,76},{14,78},{16,80}... | collective-permute-start | bytes 12296 | tf_op jit(solution)/shard_map/ppermute | solution.py:453
  107.6 4.8 %collective-permute-start.20 = (f32[8,128]{1,0:T(8,128)S(1)}, f32[8,128]{1,0:T(8,128)S(1)}, u32[]{:S(2)}, u32[]{:S(2)}) collective-permute-start(f32[8,128]{1,0:T(8,128)S(1)} %add.120), channel_id=1, source_target_pairs={{0,96},{2,98},{4,100},{6,102},{8,104},{10,106},{12,108},{14,110},{... | collective-permute-start | bytes 12296 | tf_op jit(solution)/shard_map/ppermute | solution.py:453

commit v6 on v3

--- a/solution.py
+++ b/solution.py
@@ -20,6 +20,7 @@
 KPAD = 48
 TILE = 16
 WIDE = 128
+EDGES = (0, 1, NZ - 2, NZ - 1)
 
 
 def split(array):
@@ -127,29 +128,25 @@
     return both[:CTL, :128] + (both[:CTL, 128:] + both[CTL:, :128])
 
 
-def first_kernel(half, moving, z_low, z_high, fixed, y_rows, back, xt, grad, out, planes):
-    upper = half[0] == 0
+def interior_kernel(half, moving, fixed, grad, planes, z_edges, y_edges):
     lane = lax.broadcasted_iota(jnp.int32, (TILE, NX), 1)
-
-    def plane(z, near_planes):
-        rows = y_rows[z]
-        blank = jnp.zeros_like(rows)
-        low_rows = jnp.where(upper, blank, rows)
-        high_rows = jnp.where(upper, rows, blank)
-        center = near_planes[2]
+    two = jnp.zeros((2, NX), F32)
+
+    def plane(z, shifts):
+        center = moving.at[z]
         for y in range(0, NY, TILE):
             here = slice(y, y + TILE)
             value = center[here]
 
             def at_z(k):
-                return near_planes[2 + k][here]
+                return moving[z + k, here] if k in shifts else 0.0
 
             def at_y(k):
                 first = y + k
                 if first < 0:
-                    return jnp.concatenate([low_rows[2 + first :], center[0 : TILE + first]], 0)
+                    return jnp.concatenate([two[: -first], center[0 : TILE + first]], 0)
                 if first + TILE > NY:
-                    return jnp.concatenate([center[first:NY], high_rows[: first + TILE - NY]], 0)
+                    return jnp.concatenate([center[first:NY], two[: first + TILE - NY]], 0)
                 return center[first : first + TILE]
 
             def at_x(k):
@@ -158,24 +155,19 @@
                 return jnp.where(inside, moved, 0.0)
 
             for c, near in enumerate((at_z, at_y, at_x)):
-                slope = 8.0 * (near(1) - near(-1)) - (near(2) - near(-2))
-                grad[c, z, here] = slope
-
-    def ref_of(z):
-        if z < 0:
-            return z_low.at[2 + z]
-        if z >= NZ:
-            return z_high.at[z - NZ]
-        return moving.at[z]
-
-    for z in (0, 1, NZ - 2, NZ - 1):
-        plane(z, [ref_of(z + k) for k in range(-2, 3)])
+                grad[c, z, here] = 8.0 * (near(1) - near(-1)) - (near(2) - near(-2))
+
+    every = (-2, -1, 1, 2)
 
     def body(z, carry):
-        plane(z, [moving.at[z + k] for k in range(-2, 3)])
+        plane(z, every)
         return carry
 
+    plane(0, (1, 2))
+    plane(1, (-1, 1, 2))
     lax.fori_loop(2, NZ - 2, body, 0)
+    plane(NZ - 2, (-2, -1, 1))
+    plane(NZ - 1, (-2, -1))
 
     def weight_at(z, y, lanes, slopes, carry):
         rows = pl.ds(pl.multiple_of(y * 8, 8), 8)
@@ -183,6 +175,58 @@
 
     for block in range(NZ // KNOT):
         lax.fori_loop(0, NY // 8, block_terms(block, grad, weight_at, planes), 0)
+    for e, z in enumerate(EDGES):
+        z_edges[e] = moving[z] - fixed[z]
+    rows = pl.ds(pl.multiple_of((1 - half[0]) * (NY - 8), 8), 8)
+    y_edges[...] = moving[:, rows, :] - fixed[:, rows, :]
+
+
+def edge_kernel(
+    half, z_low, z_high, y_rows, z_edges, y_edges, back, xt, grad_in, planes_in, grad, planes, out
+):
+    del grad_in, planes_in
+    weights = spline_weights()
+
+    def strip(y, carry):
+        rows = pl.ds(pl.multiple_of(y * 8, 8), 8)
+        near, far = z_low[1, rows], z_low[0, rows]
+        above, beyond = z_high[0, rows], z_high[1, rows]
+        slopes = (far - 8.0 * near, near, -above, 8.0 * above - beyond)
+        for e, z in enumerate(EDGES):
+            grad[0, z, rows] += slopes[e]
+            term = slopes[e] * z_edges[e, rows]
+            for j in range(4):
+                at = z // KNOT + j
+                planes[at, rows, 0:NX] += float(weights[j, z % KNOT]) * term
+        return carry
+
+    lax.fori_loop(0, NY // 8, strip, 0)
+
+    upper = half[0] == 0
+    rows = pl.ds(pl.multiple_of((1 - half[0]) * (NY - 8), 8), 8)
+    sub = lax.broadcasted_iota(jnp.int32, (8, NX), 0)
+
+    def coefficient(when_upper, otherwise):
+        def column(entries):
+            value = jnp.zeros((8, NX), F32)
+            for row, entry in entries.items():
+                value = jnp.where(sub == row, entry, value)
+            return value
+
+        return jnp.where(upper, column(when_upper), column(otherwise))
+
+    on_first = coefficient({6: -1.0, 7: 8.0}, {0: 1.0})
+    on_second = coefficient({7: -1.0}, {0: -8.0, 1: 1.0})
+    for block in range(NZ // KNOT):
+        sums = [0.0] * 4
+        for i in range(KNOT):
+            z = block * KNOT + i
+            slope = on_first * y_rows[z, 0:1] + on_second * y_rows[z, 1:2]
+            grad[1, z, rows] += slope
+            term = slope * y_edges[z]
+            sums = [total + float(weights[j, i]) * term for j, total in enumerate(sums)]
+        for j, total in enumerate(sums):
+            planes[block + j, rows, NX : 2 * NX] += total
     out[...] = contracted(planes, back[half[0]], xt) * (-data_weight / 12.0)
 
 
@@ -211,7 +255,7 @@
             return weight, carry + weight * weight
 
         strip = block_terms(block, grad, weight_at, planes)
-        square = lax.fori_loop(0, NY // 8, strip, square)
+        square = lax.fori_loop(0, NY // 8, strip, square, unroll=2)
 
     scale = data_weight / 144.0
     whole = ctl[...]
@@ -248,21 +292,42 @@
 VMEM_SPEC = pl.BlockSpec(memory_space=pltpu.VMEM)
 SMEM_SPEC = pl.BlockSpec(memory_space=pltpu.SMEM)
 PARAMS = pltpu.CompilerParams(vmem_limit_bytes=24 * 1024 * 1024)
-
-
-def first_pass(half, moving, z_low, z_high, fixed, y_rows, back_table, x_table):
+SMALL_PARAMS = pltpu.CompilerParams(vmem_limit_bytes=8 * 1024 * 1024)
+
+
+GRAD_SHAPE = jax.ShapeDtypeStruct((3, NZ, NY, NX), F32)
+PLANES_SHAPE = jax.ShapeDtypeStruct((PLANES, NY, 3 * NX), F32)
+CTL_SHAPE = jax.ShapeDtypeStruct((CTL, 128), F32)
+
+
+def interior_pass(half, moving, fixed):
     return pl.pallas_call(
-        first_kernel,
-        in_specs=[SMEM_SPEC] + [VMEM_SPEC] * 7,
-        out_specs=[VMEM_SPEC] * 2,
-        scratch_shapes=[pltpu.VMEM((PLANES, NY, 3 * NX), F32)],
+        interior_kernel,
+        in_specs=[SMEM_SPEC] + [VMEM_SPEC] * 2,
+        out_specs=[VMEM_SPEC] * 4,
         out_shape=[
-            jax.ShapeDtypeStruct((3, NZ, NY, NX), F32),
-            jax.ShapeDtypeStruct((CTL, 128), F32),
+            GRAD_SHAPE,
+            PLANES_SHAPE,
+            jax.ShapeDtypeStruct((len(EDGES), NY, NX), F32),
+            jax.ShapeDtypeStruct((NZ, 8, NX), F32),
         ],
+        compiler_params=SMALL_PARAMS,
+        cost_estimate=pl.CostEstimate(flops=100_000_000, bytes_accessed=40_000_000, transcendentals=0),
+        name="interior",
+    )(half, moving, fixed)
+
+
+def edge_pass(half, z_low, z_high, y_rows, z_edges, y_edges, back_table, x_table, grad, planes):
+    grad, _, part = pl.pallas_call(
+        edge_kernel,
+        in_specs=[SMEM_SPEC] + [VMEM_SPEC] * 9,
+        out_specs=[VMEM_SPEC] * 3,
+        out_shape=[GRAD_SHAPE, PLANES_SHAPE, CTL_SHAPE],
+        input_output_aliases={8: 0, 9: 1},
         compiler_params=PARAMS,
-        name="first",
-    )(half, moving, z_low, z_high, fixed, y_rows, back_table, x_table)
+        name="edge",
+    )(half, z_low, z_high, y_rows, z_edges, y_edges, back_table, x_table, grad, planes)
+    return grad, part
 
 
 def hessian_pass(half, ctl, base, grad, front_table, back_table, x_table):
@@ -284,6 +349,23 @@
     )(half, ctl, base, grad, front_table, back_table, x_table)
 
 
+def rims_kernel(*refs):
+    for source, target in zip(refs[: len(refs) // 2], refs[len(refs) // 2 :]):
+        target[...] = source[...]
+
+
+def rims_pass(*rims):
+    return pl.pallas_call(
+        rims_kernel,
+        in_specs=[VMEM_SPEC] * len(rims),
+        out_specs=[VMEM_SPEC] * len(rims),
+        out_shape=[jax.ShapeDtypeStruct(rim.shape, F32) for rim in rims],
+        compiler_params=SMALL_PARAMS,
+        cost_estimate=pl.CostEstimate(flops=20_000_000_000, bytes_accessed=60_000_000, transcendentals=0),
+        name="rims",
+    )(*rims)
+
+
 def passed_along(value, axis, steps):
     count = lax.axis_size(axis)
     initial, last = (max(0, -steps), min(count, count - steps))
@@ -299,6 +381,10 @@
     return lax.ppermute(value, "gz", [(i, i ^ mask) for i in range(count)])
 
 
+def stage(value, *masks):
+    return value + sum(paired(value, mask) for mask in masks)
+
+
 def outer_paired(value):
     count = lax.axis_size("gz")
     pairs = [(i, i + 1) for i in range(1, count - 1, 2)]
@@ -315,34 +401,42 @@
     return outer_paired(jnp.where(lower, seven[: 3 * CY], seven[4 * CY :]))
 
 
-def all_planes(lower, part):
+def all_planes(lower, inside, part):
     part = part + swapped(part)
     seven = pair_sum(lower, part, paired(part, 1))
     three = outer_terms(lower, seven)
     one = paired(jnp.where(lower, three[2 * CY :], three[:CY]), 1)
     low = jnp.concatenate([three, jnp.zeros((CY, 128), F32), one], 0) + seven[: 5 * CY]
     high = jnp.concatenate([one, jnp.zeros((CY, 128), F32), three], 0) + seven[2 * CY :]
-    row = lax.broadcasted_iota(jnp.int32, (CTL, 128), 0)
-    at = lax.axis_index("gz") * (2 * CY) - CY + row
-    inside = (at >= 0) & (at < lax.axis_size("gz") * (2 * CY))
-    return jnp.where(inside, jnp.where(lower, low, high), 0.0)
+    return inside * jnp.where(lower, low, high)
 
 
 def local(moving, fixed):
     half_id = lax.axis_index("gy").astype(jnp.int32)
     half = half_id.reshape(1)
-    lower = lax.axis_index("gz") % 2 == 0
+    slab = lax.axis_index("gz")
+    lower = slab % 2 == 0
+    at = slab * (2 * CY) - CY + lax.broadcasted_iota(jnp.int32, (CTL, 128), 0)
+    inside = ((at >= 0) & (at < lax.axis_size("gz") * (2 * CY))).astype(F32)
+    moving, half_id, half, lower, inside = lax.optimization_barrier(
+        (moving, half_id, half, lower, inside)
+    )
     front, back, xt = (jnp.asarray(a) for a in tables())
 
-    z_low = passed_along(moving[-2:], "gz", 1)
-    z_high = passed_along(moving[:2], "gz", -1)
-    y_rows = swapped(jnp.where(half_id == 0, moving[:, -2:], moving[:, :2]))
-
-    grad, part = first_pass(half, moving, z_low, z_high, fixed, y_rows, back, xt)
-    b_planes = all_planes(lower, part)
+    y_rim = jnp.where(half_id == 0, moving[:, -2:], moving[:, :2])
+    top, bottom, y_rim = rims_pass(moving[-2:], moving[:2], y_rim)
+    z_low = passed_along(top, "gz", 1)
+    z_high = passed_along(bottom, "gz", -1)
+    y_rows = swapped(y_rim)
+
+    grad, planes, z_edges, y_edges = interior_pass(half, moving, fixed)
+    grad, part = edge_pass(
+        half, z_low, z_high, y_rows, z_edges, y_edges, back, xt, grad, planes
+    )
+    b_planes = all_planes(lower, inside, part)
     b = b_planes[CY : 3 * CY]
     part, _ = hessian_pass(half, b_planes, b, grad, front, back, xt)
-    u_planes = all_planes(lower, part)
+    u_planes = all_planes(lower, inside, part)
     u = u_planes[CY : 3 * CY]
     part, sums = hessian_pass(half, u_planes, b, grad, front, back, xt)
     both = jnp.concatenate([part, sums], 0)
@@ -351,10 +445,9 @@
     seven = pair_sum(lower, both[:CTL], other[:CTL])
     sums = both[CTL:] + other[CTL:]
     three = outer_terms(lower, seven)
-    sums = sums + paired(sums, 2)
+    sums = stage(sums, 2, 4, 6)
     sums, three = lax.optimization_barrier((sums, three))
-    for mask in (6, 8, 16, 48):
-        sums = sums + paired(sums, mask)
+    sums = stage(stage(sums, 8), 16, 32, 48)
     v_low = seven[CY : 3 * CY] + three[CY:]
     v_high = seven[3 * CY : 5 * CY] + jnp.pad(three[:CY], ((CY, 0), (0, 0)))
     v = jnp.where(lower, v_low, v_high)

time: 128 us -> 109 us (0.85)
  local copies, waits for them, and re-layouts: 18 us -> 2.58 us
  starting transfers between devices: 57.6 us -> 46.4 us
  waiting for transfers between devices: 22.1 us -> 30.2 us
    unnamed x21 -> x13, local copies, waits for them, and re-layouts: 16.7 us -> 1.27 us
    ppermute x4, starting transfers between devices: 13.3 us -> 4.87 us  [swapped(): return lax.ppermute(value, 'gy', [(0, 1), (1, 0)])]
    ppermute x4, waiting for transfers between devices: 9.27 us -> 14.8 us  [swapped(): return lax.ppermute(value, 'gy', [(0, 1), (1, 0)])]
    ppermute x10 -> x12, starting transfers between devices: 39.7 us -> 36.4 us  [paired(): return lax.ppermute(value, 'gz', [(i, i ^ mask) for i in range(count)])]
    ppermute x10 -> x12, waiting for transfers between devices: 12.8 us -> 15.4 us  [paired(): return lax.ppermute(value, 'gz', [(i, i ^ mask) for i in range(count)])]
    pallas_call x2, Pallas kernels: 17.1 us -> 15.4 us  [hessian_pass(): pl.pallas_call(hessian_kernel, in_specs=[SMEM_SPEC] + [VMEM_SPEC] * 6, ou...]
    pallas_call x1 -> x3, Pallas kernels: 10.7 us -> 12.2 us  [the longest x1 10.9 us: interior_pass(): pl.pallas_call(interior_kernel, in_specs=[SMEM_SPEC] + [VMEM_SPEC] * 2, o...]
  transfers between devices with their start and end apart: 19 -> 21, of which waited for: 14 -> 13; matrix products, arithmetic and copies ran while one was open for 1% -> 0% of each run, Pallas kernels for 0% -> 10%
where the time goes in v6:
time: 109 us
  starting transfers between devices  46.4 us (43%)
  waiting for transfers between devices  30.2 us (28%)
  Pallas kernels  27.6 us (25%)
  local copies, waits for them, and re-layouts  2.58 us (2%)
  other arithmetic  1.46 us (1%)
    ppermute x12, starting transfers between devices, paired(): return lax.ppermute(value, 'gz', [(i, i ^ mask) for i in range(count)])  36.4 us
    pallas_call x2, Pallas kernels, hessian_pass(): pl.pallas_call(hessian_kernel, in_specs=[SMEM_SPEC] + [VMEM_SPEC] * 6, ou...  15.4 us
    ppermute x12, waiting for transfers between devices, paired(): return lax.ppermute(value, 'gz', [(i, i ^ mask) for i in range(count)])  15.4 us
    ppermute x4, waiting for transfers between devices, swapped(): return lax.ppermute(value, 'gy', [(0, 1), (1, 0)])  14.8 us
    pallas_call x1, Pallas kernels, interior_pass(): pl.pallas_call(interior_kernel, in_specs=[SMEM_SPEC] + [VMEM_SPEC] * 2, o...  10.9 us
    ppermute x4, starting transfers between devices, swapped(): return lax.ppermute(value, 'gy', [(0, 1), (1, 0)])  4.87 us
    ppermute x2, starting transfers between devices, passed_along(): lax.ppermute(value, axis, [(source, source + steps) for source in range(i...  3.12 us
  transfers between devices with their start and end apart: 21, of which 13 were waited for; matrix products, arithmetic and copies ran while one was open for 0% of the time, Pallas kernels for 10%

profile of v6, /device:TPU:0, one launch (start us, length us, event | category | flops | bytes accessed | tf_op | source)
XLA Modules:
  0.0 109.2 jit_solution(6164810532795493343)
XLA Ops:
  1.8 1.3 %slice_select_fusion.refs_2_ = f32[32,2,512]{2,1,0:T(2,128)S(1)} fusion(f32[32,64,512]{2,1,0:T(8,128)} %moving, pred[]{:T(512)S(6)} %eq.9), kind=kLoop, calls=%fused_computation | loop fusion | flops 32768 | bytes 393217 | tf_op jit(solution)/shard_map/jit(_where)/select_n | solution.py:426
  3.2 1.6 %collective-permute-start = (f32[2,64,512]{2,1,0:T(8,128)S(1)}, f32[2,64,512]{2,1,0:T(8,128)S(1)}, u32[]{:S(2)}, u32[]{:S(2)}) collective-permute-start(f32[2,64,512]{2,1,0:T(8,128)S(1)} %get-tuple-element.26), channel_id=1, source_target_pairs={{0,2},{2,4},{4,6},{6,8},{8,10},{10,12},{12,14},{14,16},{16,18},{18... | collective-permute-start | bytes 786440 | tf_op jit(solution)/shard_map/ppermute | solution.py:372
  4.8 1.6 %collective-permute-start.1 = (f32[2,64,512]{2,1,0:T(8,128)S(1)}, f32[2,64,512]{2,1,0:T(8,128)S(1)}, u32[]{:S(2)}, u32[]{:S(2)}) collective-permute-start(f32[2,64,512]{2,1,0:T(8,128)S(1)} %get-tuple-element.27), channel_id=1, source_target_pairs={{2,0},{4,2},{6,4},{8,6},{10,8},{12,10},{14,12},{16,14},{18,16},{20... | collective-permute-start | bytes 786440 | tf_op jit(solution)/shard_map/ppermute | solution.py:372
  6.4 3.6 %collective-permute-start.2 = (f32[32,2,512]{2,1,0:T(2,128)S(1)}, f32[32,2,512]{2,1,0:T(2,128)S(1)}, u32[]{:S(2)}, u32[]{:S(2)}) collective-permute-start(f32[32,2,512]{2,1,0:T(2,128)S(1)} %get-tuple-element.28), channel_id=1, source_target_pairs={{0,1},{1,0},{2,3},{3,2},{4,5},{5,4},{6,7},{7,6},{8,9},{9,8},{10,11... | collective-permute-start | bytes 393224 | tf_op jit(solution)/shard_map/ppermute | solution.py:376
  10.0 10.9 %interior.1 = (f32[3,32,64,512]{3,2,1,0:T(8,128)S(1)}, f32[5,64,1536]{2,1,0:T(8,128)S(1)}, f32[4,64,512]{2,1,0:T(8,128)S(1)}, f32[32,8,512]{2,1,0:T(8,128)S(1)}) custom-call(s32[1]{0:T(128)} %bitcast.half, f32[32,64,512]{2,1,0:T(8,128)S(1)} %copy-done.2, f32[32,64,512]{2,1,0:T(8,128)S(1)} %copy-done.3), custom_call_target="tpu_custom_call" | custom-call | flops 100000000 | bytes 40000000 | tf_op jit(solution)/shard_map/interior/pallas_call | solution.py:304
  21.0 1.3 %edge.1 = (f32[3,32,64,512]{3,2,1,0:T(8,128)S(1)}, f32[5,64,1536]{2,1,0:T(8,128)S(1)}, f32[40,128]{1,0:T(8,128)S(1)}) custom-call(s32[1]{0:T(128)} %bitcast.half, f32[2,64,512]{2,1,0:T(8,128)S(1)} %collective-permute-done.z_low, f32[2,64,512]{2,1,0:T(8,128)S(1)} %collective-permute-done.1.z_high, ...), custom_call_target="tpu_custom_call", output_to_operand_aliasing={{0}: (8, {}), {1}: (9, {})} | custom-call | tf_op jit(solution)/shard_map/edge/pallas_call | solution.py:321
  22.3 5.3 %collective-permute-done.3 = f32[40,128]{1,0:T(8,128)S(1)} collective-permute-done((f32[40,128]{1,0:T(8,128)S(1)}, f32[40,128]{1,0:T(8,128)S(1)}, u32[]{:S(2)}, u32[]{:S(2)}) %collective-permute-start.3) | collective-permute-done | bytes 20512 | tf_op jit(solution)/shard_map/ppermute | solution.py:376
  29.9 6.1 %collective-permute-start.6 = (f32[8,128]{1,0:T(8,128)S(1)}, f32[8,128]{1,0:T(8,128)S(1)}, u32[]{:S(2)}, u32[]{:S(2)}) collective-permute-start(f32[8,128]{1,0:T(8,128)S(1)} %slice_select_fusion.4), channel_id=1, source_target_pairs={{0,2},{2,0},{4,6},{6,4},{8,10},{10,8},{12,14},{14,12},{16,18},{18,... | collective-permute-start | bytes 12296 | tf_op jit(solution)/shard_map/ppermute | solution.py:381
  36.9 8.0 %hessian.2 = (f32[40,128]{1,0:T(8,128)S(1)}, f32[8,128]{1,0:T(8,128)}) custom-call(s32[1]{0:T(128)} %bitcast.half, f32[40,128]{1,0:T(8,128)S(1)} %fusion.3.ctl, f32[16,128]{1,0:T(8,128)S(1)} %slice.144.base, f32[3,32,64,512]{3,2,1,0:T(8,128)S(1)} %get-tuple-element.34.grad, bf16[2,2048,192]{2,1,0:T(8,128)(2,1)S(1)} %copy-done, ...), custom_call_target="tpu_custom_call" | custom-call | tf_op jit(solution)/shard_map/hessian/pallas_call | solution.py:334
  45.4 4.8 %collective-permute-done.7 = f32[40,128]{1,0:T(8,128)S(1)} collective-permute-done((f32[40,128]{1,0:T(8,128)S(1)}, f32[40,128]{1,0:T(8,128)S(1)}, u32[]{:S(2)}, u32[]{:S(2)}) %collective-permute-start.7) | collective-permute-done | bytes 20512 | tf_op jit(solution)/shard_map/ppermute | solution.py:376
  50.2 1.2 %collective-permute-done.8 = f32[40,128]{1,0:T(8,128)S(1)} collective-permute-done((f32[40,128]{1,0:T(8,128)S(1)}, f32[40,128]{1,0:T(8,128)S(1)}, u32[]{:S(2)}, u32[]{:S(2)}) %collective-permute-start.8) | collective-permute-done | bytes 20512 | tf_op jit(solution)/shard_map/ppermute | solution.py:381
  52.0 4.7 %collective-permute-start.10 = (f32[8,128]{1,0:T(8,128)S(1)}, f32[8,128]{1,0:T(8,128)S(1)}, u32[]{:S(2)}, u32[]{:S(2)}) collective-permute-start(f32[8,128]{1,0:T(8,128)S(1)} %slice_select_fusion.3), channel_id=1, source_target_pairs={{0,2},{2,0},{4,6},{6,4},{8,10},{10,8},{12,14},{14,12},{16,18},{18,... | collective-permute-start | bytes 12296 | tf_op jit(solution)/shard_map/ppermute | solution.py:381
  57.5 7.4 %hessian.3 = (f32[40,128]{1,0:T(8,128)S(1)}, f32[8,128]{1,0:T(8,128)S(1)}) custom-call(s32[1]{0:T(128)} %bitcast.half, f32[40,128]{1,0:T(8,128)S(1)} %fusion.7.ctl, f32[16,128]{1,0:T(8,128)S(1)} %slice.144.base, f32[3,32,64,512]{3,2,1,0:T(8,128)S(1)} %get-tuple-element.34.grad, bf16[2,2048,192]{2,1,0:T(8,128)(2,1)S(1)} %copy-done, ...), custom_call_target="tpu_custom_call" | custom-call | tf_op jit(solution)/shard_map/hessian/pallas_call | solution.py:334
  65.6 4.8 %collective-permute-done.11 = f32[48,128]{1,0:T(8,128)S(1)} collective-permute-done((f32[48,128]{1,0:T(8,128)S(1)}, f32[48,128]{1,0:T(8,128)S(1)}, u32[]{:S(2)}, u32[]{:S(2)}) %collective-permute-start.11) | collective-permute-done | bytes 24608 | tf_op jit(solution)/shard_map/ppermute | solution.py:376
  70.4 1.2 %collective-permute-done.12 = f32[48,128]{1,0:T(8,128)S(1)} collective-permute-done((f32[48,128]{1,0:T(8,128)S(1)}, f32[48,128]{1,0:T(8,128)S(1)}, u32[]{:S(2)}, u32[]{:S(2)}) %collective-permute-start.12) | collective-permute-done | bytes 24608 | tf_op jit(solution)/shard_map/ppermute | solution.py:381
  71.6 2.0 %collective-permute-start.13 = (f32[8,128]{1,0:T(8,128)S(1)}, f32[8,128]{1,0:T(8,128)S(1)}, u32[]{:S(2)}, u32[]{:S(2)}) collective-permute-start(f32[8,128]{1,0:T(8,128)S(1)} %slice_add_fusion), channel_id=1, source_target_pairs={{0,4},{2,6},{4,0},{6,2},{8,12},{10,14},{12,8},{14,10},{16,20},{18,... | collective-permute-start | bytes 12296 | tf_op jit(solution)/shard_map/ppermute | solution.py:381
  73.6 6.8 %collective-permute-start.14 = (f32[8,128]{1,0:T(8,128)S(1)}, f32[8,128]{1,0:T(8,128)S(1)}, u32[]{:S(2)}, u32[]{:S(2)}) collective-permute-start(f32[8,128]{1,0:T(8,128)S(1)} %slice_add_fusion), channel_id=1, source_target_pairs={{0,8},{2,10},{4,12},{6,14},{8,0},{10,2},{12,4},{14,6},{16,24},{18,... | collective-permute-start | bytes 12296 | tf_op jit(solution)/shard_map/ppermute | solution.py:381
  82.0 3.2 %collective-permute-done.15 = f32[8,128]{1,0:T(8,128)S(1)} collective-permute-done((f32[8,128]{1,0:T(8,128)S(1)}, f32[8,128]{1,0:T(8,128)S(1)}, u32[]{:S(2)}, u32[]{:S(2)}) %collective-permute-start.15) | collective-permute-done | bytes 4128 | tf_op jit(solution)/shard_map/ppermute | solution.py:381
  85.2 5.6 %collective-permute-start.17 = (f32[8,128]{1,0:T(8,128)S(1)}, f32[8,128]{1,0:T(8,128)S(1)}, u32[]{:S(2)}, u32[]{:S(2)}) collective-permute-start(f32[8,128]{1,0:T(8,128)S(1)} %add_add_fusion.1), channel_id=1, source_target_pairs={{0,16},{2,18},{4,20},{6,22},{8,24},{10,26},{12,28},{14,30},{16,0},... | collective-permute-start | bytes 12296 | tf_op jit(solution)/shard_map/ppermute | solution.py:381
  90.8 1.6 %collective-permute-done.17 = f32[8,128]{1,0:T(8,128)S(1)} collective-permute-done((f32[8,128]{1,0:T(8,128)S(1)}, f32[8,128]{1,0:T(8,128)S(1)}, u32[]{:S(2)}, u32[]{:S(2)}) %collective-permute-start.17) | collective-permute-done | bytes 4128 | tf_op jit(solution)/shard_map/ppermute | solution.py:381
  92.4 6.9 %collective-permute-start.18 = (f32[8,128]{1,0:T(8,128)S(1)}, f32[8,128]{1,0:T(8,128)S(1)}, u32[]{:S(2)}, u32[]{:S(2)}) collective-permute-start(f32[8,128]{1,0:T(8,128)S(1)} %add.118), channel_id=1, source_target_pairs={{0,32},{2,34},{4,36},{6,38},{8,40},{10,42},{12,44},{14,46},{16,48}... | collective-permute-start | bytes 12296 | tf_op jit(solution)/shard_map/ppermute | solution.py:381
  99.3 3.6 %collective-permute-start.19 = (f32[8,128]{1,0:T(8,128)S(1)}, f32[8,128]{1,0:T(8,128)S(1)}, u32[]{:S(2)}, u32[]{:S(2)}) collective-permute-start(f32[8,128]{1,0:T(8,128)S(1)} %add.118), channel_id=1, source_target_pairs={{0,64},{2,66},{4,68},{6,70},{8,72},{10,74},{12,76},{14,78},{16,80}... | collective-permute-start | bytes 12296 | tf_op jit(solution)/shard_map/ppermute | solution.py:381
  102.9 1.6 %collective-permute-done.19 = f32[8,128]{1,0:T(8,128)S(1)} collective-permute-done((f32[8,128]{1,0:T(8,128)S(1)}, f32[8,128]{1,0:T(8,128)S(1)}, u32[]{:S(2)}, u32[]{:S(2)}) %collective-permute-start.19) | collective-permute-done | bytes 4128 | tf_op jit(solution)/shard_map/ppermute | solution.py:381
  104.5 3.2 %collective-permute-done.20 = f32[8,128]{1,0:T(8,128)S(1)} collective-permute-done((f32[8,128]{1,0:T(8,128)S(1)}, f32[8,128]{1,0:T(8,128)S(1)}, u32[]{:S(2)}, u32[]{:S(2)}) %collective-permute-start.20) | collective-permute-done | bytes 4128 | tf_op jit(solution)/shard_map/ppermute | solution.py:381
  (66 shorter events, 10.2 us)
Async XLA Ops:
  3.2 17.7 %collective-permute-start = (f32[2,64,512]{2,1,0:T(8,128)S(1)}, f32[2,64,512]{2,1,0:T(8,128)S(1)}, u32[]{:S(2)}, u32[]{:S(2)}) collective-permute-start(f32[2,64,512]{2,1,0:T(8,128)S(1)} %get-tuple-element.26), channel_id=1, source_target_pairs={{0,2},{2,4},{4,6},{6,8},{8,10},{10,12},{12,14},{14,16},{16,18},{18... | collective-permute-start | bytes 786440 | tf_op jit(solution)/shard_map/ppermute | solution.py:372
  4.8 16.2 %collective-permute-start.1 = (f32[2,64,512]{2,1,0:T(8,128)S(1)}, f32[2,64,512]{2,1,0:T(8,128)S(1)}, u32[]{:S(2)}, u32[]{:S(2)}) collective-permute-start(f32[2,64,512]{2,1,0:T(8,128)S(1)} %get-tuple-element.27), channel_id=1, source_target_pairs={{2,0},{4,2},{6,4},{8,6},{10,8},{12,10},{14,12},{16,14},{18,16},{20... | collective-permute-start | bytes 786440 | tf_op jit(solution)/shard_map/ppermute | solution.py:372
  6.3 14.6 %copy-start.1 = (bf16[256,1536]{1,0:T(8,128)(2,1)S(1)}, bf16[256,1536]{1,0:T(8,128)(2,1)}, u32[]{:S(2)}) copy-start(bf16[256,1536]{1,0:T(8,128)(2,1)} %constant.45.clone.xt) | copy-start | bytes 2359300
  6.3 14.6 %copy-start.4 = (bf16[2,80,320]{2,1,0:T(8,128)(2,1)S(1)}, bf16[2,80,320]{2,1,0:T(8,128)(2,1)}, u32[]{:S(2)}) copy-start(bf16[2,80,320]{2,1,0:T(8,128)(2,1)} %constant.44.clone.back) | copy-start | bytes 307204
  6.4 14.6 %collective-permute-start.2 = (f32[32,2,512]{2,1,0:T(2,128)S(1)}, f32[32,2,512]{2,1,0:T(2,128)S(1)}, u32[]{:S(2)}, u32[]{:S(2)}) collective-permute-start(f32[32,2,512]{2,1,0:T(2,128)S(1)} %get-tuple-element.28), channel_id=1, source_target_pairs={{0,1},{1,0},{2,3},{3,2},{4,5},{5,4},{6,7},{7,6},{8,9},{9,8},{10,11... | collective-permute-start | bytes 393224 | tf_op jit(solution)/shard_map/ppermute | solution.py:376
  21.0 15.9 %copy-start = (bf16[2,2048,192]{2,1,0:T(8,128)(2,1)S(1)}, bf16[2,2048,192]{2,1,0:T(8,128)(2,1)}, u32[]{:S(2)}) copy-start(bf16[2,2048,192]{2,1,0:T(8,128)(2,1)} %constant.43.clone.front) | copy-start | bytes 4718596
  22.2 5.4 %collective-permute-start.3 = (f32[40,128]{1,0:T(8,128)S(1)}, f32[40,128]{1,0:T(8,128)S(1)}, u32[]{:S(2)}, u32[]{:S(2)}) collective-permute-start(f32[40,128]{1,0:T(8,128)S(1)} %get-tuple-element.33), channel_id=1, source_target_pairs={{0,1},{1,0},{2,3},{3,2},{4,5},{5,4},{6,7},{7,6},{8,9},{9,8},{10,11... | collective-permute-start | bytes 61448 | tf_op jit(solution)/shard_map/ppermute | solution.py:376
  27.6 1.6 %collective-permute-start.4 = (f32[40,128]{1,0:T(8,128)S(1)}, f32[40,128]{1,0:T(8,128)S(1)}, u32[]{:S(2)}, u32[]{:S(2)}) collective-permute-start(f32[40,128]{1,0:T(8,128)S(1)} %add.104), channel_id=1, source_target_pairs={{0,2},{2,0},{4,6},{6,4},{8,10},{10,8},{12,14},{14,12},{16,18},{18,... | collective-permute-start | bytes 61448 | tf_op jit(solution)/shard_map/ppermute | solution.py:381
  29.2 0.7 collective-permute-start.5
  29.9 6.9 %collective-permute-start.6 = (f32[8,128]{1,0:T(8,128)S(1)}, f32[8,128]{1,0:T(8,128)S(1)}, u32[]{:S(2)}, u32[]{:S(2)}) collective-permute-start(f32[8,128]{1,0:T(8,128)S(1)} %slice_select_fusion.4), channel_id=1, source_target_pairs={{0,2},{2,0},{4,6},{6,4},{8,10},{10,8},{12,14},{14,12},{16,18},{18,... | collective-permute-start | bytes 12296 | tf_op jit(solution)/shard_map/ppermute | solution.py:381
  44.9 5.3 %collective-permute-start.7 = (f32[40,128]{1,0:T(8,128)S(1)}, f32[40,128]{1,0:T(8,128)S(1)}, u32[]{:S(2)}, u32[]{:S(2)}) collective-permute-start(f32[40,128]{1,0:T(8,128)S(1)} %get-tuple-element.35), channel_id=1, source_target_pairs={{0,1},{1,0},{2,3},{3,2},{4,5},{5,4},{6,7},{7,6},{8,9},{9,8},{10,11... | collective-permute-start | bytes 61448 | tf_op jit(solution)/shard_map/ppermute | solution.py:376
  50.1 1.2 %collective-permute-start.8 = (f32[40,128]{1,0:T(8,128)S(1)}, f32[40,128]{1,0:T(8,128)S(1)}, u32[]{:S(2)}, u32[]{:S(2)}) collective-permute-start(f32[40,128]{1,0:T(8,128)S(1)} %add.108), channel_id=1, source_target_pairs={{0,2},{2,0},{4,6},{6,4},{8,10},{10,8},{12,14},{14,12},{16,18},{18,... | collective-permute-start | bytes 61448 | tf_op jit(solution)/shard_map/ppermute | solution.py:381
  51.4 0.7 collective-permute-start.9
  52.0 5.5 %collective-permute-start.10 = (f32[8,128]{1,0:T(8,128)S(1)}, f32[8,128]{1,0:T(8,128)S(1)}, u32[]{:S(2)}, u32[]{:S(2)}) collective-permute-start(f32[8,128]{1,0:T(8,128)S(1)} %slice_select_fusion.3), channel_id=1, source_target_pairs={{0,2},{2,0},{4,6},{6,4},{8,10},{10,8},{12,14},{14,12},{16,18},{18,... | collective-permute-start | bytes 12296 | tf_op jit(solution)/shard_map/ppermute | solution.py:381
  65.0 5.4 %collective-permute-start.11 = (f32[48,128]{1,0:T(8,128)S(1)}, f32[48,128]{1,0:T(8,128)S(1)}, u32[]{:S(2)}, u32[]{:S(2)}) collective-permute-start(f32[48,128]{1,0:T(8,128)S(1)} %constant_dynamic-update-slice_fusion), channel_id=1, source_target_pairs={{0,1},{1,0},{2,3},{3,2},{4,5},{5,4},{6,7},{7,6},{8,9},{9,8},{10,11... | collective-permute-start | bytes 73736 | tf_op jit(solution)/shard_map/ppermute | solution.py:376
  70.4 1.2 %collective-permute-start.12 = (f32[48,128]{1,0:T(8,128)S(1)}, f32[48,128]{1,0:T(8,128)S(1)}, u32[]{:S(2)}, u32[]{:S(2)}) collective-permute-start(f32[48,128]{1,0:T(8,128)S(1)} %add.112), channel_id=1, source_target_pairs={{0,2},{2,0},{4,6},{6,4},{8,10},{10,8},{12,14},{14,12},{16,18},{18,... | collective-permute-start | bytes 73736 | tf_op jit(solution)/shard_map/ppermute | solution.py:381
  71.6 9.4 %collective-permute-start.13 = (f32[8,128]{1,0:T(8,128)S(1)}, f32[8,128]{1,0:T(8,128)S(1)}, u32[]{:S(2)}, u32[]{:S(2)}) collective-permute-start(f32[8,128]{1,0:T(8,128)S(1)} %slice_add_fusion), channel_id=1, source_target_pairs={{0,4},{2,6},{4,0},{6,2},{8,12},{10,14},{12,8},{14,10},{16,20},{18,... | collective-permute-start | bytes 12296 | tf_op jit(solution)/shard_map/ppermute | solution.py:381
  73.6 8.4 %collective-permute-start.14 = (f32[8,128]{1,0:T(8,128)S(1)}, f32[8,128]{1,0:T(8,128)S(1)}, u32[]{:S(2)}, u32[]{:S(2)}) collective-permute-start(f32[8,128]{1,0:T(8,128)S(1)} %slice_add_fusion), channel_id=1, source_target_pairs={{0,8},{2,10},{4,12},{6,14},{8,0},{10,2},{12,4},{14,6},{16,24},{18,... | collective-permute-start | bytes 12296 | tf_op jit(solution)/shard_map/ppermute | solution.py:381
  80.3 4.8 %collective-permute-start.15 = (f32[8,128]{1,0:T(8,128)S(1)}, f32[8,128]{1,0:T(8,128)S(1)}, u32[]{:S(2)}, u32[]{:S(2)}) collective-permute-start(f32[8,128]{1,0:T(8,128)S(1)} %slice_add_fusion), channel_id=1, source_target_pairs={{0,12},{2,14},{4,8},{6,10},{8,4},{10,6},{12,0},{14,2},{16,28},{18,... | collective-permute-start | bytes 12296 | tf_op jit(solution)/shard_map/ppermute | solution.py:381
  80.4 4.8 %collective-permute-start.16 = (f32[24,128]{1,0:T(8,128)S(1)}, f32[24,128]{1,0:T(8,128)S(1)}, u32[]{:S(2)}, u32[]{:S(2)}) collective-permute-start(f32[24,128]{1,0:T(8,128)S(1)} %fusion.21), channel_id=1, source_target_pairs={{2,4},{6,8},{10,12},{14,16},{18,20},{22,24},{26,28},{30,32},{34,36... | collective-permute-start | bytes 36872 | tf_op jit(solution)/shard_map/ppermute | solution.py:391
  85.2 7.2 %collective-permute-start.17 = (f32[8,128]{1,0:T(8,128)S(1)}, f32[8,128]{1,0:T(8,128)S(1)}, u32[]{:S(2)}, u32[]{:S(2)}) collective-permute-start(f32[8,128]{1,0:T(8,128)S(1)} %add_add_fusion.1), channel_id=1, source_target_pairs={{0,16},{2,18},{4,20},{6,22},{8,24},{10,26},{12,28},{14,30},{16,0},... | collective-permute-start | bytes 12296 | tf_op jit(solution)/shard_map/ppermute | solution.py:381
  92.4 10.6 %collective-permute-start.18 = (f32[8,128]{1,0:T(8,128)S(1)}, f32[8,128]{1,0:T(8,128)S(1)}, u32[]{:S(2)}, u32[]{:S(2)}) collective-permute-start(f32[8,128]{1,0:T(8,128)S(1)} %add.118), channel_id=1, source_target_pairs={{0,32},{2,34},{4,36},{6,38},{8,40},{10,42},{12,44},{14,46},{16,48}... | collective-permute-start | bytes 12296 | tf_op jit(solution)/shard_map/ppermute | solution.py:381
  99.3 5.2 %collective-permute-start.19 = (f32[8,128]{1,0:T(8,128)S(1)}, f32[8,128]{1,0:T(8,128)S(1)}, u32[]{:S(2)}, u32[]{:S(2)}) collective-permute-start(f32[8,128]{1,0:T(8,128)S(1)} %add.118), channel_id=1, source_target_pairs={{0,64},{2,66},{4,68},{6,70},{8,72},{10,74},{12,76},{14,78},{16,80}... | collective-permute-start | bytes 12296 | tf_op jit(solution)/shard_map/ppermute | solution.py:381
  102.9 4.8 %collective-permute-start.20 = (f32[8,128]{1,0:T(8,128)S(1)}, f32[8,128]{1,0:T(8,128)S(1)}, u32[]{:S(2)}, u32[]{:S(2)}) collective-permute-start(f32[8,128]{1,0:T(8,128)S(1)} %add.118), channel_id=1, source_target_pairs={{0,96},{2,98},{4,100},{6,102},{8,104},{10,106},{12,108},{14,110},{... | collective-permute-start | bytes 12296 | tf_op jit(solution)/shard_map/ppermute | solution.py:381
  (2 other events, 13.8 us)

commit v7 on v6

--- a/solution.py
+++ b/solution.py
@@ -165,7 +165,7 @@
 
     plane(0, (1, 2))
     plane(1, (-1, 1, 2))
-    lax.fori_loop(2, NZ - 2, body, 0)
+    lax.fori_loop(2, NZ - 2, body, 0, unroll=2)
     plane(NZ - 2, (-2, -1, 1))
     plane(NZ - 1, (-2, -1))
 
@@ -174,7 +174,7 @@
         return moving[z, rows, lanes] - fixed[z, rows, lanes], carry
 
     for block in range(NZ // KNOT):
-        lax.fori_loop(0, NY // 8, block_terms(block, grad, weight_at, planes), 0)
+        lax.fori_loop(0, NY // 8, block_terms(block, grad, weight_at, planes), 0, unroll=2)
     for e, z in enumerate(EDGES):
         z_edges[e] = moving[z] - fixed[z]
     rows = pl.ds(pl.multiple_of((1 - half[0]) * (NY - 8), 8), 8)
@@ -182,15 +182,16 @@
 
 
 def edge_kernel(
-    half, z_low, z_high, y_rows, z_edges, y_edges, back, xt, grad_in, planes_in, grad, planes, out
+    half, inner, outer, y_rows, z_edges, y_edges, back, xt, grad_in, planes_in, grad, planes, out
 ):
     del grad_in, planes_in
+    lower = half[1] == 0
     weights = spline_weights()
 
     def strip(y, carry):
         rows = pl.ds(pl.multiple_of(y * 8, 8), 8)
-        near, far = z_low[1, rows], z_low[0, rows]
-        above, beyond = z_high[0, rows], z_high[1, rows]
+        near, far = (jnp.where(lower, outer[z, rows], inner[z, rows]) for z in (1, 0))
+        above, beyond = (jnp.where(lower, inner[z, rows], outer[z, rows]) for z in (0, 1))
         slopes = (far - 8.0 * near, near, -above, 8.0 * above - beyond)
         for e, z in enumerate(EDGES):
             grad[0, z, rows] += slopes[e]
@@ -290,8 +291,10 @@
 
 
 VMEM_SPEC = pl.BlockSpec(memory_space=pltpu.VMEM)
+HBM_SPEC = pl.BlockSpec(memory_space=pltpu.HBM)
 SMEM_SPEC = pl.BlockSpec(memory_space=pltpu.SMEM)
 PARAMS = pltpu.CompilerParams(vmem_limit_bytes=24 * 1024 * 1024)
+RIMS_MIB = 52
 SMALL_PARAMS = pltpu.CompilerParams(vmem_limit_bytes=8 * 1024 * 1024)
 
 
@@ -317,7 +320,7 @@
     )(half, moving, fixed)
 
 
-def edge_pass(half, z_low, z_high, y_rows, z_edges, y_edges, back_table, x_table, grad, planes):
+def edge_pass(half, inner, outer, y_rows, z_edges, y_edges, back_table, x_table, grad, planes):
     grad, _, part = pl.pallas_call(
         edge_kernel,
         in_specs=[SMEM_SPEC] + [VMEM_SPEC] * 9,
@@ -326,7 +329,7 @@
         input_output_aliases={8: 0, 9: 1},
         compiler_params=PARAMS,
         name="edge",
-    )(half, z_low, z_high, y_rows, z_edges, y_edges, back_table, x_table, grad, planes)
+    )(half, inner, outer, y_rows, z_edges, y_edges, back_table, x_table, grad, planes)
     return grad, part
 
 
@@ -349,27 +352,73 @@
     )(half, ctl, base, grad, front_table, back_table, x_table)
 
 
-def rims_kernel(*refs):
+def rims_kernel(place, moving, inner, outer, y_rim, tile, sems):
+    half, parity = place[0], place[1]
+    top, bottom = NZ - 2, 0
+    copies = [
+        pltpu.make_async_copy(
+            moving.at[pl.ds(jnp.where(parity == 0, top, bottom), 2)], inner, sems.at[0]
+        ),
+        pltpu.make_async_copy(
+            moving.at[pl.ds(jnp.where(parity == 0, bottom, top), 2)], outer, sems.at[1]
+        ),
+        pltpu.make_async_copy(
+            moving.at[:, pl.ds(pl.multiple_of((1 - half) * (NY - 8), 8), 8)], tile, sems.at[2]
+        ),
+    ]
+    for copy in copies:
+        copy.start()
+    for copy in copies:
+        copy.wait()
+    y_rim[...] = jnp.where(half == 0, tile[:, 6:8, :], tile[:, 0:2, :])
+
+
+def rims_pass(place, moving):
+    return pl.pallas_call(
+        rims_kernel,
+        in_specs=[SMEM_SPEC, HBM_SPEC],
+        out_specs=[VMEM_SPEC] * 3,
+        out_shape=[jax.ShapeDtypeStruct(shape, F32) for shape in ((2, NY, NX), (2, NY, NX), (NZ, 2, NX))],
+        scratch_shapes=[pltpu.VMEM((NZ, 8, NX), F32), pltpu.SemaphoreType.DMA((3,))],
+        compiler_params=pltpu.CompilerParams(vmem_limit_bytes=RIMS_MIB * 1024 * 1024),
+        name="rims",
+    )(place, moving)
+
+
+def held_kernel(*refs):
     for source, target in zip(refs[: len(refs) // 2], refs[len(refs) // 2 :]):
         target[...] = source[...]
 
 
-def rims_pass(*rims):
+def held(*rims):
     return pl.pallas_call(
-        rims_kernel,
+        held_kernel,
         in_specs=[VMEM_SPEC] * len(rims),
         out_specs=[VMEM_SPEC] * len(rims),
         out_shape=[jax.ShapeDtypeStruct(rim.shape, F32) for rim in rims],
         compiler_params=SMALL_PARAMS,
         cost_estimate=pl.CostEstimate(flops=20_000_000_000, bytes_accessed=60_000_000, transcendentals=0),
-        name="rims",
+        name="held",
     )(*rims)
 
 
-def passed_along(value, axis, steps):
-    count = lax.axis_size(axis)
-    initial, last = (max(0, -steps), min(count, count - steps))
-    return lax.ppermute(value, axis, [(source, source + steps) for source in range(initial, last)])
+def placed_kernel(solution, residual, solution_out, residual_out):
+    for value, out in ((solution[...], solution_out), (residual[...], residual_out)):
+        for c in range(3):
+            moved = pltpu.roll(value, (-c * CX) % 128, 1) if c else value
+            for plane in range(2):
+                out[c, plane] = moved[plane * CY : (plane + 1) * CY, :CX]
+
+
+def placed(solution, residual):
+    return pl.pallas_call(
+        placed_kernel,
+        in_specs=[VMEM_SPEC] * 2,
+        out_specs=[VMEM_SPEC] * 2,
+        out_shape=[jax.ShapeDtypeStruct((3, 2, CY, CX), F32)] * 2,
+        compiler_params=SMALL_PARAMS,
+        name="placed",
+    )(solution, residual)
 
 
 def swapped(value):
@@ -412,26 +461,22 @@
 
 
 def local(moving, fixed):
-    half_id = lax.axis_index("gy").astype(jnp.int32)
-    half = half_id.reshape(1)
-    slab = lax.axis_index("gz")
+    slab = lax.axis_index("gz").astype(jnp.int32)
+    half = jnp.stack([lax.axis_index("gy").astype(jnp.int32), slab % 2])
     lower = slab % 2 == 0
     at = slab * (2 * CY) - CY + lax.broadcasted_iota(jnp.int32, (CTL, 128), 0)
     inside = ((at >= 0) & (at < lax.axis_size("gz") * (2 * CY))).astype(F32)
-    moving, half_id, half, lower, inside = lax.optimization_barrier(
-        (moving, half_id, half, lower, inside)
-    )
+    moving, half, lower, inside = lax.optimization_barrier((moving, half, lower, inside))
     front, back, xt = (jnp.asarray(a) for a in tables())
 
-    y_rim = jnp.where(half_id == 0, moving[:, -2:], moving[:, :2])
-    top, bottom, y_rim = rims_pass(moving[-2:], moving[:2], y_rim)
-    z_low = passed_along(top, "gz", 1)
-    z_high = passed_along(bottom, "gz", -1)
+    inner, outer, y_rim = held(*rims_pass(half, moving))
+    inner = paired(inner, 1)
+    outer = outer_paired(outer)
     y_rows = swapped(y_rim)
 
     grad, planes, z_edges, y_edges = interior_pass(half, moving, fixed)
     grad, part = edge_pass(
-        half, z_low, z_high, y_rows, z_edges, y_edges, back, xt, grad, planes
+        half, inner, outer, y_rows, z_edges, y_edges, back, xt, grad, planes
     )
     b_planes = all_planes(lower, inside, part)
     b = b_planes[CY : 3 * CY]
@@ -461,11 +506,7 @@
     solution = a0 * b + a1 * (more * b - a0 * u)
     residual = (b - a0 * u) - a1 * (more * u - a0 * v)
 
-    def placed(value):
-        turned = value.reshape(2, CY, 128)[:, :, : 3 * CX].reshape(2, CY, 3, CX)
-        return turned.transpose(2, 0, 1, 3)
-
-    return placed(solution), placed(residual)
+    return tuple(placed(solution, residual))
 
 
 def solution(mesh):

time: 109 us -> 107 us (0.982)
  Pallas kernels: 27.6 us -> 32.1 us
  waiting for transfers between devices: 30.2 us -> 27.7 us
  local copies, waits for them, and re-layouts: 2.58 us -> 0.12 us
  other arithmetic: 1.46 us -> 0.23 us
    ppermute x2 -> x0, starting transfers between devices: 3.12 us -> none  [passed_along(): lax.ppermute(value, axis, [(source, source + steps) for source in range(i...]
    pallas_call x1 -> x3, Pallas kernels: 0.05 us -> 2.58 us  [the longest x1 1.84 us: rims_pass(): pl.pallas_call(rims_kernel, in_specs=[SMEM_SPEC, HBM_SPEC], out_specs=[VM...]
    ppermute x4, waiting for transfers between devices: 14.8 us -> 12.3 us  [swapped(): return lax.ppermute(value, 'gy', [(0, 1), (1, 0)])]
    ppermute x4, starting transfers between devices: 4.87 us -> 6.95 us  [swapped(): return lax.ppermute(value, 'gy', [(0, 1), (1, 0)])]
    select_n x1 -> x0, other arithmetic: 1.3 us -> none  [local(): y_rim = jnp.where(half_id == 0, moving[:, -2:], moving[:, :2])]
    unnamed x13 -> x11, local copies, waits for them, and re-layouts: 1.27 us -> 0.04 us
    pallas_call x2, Pallas kernels: 15.4 us -> 16.5 us  [hessian_pass(): pl.pallas_call(hessian_kernel, in_specs=[SMEM_SPEC] + [VMEM_SPEC] * 6, ou...]
    ppermute x3 -> x4, starting transfers between devices: 1.98 us -> 2.79 us  [outer_paired(): return lax.ppermute(value, 'gz', pairs + [(j, i) for i, j in pairs])]
where the time goes in v7:
time: 107 us
  starting transfers between devices  45.9 us (43%)
  Pallas kernels  32.1 us (30%)
  waiting for transfers between devices  27.7 us (26%)
    ppermute x13, starting transfers between devices, paired(): return lax.ppermute(value, 'gz', [(i, i ^ mask) for i in range(count)])  36.2 us
    pallas_call x2, Pallas kernels, hessian_pass(): pl.pallas_call(hessian_kernel, in_specs=[SMEM_SPEC] + [VMEM_SPEC] * 6, ou...  16.5 us
    ppermute x13, waiting for transfers between devices, paired(): return lax.ppermute(value, 'gz', [(i, i ^ mask) for i in range(count)])  15.4 us
    ppermute x4, waiting for transfers between devices, swapped(): return lax.ppermute(value, 'gy', [(0, 1), (1, 0)])  12.3 us
    pallas_call x1, Pallas kernels, interior_pass(): pl.pallas_call(interior_kernel, in_specs=[SMEM_SPEC] + [VMEM_SPEC] * 2, o...  11.1 us
    ppermute x4, starting transfers between devices, swapped(): return lax.ppermute(value, 'gy', [(0, 1), (1, 0)])  6.95 us
    ppermute x4, starting transfers between devices, outer_paired(): return lax.ppermute(value, 'gz', pairs + [(j, i) for i, j in pairs])  2.79 us
  transfers between devices with their start and end apart: 21, of which 13 were waited for; matrix products, arithmetic and copies ran while one was open for 0% of the time, Pallas kernels for 10%

profile of v7, /device:TPU:0, one launch (start us, length us, event | category | flops | bytes accessed | tf_op | source)
XLA Modules:
  0.0 107.0 jit_solution(8472830854178589491)
XLA Ops:
  0.8 1.8 %rims.1 = (f32[2,64,512]{2,1,0:T(8,128)S(1)}, f32[2,64,512]{2,1,0:T(8,128)S(1)}, f32[32,2,512]{2,1,0:T(2,128)S(1)}) custom-call(s32[2]{0:T(128)S(1)} %pad_add_fusion.3.place.half, f32[32,64,512]{2,1,0:T(8,128)} %moving.1), custom_call_target="tpu_custom_call" | custom-call | tf_op jit(solution)/shard_map/rims/pallas_call | solution.py:377
  3.7 3.2 %collective-permute-start.2 = (f32[32,2,512]{2,1,0:T(2,128)S(1)}, f32[32,2,512]{2,1,0:T(2,128)S(1)}, u32[]{:S(2)}, u32[]{:S(2)}) collective-permute-start(f32[32,2,512]{2,1,0:T(2,128)S(1)} %get-tuple-element.32), channel_id=1, source_target_pairs={{0,1},{1,0},{2,3},{3,2},{4,5},{5,4},{6,7},{7,6},{8,9},{9,8},{10,11... | collective-permute-start | bytes 393224 | tf_op jit(solution)/shard_map/ppermute | solution.py:425
  6.9 11.1 %interior.1 = (f32[3,32,64,512]{3,2,1,0:T(8,128)S(1)}, f32[5,64,1536]{2,1,0:T(8,128)S(1)}, f32[4,64,512]{2,1,0:T(8,128)S(1)}, f32[32,8,512]{2,1,0:T(8,128)S(1)}) custom-call(s32[2]{0:T(128)S(1)} %pad_add_fusion.3.place.half, f32[32,64,512]{2,1,0:T(8,128)S(1)} %copy-done, f32[32,64,512]{2,1,0:T(8,128)S(1)} %copy-done.3), custom_call_target="tpu_custom_call" | custom-call | flops 100000000 | bytes 40000000 | tf_op jit(solution)/shard_map/interior/pallas_call | solution.py:307
  18.1 1.9 %edge.1 = (f32[3,32,64,512]{3,2,1,0:T(8,128)S(1)}, f32[5,64,1536]{2,1,0:T(8,128)S(1)}, f32[40,128]{1,0:T(8,128)S(1)}) custom-call(s32[2]{0:T(128)S(1)} %pad_add_fusion.3.place.half, f32[2,64,512]{2,1,0:T(8,128)S(1)} %collective-permute-done.inner, f32[2,64,512]{2,1,0:T(8,128)S(1)} %collective-permute-done.1.outer, ...), custom_call_target="tpu_custom_call", output_to_operand_aliasing={{0}: (8, {}), {1}: (9, {})} | custom-call | tf_op jit(solution)/shard_map/edge/pallas_call | solution.py:324
  20.0 2.5 %collective-permute-start.3 = (f32[40,128]{1,0:T(8,128)S(1)}, f32[40,128]{1,0:T(8,128)S(1)}, u32[]{:S(2)}, u32[]{:S(2)}) collective-permute-start(f32[40,128]{1,0:T(8,128)S(1)} %get-tuple-element.37), channel_id=1, source_target_pairs={{0,1},{1,0},{2,3},{3,2},{4,5},{5,4},{6,7},{7,6},{8,9},{9,8},{10,11... | collective-permute-start | bytes 61448 | tf_op jit(solution)/shard_map/ppermute | solution.py:425
  22.4 2.9 %collective-permute-done.3 = f32[40,128]{1,0:T(8,128)S(1)} collective-permute-done((f32[40,128]{1,0:T(8,128)S(1)}, f32[40,128]{1,0:T(8,128)S(1)}, u32[]{:S(2)}, u32[]{:S(2)}) %collective-permute-start.3) | collective-permute-done | bytes 20512 | tf_op jit(solution)/shard_map/ppermute | solution.py:425
  25.3 1.6 %collective-permute-start.4 = (f32[40,128]{1,0:T(8,128)S(1)}, f32[40,128]{1,0:T(8,128)S(1)}, u32[]{:S(2)}, u32[]{:S(2)}) collective-permute-start(f32[40,128]{1,0:T(8,128)S(1)} %add.105), channel_id=1, source_target_pairs={{0,2},{2,0},{4,6},{6,4},{8,10},{10,8},{12,14},{14,12},{16,18},{18,... | collective-permute-start | bytes 61448 | tf_op jit(solution)/shard_map/ppermute | solution.py:430
  28.5 5.0 %collective-permute-start.6 = (f32[8,128]{1,0:T(8,128)S(1)}, f32[8,128]{1,0:T(8,128)S(1)}, u32[]{:S(2)}, u32[]{:S(2)}) collective-permute-start(f32[8,128]{1,0:T(8,128)S(1)} %slice_select_fusion.3), channel_id=1, source_target_pairs={{0,2},{2,0},{4,6},{6,4},{8,10},{10,8},{12,14},{14,12},{16,18},{18,... | collective-permute-start | bytes 12296 | tf_op jit(solution)/shard_map/ppermute | solution.py:430
  34.4 8.5 %hessian.2 = (f32[40,128]{1,0:T(8,128)S(1)}, f32[8,128]{1,0:T(8,128)}) custom-call(s32[2]{0:T(128)S(1)} %pad_add_fusion.3.place.half, f32[40,128]{1,0:T(8,128)S(1)} %fusion.3.ctl, f32[16,128]{1,0:T(8,128)S(1)} %slice.120.base, f32[3,32,64,512]{3,2,1,0:T(8,128)S(1)} %get-tuple-element.38.grad, bf16[2,2048,192]{2,1,0:T(8,128)(2,1)S(1)} %copy-done.1, ...), custom_call_target="tpu_custom_call" | custom-call | tf_op jit(solution)/shard_map/hessian/pallas_call | solution.py:337
  43.6 4.6 %collective-permute-done.7 = f32[40,128]{1,0:T(8,128)S(1)} collective-permute-done((f32[40,128]{1,0:T(8,128)S(1)}, f32[40,128]{1,0:T(8,128)S(1)}, u32[]{:S(2)}, u32[]{:S(2)}) %collective-permute-start.7) | collective-permute-done | bytes 20512 | tf_op jit(solution)/shard_map/ppermute | solution.py:425
  48.2 1.2 %collective-permute-done.8 = f32[40,128]{1,0:T(8,128)S(1)} collective-permute-done((f32[40,128]{1,0:T(8,128)S(1)}, f32[40,128]{1,0:T(8,128)S(1)}, u32[]{:S(2)}, u32[]{:S(2)}) %collective-permute-start.8) | collective-permute-done | bytes 20512 | tf_op jit(solution)/shard_map/ppermute | solution.py:430
  50.1 4.7 %collective-permute-start.10 = (f32[8,128]{1,0:T(8,128)S(1)}, f32[8,128]{1,0:T(8,128)S(1)}, u32[]{:S(2)}, u32[]{:S(2)}) collective-permute-start(f32[8,128]{1,0:T(8,128)S(1)} %slice_select_fusion.2), channel_id=1, source_target_pairs={{0,2},{2,0},{4,6},{6,4},{8,10},{10,8},{12,14},{14,12},{16,18},{18,... | collective-permute-start | bytes 12296 | tf_op jit(solution)/shard_map/ppermute | solution.py:430
  55.6 8.0 %hessian.3 = (f32[40,128]{1,0:T(8,128)S(1)}, f32[8,128]{1,0:T(8,128)S(1)}) custom-call(s32[2]{0:T(128)S(1)} %pad_add_fusion.3.place.half, f32[40,128]{1,0:T(8,128)S(1)} %fusion.7.ctl, f32[16,128]{1,0:T(8,128)S(1)} %slice.120.base, f32[3,32,64,512]{3,2,1,0:T(8,128)S(1)} %get-tuple-element.38.grad, bf16[2,2048,192]{2,1,0:T(8,128)(2,1)S(1)} %copy-done.1, ...), custom_call_target="tpu_custom_call" | custom-call | tf_op jit(solution)/shard_map/hessian/pallas_call | solution.py:337
  64.2 4.8 %collective-permute-done.11 = f32[48,128]{1,0:T(8,128)S(1)} collective-permute-done((f32[48,128]{1,0:T(8,128)S(1)}, f32[48,128]{1,0:T(8,128)S(1)}, u32[]{:S(2)}, u32[]{:S(2)}) %collective-permute-start.11) | collective-permute-done | bytes 24608 | tf_op jit(solution)/shard_map/ppermute | solution.py:425
  69.0 1.2 %collective-permute-done.12 = f32[48,128]{1,0:T(8,128)S(1)} collective-permute-done((f32[48,128]{1,0:T(8,128)S(1)}, f32[48,128]{1,0:T(8,128)S(1)}, u32[]{:S(2)}, u32[]{:S(2)}) %collective-permute-start.12) | collective-permute-done | bytes 24608 | tf_op jit(solution)/shard_map/ppermute | solution.py:430
  70.2 2.0 %collective-permute-start.13 = (f32[8,128]{1,0:T(8,128)S(1)}, f32[8,128]{1,0:T(8,128)S(1)}, u32[]{:S(2)}, u32[]{:S(2)}) collective-permute-start(f32[8,128]{1,0:T(8,128)S(1)} %slice_add_fusion), channel_id=1, source_target_pairs={{0,4},{2,6},{4,0},{6,2},{8,12},{10,14},{12,8},{14,10},{16,20},{18,... | collective-permute-start | bytes 12296 | tf_op jit(solution)/shard_map/ppermute | solution.py:430
  72.2 6.9 %collective-permute-start.14 = (f32[8,128]{1,0:T(8,128)S(1)}, f32[8,128]{1,0:T(8,128)S(1)}, u32[]{:S(2)}, u32[]{:S(2)}) collective-permute-start(f32[8,128]{1,0:T(8,128)S(1)} %slice_add_fusion), channel_id=1, source_target_pairs={{0,8},{2,10},{4,12},{6,14},{8,0},{10,2},{12,4},{14,6},{16,24},{18,... | collective-permute-start | bytes 12296 | tf_op jit(solution)/shard_map/ppermute | solution.py:430
  80.7 3.2 %collective-permute-done.15 = f32[8,128]{1,0:T(8,128)S(1)} collective-permute-done((f32[8,128]{1,0:T(8,128)S(1)}, f32[8,128]{1,0:T(8,128)S(1)}, u32[]{:S(2)}, u32[]{:S(2)}) %collective-permute-start.15) | collective-permute-done | bytes 4128 | tf_op jit(solution)/shard_map/ppermute | solution.py:430
  84.0 6.0 %collective-permute-start.17 = (f32[8,128]{1,0:T(8,128)S(1)}, f32[8,128]{1,0:T(8,128)S(1)}, u32[]{:S(2)}, u32[]{:S(2)}) collective-permute-start(f32[8,128]{1,0:T(8,128)S(1)} %add_add_fusion.1), channel_id=1, source_target_pairs={{0,16},{2,18},{4,20},{6,22},{8,24},{10,26},{12,28},{14,30},{16,0},... | collective-permute-start | bytes 12296 | tf_op jit(solution)/shard_map/ppermute | solution.py:430
  90.0 1.6 %collective-permute-done.17 = f32[8,128]{1,0:T(8,128)S(1)} collective-permute-done((f32[8,128]{1,0:T(8,128)S(1)}, f32[8,128]{1,0:T(8,128)S(1)}, u32[]{:S(2)}, u32[]{:S(2)}) %collective-permute-start.17) | collective-permute-done | bytes 4128 | tf_op jit(solution)/shard_map/ppermute | solution.py:430
  91.6 6.0 %collective-permute-start.18 = (f32[8,128]{1,0:T(8,128)S(1)}, f32[8,128]{1,0:T(8,128)S(1)}, u32[]{:S(2)}, u32[]{:S(2)}) collective-permute-start(f32[8,128]{1,0:T(8,128)S(1)} %add.119), channel_id=1, source_target_pairs={{0,32},{2,34},{4,36},{6,38},{8,40},{10,42},{12,44},{14,46},{16,48}... | collective-permute-start | bytes 12296 | tf_op jit(solution)/shard_map/ppermute | solution.py:430
  97.5 3.9 %collective-permute-start.19 = (f32[8,128]{1,0:T(8,128)S(1)}, f32[8,128]{1,0:T(8,128)S(1)}, u32[]{:S(2)}, u32[]{:S(2)}) collective-permute-start(f32[8,128]{1,0:T(8,128)S(1)} %add.119), channel_id=1, source_target_pairs={{0,64},{2,66},{4,68},{6,70},{8,72},{10,74},{12,76},{14,78},{16,80}... | collective-permute-start | bytes 12296 | tf_op jit(solution)/shard_map/ppermute | solution.py:430
  101.4 1.6 %collective-permute-done.19 = f32[8,128]{1,0:T(8,128)S(1)} collective-permute-done((f32[8,128]{1,0:T(8,128)S(1)}, f32[8,128]{1,0:T(8,128)S(1)}, u32[]{:S(2)}, u32[]{:S(2)}) %collective-permute-start.19) | collective-permute-done | bytes 4128 | tf_op jit(solution)/shard_map/ppermute | solution.py:430
  103.0 3.2 %collective-permute-done.20 = f32[8,128]{1,0:T(8,128)S(1)} collective-permute-done((f32[8,128]{1,0:T(8,128)S(1)}, f32[8,128]{1,0:T(8,128)S(1)}, u32[]{:S(2)}, u32[]{:S(2)}) %collective-permute-start.20) | collective-permute-done | bytes 4128 | tf_op jit(solution)/shard_map/ppermute | solution.py:430
  (63 shorter events, 8.7 us)
Async XLA Ops:
  2.7 15.3 %collective-permute-start = (f32[2,64,512]{2,1,0:T(8,128)S(1)}, f32[2,64,512]{2,1,0:T(8,128)S(1)}, u32[]{:S(2)}, u32[]{:S(2)}) collective-permute-start(f32[2,64,512]{2,1,0:T(8,128)S(1)} %get-tuple-element.30), channel_id=1, source_target_pairs={{0,2},{2,0},{4,6},{6,4},{8,10},{10,8},{12,14},{14,12},{16,18},{18,... | collective-permute-start | bytes 786440 | tf_op jit(solution)/shard_map/ppermute | solution.py:430
  2.8 15.2 %collective-permute-start.1 = (f32[2,64,512]{2,1,0:T(8,128)S(1)}, f32[2,64,512]{2,1,0:T(8,128)S(1)}, u32[]{:S(2)}, u32[]{:S(2)}) collective-permute-start(f32[2,64,512]{2,1,0:T(8,128)S(1)} %get-tuple-element.31), channel_id=1, source_target_pairs={{2,4},{6,8},{10,12},{14,16},{18,20},{22,24},{26,28},{30,32},{34,36... | collective-permute-start | bytes 786440 | tf_op jit(solution)/shard_map/ppermute | solution.py:440
  3.6 14.4 %copy-start.2 = (bf16[256,1536]{1,0:T(8,128)(2,1)S(1)}, bf16[256,1536]{1,0:T(8,128)(2,1)}, u32[]{:S(2)}) copy-start(bf16[256,1536]{1,0:T(8,128)(2,1)} %constant.47.clone.xt) | copy-start | bytes 2359300
  3.7 14.4 %copy-start.4 = (bf16[2,80,320]{2,1,0:T(8,128)(2,1)S(1)}, bf16[2,80,320]{2,1,0:T(8,128)(2,1)}, u32[]{:S(2)}) copy-start(bf16[2,80,320]{2,1,0:T(8,128)(2,1)} %constant.46.clone.back) | copy-start | bytes 307204
  3.7 14.3 %collective-permute-start.2 = (f32[32,2,512]{2,1,0:T(2,128)S(1)}, f32[32,2,512]{2,1,0:T(2,128)S(1)}, u32[]{:S(2)}, u32[]{:S(2)}) collective-permute-start(f32[32,2,512]{2,1,0:T(2,128)S(1)} %get-tuple-element.32), channel_id=1, source_target_pairs={{0,1},{1,0},{2,3},{3,2},{4,5},{5,4},{6,7},{7,6},{8,9},{9,8},{10,11... | collective-permute-start | bytes 393224 | tf_op jit(solution)/shard_map/ppermute | solution.py:425
  18.1 16.3 %copy-start.1 = (bf16[2,2048,192]{2,1,0:T(8,128)(2,1)S(1)}, bf16[2,2048,192]{2,1,0:T(8,128)(2,1)}, u32[]{:S(2)}) copy-start(bf16[2,2048,192]{2,1,0:T(8,128)(2,1)} %constant.45.clone.front) | copy-start | bytes 4718596
  20.0 5.4 %collective-permute-start.3 = (f32[40,128]{1,0:T(8,128)S(1)}, f32[40,128]{1,0:T(8,128)S(1)}, u32[]{:S(2)}, u32[]{:S(2)}) collective-permute-start(f32[40,128]{1,0:T(8,128)S(1)} %get-tuple-element.37), channel_id=1, source_target_pairs={{0,1},{1,0},{2,3},{3,2},{4,5},{5,4},{6,7},{7,6},{8,9},{9,8},{10,11... | collective-permute-start | bytes 61448 | tf_op jit(solution)/shard_map/ppermute | solution.py:425
  25.3 2.5 %collective-permute-start.4 = (f32[40,128]{1,0:T(8,128)S(1)}, f32[40,128]{1,0:T(8,128)S(1)}, u32[]{:S(2)}, u32[]{:S(2)}) collective-permute-start(f32[40,128]{1,0:T(8,128)S(1)} %add.105), channel_id=1, source_target_pairs={{0,2},{2,0},{4,6},{6,4},{8,10},{10,8},{12,14},{14,12},{16,18},{18,... | collective-permute-start | bytes 61448 | tf_op jit(solution)/shard_map/ppermute | solution.py:430
  27.8 0.7 collective-permute-start.5
  28.5 5.9 %collective-permute-start.6 = (f32[8,128]{1,0:T(8,128)S(1)}, f32[8,128]{1,0:T(8,128)S(1)}, u32[]{:S(2)}, u32[]{:S(2)}) collective-permute-start(f32[8,128]{1,0:T(8,128)S(1)} %slice_select_fusion.3), channel_id=1, source_target_pairs={{0,2},{2,0},{4,6},{6,4},{8,10},{10,8},{12,14},{14,12},{16,18},{18,... | collective-permute-start | bytes 12296 | tf_op jit(solution)/shard_map/ppermute | solution.py:430
  42.9 5.3 %collective-permute-start.7 = (f32[40,128]{1,0:T(8,128)S(1)}, f32[40,128]{1,0:T(8,128)S(1)}, u32[]{:S(2)}, u32[]{:S(2)}) collective-permute-start(f32[40,128]{1,0:T(8,128)S(1)} %get-tuple-element.39), channel_id=1, source_target_pairs={{0,1},{1,0},{2,3},{3,2},{4,5},{5,4},{6,7},{7,6},{8,9},{9,8},{10,11... | collective-permute-start | bytes 61448 | tf_op jit(solution)/shard_map/ppermute | solution.py:425
  48.2 1.2 %collective-permute-start.8 = (f32[40,128]{1,0:T(8,128)S(1)}, f32[40,128]{1,0:T(8,128)S(1)}, u32[]{:S(2)}, u32[]{:S(2)}) collective-permute-start(f32[40,128]{1,0:T(8,128)S(1)} %add.109), channel_id=1, source_target_pairs={{0,2},{2,0},{4,6},{6,4},{8,10},{10,8},{12,14},{14,12},{16,18},{18,... | collective-permute-start | bytes 61448 | tf_op jit(solution)/shard_map/ppermute | solution.py:430
  49.4 0.7 collective-permute-start.9
  50.1 5.5 %collective-permute-start.10 = (f32[8,128]{1,0:T(8,128)S(1)}, f32[8,128]{1,0:T(8,128)S(1)}, u32[]{:S(2)}, u32[]{:S(2)}) collective-permute-start(f32[8,128]{1,0:T(8,128)S(1)} %slice_select_fusion.2), channel_id=1, source_target_pairs={{0,2},{2,0},{4,6},{6,4},{8,10},{10,8},{12,14},{14,12},{16,18},{18,... | collective-permute-start | bytes 12296 | tf_op jit(solution)/shard_map/ppermute | solution.py:430
  63.6 5.4 %collective-permute-start.11 = (f32[48,128]{1,0:T(8,128)S(1)}, f32[48,128]{1,0:T(8,128)S(1)}, u32[]{:S(2)}, u32[]{:S(2)}) collective-permute-start(f32[48,128]{1,0:T(8,128)S(1)} %constant_dynamic-update-slice_fusion), channel_id=1, source_target_pairs={{0,1},{1,0},{2,3},{3,2},{4,5},{5,4},{6,7},{7,6},{8,9},{9,8},{10,11... | collective-permute-start | bytes 73736 | tf_op jit(solution)/shard_map/ppermute | solution.py:425
  69.0 1.2 %collective-permute-start.12 = (f32[48,128]{1,0:T(8,128)S(1)}, f32[48,128]{1,0:T(8,128)S(1)}, u32[]{:S(2)}, u32[]{:S(2)}) collective-permute-start(f32[48,128]{1,0:T(8,128)S(1)} %add.113), channel_id=1, source_target_pairs={{0,2},{2,0},{4,6},{6,4},{8,10},{10,8},{12,14},{14,12},{16,18},{18,... | collective-permute-start | bytes 73736 | tf_op jit(solution)/shard_map/ppermute | solution.py:430
  70.2 9.6 %collective-permute-start.13 = (f32[8,128]{1,0:T(8,128)S(1)}, f32[8,128]{1,0:T(8,128)S(1)}, u32[]{:S(2)}, u32[]{:S(2)}) collective-permute-start(f32[8,128]{1,0:T(8,128)S(1)} %slice_add_fusion), channel_id=1, source_target_pairs={{0,4},{2,6},{4,0},{6,2},{8,12},{10,14},{12,8},{14,10},{16,20},{18,... | collective-permute-start | bytes 12296 | tf_op jit(solution)/shard_map/ppermute | solution.py:430
  72.2 8.6 %collective-permute-start.14 = (f32[8,128]{1,0:T(8,128)S(1)}, f32[8,128]{1,0:T(8,128)S(1)}, u32[]{:S(2)}, u32[]{:S(2)}) collective-permute-start(f32[8,128]{1,0:T(8,128)S(1)} %slice_add_fusion), channel_id=1, source_target_pairs={{0,8},{2,10},{4,12},{6,14},{8,0},{10,2},{12,4},{14,6},{16,24},{18,... | collective-permute-start | bytes 12296 | tf_op jit(solution)/shard_map/ppermute | solution.py:430
  79.1 4.8 %collective-permute-start.15 = (f32[8,128]{1,0:T(8,128)S(1)}, f32[8,128]{1,0:T(8,128)S(1)}, u32[]{:S(2)}, u32[]{:S(2)}) collective-permute-start(f32[8,128]{1,0:T(8,128)S(1)} %slice_add_fusion), channel_id=1, source_target_pairs={{0,12},{2,14},{4,8},{6,10},{8,4},{10,6},{12,0},{14,2},{16,28},{18,... | collective-permute-start | bytes 12296 | tf_op jit(solution)/shard_map/ppermute | solution.py:430
  79.1 4.8 %collective-permute-start.16 = (f32[24,128]{1,0:T(8,128)S(1)}, f32[24,128]{1,0:T(8,128)S(1)}, u32[]{:S(2)}, u32[]{:S(2)}) collective-permute-start(f32[24,128]{1,0:T(8,128)S(1)} %fusion.21), channel_id=1, source_target_pairs={{2,4},{6,8},{10,12},{14,16},{18,20},{22,24},{26,28},{30,32},{34,36... | collective-permute-start | bytes 36872 | tf_op jit(solution)/shard_map/ppermute | solution.py:440
  84.0 7.6 %collective-permute-start.17 = (f32[8,128]{1,0:T(8,128)S(1)}, f32[8,128]{1,0:T(8,128)S(1)}, u32[]{:S(2)}, u32[]{:S(2)}) collective-permute-start(f32[8,128]{1,0:T(8,128)S(1)} %add_add_fusion.1), channel_id=1, source_target_pairs={{0,16},{2,18},{4,20},{6,22},{8,24},{10,26},{12,28},{14,30},{16,0},... | collective-permute-start | bytes 12296 | tf_op jit(solution)/shard_map/ppermute | solution.py:430
  91.6 9.8 %collective-permute-start.18 = (f32[8,128]{1,0:T(8,128)S(1)}, f32[8,128]{1,0:T(8,128)S(1)}, u32[]{:S(2)}, u32[]{:S(2)}) collective-permute-start(f32[8,128]{1,0:T(8,128)S(1)} %add.119), channel_id=1, source_target_pairs={{0,32},{2,34},{4,36},{6,38},{8,40},{10,42},{12,44},{14,46},{16,48}... | collective-permute-start | bytes 12296 | tf_op jit(solution)/shard_map/ppermute | solution.py:430
  97.5 5.5 %collective-permute-start.19 = (f32[8,128]{1,0:T(8,128)S(1)}, f32[8,128]{1,0:T(8,128)S(1)}, u32[]{:S(2)}, u32[]{:S(2)}) collective-permute-start(f32[8,128]{1,0:T(8,128)S(1)} %add.119), channel_id=1, source_target_pairs={{0,64},{2,66},{4,68},{6,70},{8,72},{10,74},{12,76},{14,78},{16,80}... | collective-permute-start | bytes 12296 | tf_op jit(solution)/shard_map/ppermute | solution.py:430
  101.4 4.8 %collective-permute-start.20 = (f32[8,128]{1,0:T(8,128)S(1)}, f32[8,128]{1,0:T(8,128)S(1)}, u32[]{:S(2)}, u32[]{:S(2)}) collective-permute-start(f32[8,128]{1,0:T(8,128)S(1)} %add.119), channel_id=1, source_target_pairs={{0,96},{2,98},{4,100},{6,102},{8,104},{10,106},{12,108},{14,110},{... | collective-permute-start | bytes 12296 | tf_op jit(solution)/shard_map/ppermute | solution.py:430
  (2 other events, 8.4 us)

commit v8 on v7

--- a/solution.py
+++ b/solution.py
@@ -182,10 +182,10 @@
 
 
 def edge_kernel(
-    half, inner, outer, y_rows, z_edges, y_edges, back, xt, grad_in, planes_in, grad, planes, out
+    half, parity, inner, outer, y_rows, z_edges, y_edges, back, xt, grad_in, planes_in, grad, planes, out
 ):
     del grad_in, planes_in
-    lower = half[1] == 0
+    lower = parity[0] == 0
     weights = spline_weights()
 
     def strip(y, carry):
@@ -231,7 +231,7 @@
     out[...] = contracted(planes, back[half[0]], xt) * (-data_weight / 12.0)
 
 
-def hessian_kernel(half, ctl, base, grad, front, back, xt, out, sums, spread, field, planes):
+def hessian_kernel(half, ctl, base, grad, front, back, xt, out, spread, field, planes):
     high, low = halves_of(ctl[...])
     first, second = xt[:128], xt[128:]
     value = jnp.dot(high, first, preferred_element_type=F32)
@@ -269,7 +269,7 @@
     near += jnp.where(lane > 0, pltpu.roll(owned, 1, 1), 0.0)
     near += jnp.where(lane < CX - 1, pltpu.roll(owned, 127, 1), 0.0)
     smooth = (0.5 * smooth_weight) * (6.0 * owned - near)
-    out[...] = contracted(planes, back[half[0]], xt) * scale
+    out[:CTL] = contracted(planes, back[half[0]], xt) * scale
     out[CY : 3 * CY] += smooth
     first = base[...]
 
@@ -287,7 +287,7 @@
     tile = jnp.zeros((8, 128), F32)
     for j, line in enumerate(lines):
         tile = jnp.where(which == j, line, tile)
-    sums[...] = tile
+    out[CTL:] = tile
 
 
 VMEM_SPEC = pl.BlockSpec(memory_space=pltpu.VMEM)
@@ -320,16 +320,16 @@
     )(half, moving, fixed)
 
 
-def edge_pass(half, inner, outer, y_rows, z_edges, y_edges, back_table, x_table, grad, planes):
+def edge_pass(half, parity, inner, outer, y_rows, z_edges, y_edges, back_table, x_table, grad, planes):
     grad, _, part = pl.pallas_call(
         edge_kernel,
-        in_specs=[SMEM_SPEC] + [VMEM_SPEC] * 9,
+        in_specs=[SMEM_SPEC] * 2 + [VMEM_SPEC] * 9,
         out_specs=[VMEM_SPEC] * 3,
         out_shape=[GRAD_SHAPE, PLANES_SHAPE, CTL_SHAPE],
-        input_output_aliases={8: 0, 9: 1},
+        input_output_aliases={9: 0, 10: 1},
         compiler_params=PARAMS,
         name="edge",
-    )(half, inner, outer, y_rows, z_edges, y_edges, back_table, x_table, grad, planes)
+    )(half, parity, inner, outer, y_rows, z_edges, y_edges, back_table, x_table, grad, planes)
     return grad, part
 
 
@@ -337,23 +337,20 @@
     return pl.pallas_call(
         hessian_kernel,
         in_specs=[SMEM_SPEC] + [VMEM_SPEC] * 6,
-        out_specs=[VMEM_SPEC] * 2,
+        out_specs=VMEM_SPEC,
         scratch_shapes=[
             pltpu.VMEM((4 * KPAD, 3 * NX), BF),
             pltpu.VMEM((ROWS, 3 * NX), F32),
             pltpu.VMEM((PLANES, NY, 3 * NX), F32),
         ],
-        out_shape=[
-            jax.ShapeDtypeStruct((CTL, 128), F32),
-            jax.ShapeDtypeStruct((8, 128), F32),
-        ],
+        out_shape=jax.ShapeDtypeStruct((CTL + 8, 128), F32),
         compiler_params=PARAMS,
         name="hessian",
     )(half, ctl, base, grad, front_table, back_table, x_table)
 
 
-def rims_kernel(place, moving, inner, outer, y_rim, tile, sems):
-    half, parity = place[0], place[1]
+def rims_kernel(half, parity, moving, inner, outer, y_rim, tile, sems):
+    half, parity = half[0], parity[0]
     top, bottom = NZ - 2, 0
     copies = [
         pltpu.make_async_copy(
@@ -373,16 +370,16 @@
     y_rim[...] = jnp.where(half == 0, tile[:, 6:8, :], tile[:, 0:2, :])
 
 
-def rims_pass(place, moving):
+def rims_pass(half, parity, moving):
     return pl.pallas_call(
         rims_kernel,
-        in_specs=[SMEM_SPEC, HBM_SPEC],
+        in_specs=[SMEM_SPEC, SMEM_SPEC, HBM_SPEC],
         out_specs=[VMEM_SPEC] * 3,
         out_shape=[jax.ShapeDtypeStruct(shape, F32) for shape in ((2, NY, NX), (2, NY, NX), (NZ, 2, NX))],
         scratch_shapes=[pltpu.VMEM((NZ, 8, NX), F32), pltpu.SemaphoreType.DMA((3,))],
         compiler_params=pltpu.CompilerParams(vmem_limit_bytes=RIMS_MIB * 1024 * 1024),
         name="rims",
-    )(place, moving)
+    )(half, parity, moving)
 
 
 def held_kernel(*refs):
@@ -451,7 +448,7 @@
 
 
 def all_planes(lower, inside, part):
-    part = part + swapped(part)
+    part = (part + swapped(part))[:CTL]
     seven = pair_sum(lower, part, paired(part, 1))
     three = outer_terms(lower, seven)
     one = paired(jnp.where(lower, three[2 * CY :], three[:CY]), 1)
@@ -462,29 +459,31 @@
 
 def local(moving, fixed):
     slab = lax.axis_index("gz").astype(jnp.int32)
-    half = jnp.stack([lax.axis_index("gy").astype(jnp.int32), slab % 2])
+    half = lax.axis_index("gy").astype(jnp.int32).reshape(1)
+    parity = (slab % 2).reshape(1)
     lower = slab % 2 == 0
     at = slab * (2 * CY) - CY + lax.broadcasted_iota(jnp.int32, (CTL, 128), 0)
     inside = ((at >= 0) & (at < lax.axis_size("gz") * (2 * CY))).astype(F32)
-    moving, half, lower, inside = lax.optimization_barrier((moving, half, lower, inside))
+    moving, half, parity, lower, inside = lax.optimization_barrier(
+        (moving, half, parity, lower, inside)
+    )
     front, back, xt = (jnp.asarray(a) for a in tables())
 
-    inner, outer, y_rim = held(*rims_pass(half, moving))
+    inner, outer, y_rim = held(*rims_pass(half, parity, moving))
     inner = paired(inner, 1)
     outer = outer_paired(outer)
     y_rows = swapped(y_rim)
 
     grad, planes, z_edges, y_edges = interior_pass(half, moving, fixed)
     grad, part = edge_pass(
-        half, inner, outer, y_rows, z_edges, y_edges, back, xt, grad, planes
+        half, parity, inner, outer, y_rows, z_edges, y_edges, back, xt, grad, planes
     )
     b_planes = all_planes(lower, inside, part)
     b = b_planes[CY : 3 * CY]
-    part, _ = hessian_pass(half, b_planes, b, grad, front, back, xt)
+    part = hessian_pass(half, b_planes, b, grad, front, back, xt)
     u_planes = all_planes(lower, inside, part)
     u = u_planes[CY : 3 * CY]
-    part, sums = hessian_pass(half, u_planes, b, grad, front, back, xt)
-    both = jnp.concatenate([part, sums], 0)
+    both = hessian_pass(half, u_planes, b, grad, front, back, xt)
     both = both + swapped(both)
     other = paired(both, 1)
     seven = pair_sum(lower, both[:CTL], other[:CTL])

time: 107 us -> 104 us (0.972)
  Pallas kernels: 32.1 us -> 28.9 us
    pallas_call x2, Pallas kernels: 16.5 us -> 14.9 us  [hessian_pass(): pl.pallas_call(hessian_kernel, in_specs=[SMEM_SPEC] + [VMEM_SPEC] * 6, ou...]
    pallas_call x2, Pallas kernels: 3.74 us -> 2.64 us  [the longest x1 1.34 us: edge_pass(): pl.pallas_call(edge_kernel, in_specs=[SMEM_SPEC] * 2 + [VMEM_SPEC] * 9, o...]
where the time goes in v8:
time: 104 us
  starting transfers between devices  46 us (44%)
  Pallas kernels  28.9 us (28%)
  waiting for transfers between devices  27.7 us (27%)
    ppermute x13, starting transfers between devices, paired(): return lax.ppermute(value, 'gz', [(i, i ^ mask) for i in range(count)])  36.2 us
    ppermute x13, waiting for transfers between devices, paired(): return lax.ppermute(value, 'gz', [(i, i ^ mask) for i in range(count)])  15.4 us
    pallas_call x2, Pallas kernels, hessian_pass(): pl.pallas_call(hessian_kernel, in_specs=[SMEM_SPEC] + [VMEM_SPEC] * 6, ou...  14.9 us
    ppermute x4, waiting for transfers between devices, swapped(): return lax.ppermute(value, 'gy', [(0, 1), (1, 0)])  12.3 us
    pallas_call x1, Pallas kernels, interior_pass(): pl.pallas_call(interior_kernel, in_specs=[SMEM_SPEC] + [VMEM_SPEC] * 2, o...  10.6 us
    ppermute x4, starting transfers between devices, swapped(): return lax.ppermute(value, 'gy', [(0, 1), (1, 0)])  7.08 us
    ppermute x4, starting transfers between devices, outer_paired(): return lax.ppermute(value, 'gz', pairs + [(j, i) for i, j in pairs])  2.79 us
  transfers between devices with their start and end apart: 21, of which 13 were waited for; matrix products, arithmetic and copies ran while one was open for 0% of the time, Pallas kernels for 10%

profile of v8, /device:TPU:0, one launch (start us, length us, event | category | flops | bytes accessed | tf_op | source)
XLA Modules:
  0.0 103.8 jit_solution(14811843018690518695)
XLA Ops:
  0.7 1.3 %rims.1 = (f32[2,64,512]{2,1,0:T(8,128)S(1)}, f32[2,64,512]{2,1,0:T(8,128)S(1)}, f32[32,2,512]{2,1,0:T(2,128)S(1)}) custom-call(s32[1]{0:T(128)} %bitcast.half, s32[1]{0:T(128)} %bitcast.1.parity, f32[32,64,512]{2,1,0:T(8,128)} %moving.1), custom_call_target="tpu_custom_call" | custom-call | tf_op jit(solution)/shard_map/rims/pallas_call | solution.py:374
  3.0 3.2 %collective-permute-start.2 = (f32[32,2,512]{2,1,0:T(2,128)S(1)}, f32[32,2,512]{2,1,0:T(2,128)S(1)}, u32[]{:S(2)}, u32[]{:S(2)}) collective-permute-start(f32[32,2,512]{2,1,0:T(2,128)S(1)} %get-tuple-element.31), channel_id=1, source_target_pairs={{0,1},{1,0},{2,3},{3,2},{4,5},{5,4},{6,7},{7,6},{8,9},{9,8},{10,11... | collective-permute-start | bytes 393224 | tf_op jit(solution)/shard_map/ppermute | solution.py:422
  6.2 10.6 %interior.1 = (f32[3,32,64,512]{3,2,1,0:T(8,128)S(1)}, f32[5,64,1536]{2,1,0:T(8,128)S(1)}, f32[4,64,512]{2,1,0:T(8,128)S(1)}, f32[32,8,512]{2,1,0:T(8,128)S(1)}) custom-call(s32[1]{0:T(128)} %bitcast.half, f32[32,64,512]{2,1,0:T(8,128)S(1)} %copy-done, f32[32,64,512]{2,1,0:T(8,128)S(1)} %copy-done.3), custom_call_target="tpu_custom_call" | custom-call | flops 100000000 | bytes 40000000 | tf_op jit(solution)/shard_map/interior/pallas_call | solution.py:307
  16.9 1.3 %edge.1 = (f32[3,32,64,512]{3,2,1,0:T(8,128)S(1)}, f32[5,64,1536]{2,1,0:T(8,128)S(1)}, f32[40,128]{1,0:T(8,128)S(1)}) custom-call(s32[1]{0:T(128)} %bitcast.half, s32[1]{0:T(128)} %bitcast.1.parity, f32[2,64,512]{2,1,0:T(8,128)S(1)} %collective-permute-done.inner, ...), custom_call_target="tpu_custom_call", output_to_operand_aliasing={{0}: (9, {}), {1}: (10, {})} | custom-call | tf_op jit(solution)/shard_map/edge/pallas_call | solution.py:324
  18.3 2.5 %collective-permute-start.3 = (f32[40,128]{1,0:T(8,128)S(1)}, f32[40,128]{1,0:T(8,128)S(1)}, u32[]{:S(2)}, u32[]{:S(2)}) collective-permute-start(f32[40,128]{1,0:T(8,128)S(1)} %get-tuple-element.36), channel_id=1, source_target_pairs={{0,1},{1,0},{2,3},{3,2},{4,5},{5,4},{6,7},{7,6},{8,9},{9,8},{10,11... | collective-permute-start | bytes 61448 | tf_op jit(solution)/shard_map/ppermute | solution.py:422
  20.7 2.9 %collective-permute-done.3 = f32[40,128]{1,0:T(8,128)S(1)} collective-permute-done((f32[40,128]{1,0:T(8,128)S(1)}, f32[40,128]{1,0:T(8,128)S(1)}, u32[]{:S(2)}, u32[]{:S(2)}) %collective-permute-start.3) | collective-permute-done | bytes 20512 | tf_op jit(solution)/shard_map/ppermute | solution.py:422
  23.7 1.6 %collective-permute-start.4 = (f32[40,128]{1,0:T(8,128)S(1)}, f32[40,128]{1,0:T(8,128)S(1)}, u32[]{:S(2)}, u32[]{:S(2)}) collective-permute-start(f32[40,128]{1,0:T(8,128)S(1)} %add.105), channel_id=1, source_target_pairs={{0,2},{2,0},{4,6},{6,4},{8,10},{10,8},{12,14},{14,12},{16,18},{18,... | collective-permute-start | bytes 61448 | tf_op jit(solution)/shard_map/ppermute | solution.py:427
  26.8 5.0 %collective-permute-start.6 = (f32[8,128]{1,0:T(8,128)S(1)}, f32[8,128]{1,0:T(8,128)S(1)}, u32[]{:S(2)}, u32[]{:S(2)}) collective-permute-start(f32[8,128]{1,0:T(8,128)S(1)} %slice_select_fusion.3), channel_id=1, source_target_pairs={{0,2},{2,0},{4,6},{6,4},{8,10},{10,8},{12,14},{14,12},{16,18},{18,... | collective-permute-start | bytes 12296 | tf_op jit(solution)/shard_map/ppermute | solution.py:427
  32.7 7.5 %hessian.2 = f32[48,128]{1,0:T(8,128)S(1)} custom-call(s32[1]{0:T(128)} %bitcast.half, f32[40,128]{1,0:T(8,128)S(1)} %fusion.3.ctl, f32[16,128]{1,0:T(8,128)S(1)} %slice.124.base, f32[3,32,64,512]{3,2,1,0:T(8,128)S(1)} %get-tuple-element.37.grad, bf16[2,2048,192]{2,1,0:T(8,128)(2,1)S(1)} %copy-done.1, bf16[2,80,320]{2,1,0:T(8,128)(2,1)S(1)} %copy-done.4, ...), custom_call_target="tpu_custom_call" | custom-call | tf_op jit(solution)/shard_map/hessian/pallas_call | solution.py:337
  41.0 4.6 %collective-permute-done.7 = f32[48,128]{1,0:T(8,128)S(1)} collective-permute-done((f32[48,128]{1,0:T(8,128)S(1)}, f32[48,128]{1,0:T(8,128)S(1)}, u32[]{:S(2)}, u32[]{:S(2)}) %collective-permute-start.7) | collective-permute-done | bytes 24608 | tf_op jit(solution)/shard_map/ppermute | solution.py:422
  45.6 1.2 %collective-permute-done.8 = f32[40,128]{1,0:T(8,128)S(1)} collective-permute-done((f32[40,128]{1,0:T(8,128)S(1)}, f32[40,128]{1,0:T(8,128)S(1)}, u32[]{:S(2)}, u32[]{:S(2)}) %collective-permute-start.8) | collective-permute-done | bytes 20512 | tf_op jit(solution)/shard_map/ppermute | solution.py:427
  47.5 4.7 %collective-permute-start.10 = (f32[8,128]{1,0:T(8,128)S(1)}, f32[8,128]{1,0:T(8,128)S(1)}, u32[]{:S(2)}, u32[]{:S(2)}) collective-permute-start(f32[8,128]{1,0:T(8,128)S(1)} %slice_select_fusion.2), channel_id=1, source_target_pairs={{0,2},{2,0},{4,6},{6,4},{8,10},{10,8},{12,14},{14,12},{16,18},{18,... | collective-permute-start | bytes 12296 | tf_op jit(solution)/shard_map/ppermute | solution.py:427
  53.0 7.4 %hessian.3 = f32[48,128]{1,0:T(8,128)S(1)} custom-call(s32[1]{0:T(128)} %bitcast.half, f32[40,128]{1,0:T(8,128)S(1)} %fusion.7.ctl, f32[16,128]{1,0:T(8,128)S(1)} %slice.124.base, f32[3,32,64,512]{3,2,1,0:T(8,128)S(1)} %get-tuple-element.37.grad, bf16[2,2048,192]{2,1,0:T(8,128)(2,1)S(1)} %copy-done.1, bf16[2,80,320]{2,1,0:T(8,128)(2,1)S(1)} %copy-done.4, ...), custom_call_target="tpu_custom_call" | custom-call | tf_op jit(solution)/shard_map/hessian/pallas_call | solution.py:337
  61.1 4.8 %collective-permute-done.11 = f32[48,128]{1,0:T(8,128)S(1)} collective-permute-done((f32[48,128]{1,0:T(8,128)S(1)}, f32[48,128]{1,0:T(8,128)S(1)}, u32[]{:S(2)}, u32[]{:S(2)}) %collective-permute-start.11) | collective-permute-done | bytes 24608 | tf_op jit(solution)/shard_map/ppermute | solution.py:422
  65.9 1.2 %collective-permute-done.12 = f32[48,128]{1,0:T(8,128)S(1)} collective-permute-done((f32[48,128]{1,0:T(8,128)S(1)}, f32[48,128]{1,0:T(8,128)S(1)}, u32[]{:S(2)}, u32[]{:S(2)}) %collective-permute-start.12) | collective-permute-done | bytes 24608 | tf_op jit(solution)/shard_map/ppermute | solution.py:427
  67.1 2.0 %collective-permute-start.13 = (f32[8,128]{1,0:T(8,128)S(1)}, f32[8,128]{1,0:T(8,128)S(1)}, u32[]{:S(2)}, u32[]{:S(2)}) collective-permute-start(f32[8,128]{1,0:T(8,128)S(1)} %slice_add_fusion.1), channel_id=1, source_target_pairs={{0,4},{2,6},{4,0},{6,2},{8,12},{10,14},{12,8},{14,10},{16,20},{18,... | collective-permute-start | bytes 12296 | tf_op jit(solution)/shard_map/ppermute | solution.py:427
  69.0 6.9 %collective-permute-start.14 = (f32[8,128]{1,0:T(8,128)S(1)}, f32[8,128]{1,0:T(8,128)S(1)}, u32[]{:S(2)}, u32[]{:S(2)}) collective-permute-start(f32[8,128]{1,0:T(8,128)S(1)} %slice_add_fusion.1), channel_id=1, source_target_pairs={{0,8},{2,10},{4,12},{6,14},{8,0},{10,2},{12,4},{14,6},{16,24},{18,... | collective-permute-start | bytes 12296 | tf_op jit(solution)/shard_map/ppermute | solution.py:427
  77.6 3.2 %collective-permute-done.15 = f32[8,128]{1,0:T(8,128)S(1)} collective-permute-done((f32[8,128]{1,0:T(8,128)S(1)}, f32[8,128]{1,0:T(8,128)S(1)}, u32[]{:S(2)}, u32[]{:S(2)}) %collective-permute-start.15) | collective-permute-done | bytes 4128 | tf_op jit(solution)/shard_map/ppermute | solution.py:427
  80.8 6.0 %collective-permute-start.17 = (f32[8,128]{1,0:T(8,128)S(1)}, f32[8,128]{1,0:T(8,128)S(1)}, u32[]{:S(2)}, u32[]{:S(2)}) collective-permute-start(f32[8,128]{1,0:T(8,128)S(1)} %add_add_fusion.1), channel_id=1, source_target_pairs={{0,16},{2,18},{4,20},{6,22},{8,24},{10,26},{12,28},{14,30},{16,0},... | collective-permute-start | bytes 12296 | tf_op jit(solution)/shard_map/ppermute | solution.py:427
  86.8 1.6 %collective-permute-done.17 = f32[8,128]{1,0:T(8,128)S(1)} collective-permute-done((f32[8,128]{1,0:T(8,128)S(1)}, f32[8,128]{1,0:T(8,128)S(1)}, u32[]{:S(2)}, u32[]{:S(2)}) %collective-permute-start.17) | collective-permute-done | bytes 4128 | tf_op jit(solution)/shard_map/ppermute | solution.py:427
  88.4 6.0 %collective-permute-start.18 = (f32[8,128]{1,0:T(8,128)S(1)}, f32[8,128]{1,0:T(8,128)S(1)}, u32[]{:S(2)}, u32[]{:S(2)}) collective-permute-start(f32[8,128]{1,0:T(8,128)S(1)} %add.119), channel_id=1, source_target_pairs={{0,32},{2,34},{4,36},{6,38},{8,40},{10,42},{12,44},{14,46},{16,48}... | collective-permute-start | bytes 12296 | tf_op jit(solution)/shard_map/ppermute | solution.py:427
  94.4 3.9 %collective-permute-start.19 = (f32[8,128]{1,0:T(8,128)S(1)}, f32[8,128]{1,0:T(8,128)S(1)}, u32[]{:S(2)}, u32[]{:S(2)}) collective-permute-start(f32[8,128]{1,0:T(8,128)S(1)} %add.119), channel_id=1, source_target_pairs={{0,64},{2,66},{4,68},{6,70},{8,72},{10,74},{12,76},{14,78},{16,80}... | collective-permute-start | bytes 12296 | tf_op jit(solution)/shard_map/ppermute | solution.py:427
  98.3 1.6 %collective-permute-done.19 = f32[8,128]{1,0:T(8,128)S(1)} collective-permute-done((f32[8,128]{1,0:T(8,128)S(1)}, f32[8,128]{1,0:T(8,128)S(1)}, u32[]{:S(2)}, u32[]{:S(2)}) %collective-permute-start.19) | collective-permute-done | bytes 4128 | tf_op jit(solution)/shard_map/ppermute | solution.py:427
  99.9 3.2 %collective-permute-done.20 = f32[8,128]{1,0:T(8,128)S(1)} collective-permute-done((f32[8,128]{1,0:T(8,128)S(1)}, f32[8,128]{1,0:T(8,128)S(1)}, u32[]{:S(2)}, u32[]{:S(2)}) %collective-permute-start.20) | collective-permute-done | bytes 4128 | tf_op jit(solution)/shard_map/ppermute | solution.py:427
  (60 shorter events, 8.8 us)
Async XLA Ops:
  2.1 14.8 %collective-permute-start = (f32[2,64,512]{2,1,0:T(8,128)S(1)}, f32[2,64,512]{2,1,0:T(8,128)S(1)}, u32[]{:S(2)}, u32[]{:S(2)}) collective-permute-start(f32[2,64,512]{2,1,0:T(8,128)S(1)} %get-tuple-element.29), channel_id=1, source_target_pairs={{0,2},{2,0},{4,6},{6,4},{8,10},{10,8},{12,14},{14,12},{16,18},{18,... | collective-permute-start | bytes 786440 | tf_op jit(solution)/shard_map/ppermute | solution.py:427
  2.2 14.7 %collective-permute-start.1 = (f32[2,64,512]{2,1,0:T(8,128)S(1)}, f32[2,64,512]{2,1,0:T(8,128)S(1)}, u32[]{:S(2)}, u32[]{:S(2)}) collective-permute-start(f32[2,64,512]{2,1,0:T(8,128)S(1)} %get-tuple-element.30), channel_id=1, source_target_pairs={{2,4},{6,8},{10,12},{14,16},{18,20},{22,24},{26,28},{30,32},{34,36... | collective-permute-start | bytes 786440 | tf_op jit(solution)/shard_map/ppermute | solution.py:437
  3.0 13.9 %copy-start.2 = (bf16[256,1536]{1,0:T(8,128)(2,1)S(1)}, bf16[256,1536]{1,0:T(8,128)(2,1)}, u32[]{:S(2)}) copy-start(bf16[256,1536]{1,0:T(8,128)(2,1)} %constant.47.clone.xt) | copy-start | bytes 2359300
  3.0 13.9 %copy-start.4 = (bf16[2,80,320]{2,1,0:T(8,128)(2,1)S(1)}, bf16[2,80,320]{2,1,0:T(8,128)(2,1)}, u32[]{:S(2)}) copy-start(bf16[2,80,320]{2,1,0:T(8,128)(2,1)} %constant.46.clone.back) | copy-start | bytes 307204
  3.0 13.8 %collective-permute-start.2 = (f32[32,2,512]{2,1,0:T(2,128)S(1)}, f32[32,2,512]{2,1,0:T(2,128)S(1)}, u32[]{:S(2)}, u32[]{:S(2)}) collective-permute-start(f32[32,2,512]{2,1,0:T(2,128)S(1)} %get-tuple-element.31), channel_id=1, source_target_pairs={{0,1},{1,0},{2,3},{3,2},{4,5},{5,4},{6,7},{7,6},{8,9},{9,8},{10,11... | collective-permute-start | bytes 393224 | tf_op jit(solution)/shard_map/ppermute | solution.py:422
  16.9 15.8 %copy-start.1 = (bf16[2,2048,192]{2,1,0:T(8,128)(2,1)S(1)}, bf16[2,2048,192]{2,1,0:T(8,128)(2,1)}, u32[]{:S(2)}) copy-start(bf16[2,2048,192]{2,1,0:T(8,128)(2,1)} %constant.45.clone.front) | copy-start | bytes 4718596
  18.3 5.4 %collective-permute-start.3 = (f32[40,128]{1,0:T(8,128)S(1)}, f32[40,128]{1,0:T(8,128)S(1)}, u32[]{:S(2)}, u32[]{:S(2)}) collective-permute-start(f32[40,128]{1,0:T(8,128)S(1)} %get-tuple-element.36), channel_id=1, source_target_pairs={{0,1},{1,0},{2,3},{3,2},{4,5},{5,4},{6,7},{7,6},{8,9},{9,8},{10,11... | collective-permute-start | bytes 61448 | tf_op jit(solution)/shard_map/ppermute | solution.py:422
  23.7 2.5 %collective-permute-start.4 = (f32[40,128]{1,0:T(8,128)S(1)}, f32[40,128]{1,0:T(8,128)S(1)}, u32[]{:S(2)}, u32[]{:S(2)}) collective-permute-start(f32[40,128]{1,0:T(8,128)S(1)} %add.105), channel_id=1, source_target_pairs={{0,2},{2,0},{4,6},{6,4},{8,10},{10,8},{12,14},{14,12},{16,18},{18,... | collective-permute-start | bytes 61448 | tf_op jit(solution)/shard_map/ppermute | solution.py:427
  26.1 0.7 collective-permute-start.5
  26.8 5.9 %collective-permute-start.6 = (f32[8,128]{1,0:T(8,128)S(1)}, f32[8,128]{1,0:T(8,128)S(1)}, u32[]{:S(2)}, u32[]{:S(2)}) collective-permute-start(f32[8,128]{1,0:T(8,128)S(1)} %slice_select_fusion.3), channel_id=1, source_target_pairs={{0,2},{2,0},{4,6},{6,4},{8,10},{10,8},{12,14},{14,12},{16,18},{18,... | collective-permute-start | bytes 12296 | tf_op jit(solution)/shard_map/ppermute | solution.py:427
  40.2 5.4 %collective-permute-start.7 = (f32[48,128]{1,0:T(8,128)S(1)}, f32[48,128]{1,0:T(8,128)S(1)}, u32[]{:S(2)}, u32[]{:S(2)}) collective-permute-start(f32[48,128]{1,0:T(8,128)S(1)} %hessian.2), channel_id=1, source_target_pairs={{0,1},{1,0},{2,3},{3,2},{4,5},{5,4},{6,7},{7,6},{8,9},{9,8},{10,11... | collective-permute-start | bytes 73736 | tf_op jit(solution)/shard_map/ppermute | solution.py:422
  45.6 1.2 %collective-permute-start.8 = (f32[40,128]{1,0:T(8,128)S(1)}, f32[40,128]{1,0:T(8,128)S(1)}, u32[]{:S(2)}, u32[]{:S(2)}) collective-permute-start(f32[40,128]{1,0:T(8,128)S(1)} %slice_add_fusion), channel_id=1, source_target_pairs={{0,2},{2,0},{4,6},{6,4},{8,10},{10,8},{12,14},{14,12},{16,18},{18,... | collective-permute-start | bytes 61448 | tf_op jit(solution)/shard_map/ppermute | solution.py:427
  46.8 0.7 collective-permute-start.9
  47.5 5.5 %collective-permute-start.10 = (f32[8,128]{1,0:T(8,128)S(1)}, f32[8,128]{1,0:T(8,128)S(1)}, u32[]{:S(2)}, u32[]{:S(2)}) collective-permute-start(f32[8,128]{1,0:T(8,128)S(1)} %slice_select_fusion.2), channel_id=1, source_target_pairs={{0,2},{2,0},{4,6},{6,4},{8,10},{10,8},{12,14},{14,12},{16,18},{18,... | collective-permute-start | bytes 12296 | tf_op jit(solution)/shard_map/ppermute | solution.py:427
  60.5 5.4 %collective-permute-start.11 = (f32[48,128]{1,0:T(8,128)S(1)}, f32[48,128]{1,0:T(8,128)S(1)}, u32[]{:S(2)}, u32[]{:S(2)}) collective-permute-start(f32[48,128]{1,0:T(8,128)S(1)} %hessian.3), channel_id=1, source_target_pairs={{0,1},{1,0},{2,3},{3,2},{4,5},{5,4},{6,7},{7,6},{8,9},{9,8},{10,11... | collective-permute-start | bytes 73736 | tf_op jit(solution)/shard_map/ppermute | solution.py:422
  65.9 1.2 %collective-permute-start.12 = (f32[48,128]{1,0:T(8,128)S(1)}, f32[48,128]{1,0:T(8,128)S(1)}, u32[]{:S(2)}, u32[]{:S(2)}) collective-permute-start(f32[48,128]{1,0:T(8,128)S(1)} %add.113), channel_id=1, source_target_pairs={{0,2},{2,0},{4,6},{6,4},{8,10},{10,8},{12,14},{14,12},{16,18},{18,... | collective-permute-start | bytes 73736 | tf_op jit(solution)/shard_map/ppermute | solution.py:427
  67.1 9.6 %collective-permute-start.13 = (f32[8,128]{1,0:T(8,128)S(1)}, f32[8,128]{1,0:T(8,128)S(1)}, u32[]{:S(2)}, u32[]{:S(2)}) collective-permute-start(f32[8,128]{1,0:T(8,128)S(1)} %slice_add_fusion.1), channel_id=1, source_target_pairs={{0,4},{2,6},{4,0},{6,2},{8,12},{10,14},{12,8},{14,10},{16,20},{18,... | collective-permute-start | bytes 12296 | tf_op jit(solution)/shard_map/ppermute | solution.py:427
  69.0 8.5 %collective-permute-start.14 = (f32[8,128]{1,0:T(8,128)S(1)}, f32[8,128]{1,0:T(8,128)S(1)}, u32[]{:S(2)}, u32[]{:S(2)}) collective-permute-start(f32[8,128]{1,0:T(8,128)S(1)} %slice_add_fusion.1), channel_id=1, source_target_pairs={{0,8},{2,10},{4,12},{6,14},{8,0},{10,2},{12,4},{14,6},{16,24},{18,... | collective-permute-start | bytes 12296 | tf_op jit(solution)/shard_map/ppermute | solution.py:427
  76.0 4.8 %collective-permute-start.15 = (f32[8,128]{1,0:T(8,128)S(1)}, f32[8,128]{1,0:T(8,128)S(1)}, u32[]{:S(2)}, u32[]{:S(2)}) collective-permute-start(f32[8,128]{1,0:T(8,128)S(1)} %slice_add_fusion.1), channel_id=1, source_target_pairs={{0,12},{2,14},{4,8},{6,10},{8,4},{10,6},{12,0},{14,2},{16,28},{18,... | collective-permute-start | bytes 12296 | tf_op jit(solution)/shard_map/ppermute | solution.py:427
  76.0 4.8 %collective-permute-start.16 = (f32[24,128]{1,0:T(8,128)S(1)}, f32[24,128]{1,0:T(8,128)S(1)}, u32[]{:S(2)}, u32[]{:S(2)}) collective-permute-start(f32[24,128]{1,0:T(8,128)S(1)} %fusion.21), channel_id=1, source_target_pairs={{2,4},{6,8},{10,12},{14,16},{18,20},{22,24},{26,28},{30,32},{34,36... | collective-permute-start | bytes 36872 | tf_op jit(solution)/shard_map/ppermute | solution.py:437
  80.8 7.6 %collective-permute-start.17 = (f32[8,128]{1,0:T(8,128)S(1)}, f32[8,128]{1,0:T(8,128)S(1)}, u32[]{:S(2)}, u32[]{:S(2)}) collective-permute-start(f32[8,128]{1,0:T(8,128)S(1)} %add_add_fusion.1), channel_id=1, source_target_pairs={{0,16},{2,18},{4,20},{6,22},{8,24},{10,26},{12,28},{14,30},{16,0},... | collective-permute-start | bytes 12296 | tf_op jit(solution)/shard_map/ppermute | solution.py:427
  88.4 9.8 %collective-permute-start.18 = (f32[8,128]{1,0:T(8,128)S(1)}, f32[8,128]{1,0:T(8,128)S(1)}, u32[]{:S(2)}, u32[]{:S(2)}) collective-permute-start(f32[8,128]{1,0:T(8,128)S(1)} %add.119), channel_id=1, source_target_pairs={{0,32},{2,34},{4,36},{6,38},{8,40},{10,42},{12,44},{14,46},{16,48}... | collective-permute-start | bytes 12296 | tf_op jit(solution)/shard_map/ppermute | solution.py:427
  94.4 5.5 %collective-permute-start.19 = (f32[8,128]{1,0:T(8,128)S(1)}, f32[8,128]{1,0:T(8,128)S(1)}, u32[]{:S(2)}, u32[]{:S(2)}) collective-permute-start(f32[8,128]{1,0:T(8,128)S(1)} %add.119), channel_id=1, source_target_pairs={{0,64},{2,66},{4,68},{6,70},{8,72},{10,74},{12,76},{14,78},{16,80}... | collective-permute-start | bytes 12296 | tf_op jit(solution)/shard_map/ppermute | solution.py:427
  98.2 4.8 %collective-permute-start.20 = (f32[8,128]{1,0:T(8,128)S(1)}, f32[8,128]{1,0:T(8,128)S(1)}, u32[]{:S(2)}, u32[]{:S(2)}) collective-permute-start(f32[8,128]{1,0:T(8,128)S(1)} %add.119), channel_id=1, source_target_pairs={{0,96},{2,98},{4,100},{6,102},{8,104},{10,106},{12,108},{14,110},{... | collective-permute-start | bytes 12296 | tf_op jit(solution)/shard_map/ppermute | solution.py:427
  (2 other events, 8.4 us)

commit v9 on v8

--- a/solution.py
+++ b/solution.py
@@ -165,7 +165,7 @@
 
     plane(0, (1, 2))
     plane(1, (-1, 1, 2))
-    lax.fori_loop(2, NZ - 2, body, 0, unroll=2)
+    lax.fori_loop(2, NZ - 2, body, 0, unroll=4)
     plane(NZ - 2, (-2, -1, 1))
     plane(NZ - 1, (-2, -1))
 
@@ -234,9 +234,8 @@
 def hessian_kernel(half, ctl, base, grad, front, back, xt, out, spread, field, planes):
     high, low = halves_of(ctl[...])
     first, second = xt[:128], xt[128:]
-    value = jnp.dot(high, first, preferred_element_type=F32)
-    value += jnp.dot(low, first, preferred_element_type=F32)
-    value += jnp.dot(high, second, preferred_element_type=F32)
+    value = jnp.dot(jnp.concatenate([high, low], 0), first, preferred_element_type=F32)
+    value = value[:CTL] + (value[CTL:] + jnp.dot(high, second, preferred_element_type=F32))
     value = jnp.concatenate([value, jnp.zeros((KPAD - CTL, 3 * NX), F32)], 0)
     high, low = halves_of(value)
     for j, part in enumerate((high, high, low, low)):
@@ -256,7 +255,7 @@
             return weight, carry + weight * weight
 
         strip = block_terms(block, grad, weight_at, planes)
-        square = lax.fori_loop(0, NY // 8, strip, square, unroll=2)
+        square = lax.fori_loop(0, NY // 8, strip, square, unroll=True)
 
     scale = data_weight / 144.0
     whole = ctl[...]

time: 104 us -> 104 us (level)
  no operation moved by 1% of the time
where the time goes in v9:
time: 104 us; the launch traced here: 103 us
  starting transfers between devices  46 us (44%)
  Pallas kernels  28.5 us (27%)
  waiting for transfers between devices  27.7 us (27%)
    ppermute x13, starting transfers between devices, paired(): return lax.ppermute(value, 'gz', [(i, i ^ mask) for i in range(count)])  36.2 us
    ppermute x13, waiting for transfers between devices, paired(): return lax.ppermute(value, 'gz', [(i, i ^ mask) for i in range(count)])  15.4 us
    pallas_call x2, Pallas kernels, hessian_pass(): pl.pallas_call(hessian_kernel, in_specs=[SMEM_SPEC] + [VMEM_SPEC] * 6, ou...  14.6 us
    ppermute x4, waiting for transfers between devices, swapped(): return lax.ppermute(value, 'gy', [(0, 1), (1, 0)])  12.3 us
    pallas_call x1, Pallas kernels, interior_pass(): pl.pallas_call(interior_kernel, in_specs=[SMEM_SPEC] + [VMEM_SPEC] * 2, o...  10.4 us
    ppermute x4, starting transfers between devices, swapped(): return lax.ppermute(value, 'gy', [(0, 1), (1, 0)])  7.06 us
    ppermute x4, starting transfers between devices, outer_paired(): return lax.ppermute(value, 'gz', pairs + [(j, i) for i, j in pairs])  2.79 us
  transfers between devices with their start and end apart: 21, of which 13 were waited for; matrix products, arithmetic and copies ran while one was open for 0% of the time, Pallas kernels for 10%

profile of v9, /device:TPU:0, one launch (start us, length us, event | category | flops | bytes accessed | tf_op | source)
XLA Modules:
  0.0 103.4 jit_solution(363383182974239143)
XLA Ops:
  0.7 1.3 %rims.1 = (f32[2,64,512]{2,1,0:T(8,128)S(1)}, f32[2,64,512]{2,1,0:T(8,128)S(1)}, f32[32,2,512]{2,1,0:T(2,128)S(1)}) custom-call(s32[1]{0:T(128)} %bitcast.half, s32[1]{0:T(128)} %bitcast.1.parity, f32[32,64,512]{2,1,0:T(8,128)} %moving.1), custom_call_target="tpu_custom_call" | custom-call | tf_op jit(solution)/shard_map/rims/pallas_call | solution.py:373
  3.0 3.2 %collective-permute-start.2 = (f32[32,2,512]{2,1,0:T(2,128)S(1)}, f32[32,2,512]{2,1,0:T(2,128)S(1)}, u32[]{:S(2)}, u32[]{:S(2)}) collective-permute-start(f32[32,2,512]{2,1,0:T(2,128)S(1)} %get-tuple-element.31), channel_id=1, source_target_pairs={{0,1},{1,0},{2,3},{3,2},{4,5},{5,4},{6,7},{7,6},{8,9},{9,8},{10,11... | collective-permute-start | bytes 393224 | tf_op jit(solution)/shard_map/ppermute | solution.py:421
  6.2 10.4 %interior.1 = (f32[3,32,64,512]{3,2,1,0:T(8,128)S(1)}, f32[5,64,1536]{2,1,0:T(8,128)S(1)}, f32[4,64,512]{2,1,0:T(8,128)S(1)}, f32[32,8,512]{2,1,0:T(8,128)S(1)}) custom-call(s32[1]{0:T(128)} %bitcast.half, f32[32,64,512]{2,1,0:T(8,128)S(1)} %copy-done, f32[32,64,512]{2,1,0:T(8,128)S(1)} %copy-done.3), custom_call_target="tpu_custom_call" | custom-call | flops 100000000 | bytes 40000000 | tf_op jit(solution)/shard_map/interior/pallas_call | solution.py:306
  16.8 1.3 %edge.1 = (f32[3,32,64,512]{3,2,1,0:T(8,128)S(1)}, f32[5,64,1536]{2,1,0:T(8,128)S(1)}, f32[40,128]{1,0:T(8,128)S(1)}) custom-call(s32[1]{0:T(128)} %bitcast.half, s32[1]{0:T(128)} %bitcast.1.parity, f32[2,64,512]{2,1,0:T(8,128)S(1)} %collective-permute-done.inner, ...), custom_call_target="tpu_custom_call", output_to_operand_aliasing={{0}: (9, {}), {1}: (10, {})} | custom-call | tf_op jit(solution)/shard_map/edge/pallas_call | solution.py:323
  18.1 2.5 %collective-permute-start.3 = (f32[40,128]{1,0:T(8,128)S(1)}, f32[40,128]{1,0:T(8,128)S(1)}, u32[]{:S(2)}, u32[]{:S(2)}) collective-permute-start(f32[40,128]{1,0:T(8,128)S(1)} %get-tuple-element.36), channel_id=1, source_target_pairs={{0,1},{1,0},{2,3},{3,2},{4,5},{5,4},{6,7},{7,6},{8,9},{9,8},{10,11... | collective-permute-start | bytes 61448 | tf_op jit(solution)/shard_map/ppermute | solution.py:421
  20.6 2.9 %collective-permute-done.3 = f32[40,128]{1,0:T(8,128)S(1)} collective-permute-done((f32[40,128]{1,0:T(8,128)S(1)}, f32[40,128]{1,0:T(8,128)S(1)}, u32[]{:S(2)}, u32[]{:S(2)}) %collective-permute-start.3) | collective-permute-done | bytes 20512 | tf_op jit(solution)/shard_map/ppermute | solution.py:421
  23.5 1.6 %collective-permute-start.4 = (f32[40,128]{1,0:T(8,128)S(1)}, f32[40,128]{1,0:T(8,128)S(1)}, u32[]{:S(2)}, u32[]{:S(2)}) collective-permute-start(f32[40,128]{1,0:T(8,128)S(1)} %add.105), channel_id=1, source_target_pairs={{0,2},{2,0},{4,6},{6,4},{8,10},{10,8},{12,14},{14,12},{16,18},{18,... | collective-permute-start | bytes 61448 | tf_op jit(solution)/shard_map/ppermute | solution.py:426
  26.6 5.0 %collective-permute-start.6 = (f32[8,128]{1,0:T(8,128)S(1)}, f32[8,128]{1,0:T(8,128)S(1)}, u32[]{:S(2)}, u32[]{:S(2)}) collective-permute-start(f32[8,128]{1,0:T(8,128)S(1)} %slice_select_fusion.3), channel_id=1, source_target_pairs={{0,2},{2,0},{4,6},{6,4},{8,10},{10,8},{12,14},{14,12},{16,18},{18,... | collective-permute-start | bytes 12296 | tf_op jit(solution)/shard_map/ppermute | solution.py:426
  32.5 7.3 %hessian.2 = f32[48,128]{1,0:T(8,128)S(1)} custom-call(s32[1]{0:T(128)} %bitcast.half, f32[40,128]{1,0:T(8,128)S(1)} %fusion.3.ctl, f32[16,128]{1,0:T(8,128)S(1)} %slice.124.base, f32[3,32,64,512]{3,2,1,0:T(8,128)S(1)} %get-tuple-element.37.grad, bf16[2,2048,192]{2,1,0:T(8,128)(2,1)S(1)} %copy-done.1, bf16[2,80,320]{2,1,0:T(8,128)(2,1)S(1)} %copy-done.4, ...), custom_call_target="tpu_custom_call" | custom-call | tf_op jit(solution)/shard_map/hessian/pallas_call | solution.py:336
  40.7 4.6 %collective-permute-done.7 = f32[48,128]{1,0:T(8,128)S(1)} collective-permute-done((f32[48,128]{1,0:T(8,128)S(1)}, f32[48,128]{1,0:T(8,128)S(1)}, u32[]{:S(2)}, u32[]{:S(2)}) %collective-permute-start.7) | collective-permute-done | bytes 24608 | tf_op jit(solution)/shard_map/ppermute | solution.py:421
  45.3 1.2 %collective-permute-done.8 = f32[40,128]{1,0:T(8,128)S(1)} collective-permute-done((f32[40,128]{1,0:T(8,128)S(1)}, f32[40,128]{1,0:T(8,128)S(1)}, u32[]{:S(2)}, u32[]{:S(2)}) %collective-permute-start.8) | collective-permute-done | bytes 20512 | tf_op jit(solution)/shard_map/ppermute | solution.py:426
  47.2 4.7 %collective-permute-start.10 = (f32[8,128]{1,0:T(8,128)S(1)}, f32[8,128]{1,0:T(8,128)S(1)}, u32[]{:S(2)}, u32[]{:S(2)}) collective-permute-start(f32[8,128]{1,0:T(8,128)S(1)} %slice_select_fusion.2), channel_id=1, source_target_pairs={{0,2},{2,0},{4,6},{6,4},{8,10},{10,8},{12,14},{14,12},{16,18},{18,... | collective-permute-start | bytes 12296 | tf_op jit(solution)/shard_map/ppermute | solution.py:426
  52.7 7.3 %hessian.3 = f32[48,128]{1,0:T(8,128)S(1)} custom-call(s32[1]{0:T(128)} %bitcast.half, f32[40,128]{1,0:T(8,128)S(1)} %fusion.7.ctl, f32[16,128]{1,0:T(8,128)S(1)} %slice.124.base, f32[3,32,64,512]{3,2,1,0:T(8,128)S(1)} %get-tuple-element.37.grad, bf16[2,2048,192]{2,1,0:T(8,128)(2,1)S(1)} %copy-done.1, bf16[2,80,320]{2,1,0:T(8,128)(2,1)S(1)} %copy-done.4, ...), custom_call_target="tpu_custom_call" | custom-call | tf_op jit(solution)/shard_map/hessian/pallas_call | solution.py:336
  60.6 4.8 %collective-permute-done.11 = f32[48,128]{1,0:T(8,128)S(1)} collective-permute-done((f32[48,128]{1,0:T(8,128)S(1)}, f32[48,128]{1,0:T(8,128)S(1)}, u32[]{:S(2)}, u32[]{:S(2)}) %collective-permute-start.11) | collective-permute-done | bytes 24608 | tf_op jit(solution)/shard_map/ppermute | solution.py:421
  65.4 1.2 %collective-permute-done.12 = f32[48,128]{1,0:T(8,128)S(1)} collective-permute-done((f32[48,128]{1,0:T(8,128)S(1)}, f32[48,128]{1,0:T(8,128)S(1)}, u32[]{:S(2)}, u32[]{:S(2)}) %collective-permute-start.12) | collective-permute-done | bytes 24608 | tf_op jit(solution)/shard_map/ppermute | solution.py:426
  66.6 2.0 %collective-permute-start.13 = (f32[8,128]{1,0:T(8,128)S(1)}, f32[8,128]{1,0:T(8,128)S(1)}, u32[]{:S(2)}, u32[]{:S(2)}) collective-permute-start(f32[8,128]{1,0:T(8,128)S(1)} %slice_add_fusion.1), channel_id=1, source_target_pairs={{0,4},{2,6},{4,0},{6,2},{8,12},{10,14},{12,8},{14,10},{16,20},{18,... | collective-permute-start | bytes 12296 | tf_op jit(solution)/shard_map/ppermute | solution.py:426
  68.6 6.9 %collective-permute-start.14 = (f32[8,128]{1,0:T(8,128)S(1)}, f32[8,128]{1,0:T(8,128)S(1)}, u32[]{:S(2)}, u32[]{:S(2)}) collective-permute-start(f32[8,128]{1,0:T(8,128)S(1)} %slice_add_fusion.1), channel_id=1, source_target_pairs={{0,8},{2,10},{4,12},{6,14},{8,0},{10,2},{12,4},{14,6},{16,24},{18,... | collective-permute-start | bytes 12296 | tf_op jit(solution)/shard_map/ppermute | solution.py:426
  77.1 3.2 %collective-permute-done.15 = f32[8,128]{1,0:T(8,128)S(1)} collective-permute-done((f32[8,128]{1,0:T(8,128)S(1)}, f32[8,128]{1,0:T(8,128)S(1)}, u32[]{:S(2)}, u32[]{:S(2)}) %collective-permute-start.15) | collective-permute-done | bytes 4128 | tf_op jit(solution)/shard_map/ppermute | solution.py:426
  80.3 6.0 %collective-permute-start.17 = (f32[8,128]{1,0:T(8,128)S(1)}, f32[8,128]{1,0:T(8,128)S(1)}, u32[]{:S(2)}, u32[]{:S(2)}) collective-permute-start(f32[8,128]{1,0:T(8,128)S(1)} %add_add_fusion.1), channel_id=1, source_target_pairs={{0,16},{2,18},{4,20},{6,22},{8,24},{10,26},{12,28},{14,30},{16,0},... | collective-permute-start | bytes 12296 | tf_op jit(solution)/shard_map/ppermute | solution.py:426
  86.4 1.6 %collective-permute-done.17 = f32[8,128]{1,0:T(8,128)S(1)} collective-permute-done((f32[8,128]{1,0:T(8,128)S(1)}, f32[8,128]{1,0:T(8,128)S(1)}, u32[]{:S(2)}, u32[]{:S(2)}) %collective-permute-start.17) | collective-permute-done | bytes 4128 | tf_op jit(solution)/shard_map/ppermute | solution.py:426
  87.9 6.0 %collective-permute-start.18 = (f32[8,128]{1,0:T(8,128)S(1)}, f32[8,128]{1,0:T(8,128)S(1)}, u32[]{:S(2)}, u32[]{:S(2)}) collective-permute-start(f32[8,128]{1,0:T(8,128)S(1)} %add.119), channel_id=1, source_target_pairs={{0,32},{2,34},{4,36},{6,38},{8,40},{10,42},{12,44},{14,46},{16,48}... | collective-permute-start | bytes 12296 | tf_op jit(solution)/shard_map/ppermute | solution.py:426
  93.9 3.9 %collective-permute-start.19 = (f32[8,128]{1,0:T(8,128)S(1)}, f32[8,128]{1,0:T(8,128)S(1)}, u32[]{:S(2)}, u32[]{:S(2)}) collective-permute-start(f32[8,128]{1,0:T(8,128)S(1)} %add.119), channel_id=1, source_target_pairs={{0,64},{2,66},{4,68},{6,70},{8,72},{10,74},{12,76},{14,78},{16,80}... | collective-permute-start | bytes 12296 | tf_op jit(solution)/shard_map/ppermute | solution.py:426
  97.8 1.6 %collective-permute-done.19 = f32[8,128]{1,0:T(8,128)S(1)} collective-permute-done((f32[8,128]{1,0:T(8,128)S(1)}, f32[8,128]{1,0:T(8,128)S(1)}, u32[]{:S(2)}, u32[]{:S(2)}) %collective-permute-start.19) | collective-permute-done | bytes 4128 | tf_op jit(solution)/shard_map/ppermute | solution.py:426
  99.4 3.2 %collective-permute-done.20 = f32[8,128]{1,0:T(8,128)S(1)} collective-permute-done((f32[8,128]{1,0:T(8,128)S(1)}, f32[8,128]{1,0:T(8,128)S(1)}, u32[]{:S(2)}, u32[]{:S(2)}) %collective-permute-start.20) | collective-permute-done | bytes 4128 | tf_op jit(solution)/shard_map/ppermute | solution.py:426
  (60 shorter events, 8.7 us)
Async XLA Ops:
  2.1 14.6 %collective-permute-start = (f32[2,64,512]{2,1,0:T(8,128)S(1)}, f32[2,64,512]{2,1,0:T(8,128)S(1)}, u32[]{:S(2)}, u32[]{:S(2)}) collective-permute-start(f32[2,64,512]{2,1,0:T(8,128)S(1)} %get-tuple-element.29), channel_id=1, source_target_pairs={{0,2},{2,0},{4,6},{6,4},{8,10},{10,8},{12,14},{14,12},{16,18},{18,... | collective-permute-start | bytes 786440 | tf_op jit(solution)/shard_map/ppermute | solution.py:426
  2.2 14.5 %collective-permute-start.1 = (f32[2,64,512]{2,1,0:T(8,128)S(1)}, f32[2,64,512]{2,1,0:T(8,128)S(1)}, u32[]{:S(2)}, u32[]{:S(2)}) collective-permute-start(f32[2,64,512]{2,1,0:T(8,128)S(1)} %get-tuple-element.30), channel_id=1, source_target_pairs={{2,4},{6,8},{10,12},{14,16},{18,20},{22,24},{26,28},{30,32},{34,36... | collective-permute-start | bytes 786440 | tf_op jit(solution)/shard_map/ppermute | solution.py:436
  3.0 13.7 %copy-start.2 = (bf16[256,1536]{1,0:T(8,128)(2,1)S(1)}, bf16[256,1536]{1,0:T(8,128)(2,1)}, u32[]{:S(2)}) copy-start(bf16[256,1536]{1,0:T(8,128)(2,1)} %constant.47.clone.xt) | copy-start | bytes 2359300
  3.0 13.7 %copy-start.4 = (bf16[2,80,320]{2,1,0:T(8,128)(2,1)S(1)}, bf16[2,80,320]{2,1,0:T(8,128)(2,1)}, u32[]{:S(2)}) copy-start(bf16[2,80,320]{2,1,0:T(8,128)(2,1)} %constant.46.clone.back) | copy-start | bytes 307204
  3.0 13.6 %collective-permute-start.2 = (f32[32,2,512]{2,1,0:T(2,128)S(1)}, f32[32,2,512]{2,1,0:T(2,128)S(1)}, u32[]{:S(2)}, u32[]{:S(2)}) collective-permute-start(f32[32,2,512]{2,1,0:T(2,128)S(1)} %get-tuple-element.31), channel_id=1, source_target_pairs={{0,1},{1,0},{2,3},{3,2},{4,5},{5,4},{6,7},{7,6},{8,9},{9,8},{10,11... | collective-permute-start | bytes 393224 | tf_op jit(solution)/shard_map/ppermute | solution.py:421
  16.7 15.8 %copy-start.1 = (bf16[2,2048,192]{2,1,0:T(8,128)(2,1)S(1)}, bf16[2,2048,192]{2,1,0:T(8,128)(2,1)}, u32[]{:S(2)}) copy-start(bf16[2,2048,192]{2,1,0:T(8,128)(2,1)} %constant.45.clone.front) | copy-start | bytes 4718596
  18.1 5.4 %collective-permute-start.3 = (f32[40,128]{1,0:T(8,128)S(1)}, f32[40,128]{1,0:T(8,128)S(1)}, u32[]{:S(2)}, u32[]{:S(2)}) collective-permute-start(f32[40,128]{1,0:T(8,128)S(1)} %get-tuple-element.36), channel_id=1, source_target_pairs={{0,1},{1,0},{2,3},{3,2},{4,5},{5,4},{6,7},{7,6},{8,9},{9,8},{10,11... | collective-permute-start | bytes 61448 | tf_op jit(solution)/shard_map/ppermute | solution.py:421
  23.5 2.5 %collective-permute-start.4 = (f32[40,128]{1,0:T(8,128)S(1)}, f32[40,128]{1,0:T(8,128)S(1)}, u32[]{:S(2)}, u32[]{:S(2)}) collective-permute-start(f32[40,128]{1,0:T(8,128)S(1)} %add.105), channel_id=1, source_target_pairs={{0,2},{2,0},{4,6},{6,4},{8,10},{10,8},{12,14},{14,12},{16,18},{18,... | collective-permute-start | bytes 61448 | tf_op jit(solution)/shard_map/ppermute | solution.py:426
  26.0 0.7 collective-permute-start.5
  26.6 5.9 %collective-permute-start.6 = (f32[8,128]{1,0:T(8,128)S(1)}, f32[8,128]{1,0:T(8,128)S(1)}, u32[]{:S(2)}, u32[]{:S(2)}) collective-permute-start(f32[8,128]{1,0:T(8,128)S(1)} %slice_select_fusion.3), channel_id=1, source_target_pairs={{0,2},{2,0},{4,6},{6,4},{8,10},{10,8},{12,14},{14,12},{16,18},{18,... | collective-permute-start | bytes 12296 | tf_op jit(solution)/shard_map/ppermute | solution.py:426
  39.9 5.4 %collective-permute-start.7 = (f32[48,128]{1,0:T(8,128)S(1)}, f32[48,128]{1,0:T(8,128)S(1)}, u32[]{:S(2)}, u32[]{:S(2)}) collective-permute-start(f32[48,128]{1,0:T(8,128)S(1)} %hessian.2), channel_id=1, source_target_pairs={{0,1},{1,0},{2,3},{3,2},{4,5},{5,4},{6,7},{7,6},{8,9},{9,8},{10,11... | collective-permute-start | bytes 73736 | tf_op jit(solution)/shard_map/ppermute | solution.py:421
  45.3 1.2 %collective-permute-start.8 = (f32[40,128]{1,0:T(8,128)S(1)}, f32[40,128]{1,0:T(8,128)S(1)}, u32[]{:S(2)}, u32[]{:S(2)}) collective-permute-start(f32[40,128]{1,0:T(8,128)S(1)} %slice_add_fusion), channel_id=1, source_target_pairs={{0,2},{2,0},{4,6},{6,4},{8,10},{10,8},{12,14},{14,12},{16,18},{18,... | collective-permute-start | bytes 61448 | tf_op jit(solution)/shard_map/ppermute | solution.py:426
  46.5 0.7 collective-permute-start.9
  47.2 5.5 %collective-permute-start.10 = (f32[8,128]{1,0:T(8,128)S(1)}, f32[8,128]{1,0:T(8,128)S(1)}, u32[]{:S(2)}, u32[]{:S(2)}) collective-permute-start(f32[8,128]{1,0:T(8,128)S(1)} %slice_select_fusion.2), channel_id=1, source_target_pairs={{0,2},{2,0},{4,6},{6,4},{8,10},{10,8},{12,14},{14,12},{16,18},{18,... | collective-permute-start | bytes 12296 | tf_op jit(solution)/shard_map/ppermute | solution.py:426
  60.0 5.4 %collective-permute-start.11 = (f32[48,128]{1,0:T(8,128)S(1)}, f32[48,128]{1,0:T(8,128)S(1)}, u32[]{:S(2)}, u32[]{:S(2)}) collective-permute-start(f32[48,128]{1,0:T(8,128)S(1)} %hessian.3), channel_id=1, source_target_pairs={{0,1},{1,0},{2,3},{3,2},{4,5},{5,4},{6,7},{7,6},{8,9},{9,8},{10,11... | collective-permute-start | bytes 73736 | tf_op jit(solution)/shard_map/ppermute | solution.py:421
  65.4 1.2 %collective-permute-start.12 = (f32[48,128]{1,0:T(8,128)S(1)}, f32[48,128]{1,0:T(8,128)S(1)}, u32[]{:S(2)}, u32[]{:S(2)}) collective-permute-start(f32[48,128]{1,0:T(8,128)S(1)} %add.113), channel_id=1, source_target_pairs={{0,2},{2,0},{4,6},{6,4},{8,10},{10,8},{12,14},{14,12},{16,18},{18,... | collective-permute-start | bytes 73736 | tf_op jit(solution)/shard_map/ppermute | solution.py:426
  66.6 9.6 %collective-permute-start.13 = (f32[8,128]{1,0:T(8,128)S(1)}, f32[8,128]{1,0:T(8,128)S(1)}, u32[]{:S(2)}, u32[]{:S(2)}) collective-permute-start(f32[8,128]{1,0:T(8,128)S(1)} %slice_add_fusion.1), channel_id=1, source_target_pairs={{0,4},{2,6},{4,0},{6,2},{8,12},{10,14},{12,8},{14,10},{16,20},{18,... | collective-permute-start | bytes 12296 | tf_op jit(solution)/shard_map/ppermute | solution.py:426
  68.6 8.5 %collective-permute-start.14 = (f32[8,128]{1,0:T(8,128)S(1)}, f32[8,128]{1,0:T(8,128)S(1)}, u32[]{:S(2)}, u32[]{:S(2)}) collective-permute-start(f32[8,128]{1,0:T(8,128)S(1)} %slice_add_fusion.1), channel_id=1, source_target_pairs={{0,8},{2,10},{4,12},{6,14},{8,0},{10,2},{12,4},{14,6},{16,24},{18,... | collective-permute-start | bytes 12296 | tf_op jit(solution)/shard_map/ppermute | solution.py:426
  75.5 4.8 %collective-permute-start.15 = (f32[8,128]{1,0:T(8,128)S(1)}, f32[8,128]{1,0:T(8,128)S(1)}, u32[]{:S(2)}, u32[]{:S(2)}) collective-permute-start(f32[8,128]{1,0:T(8,128)S(1)} %slice_add_fusion.1), channel_id=1, source_target_pairs={{0,12},{2,14},{4,8},{6,10},{8,4},{10,6},{12,0},{14,2},{16,28},{18,... | collective-permute-start | bytes 12296 | tf_op jit(solution)/shard_map/ppermute | solution.py:426
  75.5 4.8 %collective-permute-start.16 = (f32[24,128]{1,0:T(8,128)S(1)}, f32[24,128]{1,0:T(8,128)S(1)}, u32[]{:S(2)}, u32[]{:S(2)}) collective-permute-start(f32[24,128]{1,0:T(8,128)S(1)} %fusion.21), channel_id=1, source_target_pairs={{2,4},{6,8},{10,12},{14,16},{18,20},{22,24},{26,28},{30,32},{34,36... | collective-permute-start | bytes 36872 | tf_op jit(solution)/shard_map/ppermute | solution.py:436
  80.3 7.6 %collective-permute-start.17 = (f32[8,128]{1,0:T(8,128)S(1)}, f32[8,128]{1,0:T(8,128)S(1)}, u32[]{:S(2)}, u32[]{:S(2)}) collective-permute-start(f32[8,128]{1,0:T(8,128)S(1)} %add_add_fusion.1), channel_id=1, source_target_pairs={{0,16},{2,18},{4,20},{6,22},{8,24},{10,26},{12,28},{14,30},{16,0},... | collective-permute-start | bytes 12296 | tf_op jit(solution)/shard_map/ppermute | solution.py:426
  87.9 9.8 %collective-permute-start.18 = (f32[8,128]{1,0:T(8,128)S(1)}, f32[8,128]{1,0:T(8,128)S(1)}, u32[]{:S(2)}, u32[]{:S(2)}) collective-permute-start(f32[8,128]{1,0:T(8,128)S(1)} %add.119), channel_id=1, source_target_pairs={{0,32},{2,34},{4,36},{6,38},{8,40},{10,42},{12,44},{14,46},{16,48}... | collective-permute-start | bytes 12296 | tf_op jit(solution)/shard_map/ppermute | solution.py:426
  93.9 5.5 %collective-permute-start.19 = (f32[8,128]{1,0:T(8,128)S(1)}, f32[8,128]{1,0:T(8,128)S(1)}, u32[]{:S(2)}, u32[]{:S(2)}) collective-permute-start(f32[8,128]{1,0:T(8,128)S(1)} %add.119), channel_id=1, source_target_pairs={{0,64},{2,66},{4,68},{6,70},{8,72},{10,74},{12,76},{14,78},{16,80}... | collective-permute-start | bytes 12296 | tf_op jit(solution)/shard_map/ppermute | solution.py:426
  97.8 4.8 %collective-permute-start.20 = (f32[8,128]{1,0:T(8,128)S(1)}, f32[8,128]{1,0:T(8,128)S(1)}, u32[]{:S(2)}, u32[]{:S(2)}) collective-permute-start(f32[8,128]{1,0:T(8,128)S(1)} %add.119), channel_id=1, source_target_pairs={{0,96},{2,98},{4,100},{6,102},{8,104},{10,106},{12,108},{14,110},{... | collective-permute-start | bytes 12296 | tf_op jit(solution)/shard_map/ppermute | solution.py:426
  (2 other events, 8.4 us)

commit v10 on v8

--- a/solution.py
+++ b/solution.py
@@ -437,6 +437,12 @@
     return lax.ppermute(value, "gz", pairs + [(j, i) for i, j in pairs])
 
 
+def far_paired(value):
+    count = lax.axis_size("gz")
+    pairs = [(i, i + 3) for i in range(0, count - 3, 2)]
+    return lax.ppermute(value, "gz", pairs + [(j, i) for i, j in pairs])
+
+
 def pair_sum(lower, own, other):
     first, second = jnp.where(lower, own, other), jnp.where(lower, other, own)
     widths = ((0, 2 * CY), (0, 0)), ((2 * CY, 0), (0, 0))
@@ -451,7 +457,7 @@
     part = (part + swapped(part))[:CTL]
     seven = pair_sum(lower, part, paired(part, 1))
     three = outer_terms(lower, seven)
-    one = paired(jnp.where(lower, three[2 * CY :], three[:CY]), 1)
+    one = far_paired(jnp.where(lower, seven[6 * CY :], seven[:CY]))
     low = jnp.concatenate([three, jnp.zeros((CY, 128), F32), one], 0) + seven[: 5 * CY]
     high = jnp.concatenate([one, jnp.zeros((CY, 128), F32), three], 0) + seven[2 * CY :]
     return inside * jnp.where(lower, low, high)

time: 104 us -> 103 us (level)
    ppermute x13 -> x11, starting transfers between devices: 36.2 us -> 20.2 us  [paired(): return lax.ppermute(value, 'gz', [(i, i ^ mask) for i in range(count)])]
    ppermute x0 -> x2, starting transfers between devices: none -> 14.1 us  [far_paired(): return lax.ppermute(value, 'gz', pairs + [(j, i) for i, j in pairs])]
    ppermute x0 -> x2, waiting for transfers between devices: none -> 2.43 us  [far_paired(): return lax.ppermute(value, 'gz', pairs + [(j, i) for i, j in pairs])]
    ppermute x13 -> x11, waiting for transfers between devices: 15.4 us -> 13.7 us  [paired(): return lax.ppermute(value, 'gz', [(i, i ^ mask) for i in range(count)])]
where the time goes in v10:
time: 103 us
  starting transfers between devices  45.1 us (44%)
  Pallas kernels  28.9 us (28%)
  waiting for transfers between devices  27.5 us (27%)
    ppermute x11, starting transfers between devices, paired(): return lax.ppermute(value, 'gz', [(i, i ^ mask) for i in range(count)])  20.2 us
    pallas_call x2, Pallas kernels, hessian_pass(): pl.pallas_call(hessian_kernel, in_specs=[SMEM_SPEC] + [VMEM_SPEC] * 6, ou...  14.9 us
    ppermute x2, starting transfers between devices, far_paired(): return lax.ppermute(value, 'gz', pairs + [(j, i) for i, j in pairs])  14.1 us
    ppermute x11, waiting for transfers between devices, paired(): return lax.ppermute(value, 'gz', [(i, i ^ mask) for i in range(count)])  13.7 us
    ppermute x4, waiting for transfers between devices, swapped(): return lax.ppermute(value, 'gy', [(0, 1), (1, 0)])  11.3 us
    pallas_call x1, Pallas kernels, interior_pass(): pl.pallas_call(interior_kernel, in_specs=[SMEM_SPEC] + [VMEM_SPEC] * 2, o...  10.6 us
    ppermute x4, starting transfers between devices, swapped(): return lax.ppermute(value, 'gy', [(0, 1), (1, 0)])  8.04 us
    ppermute x4, starting transfers between devices, outer_paired(): return lax.ppermute(value, 'gz', pairs + [(j, i) for i, j in pairs])  2.79 us
  transfers between devices with their start and end apart: 21, of which 13 were waited for; matrix products, arithmetic and copies ran while one was open for 0% of the time, Pallas kernels for 10%

profile of v10, /device:TPU:0, one launch (start us, length us, event | category | flops | bytes accessed | tf_op | source)
XLA Modules:
  0.0 102.7 jit_solution(6872624966877866594)
XLA Ops:
  0.7 1.3 %rims.1 = (f32[2,64,512]{2,1,0:T(8,128)S(1)}, f32[2,64,512]{2,1,0:T(8,128)S(1)}, f32[32,2,512]{2,1,0:T(2,128)S(1)}) custom-call(s32[1]{0:T(128)} %bitcast.half, s32[1]{0:T(128)} %bitcast.1.parity, f32[32,64,512]{2,1,0:T(8,128)} %moving.1), custom_call_target="tpu_custom_call" | custom-call | tf_op jit(solution)/shard_map/rims/pallas_call | solution.py:374
  3.0 3.2 %collective-permute-start.2 = (f32[32,2,512]{2,1,0:T(2,128)S(1)}, f32[32,2,512]{2,1,0:T(2,128)S(1)}, u32[]{:S(2)}, u32[]{:S(2)}) collective-permute-start(f32[32,2,512]{2,1,0:T(2,128)S(1)} %get-tuple-element.31), channel_id=1, source_target_pairs={{0,1},{1,0},{2,3},{3,2},{4,5},{5,4},{6,7},{7,6},{8,9},{9,8},{10,11... | collective-permute-start | bytes 393224 | tf_op jit(solution)/shard_map/ppermute | solution.py:422
  6.2 10.6 %interior.1 = (f32[3,32,64,512]{3,2,1,0:T(8,128)S(1)}, f32[5,64,1536]{2,1,0:T(8,128)S(1)}, f32[4,64,512]{2,1,0:T(8,128)S(1)}, f32[32,8,512]{2,1,0:T(8,128)S(1)}) custom-call(s32[1]{0:T(128)} %bitcast.half, f32[32,64,512]{2,1,0:T(8,128)S(1)} %copy-done, f32[32,64,512]{2,1,0:T(8,128)S(1)} %copy-done.3), custom_call_target="tpu_custom_call" | custom-call | flops 100000000 | bytes 40000000 | tf_op jit(solution)/shard_map/interior/pallas_call | solution.py:307
  16.9 1.3 %edge.1 = (f32[3,32,64,512]{3,2,1,0:T(8,128)S(1)}, f32[5,64,1536]{2,1,0:T(8,128)S(1)}, f32[40,128]{1,0:T(8,128)S(1)}) custom-call(s32[1]{0:T(128)} %bitcast.half, s32[1]{0:T(128)} %bitcast.1.parity, f32[2,64,512]{2,1,0:T(8,128)S(1)} %collective-permute-done.inner, ...), custom_call_target="tpu_custom_call", output_to_operand_aliasing={{0}: (9, {}), {1}: (10, {})} | custom-call | tf_op jit(solution)/shard_map/edge/pallas_call | solution.py:324
  18.3 2.5 %collective-permute-start.3 = (f32[40,128]{1,0:T(8,128)S(1)}, f32[40,128]{1,0:T(8,128)S(1)}, u32[]{:S(2)}, u32[]{:S(2)}) collective-permute-start(f32[40,128]{1,0:T(8,128)S(1)} %get-tuple-element.36), channel_id=1, source_target_pairs={{0,1},{1,0},{2,3},{3,2},{4,5},{5,4},{6,7},{7,6},{8,9},{9,8},{10,11... | collective-permute-start | bytes 61448 | tf_op jit(solution)/shard_map/ppermute | solution.py:422
  20.7 2.9 %collective-permute-done.3 = f32[40,128]{1,0:T(8,128)S(1)} collective-permute-done((f32[40,128]{1,0:T(8,128)S(1)}, f32[40,128]{1,0:T(8,128)S(1)}, u32[]{:S(2)}, u32[]{:S(2)}) %collective-permute-start.3) | collective-permute-done | bytes 20512 | tf_op jit(solution)/shard_map/ppermute | solution.py:422
  23.7 1.6 %collective-permute-start.4 = (f32[40,128]{1,0:T(8,128)S(1)}, f32[40,128]{1,0:T(8,128)S(1)}, u32[]{:S(2)}, u32[]{:S(2)}) collective-permute-start(f32[40,128]{1,0:T(8,128)S(1)} %add.105), channel_id=1, source_target_pairs={{0,2},{2,0},{4,6},{6,4},{8,10},{10,8},{12,14},{14,12},{16,18},{18,... | collective-permute-start | bytes 61448 | tf_op jit(solution)/shard_map/ppermute | solution.py:427
  26.8 6.8 %collective-permute-start.6 = (f32[8,128]{1,0:T(8,128)S(1)}, f32[8,128]{1,0:T(8,128)S(1)}, u32[]{:S(2)}, u32[]{:S(2)}) collective-permute-start(f32[8,128]{1,0:T(8,128)S(1)} %fusion.32), channel_id=1, source_target_pairs={{0,6},{4,10},{8,14},{12,18},{16,22},{20,26},{24,30},{28,34},{32,38... | collective-permute-start | bytes 12296 | tf_op jit(solution)/shard_map/ppermute | solution.py:443
  33.6 1.3 %collective-permute-done.6 = f32[8,128]{1,0:T(8,128)S(1)} collective-permute-done((f32[8,128]{1,0:T(8,128)S(1)}, f32[8,128]{1,0:T(8,128)S(1)}, u32[]{:S(2)}, u32[]{:S(2)}) %collective-permute-start.6) | collective-permute-done | bytes 4128 | tf_op jit(solution)/shard_map/ppermute | solution.py:443
  35.0 7.5 %hessian.2 = f32[48,128]{1,0:T(8,128)S(1)} custom-call(s32[1]{0:T(128)} %bitcast.half, f32[40,128]{1,0:T(8,128)S(1)} %fusion.3.ctl, f32[16,128]{1,0:T(8,128)S(1)} %slice.126.base, f32[3,32,64,512]{3,2,1,0:T(8,128)S(1)} %get-tuple-element.37.grad, bf16[2,2048,192]{2,1,0:T(8,128)(2,1)S(1)} %copy-done.1, bf16[2,80,320]{2,1,0:T(8,128)(2,1)S(1)} %copy-done.4, ...), custom_call_target="tpu_custom_call" | custom-call | tf_op jit(solution)/shard_map/hessian/pallas_call | solution.py:337
  43.0 4.8 %collective-permute-done.7 = f32[48,128]{1,0:T(8,128)S(1)} collective-permute-done((f32[48,128]{1,0:T(8,128)S(1)}, f32[48,128]{1,0:T(8,128)S(1)}, u32[]{:S(2)}, u32[]{:S(2)}) %collective-permute-start.7) | collective-permute-done | bytes 24608 | tf_op jit(solution)/shard_map/ppermute | solution.py:422
  49.7 7.3 %collective-permute-start.10 = (f32[8,128]{1,0:T(8,128)S(1)}, f32[8,128]{1,0:T(8,128)S(1)}, u32[]{:S(2)}, u32[]{:S(2)}) collective-permute-start(f32[8,128]{1,0:T(8,128)S(1)} %fusion.35), channel_id=1, source_target_pairs={{0,6},{4,10},{8,14},{12,18},{16,22},{20,26},{24,30},{28,34},{32,38... | collective-permute-start | bytes 12296 | tf_op jit(solution)/shard_map/ppermute | solution.py:443
  58.2 7.5 %hessian.3 = f32[48,128]{1,0:T(8,128)S(1)} custom-call(s32[1]{0:T(128)} %bitcast.half, f32[40,128]{1,0:T(8,128)S(1)} %fusion.7.ctl, f32[16,128]{1,0:T(8,128)S(1)} %slice.126.base, f32[3,32,64,512]{3,2,1,0:T(8,128)S(1)} %get-tuple-element.37.grad, bf16[2,2048,192]{2,1,0:T(8,128)(2,1)S(1)} %copy-done.1, bf16[2,80,320]{2,1,0:T(8,128)(2,1)S(1)} %copy-done.4, ...), custom_call_target="tpu_custom_call" | custom-call | tf_op jit(solution)/shard_map/hessian/pallas_call | solution.py:337
  65.6 1.8 %collective-permute-start.11 = (f32[48,128]{1,0:T(8,128)S(1)}, f32[48,128]{1,0:T(8,128)S(1)}, u32[]{:S(2)}, u32[]{:S(2)}) collective-permute-start(f32[48,128]{1,0:T(8,128)S(1)} %hessian.3), channel_id=1, source_target_pairs={{0,1},{1,0},{2,3},{3,2},{4,5},{5,4},{6,7},{7,6},{8,9},{9,8},{10,11... | collective-permute-start | bytes 73736 | tf_op jit(solution)/shard_map/ppermute | solution.py:422
  67.4 3.6 %collective-permute-done.11 = f32[48,128]{1,0:T(8,128)S(1)} collective-permute-done((f32[48,128]{1,0:T(8,128)S(1)}, f32[48,128]{1,0:T(8,128)S(1)}, u32[]{:S(2)}, u32[]{:S(2)}) %collective-permute-start.11) | collective-permute-done | bytes 24608 | tf_op jit(solution)/shard_map/ppermute | solution.py:422
  72.2 1.7 %collective-permute-start.13 = (f32[8,128]{1,0:T(8,128)S(1)}, f32[8,128]{1,0:T(8,128)S(1)}, u32[]{:S(2)}, u32[]{:S(2)}) collective-permute-start(f32[8,128]{1,0:T(8,128)S(1)} %slice_add_fusion.1), channel_id=1, source_target_pairs={{0,4},{2,6},{4,0},{6,2},{8,12},{10,14},{12,8},{14,10},{16,20},{18,... | collective-permute-start | bytes 12296 | tf_op jit(solution)/shard_map/ppermute | solution.py:427
  73.9 4.3 %collective-permute-start.14 = (f32[8,128]{1,0:T(8,128)S(1)}, f32[8,128]{1,0:T(8,128)S(1)}, u32[]{:S(2)}, u32[]{:S(2)}) collective-permute-start(f32[8,128]{1,0:T(8,128)S(1)} %slice_add_fusion.1), channel_id=1, source_target_pairs={{0,8},{2,10},{4,12},{6,14},{8,0},{10,2},{12,4},{14,6},{16,24},{18,... | collective-permute-start | bytes 12296 | tf_op jit(solution)/shard_map/ppermute | solution.py:427
  79.8 3.2 %collective-permute-done.15 = f32[8,128]{1,0:T(8,128)S(1)} collective-permute-done((f32[8,128]{1,0:T(8,128)S(1)}, f32[8,128]{1,0:T(8,128)S(1)}, u32[]{:S(2)}, u32[]{:S(2)}) %collective-permute-start.15) | collective-permute-done | bytes 4128 | tf_op jit(solution)/shard_map/ppermute | solution.py:427
  83.0 5.9 %collective-permute-start.17 = (f32[8,128]{1,0:T(8,128)S(1)}, f32[8,128]{1,0:T(8,128)S(1)}, u32[]{:S(2)}, u32[]{:S(2)}) collective-permute-start(f32[8,128]{1,0:T(8,128)S(1)} %add_add_fusion.1), channel_id=1, source_target_pairs={{0,16},{2,18},{4,20},{6,22},{8,24},{10,26},{12,28},{14,30},{16,0},... | collective-permute-start | bytes 12296 | tf_op jit(solution)/shard_map/ppermute | solution.py:427
  88.9 1.6 %collective-permute-done.17 = f32[8,128]{1,0:T(8,128)S(1)} collective-permute-done((f32[8,128]{1,0:T(8,128)S(1)}, f32[8,128]{1,0:T(8,128)S(1)}, u32[]{:S(2)}, u32[]{:S(2)}) %collective-permute-start.17) | collective-permute-done | bytes 4128 | tf_op jit(solution)/shard_map/ppermute | solution.py:427
  90.5 2.8 %collective-permute-start.18 = (f32[8,128]{1,0:T(8,128)S(1)}, f32[8,128]{1,0:T(8,128)S(1)}, u32[]{:S(2)}, u32[]{:S(2)}) collective-permute-start(f32[8,128]{1,0:T(8,128)S(1)} %add.119), channel_id=1, source_target_pairs={{0,32},{2,34},{4,36},{6,38},{8,40},{10,42},{12,44},{14,46},{16,48}... | collective-permute-start | bytes 12296 | tf_op jit(solution)/shard_map/ppermute | solution.py:427
  93.3 3.9 %collective-permute-start.19 = (f32[8,128]{1,0:T(8,128)S(1)}, f32[8,128]{1,0:T(8,128)S(1)}, u32[]{:S(2)}, u32[]{:S(2)}) collective-permute-start(f32[8,128]{1,0:T(8,128)S(1)} %add.119), channel_id=1, source_target_pairs={{0,64},{2,66},{4,68},{6,70},{8,72},{10,74},{12,76},{14,78},{16,80}... | collective-permute-start | bytes 12296 | tf_op jit(solution)/shard_map/ppermute | solution.py:427
  97.2 1.6 %collective-permute-done.19 = f32[8,128]{1,0:T(8,128)S(1)} collective-permute-done((f32[8,128]{1,0:T(8,128)S(1)}, f32[8,128]{1,0:T(8,128)S(1)}, u32[]{:S(2)}, u32[]{:S(2)}) %collective-permute-start.19) | collective-permute-done | bytes 4128 | tf_op jit(solution)/shard_map/ppermute | solution.py:427
  98.8 3.2 %collective-permute-done.20 = f32[8,128]{1,0:T(8,128)S(1)} collective-permute-done((f32[8,128]{1,0:T(8,128)S(1)}, f32[8,128]{1,0:T(8,128)S(1)}, u32[]{:S(2)}, u32[]{:S(2)}) %collective-permute-start.20) | collective-permute-done | bytes 4128 | tf_op jit(solution)/shard_map/ppermute | solution.py:427
  (60 shorter events, 9.8 us)
Async XLA Ops:
  2.1 14.8 %collective-permute-start = (f32[2,64,512]{2,1,0:T(8,128)S(1)}, f32[2,64,512]{2,1,0:T(8,128)S(1)}, u32[]{:S(2)}, u32[]{:S(2)}) collective-permute-start(f32[2,64,512]{2,1,0:T(8,128)S(1)} %get-tuple-element.29), channel_id=1, source_target_pairs={{0,2},{2,0},{4,6},{6,4},{8,10},{10,8},{12,14},{14,12},{16,18},{18,... | collective-permute-start | bytes 786440 | tf_op jit(solution)/shard_map/ppermute | solution.py:427
  2.2 14.7 %collective-permute-start.1 = (f32[2,64,512]{2,1,0:T(8,128)S(1)}, f32[2,64,512]{2,1,0:T(8,128)S(1)}, u32[]{:S(2)}, u32[]{:S(2)}) collective-permute-start(f32[2,64,512]{2,1,0:T(8,128)S(1)} %get-tuple-element.30), channel_id=1, source_target_pairs={{2,4},{6,8},{10,12},{14,16},{18,20},{22,24},{26,28},{30,32},{34,36... | collective-permute-start | bytes 786440 | tf_op jit(solution)/shard_map/ppermute | solution.py:437
  3.0 13.9 %copy-start.2 = (bf16[256,1536]{1,0:T(8,128)(2,1)S(1)}, bf16[256,1536]{1,0:T(8,128)(2,1)}, u32[]{:S(2)}) copy-start(bf16[256,1536]{1,0:T(8,128)(2,1)} %constant.47.clone.xt) | copy-start | bytes 2359300
  3.0 13.9 %copy-start.4 = (bf16[2,80,320]{2,1,0:T(8,128)(2,1)S(1)}, bf16[2,80,320]{2,1,0:T(8,128)(2,1)}, u32[]{:S(2)}) copy-start(bf16[2,80,320]{2,1,0:T(8,128)(2,1)} %constant.46.clone.back) | copy-start | bytes 307204
  3.0 13.8 %collective-permute-start.2 = (f32[32,2,512]{2,1,0:T(2,128)S(1)}, f32[32,2,512]{2,1,0:T(2,128)S(1)}, u32[]{:S(2)}, u32[]{:S(2)}) collective-permute-start(f32[32,2,512]{2,1,0:T(2,128)S(1)} %get-tuple-element.31), channel_id=1, source_target_pairs={{0,1},{1,0},{2,3},{3,2},{4,5},{5,4},{6,7},{7,6},{8,9},{9,8},{10,11... | collective-permute-start | bytes 393224 | tf_op jit(solution)/shard_map/ppermute | solution.py:422
  16.9 18.0 %copy-start.1 = (bf16[2,2048,192]{2,1,0:T(8,128)(2,1)S(1)}, bf16[2,2048,192]{2,1,0:T(8,128)(2,1)}, u32[]{:S(2)}) copy-start(bf16[2,2048,192]{2,1,0:T(8,128)(2,1)} %constant.45.clone.front) | copy-start | bytes 4718596
  18.3 5.4 %collective-permute-start.3 = (f32[40,128]{1,0:T(8,128)S(1)}, f32[40,128]{1,0:T(8,128)S(1)}, u32[]{:S(2)}, u32[]{:S(2)}) collective-permute-start(f32[40,128]{1,0:T(8,128)S(1)} %get-tuple-element.36), channel_id=1, source_target_pairs={{0,1},{1,0},{2,3},{3,2},{4,5},{5,4},{6,7},{7,6},{8,9},{9,8},{10,11... | collective-permute-start | bytes 61448 | tf_op jit(solution)/shard_map/ppermute | solution.py:422
  23.7 2.5 %collective-permute-start.4 = (f32[40,128]{1,0:T(8,128)S(1)}, f32[40,128]{1,0:T(8,128)S(1)}, u32[]{:S(2)}, u32[]{:S(2)}) collective-permute-start(f32[40,128]{1,0:T(8,128)S(1)} %add.105), channel_id=1, source_target_pairs={{0,2},{2,0},{4,6},{6,4},{8,10},{10,8},{12,14},{14,12},{16,18},{18,... | collective-permute-start | bytes 61448 | tf_op jit(solution)/shard_map/ppermute | solution.py:427
  26.1 8.8 %collective-permute-start.5 = (f32[24,128]{1,0:T(8,128)S(1)}, f32[24,128]{1,0:T(8,128)S(1)}, u32[]{:S(2)}, u32[]{:S(2)}) collective-permute-start(f32[24,128]{1,0:T(8,128)S(1)} %fusion.18), channel_id=1, source_target_pairs={{2,4},{6,8},{10,12},{14,16},{18,20},{22,24},{26,28},{30,32},{34,36... | collective-permute-start | bytes 36872 | tf_op jit(solution)/shard_map/ppermute | solution.py:437
  26.8 8.1 %collective-permute-start.6 = (f32[8,128]{1,0:T(8,128)S(1)}, f32[8,128]{1,0:T(8,128)S(1)}, u32[]{:S(2)}, u32[]{:S(2)}) collective-permute-start(f32[8,128]{1,0:T(8,128)S(1)} %fusion.32), channel_id=1, source_target_pairs={{0,6},{4,10},{8,14},{12,18},{16,22},{20,26},{24,30},{28,34},{32,38... | collective-permute-start | bytes 12296 | tf_op jit(solution)/shard_map/ppermute | solution.py:443
  42.4 5.4 %collective-permute-start.7 = (f32[48,128]{1,0:T(8,128)S(1)}, f32[48,128]{1,0:T(8,128)S(1)}, u32[]{:S(2)}, u32[]{:S(2)}) collective-permute-start(f32[48,128]{1,0:T(8,128)S(1)} %hessian.2), channel_id=1, source_target_pairs={{0,1},{1,0},{2,3},{3,2},{4,5},{5,4},{6,7},{7,6},{8,9},{9,8},{10,11... | collective-permute-start | bytes 73736 | tf_op jit(solution)/shard_map/ppermute | solution.py:422
  47.8 1.2 %collective-permute-start.8 = (f32[40,128]{1,0:T(8,128)S(1)}, f32[40,128]{1,0:T(8,128)S(1)}, u32[]{:S(2)}, u32[]{:S(2)}) collective-permute-start(f32[40,128]{1,0:T(8,128)S(1)} %slice_add_fusion), channel_id=1, source_target_pairs={{0,2},{2,0},{4,6},{6,4},{8,10},{10,8},{12,14},{14,12},{16,18},{18,... | collective-permute-start | bytes 61448 | tf_op jit(solution)/shard_map/ppermute | solution.py:427
  49.0 9.1 %collective-permute-start.9 = (f32[24,128]{1,0:T(8,128)S(1)}, f32[24,128]{1,0:T(8,128)S(1)}, u32[]{:S(2)}, u32[]{:S(2)}) collective-permute-start(f32[24,128]{1,0:T(8,128)S(1)} %fusion.21), channel_id=1, source_target_pairs={{2,4},{6,8},{10,12},{14,16},{18,20},{22,24},{26,28},{30,32},{34,36... | collective-permute-start | bytes 36872 | tf_op jit(solution)/shard_map/ppermute | solution.py:437
  49.7 8.4 %collective-permute-start.10 = (f32[8,128]{1,0:T(8,128)S(1)}, f32[8,128]{1,0:T(8,128)S(1)}, u32[]{:S(2)}, u32[]{:S(2)}) collective-permute-start(f32[8,128]{1,0:T(8,128)S(1)} %fusion.35), channel_id=1, source_target_pairs={{0,6},{4,10},{8,14},{12,18},{16,22},{20,26},{24,30},{28,34},{32,38... | collective-permute-start | bytes 12296 | tf_op jit(solution)/shard_map/ppermute | solution.py:443
  65.6 5.4 %collective-permute-start.11 = (f32[48,128]{1,0:T(8,128)S(1)}, f32[48,128]{1,0:T(8,128)S(1)}, u32[]{:S(2)}, u32[]{:S(2)}) collective-permute-start(f32[48,128]{1,0:T(8,128)S(1)} %hessian.3), channel_id=1, source_target_pairs={{0,1},{1,0},{2,3},{3,2},{4,5},{5,4},{6,7},{7,6},{8,9},{9,8},{10,11... | collective-permute-start | bytes 73736 | tf_op jit(solution)/shard_map/ppermute | solution.py:422
  71.0 1.2 %collective-permute-start.12 = (f32[48,128]{1,0:T(8,128)S(1)}, f32[48,128]{1,0:T(8,128)S(1)}, u32[]{:S(2)}, u32[]{:S(2)}) collective-permute-start(f32[48,128]{1,0:T(8,128)S(1)} %add.113), channel_id=1, source_target_pairs={{0,2},{2,0},{4,6},{6,4},{8,10},{10,8},{12,14},{14,12},{16,18},{18,... | collective-permute-start | bytes 73736 | tf_op jit(solution)/shard_map/ppermute | solution.py:427
  72.2 6.6 %collective-permute-start.13 = (f32[8,128]{1,0:T(8,128)S(1)}, f32[8,128]{1,0:T(8,128)S(1)}, u32[]{:S(2)}, u32[]{:S(2)}) collective-permute-start(f32[8,128]{1,0:T(8,128)S(1)} %slice_add_fusion.1), channel_id=1, source_target_pairs={{0,4},{2,6},{4,0},{6,2},{8,12},{10,14},{12,8},{14,10},{16,20},{18,... | collective-permute-start | bytes 12296 | tf_op jit(solution)/shard_map/ppermute | solution.py:427
  73.9 5.9 %collective-permute-start.14 = (f32[8,128]{1,0:T(8,128)S(1)}, f32[8,128]{1,0:T(8,128)S(1)}, u32[]{:S(2)}, u32[]{:S(2)}) collective-permute-start(f32[8,128]{1,0:T(8,128)S(1)} %slice_add_fusion.1), channel_id=1, source_target_pairs={{0,8},{2,10},{4,12},{6,14},{8,0},{10,2},{12,4},{14,6},{16,24},{18,... | collective-permute-start | bytes 12296 | tf_op jit(solution)/shard_map/ppermute | solution.py:427
  78.2 4.8 %collective-permute-start.15 = (f32[8,128]{1,0:T(8,128)S(1)}, f32[8,128]{1,0:T(8,128)S(1)}, u32[]{:S(2)}, u32[]{:S(2)}) collective-permute-start(f32[8,128]{1,0:T(8,128)S(1)} %slice_add_fusion.1), channel_id=1, source_target_pairs={{0,12},{2,14},{4,8},{6,10},{8,4},{10,6},{12,0},{14,2},{16,28},{18,... | collective-permute-start | bytes 12296 | tf_op jit(solution)/shard_map/ppermute | solution.py:427
  78.2 4.8 %collective-permute-start.16 = (f32[24,128]{1,0:T(8,128)S(1)}, f32[24,128]{1,0:T(8,128)S(1)}, u32[]{:S(2)}, u32[]{:S(2)}) collective-permute-start(f32[24,128]{1,0:T(8,128)S(1)} %fusion.15), channel_id=1, source_target_pairs={{2,4},{6,8},{10,12},{14,16},{18,20},{22,24},{26,28},{30,32},{34,36... | collective-permute-start | bytes 36872 | tf_op jit(solution)/shard_map/ppermute | solution.py:437
  83.0 7.5 %collective-permute-start.17 = (f32[8,128]{1,0:T(8,128)S(1)}, f32[8,128]{1,0:T(8,128)S(1)}, u32[]{:S(2)}, u32[]{:S(2)}) collective-permute-start(f32[8,128]{1,0:T(8,128)S(1)} %add_add_fusion.1), channel_id=1, source_target_pairs={{0,16},{2,18},{4,20},{6,22},{8,24},{10,26},{12,28},{14,30},{16,0},... | collective-permute-start | bytes 12296 | tf_op jit(solution)/shard_map/ppermute | solution.py:427
  90.5 6.7 %collective-permute-start.18 = (f32[8,128]{1,0:T(8,128)S(1)}, f32[8,128]{1,0:T(8,128)S(1)}, u32[]{:S(2)}, u32[]{:S(2)}) collective-permute-start(f32[8,128]{1,0:T(8,128)S(1)} %add.119), channel_id=1, source_target_pairs={{0,32},{2,34},{4,36},{6,38},{8,40},{10,42},{12,44},{14,46},{16,48}... | collective-permute-start | bytes 12296 | tf_op jit(solution)/shard_map/ppermute | solution.py:427
  93.3 5.5 %collective-permute-start.19 = (f32[8,128]{1,0:T(8,128)S(1)}, f32[8,128]{1,0:T(8,128)S(1)}, u32[]{:S(2)}, u32[]{:S(2)}) collective-permute-start(f32[8,128]{1,0:T(8,128)S(1)} %add.119), channel_id=1, source_target_pairs={{0,64},{2,66},{4,68},{6,70},{8,72},{10,74},{12,76},{14,78},{16,80}... | collective-permute-start | bytes 12296 | tf_op jit(solution)/shard_map/ppermute | solution.py:427
  97.2 4.8 %collective-permute-start.20 = (f32[8,128]{1,0:T(8,128)S(1)}, f32[8,128]{1,0:T(8,128)S(1)}, u32[]{:S(2)}, u32[]{:S(2)}) collective-permute-start(f32[8,128]{1,0:T(8,128)S(1)} %add.119), channel_id=1, source_target_pairs={{0,96},{2,98},{4,100},{6,102},{8,104},{10,106},{12,108},{14,110},{... | collective-permute-start | bytes 12296 | tf_op jit(solution)/shard_map/ppermute | solution.py:427
  (2 other events, 8.4 us)

commit v11 on v10

--- a/solution.py
+++ b/solution.py
@@ -165,7 +165,7 @@
 
     plane(0, (1, 2))
     plane(1, (-1, 1, 2))
-    lax.fori_loop(2, NZ - 2, body, 0, unroll=2)
+    lax.fori_loop(2, NZ - 2, body, 0, unroll=4)
     plane(NZ - 2, (-2, -1, 1))
     plane(NZ - 1, (-2, -1))
 
@@ -234,9 +234,8 @@
 def hessian_kernel(half, ctl, base, grad, front, back, xt, out, spread, field, planes):
     high, low = halves_of(ctl[...])
     first, second = xt[:128], xt[128:]
-    value = jnp.dot(high, first, preferred_element_type=F32)
-    value += jnp.dot(low, first, preferred_element_type=F32)
-    value += jnp.dot(high, second, preferred_element_type=F32)
+    value = jnp.dot(jnp.concatenate([high, low], 0), first, preferred_element_type=F32)
+    value = value[:CTL] + (value[CTL:] + jnp.dot(high, second, preferred_element_type=F32))
     value = jnp.concatenate([value, jnp.zeros((KPAD - CTL, 3 * NX), F32)], 0)
     high, low = halves_of(value)
     for j, part in enumerate((high, high, low, low)):

time: 103 us -> 103 us (level)
  no operation moved by 1% of the time
where the time goes in v11:
time: 103 us
  starting transfers between devices  45.2 us (44%)
  Pallas kernels  28.7 us (28%)
  waiting for transfers between devices  27.5 us (27%)
    ppermute x11, starting transfers between devices, paired(): return lax.ppermute(value, 'gz', [(i, i ^ mask) for i in range(count)])  20.3 us
    pallas_call x2, Pallas kernels, hessian_pass(): pl.pallas_call(hessian_kernel, in_specs=[SMEM_SPEC] + [VMEM_SPEC] * 6, ou...  14.9 us
    ppermute x2, starting transfers between devices, far_paired(): return lax.ppermute(value, 'gz', pairs + [(j, i) for i, j in pairs])  14.1 us
    ppermute x11, waiting for transfers between devices, paired(): return lax.ppermute(value, 'gz', [(i, i ^ mask) for i in range(count)])  13.7 us
    ppermute x4, waiting for transfers between devices, swapped(): return lax.ppermute(value, 'gy', [(0, 1), (1, 0)])  11.3 us
    pallas_call x1, Pallas kernels, interior_pass(): pl.pallas_call(interior_kernel, in_specs=[SMEM_SPEC] + [VMEM_SPEC] * 2, o...  10.4 us
    ppermute x4, starting transfers between devices, swapped(): return lax.ppermute(value, 'gy', [(0, 1), (1, 0)])  8.06 us
    ppermute x4, starting transfers between devices, outer_paired(): return lax.ppermute(value, 'gz', pairs + [(j, i) for i, j in pairs])  2.79 us
  transfers between devices with their start and end apart: 21, of which 13 were waited for; matrix products, arithmetic and copies ran while one was open for 0% of the time, Pallas kernels for 10%

profile of v11, /device:TPU:0, one launch (start us, length us, event | category | flops | bytes accessed | tf_op | source)
XLA Modules:
  0.0 102.5 jit_solution(3654839857016873533)
XLA Ops:
  0.7 1.3 %rims.1 = (f32[2,64,512]{2,1,0:T(8,128)S(1)}, f32[2,64,512]{2,1,0:T(8,128)S(1)}, f32[32,2,512]{2,1,0:T(2,128)S(1)}) custom-call(s32[1]{0:T(128)} %bitcast.half, s32[1]{0:T(128)} %bitcast.1.parity, f32[32,64,512]{2,1,0:T(8,128)} %moving.1), custom_call_target="tpu_custom_call" | custom-call | tf_op jit(solution)/shard_map/rims/pallas_call | solution.py:373
  3.0 3.2 %collective-permute-start.2 = (f32[32,2,512]{2,1,0:T(2,128)S(1)}, f32[32,2,512]{2,1,0:T(2,128)S(1)}, u32[]{:S(2)}, u32[]{:S(2)}) collective-permute-start(f32[32,2,512]{2,1,0:T(2,128)S(1)} %get-tuple-element.31), channel_id=1, source_target_pairs={{0,1},{1,0},{2,3},{3,2},{4,5},{5,4},{6,7},{7,6},{8,9},{9,8},{10,11... | collective-permute-start | bytes 393224 | tf_op jit(solution)/shard_map/ppermute | solution.py:421
  6.2 10.4 %interior.1 = (f32[3,32,64,512]{3,2,1,0:T(8,128)S(1)}, f32[5,64,1536]{2,1,0:T(8,128)S(1)}, f32[4,64,512]{2,1,0:T(8,128)S(1)}, f32[32,8,512]{2,1,0:T(8,128)S(1)}) custom-call(s32[1]{0:T(128)} %bitcast.half, f32[32,64,512]{2,1,0:T(8,128)S(1)} %copy-done, f32[32,64,512]{2,1,0:T(8,128)S(1)} %copy-done.3), custom_call_target="tpu_custom_call" | custom-call | flops 100000000 | bytes 40000000 | tf_op jit(solution)/shard_map/interior/pallas_call | solution.py:306
  16.8 1.3 %edge.1 = (f32[3,32,64,512]{3,2,1,0:T(8,128)S(1)}, f32[5,64,1536]{2,1,0:T(8,128)S(1)}, f32[40,128]{1,0:T(8,128)S(1)}) custom-call(s32[1]{0:T(128)} %bitcast.half, s32[1]{0:T(128)} %bitcast.1.parity, f32[2,64,512]{2,1,0:T(8,128)S(1)} %collective-permute-done.inner, ...), custom_call_target="tpu_custom_call", output_to_operand_aliasing={{0}: (9, {}), {1}: (10, {})} | custom-call | tf_op jit(solution)/shard_map/edge/pallas_call | solution.py:323
  18.1 2.5 %collective-permute-start.3 = (f32[40,128]{1,0:T(8,128)S(1)}, f32[40,128]{1,0:T(8,128)S(1)}, u32[]{:S(2)}, u32[]{:S(2)}) collective-permute-start(f32[40,128]{1,0:T(8,128)S(1)} %get-tuple-element.36), channel_id=1, source_target_pairs={{0,1},{1,0},{2,3},{3,2},{4,5},{5,4},{6,7},{7,6},{8,9},{9,8},{10,11... | collective-permute-start | bytes 61448 | tf_op jit(solution)/shard_map/ppermute | solution.py:421
  20.6 2.9 %collective-permute-done.3 = f32[40,128]{1,0:T(8,128)S(1)} collective-permute-done((f32[40,128]{1,0:T(8,128)S(1)}, f32[40,128]{1,0:T(8,128)S(1)}, u32[]{:S(2)}, u32[]{:S(2)}) %collective-permute-start.3) | collective-permute-done | bytes 20512 | tf_op jit(solution)/shard_map/ppermute | solution.py:421
  23.5 1.6 %collective-permute-start.4 = (f32[40,128]{1,0:T(8,128)S(1)}, f32[40,128]{1,0:T(8,128)S(1)}, u32[]{:S(2)}, u32[]{:S(2)}) collective-permute-start(f32[40,128]{1,0:T(8,128)S(1)} %add.105), channel_id=1, source_target_pairs={{0,2},{2,0},{4,6},{6,4},{8,10},{10,8},{12,14},{14,12},{16,18},{18,... | collective-permute-start | bytes 61448 | tf_op jit(solution)/shard_map/ppermute | solution.py:426
  26.6 6.8 %collective-permute-start.6 = (f32[8,128]{1,0:T(8,128)S(1)}, f32[8,128]{1,0:T(8,128)S(1)}, u32[]{:S(2)}, u32[]{:S(2)}) collective-permute-start(f32[8,128]{1,0:T(8,128)S(1)} %fusion.32), channel_id=1, source_target_pairs={{0,6},{4,10},{8,14},{12,18},{16,22},{20,26},{24,30},{28,34},{32,38... | collective-permute-start | bytes 12296 | tf_op jit(solution)/shard_map/ppermute | solution.py:442
  33.4 1.3 %collective-permute-done.6 = f32[8,128]{1,0:T(8,128)S(1)} collective-permute-done((f32[8,128]{1,0:T(8,128)S(1)}, f32[8,128]{1,0:T(8,128)S(1)}, u32[]{:S(2)}, u32[]{:S(2)}) %collective-permute-start.6) | collective-permute-done | bytes 4128 | tf_op jit(solution)/shard_map/ppermute | solution.py:442
  34.8 7.4 %hessian.2 = f32[48,128]{1,0:T(8,128)S(1)} custom-call(s32[1]{0:T(128)} %bitcast.half, f32[40,128]{1,0:T(8,128)S(1)} %fusion.3.ctl, f32[16,128]{1,0:T(8,128)S(1)} %slice.126.base, f32[3,32,64,512]{3,2,1,0:T(8,128)S(1)} %get-tuple-element.37.grad, bf16[2,2048,192]{2,1,0:T(8,128)(2,1)S(1)} %copy-done.1, bf16[2,80,320]{2,1,0:T(8,128)(2,1)S(1)} %copy-done.4, ...), custom_call_target="tpu_custom_call" | custom-call | tf_op jit(solution)/shard_map/hessian/pallas_call | solution.py:336
  42.8 4.8 %collective-permute-done.7 = f32[48,128]{1,0:T(8,128)S(1)} collective-permute-done((f32[48,128]{1,0:T(8,128)S(1)}, f32[48,128]{1,0:T(8,128)S(1)}, u32[]{:S(2)}, u32[]{:S(2)}) %collective-permute-start.7) | collective-permute-done | bytes 24608 | tf_op jit(solution)/shard_map/ppermute | solution.py:421
  49.5 7.3 %collective-permute-start.10 = (f32[8,128]{1,0:T(8,128)S(1)}, f32[8,128]{1,0:T(8,128)S(1)}, u32[]{:S(2)}, u32[]{:S(2)}) collective-permute-start(f32[8,128]{1,0:T(8,128)S(1)} %fusion.35), channel_id=1, source_target_pairs={{0,6},{4,10},{8,14},{12,18},{16,22},{20,26},{24,30},{28,34},{32,38... | collective-permute-start | bytes 12296 | tf_op jit(solution)/shard_map/ppermute | solution.py:442
  58.0 7.4 %hessian.3 = f32[48,128]{1,0:T(8,128)S(1)} custom-call(s32[1]{0:T(128)} %bitcast.half, f32[40,128]{1,0:T(8,128)S(1)} %fusion.7.ctl, f32[16,128]{1,0:T(8,128)S(1)} %slice.126.base, f32[3,32,64,512]{3,2,1,0:T(8,128)S(1)} %get-tuple-element.37.grad, bf16[2,2048,192]{2,1,0:T(8,128)(2,1)S(1)} %copy-done.1, bf16[2,80,320]{2,1,0:T(8,128)(2,1)S(1)} %copy-done.4, ...), custom_call_target="tpu_custom_call" | custom-call | tf_op jit(solution)/shard_map/hessian/pallas_call | solution.py:336
  65.4 1.8 %collective-permute-start.11 = (f32[48,128]{1,0:T(8,128)S(1)}, f32[48,128]{1,0:T(8,128)S(1)}, u32[]{:S(2)}, u32[]{:S(2)}) collective-permute-start(f32[48,128]{1,0:T(8,128)S(1)} %hessian.3), channel_id=1, source_target_pairs={{0,1},{1,0},{2,3},{3,2},{4,5},{5,4},{6,7},{7,6},{8,9},{9,8},{10,11... | collective-permute-start | bytes 73736 | tf_op jit(solution)/shard_map/ppermute | solution.py:421
  67.2 3.6 %collective-permute-done.11 = f32[48,128]{1,0:T(8,128)S(1)} collective-permute-done((f32[48,128]{1,0:T(8,128)S(1)}, f32[48,128]{1,0:T(8,128)S(1)}, u32[]{:S(2)}, u32[]{:S(2)}) %collective-permute-start.11) | collective-permute-done | bytes 24608 | tf_op jit(solution)/shard_map/ppermute | solution.py:421
  72.0 1.7 %collective-permute-start.13 = (f32[8,128]{1,0:T(8,128)S(1)}, f32[8,128]{1,0:T(8,128)S(1)}, u32[]{:S(2)}, u32[]{:S(2)}) collective-permute-start(f32[8,128]{1,0:T(8,128)S(1)} %slice_add_fusion.1), channel_id=1, source_target_pairs={{0,4},{2,6},{4,0},{6,2},{8,12},{10,14},{12,8},{14,10},{16,20},{18,... | collective-permute-start | bytes 12296 | tf_op jit(solution)/shard_map/ppermute | solution.py:426
  73.7 4.3 %collective-permute-start.14 = (f32[8,128]{1,0:T(8,128)S(1)}, f32[8,128]{1,0:T(8,128)S(1)}, u32[]{:S(2)}, u32[]{:S(2)}) collective-permute-start(f32[8,128]{1,0:T(8,128)S(1)} %slice_add_fusion.1), channel_id=1, source_target_pairs={{0,8},{2,10},{4,12},{6,14},{8,0},{10,2},{12,4},{14,6},{16,24},{18,... | collective-permute-start | bytes 12296 | tf_op jit(solution)/shard_map/ppermute | solution.py:426
  79.6 3.2 %collective-permute-done.15 = f32[8,128]{1,0:T(8,128)S(1)} collective-permute-done((f32[8,128]{1,0:T(8,128)S(1)}, f32[8,128]{1,0:T(8,128)S(1)}, u32[]{:S(2)}, u32[]{:S(2)}) %collective-permute-start.15) | collective-permute-done | bytes 4128 | tf_op jit(solution)/shard_map/ppermute | solution.py:426
  82.8 5.9 %collective-permute-start.17 = (f32[8,128]{1,0:T(8,128)S(1)}, f32[8,128]{1,0:T(8,128)S(1)}, u32[]{:S(2)}, u32[]{:S(2)}) collective-permute-start(f32[8,128]{1,0:T(8,128)S(1)} %add_add_fusion.1), channel_id=1, source_target_pairs={{0,16},{2,18},{4,20},{6,22},{8,24},{10,26},{12,28},{14,30},{16,0},... | collective-permute-start | bytes 12296 | tf_op jit(solution)/shard_map/ppermute | solution.py:426
  88.7 1.6 %collective-permute-done.17 = f32[8,128]{1,0:T(8,128)S(1)} collective-permute-done((f32[8,128]{1,0:T(8,128)S(1)}, f32[8,128]{1,0:T(8,128)S(1)}, u32[]{:S(2)}, u32[]{:S(2)}) %collective-permute-start.17) | collective-permute-done | bytes 4128 | tf_op jit(solution)/shard_map/ppermute | solution.py:426
  90.3 2.8 %collective-permute-start.18 = (f32[8,128]{1,0:T(8,128)S(1)}, f32[8,128]{1,0:T(8,128)S(1)}, u32[]{:S(2)}, u32[]{:S(2)}) collective-permute-start(f32[8,128]{1,0:T(8,128)S(1)} %add.119), channel_id=1, source_target_pairs={{0,32},{2,34},{4,36},{6,38},{8,40},{10,42},{12,44},{14,46},{16,48}... | collective-permute-start | bytes 12296 | tf_op jit(solution)/shard_map/ppermute | solution.py:426
  93.1 3.9 %collective-permute-start.19 = (f32[8,128]{1,0:T(8,128)S(1)}, f32[8,128]{1,0:T(8,128)S(1)}, u32[]{:S(2)}, u32[]{:S(2)}) collective-permute-start(f32[8,128]{1,0:T(8,128)S(1)} %add.119), channel_id=1, source_target_pairs={{0,64},{2,66},{4,68},{6,70},{8,72},{10,74},{12,76},{14,78},{16,80}... | collective-permute-start | bytes 12296 | tf_op jit(solution)/shard_map/ppermute | solution.py:426
  97.0 1.6 %collective-permute-done.19 = f32[8,128]{1,0:T(8,128)S(1)} collective-permute-done((f32[8,128]{1,0:T(8,128)S(1)}, f32[8,128]{1,0:T(8,128)S(1)}, u32[]{:S(2)}, u32[]{:S(2)}) %collective-permute-start.19) | collective-permute-done | bytes 4128 | tf_op jit(solution)/shard_map/ppermute | solution.py:426
  98.6 3.2 %collective-permute-done.20 = f32[8,128]{1,0:T(8,128)S(1)} collective-permute-done((f32[8,128]{1,0:T(8,128)S(1)}, f32[8,128]{1,0:T(8,128)S(1)}, u32[]{:S(2)}, u32[]{:S(2)}) %collective-permute-start.20) | collective-permute-done | bytes 4128 | tf_op jit(solution)/shard_map/ppermute | solution.py:426
  (60 shorter events, 9.8 us)
Async XLA Ops:
  2.1 14.6 %collective-permute-start = (f32[2,64,512]{2,1,0:T(8,128)S(1)}, f32[2,64,512]{2,1,0:T(8,128)S(1)}, u32[]{:S(2)}, u32[]{:S(2)}) collective-permute-start(f32[2,64,512]{2,1,0:T(8,128)S(1)} %get-tuple-element.29), channel_id=1, source_target_pairs={{0,2},{2,0},{4,6},{6,4},{8,10},{10,8},{12,14},{14,12},{16,18},{18,... | collective-permute-start | bytes 786440 | tf_op jit(solution)/shard_map/ppermute | solution.py:426
  2.2 14.5 %collective-permute-start.1 = (f32[2,64,512]{2,1,0:T(8,128)S(1)}, f32[2,64,512]{2,1,0:T(8,128)S(1)}, u32[]{:S(2)}, u32[]{:S(2)}) collective-permute-start(f32[2,64,512]{2,1,0:T(8,128)S(1)} %get-tuple-element.30), channel_id=1, source_target_pairs={{2,4},{6,8},{10,12},{14,16},{18,20},{22,24},{26,28},{30,32},{34,36... | collective-permute-start | bytes 786440 | tf_op jit(solution)/shard_map/ppermute | solution.py:436
  3.0 13.7 %copy-start.2 = (bf16[256,1536]{1,0:T(8,128)(2,1)S(1)}, bf16[256,1536]{1,0:T(8,128)(2,1)}, u32[]{:S(2)}) copy-start(bf16[256,1536]{1,0:T(8,128)(2,1)} %constant.47.clone.xt) | copy-start | bytes 2359300
  3.0 13.7 %copy-start.4 = (bf16[2,80,320]{2,1,0:T(8,128)(2,1)S(1)}, bf16[2,80,320]{2,1,0:T(8,128)(2,1)}, u32[]{:S(2)}) copy-start(bf16[2,80,320]{2,1,0:T(8,128)(2,1)} %constant.46.clone.back) | copy-start | bytes 307204
  3.0 13.6 %collective-permute-start.2 = (f32[32,2,512]{2,1,0:T(2,128)S(1)}, f32[32,2,512]{2,1,0:T(2,128)S(1)}, u32[]{:S(2)}, u32[]{:S(2)}) collective-permute-start(f32[32,2,512]{2,1,0:T(2,128)S(1)} %get-tuple-element.31), channel_id=1, source_target_pairs={{0,1},{1,0},{2,3},{3,2},{4,5},{5,4},{6,7},{7,6},{8,9},{9,8},{10,11... | collective-permute-start | bytes 393224 | tf_op jit(solution)/shard_map/ppermute | solution.py:421
  16.7 18.0 %copy-start.1 = (bf16[2,2048,192]{2,1,0:T(8,128)(2,1)S(1)}, bf16[2,2048,192]{2,1,0:T(8,128)(2,1)}, u32[]{:S(2)}) copy-start(bf16[2,2048,192]{2,1,0:T(8,128)(2,1)} %constant.45.clone.front) | copy-start | bytes 4718596
  18.1 5.4 %collective-permute-start.3 = (f32[40,128]{1,0:T(8,128)S(1)}, f32[40,128]{1,0:T(8,128)S(1)}, u32[]{:S(2)}, u32[]{:S(2)}) collective-permute-start(f32[40,128]{1,0:T(8,128)S(1)} %get-tuple-element.36), channel_id=1, source_target_pairs={{0,1},{1,0},{2,3},{3,2},{4,5},{5,4},{6,7},{7,6},{8,9},{9,8},{10,11... | collective-permute-start | bytes 61448 | tf_op jit(solution)/shard_map/ppermute | solution.py:421
  23.5 2.5 %collective-permute-start.4 = (f32[40,128]{1,0:T(8,128)S(1)}, f32[40,128]{1,0:T(8,128)S(1)}, u32[]{:S(2)}, u32[]{:S(2)}) collective-permute-start(f32[40,128]{1,0:T(8,128)S(1)} %add.105), channel_id=1, source_target_pairs={{0,2},{2,0},{4,6},{6,4},{8,10},{10,8},{12,14},{14,12},{16,18},{18,... | collective-permute-start | bytes 61448 | tf_op jit(solution)/shard_map/ppermute | solution.py:426
  26.0 8.8 %collective-permute-start.5 = (f32[24,128]{1,0:T(8,128)S(1)}, f32[24,128]{1,0:T(8,128)S(1)}, u32[]{:S(2)}, u32[]{:S(2)}) collective-permute-start(f32[24,128]{1,0:T(8,128)S(1)} %fusion.18), channel_id=1, source_target_pairs={{2,4},{6,8},{10,12},{14,16},{18,20},{22,24},{26,28},{30,32},{34,36... | collective-permute-start | bytes 36872 | tf_op jit(solution)/shard_map/ppermute | solution.py:436
  26.6 8.1 %collective-permute-start.6 = (f32[8,128]{1,0:T(8,128)S(1)}, f32[8,128]{1,0:T(8,128)S(1)}, u32[]{:S(2)}, u32[]{:S(2)}) collective-permute-start(f32[8,128]{1,0:T(8,128)S(1)} %fusion.32), channel_id=1, source_target_pairs={{0,6},{4,10},{8,14},{12,18},{16,22},{20,26},{24,30},{28,34},{32,38... | collective-permute-start | bytes 12296 | tf_op jit(solution)/shard_map/ppermute | solution.py:442
  42.2 5.4 %collective-permute-start.7 = (f32[48,128]{1,0:T(8,128)S(1)}, f32[48,128]{1,0:T(8,128)S(1)}, u32[]{:S(2)}, u32[]{:S(2)}) collective-permute-start(f32[48,128]{1,0:T(8,128)S(1)} %hessian.2), channel_id=1, source_target_pairs={{0,1},{1,0},{2,3},{3,2},{4,5},{5,4},{6,7},{7,6},{8,9},{9,8},{10,11... | collective-permute-start | bytes 73736 | tf_op jit(solution)/shard_map/ppermute | solution.py:421
  47.6 1.2 %collective-permute-start.8 = (f32[40,128]{1,0:T(8,128)S(1)}, f32[40,128]{1,0:T(8,128)S(1)}, u32[]{:S(2)}, u32[]{:S(2)}) collective-permute-start(f32[40,128]{1,0:T(8,128)S(1)} %slice_add_fusion), channel_id=1, source_target_pairs={{0,2},{2,0},{4,6},{6,4},{8,10},{10,8},{12,14},{14,12},{16,18},{18,... | collective-permute-start | bytes 61448 | tf_op jit(solution)/shard_map/ppermute | solution.py:426
  48.8 9.1 %collective-permute-start.9 = (f32[24,128]{1,0:T(8,128)S(1)}, f32[24,128]{1,0:T(8,128)S(1)}, u32[]{:S(2)}, u32[]{:S(2)}) collective-permute-start(f32[24,128]{1,0:T(8,128)S(1)} %fusion.21), channel_id=1, source_target_pairs={{2,4},{6,8},{10,12},{14,16},{18,20},{22,24},{26,28},{30,32},{34,36... | collective-permute-start | bytes 36872 | tf_op jit(solution)/shard_map/ppermute | solution.py:436
  49.5 8.4 %collective-permute-start.10 = (f32[8,128]{1,0:T(8,128)S(1)}, f32[8,128]{1,0:T(8,128)S(1)}, u32[]{:S(2)}, u32[]{:S(2)}) collective-permute-start(f32[8,128]{1,0:T(8,128)S(1)} %fusion.35), channel_id=1, source_target_pairs={{0,6},{4,10},{8,14},{12,18},{16,22},{20,26},{24,30},{28,34},{32,38... | collective-permute-start | bytes 12296 | tf_op jit(solution)/shard_map/ppermute | solution.py:442
  65.4 5.4 %collective-permute-start.11 = (f32[48,128]{1,0:T(8,128)S(1)}, f32[48,128]{1,0:T(8,128)S(1)}, u32[]{:S(2)}, u32[]{:S(2)}) collective-permute-start(f32[48,128]{1,0:T(8,128)S(1)} %hessian.3), channel_id=1, source_target_pairs={{0,1},{1,0},{2,3},{3,2},{4,5},{5,4},{6,7},{7,6},{8,9},{9,8},{10,11... | collective-permute-start | bytes 73736 | tf_op jit(solution)/shard_map/ppermute | solution.py:421
  70.8 1.2 %collective-permute-start.12 = (f32[48,128]{1,0:T(8,128)S(1)}, f32[48,128]{1,0:T(8,128)S(1)}, u32[]{:S(2)}, u32[]{:S(2)}) collective-permute-start(f32[48,128]{1,0:T(8,128)S(1)} %add.113), channel_id=1, source_target_pairs={{0,2},{2,0},{4,6},{6,4},{8,10},{10,8},{12,14},{14,12},{16,18},{18,... | collective-permute-start | bytes 73736 | tf_op jit(solution)/shard_map/ppermute | solution.py:426
  72.0 6.6 %collective-permute-start.13 = (f32[8,128]{1,0:T(8,128)S(1)}, f32[8,128]{1,0:T(8,128)S(1)}, u32[]{:S(2)}, u32[]{:S(2)}) collective-permute-start(f32[8,128]{1,0:T(8,128)S(1)} %slice_add_fusion.1), channel_id=1, source_target_pairs={{0,4},{2,6},{4,0},{6,2},{8,12},{10,14},{12,8},{14,10},{16,20},{18,... | collective-permute-start | bytes 12296 | tf_op jit(solution)/shard_map/ppermute | solution.py:426
  73.7 5.9 %collective-permute-start.14 = (f32[8,128]{1,0:T(8,128)S(1)}, f32[8,128]{1,0:T(8,128)S(1)}, u32[]{:S(2)}, u32[]{:S(2)}) collective-permute-start(f32[8,128]{1,0:T(8,128)S(1)} %slice_add_fusion.1), channel_id=1, source_target_pairs={{0,8},{2,10},{4,12},{6,14},{8,0},{10,2},{12,4},{14,6},{16,24},{18,... | collective-permute-start | bytes 12296 | tf_op jit(solution)/shard_map/ppermute | solution.py:426
  77.9 4.8 %collective-permute-start.15 = (f32[8,128]{1,0:T(8,128)S(1)}, f32[8,128]{1,0:T(8,128)S(1)}, u32[]{:S(2)}, u32[]{:S(2)}) collective-permute-start(f32[8,128]{1,0:T(8,128)S(1)} %slice_add_fusion.1), channel_id=1, source_target_pairs={{0,12},{2,14},{4,8},{6,10},{8,4},{10,6},{12,0},{14,2},{16,28},{18,... | collective-permute-start | bytes 12296 | tf_op jit(solution)/shard_map/ppermute | solution.py:426
  78.0 4.8 %collective-permute-start.16 = (f32[24,128]{1,0:T(8,128)S(1)}, f32[24,128]{1,0:T(8,128)S(1)}, u32[]{:S(2)}, u32[]{:S(2)}) collective-permute-start(f32[24,128]{1,0:T(8,128)S(1)} %fusion.15), channel_id=1, source_target_pairs={{2,4},{6,8},{10,12},{14,16},{18,20},{22,24},{26,28},{30,32},{34,36... | collective-permute-start | bytes 36872 | tf_op jit(solution)/shard_map/ppermute | solution.py:436
  82.8 7.5 %collective-permute-start.17 = (f32[8,128]{1,0:T(8,128)S(1)}, f32[8,128]{1,0:T(8,128)S(1)}, u32[]{:S(2)}, u32[]{:S(2)}) collective-permute-start(f32[8,128]{1,0:T(8,128)S(1)} %add_add_fusion.1), channel_id=1, source_target_pairs={{0,16},{2,18},{4,20},{6,22},{8,24},{10,26},{12,28},{14,30},{16,0},... | collective-permute-start | bytes 12296 | tf_op jit(solution)/shard_map/ppermute | solution.py:426
  90.3 6.7 %collective-permute-start.18 = (f32[8,128]{1,0:T(8,128)S(1)}, f32[8,128]{1,0:T(8,128)S(1)}, u32[]{:S(2)}, u32[]{:S(2)}) collective-permute-start(f32[8,128]{1,0:T(8,128)S(1)} %add.119), channel_id=1, source_target_pairs={{0,32},{2,34},{4,36},{6,38},{8,40},{10,42},{12,44},{14,46},{16,48}... | collective-permute-start | bytes 12296 | tf_op jit(solution)/shard_map/ppermute | solution.py:426
  93.1 5.5 %collective-permute-start.19 = (f32[8,128]{1,0:T(8,128)S(1)}, f32[8,128]{1,0:T(8,128)S(1)}, u32[]{:S(2)}, u32[]{:S(2)}) collective-permute-start(f32[8,128]{1,0:T(8,128)S(1)} %add.119), channel_id=1, source_target_pairs={{0,64},{2,66},{4,68},{6,70},{8,72},{10,74},{12,76},{14,78},{16,80}... | collective-permute-start | bytes 12296 | tf_op jit(solution)/shard_map/ppermute | solution.py:426
  97.0 4.8 %collective-permute-start.20 = (f32[8,128]{1,0:T(8,128)S(1)}, f32[8,128]{1,0:T(8,128)S(1)}, u32[]{:S(2)}, u32[]{:S(2)}) collective-permute-start(f32[8,128]{1,0:T(8,128)S(1)} %add.119), channel_id=1, source_target_pairs={{0,96},{2,98},{4,100},{6,102},{8,104},{10,106},{12,108},{14,110},{... | collective-permute-start | bytes 12296 | tf_op jit(solution)/shard_map/ppermute | solution.py:426
  (2 other events, 8.4 us)
